TPU v7x, 32 devices: a whole 2x2x4 slice. The times are simulated.
32 devices in a mesh: ctx: 8 (over y, x, core), fsdp: 4 (over z).
Axes of the slice: x: 2, y: 2, z: 4, core: 2. Of those that a mesh axis runs over, the one named last changes fastest.
Arguments:
- inputs: bfloat16 [4, 3072, 1024], P('fsdp', 'ctx'), may hold values from -6 to 6
- cotangent: bfloat16 [4, 3072, 1024], P('fsdp', 'ctx'), may hold values from -6 to 6
- lengths: int32 [4, 6], P('fsdp'), may hold values from 1 to 1536, 2688 in all within a row
- piece_route: int32 [4, 8, 8], P('fsdp', 'ctx'), may hold values from 0 to 7, each once within a row
- gain_one: bfloat16 [1024], P('fsdp'), may hold values from 0.5 to 1.5
- qkv_weight: bfloat16 [1024, 3072], P('fsdp'), may hold values from -0.1875 to 0.1875
- attn_out: bfloat16 [1024, 1024], P('fsdp'), may hold values from -1.5 to 1.5
- gain_two: bfloat16 [1024], P('fsdp'), may hold values from 0.5 to 1.5
- geglu_in: bfloat16 [1024, 5248], P('fsdp'), may hold values from -0.1875 to 0.1875
- geglu_out: bfloat16 [2624, 1024], P('fsdp'), may hold values from -0.15625 to 0.15625
Outputs:
- block_out: bfloat16 [4, 3072, 1024], P('fsdp', 'ctx')
- grad_inputs: bfloat16 [4, 3072, 1024], P('fsdp', 'ctx')
- grad_gain_one: float32 [1024], P('fsdp')
- grad_qkv_weight: float32 [1024, 3072], P('fsdp')
- grad_attn_out: float32 [1024, 1024], P('fsdp')
- grad_gain_two: float32 [1024], P('fsdp')
- grad_geglu_in: float32 [1024, 5248], P('fsdp')
- grad_geglu_out: float32 [2624, 1024], P('fsdp')
- rms_stats: float32 [4, 3], P('fsdp')
Inputs may be any that keep to these rules, and one draw needn't show every extreme that they name: In each pack the 6 lengths sum to 2688 and the largest is 1536. Each row piece_route[b, s, :] names every index of ctx exactly once.
All inputs are finite; a program needn't handle non-finite values.
Results may differ from a plain program's by a relative error of at most 0.02.
Values may be sent and summed in bfloat16 or wider, within the bound.
A program may use at most 192 MiB of HBM per device.

v0:
```python
import functools
import math
import jax
import jax.numpy as jnp
from jax import lax
from jax.experimental import pallas as pl
from jax.experimental.pallas import tpu as pltpu
from jax.sharding import PartitionSpec as P

HEAD_WIDTH = 64
norm_eps = 1e-05
masked_score = -1e30


def head_stack(rows_in, head_count):
    if head_count == 1:
        return rows_in
    lane_head = lax.broadcasted_iota(jnp.int32, rows_in.shape, 1) // HEAD_WIDTH
    zero = jnp.zeros_like(rows_in)
    return jnp.concatenate(
        [jnp.where(lane_head == h, rows_in, zero) for h in range(head_count)], axis=0
    )


def head_pick(stacked_t, head_count, block):
    return jnp.concatenate(
        [
            stacked_t[h * HEAD_WIDTH : (h + 1) * HEAD_WIDTH, h * block : (h + 1) * block]
            for h in range(head_count)
        ],
        axis=0,
    ).T


NT = (((1,), (1,)), ((), ()))


def forward_kernel(
    head_count, block_q, block_k, low_ref, high_ref, begin_ref, end_ref, qkv_ref, out_ref, log_ref, turned_ref
):
    width = out_ref.shape[1]
    step = pl.program_id(0)

    @pl.when(step == 0)
    def prepare():
        turned_ref[...] = qkv_ref[:, 2 * width :].astype(jnp.float32).T.astype(jnp.bfloat16)

    rows = pl.ds(pl.multiple_of(step * block_q, block_q), block_q)
    scale = 1.0 / math.sqrt(HEAD_WIDTH)
    stacked = head_stack(qkv_ref[rows, :width] * jnp.asarray(scale, jnp.bfloat16), head_count)
    begin = jnp.concatenate([begin_ref[:, rows]] * head_count, axis=1)
    end = jnp.concatenate([end_ref[:, rows]] * head_count, axis=1)

    def body(index, carried):
        top, total, acc = carried
        first = pl.multiple_of(index * block_k, block_k)
        keys = qkv_ref[pl.ds(first, block_k), width : 2 * width]
        scores = lax.dot_general(keys, stacked, NT, preferred_element_type=jnp.float32)
        place = first + lax.broadcasted_iota(jnp.int32, scores.shape, 0)
        scores = jnp.where((place >= begin) & (place < end), scores, masked_score)
        new_top = jnp.maximum(top, jnp.max(scores, axis=0, keepdims=True))
        fresh = jnp.exp(scores - new_top)
        fade = jnp.exp(top - new_top)
        total = total * fade + jnp.sum(fresh, axis=0, keepdims=True)
        acc = acc * fade + jnp.dot(
            turned_ref[:, pl.ds(first, block_k)],
            fresh.astype(jnp.bfloat16),
            preferred_element_type=jnp.float32,
        )
        return (new_top, total, acc)

    lanes = head_count * block_q
    top, total, acc = lax.fori_loop(
        low_ref[step],
        high_ref[step],
        body,
        (
            jnp.full((1, lanes), masked_score, jnp.float32),
            jnp.zeros((1, lanes), jnp.float32),
            jnp.zeros((width, lanes), jnp.float32),
        ),
    )
    valid = end > begin
    safe = jnp.where(valid, total, 1.0)
    acc = jnp.where(valid, acc / safe, 0.0)
    log_total = jnp.where(valid, top + jnp.log(safe), 0.0)
    out_ref[...] = head_pick(acc, head_count, block_q)
    log_ref[0] = log_total


def attention_forward(qkv, begin, end, low, high, head_count, block_q, block_k):
    tokens = qkv.shape[0]
    width = head_count * HEAD_WIDTH
    steps = tokens // block_q
    whole = lambda shape: pl.BlockSpec(shape, lambda i, *_: (0,) * len(shape))
    pairs = tokens * tokens // 4 * head_count
    return pl.pallas_call(
        functools.partial(forward_kernel, head_count, block_q, block_k),
        out_shape=(
            jax.ShapeDtypeStruct((tokens, width), jnp.float32),
            jax.ShapeDtypeStruct((steps, 1, head_count * block_q), jnp.float32),
        ),
        grid_spec=pltpu.PrefetchScalarGridSpec(
            num_scalar_prefetch=2,
            grid=(steps,),
            in_specs=[whole((1, tokens)), whole((1, tokens)), whole((tokens, 3 * width))],
            out_specs=(
                pl.BlockSpec((block_q, width), lambda i, *_: (i, 0)),
                pl.BlockSpec((1, 1, head_count * block_q), lambda i, *_: (i, 0, 0)),
            ),
            scratch_shapes=[pltpu.VMEM((width, tokens), jnp.bfloat16)],
        ),
        cost_estimate=pl.CostEstimate(
            flops=pairs * 512, bytes_accessed=tokens * width * 12, transcendentals=pairs
        ),
        name="attention_forward",
    )(low, high, begin, end, qkv)


def turn_back(grads, cosine, sine, head_count):
    half = HEAD_WIDTH // 2
    pieces = []
    for h in range(head_count):
        base = h * HEAD_WIDTH
        pieces += [grads[:, base + half : base + HEAD_WIDTH], grads[:, base : base + half]]
    return grads * cosine + jnp.concatenate(pieces, axis=1) * sine


def backward_kernel(
    head_count,
    block_q,
    block_k,
    low_ref,
    high_ref,
    begin_ref,
    end_ref,
    qkv_ref,
    attended_ref,
    grad_ref,
    log_ref,
    cosine_ref,
    sine_ref,
    out_ref,
    turned_ref,
    key_acc,
    value_acc,
):
    width = attended_ref.shape[1]
    step = pl.program_id(0)

    @pl.when(step == 0)
    def prepare():
        turned_ref[...] = qkv_ref[:, width : 2 * width].astype(jnp.float32).T.astype(jnp.bfloat16)
        key_acc[...] = jnp.zeros_like(key_acc)
        value_acc[...] = jnp.zeros_like(value_acc)

    rows = pl.ds(pl.multiple_of(step * block_q, block_q), block_q)
    scale = 1.0 / math.sqrt(HEAD_WIDTH)
    stacked = head_stack(qkv_ref[rows, :width] * jnp.asarray(scale, jnp.bfloat16), head_count)
    grads = grad_ref[rows, :]
    grad_stacked = head_stack(grads, head_count)
    begin = jnp.concatenate([begin_ref[:, rows]] * head_count, axis=1)
    end = jnp.concatenate([end_ref[:, rows]] * head_count, axis=1)
    product = (grads.astype(jnp.float32) * attended_ref[rows, :]).T
    delta = jnp.concatenate(
        [
            jnp.sum(product[h * HEAD_WIDTH : (h + 1) * HEAD_WIDTH], axis=0, keepdims=True)
            for h in range(head_count)
        ],
        axis=1,
    )
    log_total = log_ref[0]

    def body(index, acc):
        first = pl.multiple_of(index * block_k, block_k)
        span = pl.ds(first, block_k)
        keys = qkv_ref[span, width : 2 * width]
        values = qkv_ref[span, 2 * width :]
        scores = lax.dot_general(keys, stacked, NT, preferred_element_type=jnp.float32)
        grad_probs = lax.dot_general(values, grad_stacked, NT, preferred_element_type=jnp.float32)
        place = first + lax.broadcasted_iota(jnp.int32, scores.shape, 0)
        scores = jnp.where((place >= begin) & (place < end), scores, masked_score)
        probs = jnp.exp(scores - log_total)
        grad_scores = (probs * (grad_probs - delta)).astype(jnp.bfloat16)
        value_acc[span, :] += jnp.dot(
            probs.astype(jnp.bfloat16), grad_stacked, preferred_element_type=jnp.float32
        )
        key_acc[span, :] += jnp.dot(grad_scores, stacked, preferred_element_type=jnp.float32)
        return acc + jnp.dot(
            turned_ref[:, span], grad_scores, preferred_element_type=jnp.float32
        )

    acc = lax.fori_loop(
        low_ref[step],
        high_ref[step],
        body,
        jnp.zeros((width, head_count * block_q), jnp.float32),
    )
    grad_queries = head_pick(acc, head_count, block_q) * scale
    out_ref[rows, :width] = turn_back(
        grad_queries, cosine_ref[rows, :], sine_ref[rows, :], head_count
    ).astype(jnp.bfloat16)

    @pl.when(step == pl.num_programs(0) - 1)
    def finish():
        @pl.loop(0, pl.num_programs(0))
        def each(index):
            span = pl.ds(pl.multiple_of(index * block_q, block_q), block_q)
            out_ref[span, width : 2 * width] = turn_back(
                key_acc[span, :], cosine_ref[span, :], sine_ref[span, :], head_count
            ).astype(jnp.bfloat16)
            out_ref[span, 2 * width :] = value_acc[span, :].astype(jnp.bfloat16)


def attention_backward(
    qkv, attended, grads, log_total, begin, end, low, high, cosine, sine, head_count, block_q, block_k
):
    tokens = qkv.shape[0]
    width = head_count * HEAD_WIDTH
    steps = tokens // block_q
    whole = lambda shape: pl.BlockSpec(shape, lambda i, *_: (0,) * len(shape))
    pairs = tokens * tokens // 4 * head_count
    return pl.pallas_call(
        functools.partial(backward_kernel, head_count, block_q, block_k),
        out_shape=jax.ShapeDtypeStruct((tokens, 3 * width), jnp.bfloat16),
        grid_spec=pltpu.PrefetchScalarGridSpec(
            num_scalar_prefetch=2,
            grid=(steps,),
            in_specs=[
                whole((1, tokens)),
                whole((1, tokens)),
                whole((tokens, 3 * width)),
                whole((tokens, width)),
                whole((tokens, width)),
                pl.BlockSpec((1, 1, head_count * block_q), lambda i, *_: (i, 0, 0)),
                whole((tokens, width)),
                whole((tokens, width)),
            ],
            out_specs=whole((tokens, 3 * width)),
            scratch_shapes=[
                pltpu.VMEM((width, tokens), jnp.bfloat16),
                pltpu.VMEM((tokens, width), jnp.float32),
                pltpu.VMEM((tokens, width), jnp.float32),
            ],
        ),
        cost_estimate=pl.CostEstimate(
            flops=pairs * 1280, bytes_accessed=tokens * width * 30, transcendentals=pairs
        ),
        name="attention_backward",
    )(low, high, begin, end, qkv, attended, grads, log_total, cosine, sine)


def spans(places, lengths_row):
    ends = jnp.cumsum(lengths_row)
    past = (places[:, None] >= ends[None, :]).astype(jnp.int32)
    begin = jnp.sum(past * lengths_row[None, :], axis=1)
    before = (places[:, None] >= (ends - lengths_row)[None, :]).astype(jnp.int32)
    end = jnp.sum(before * lengths_row[None, :], axis=1)
    valid = places < ends[-1]
    return (jnp.where(valid, begin, 0), jnp.where(valid, end, 0), places - begin, valid)


def key_range(begin, end, block_q, block_k):
    begin_blocks = jnp.where(end > begin, begin, jnp.int32(1 << 30)).reshape(-1, block_q)
    high = (jnp.max(end.reshape(-1, block_q), axis=1) + block_k - 1) // block_k
    low = jnp.minimum(jnp.min(begin_blocks, axis=1) // block_k, high)
    return (low, high)


def rotary_tables(offset, head_count):
    half = HEAD_WIDTH // 2
    inverse = 160000.0 ** (-2.0 * jnp.arange(half, dtype=jnp.float32) / HEAD_WIDTH)
    angles = offset.astype(jnp.float32)[:, None] * inverse[None, :]
    cosine, sine = (jnp.cos(angles), jnp.sin(angles))
    return (
        jnp.concatenate([cosine, cosine] * head_count, axis=1),
        jnp.concatenate([sine, -sine] * head_count, axis=1),
    )


def toggled(index, bit):
    return index + bit - 2 * bit * ((index // bit) % 2)


def gather_kernel(shapes, projects, *refs):
    count = len(shapes)
    shard_refs, refs = (refs[:count], refs[count:])
    if projects:
        act_ref, qkv_ref, cosine_ref, sine_ref = refs[:4]
        heads_ref = refs[4 + count]
        columns_ref, held_ref, load_sem, head_send, head_recv, own_sem = refs[count + 8 :]
        refs = refs[4 : 4 + count] + refs[count + 5 : count + 8]
    full_refs = refs[:count]
    send_sem, recv_sem, local_sem = refs[count:]
    shards = lax.axis_size("fsdp")
    slices = lax.axis_size("ctx") // 2
    own_ctx, own_shard = (lax.axis_index("ctx"), lax.axis_index("fsdp"))
    core, chip = (own_ctx % 2, own_ctx // 2)
    barrier = pltpu.get_barrier_semaphore()
    partners = [{"fsdp": toggled(own_shard, bit)} for bit in (1, 2)]
    partners += [{"ctx": toggled(own_ctx, bit)} for bit in (1, 2, 4)]

    def owner_at(relation):
        owner = own_ctx
        for bit in (1, 2, 4):
            if relation & bit:
                owner = toggled(owner, bit)
        return owner

    if projects:
        partners += [{"ctx": owner_at(relation)} for relation in (3, 5, 6, 7)]
    for partner in partners:
        pl.semaphore_signal(
            barrier, inc=1, device_id=partner, device_id_type=pl.DeviceIdType.MESH
        )
    pl.semaphore_wait(barrier, len(partners))
    to_one, to_two, to_core, to_x, to_y = partners[:5]

    def shard_at(step):
        if step == 0:
            return own_shard
        if step == 3:
            return toggled(toggled(own_shard, 1), 2)
        return toggled(own_shard, step)

    def region(ref, weight, step, chip_at, half):
        if shapes[weight] == "small":
            return ref if len(ref.shape) == 2 else ref.at[shard_at(step)]
        if shapes[weight] == "rows":
            rows = ref.shape[-2]
            span = pl.ds(0, rows) if half is None else pl.ds(half * (rows // 2), rows // 2)
            if len(ref.shape) == 4:
                return ref.at[core, chip_at, span, :]
            return ref.at[shard_at(step), core, chip_at, span, :]
        rows = ref.shape[-2]
        first = (rows // 2) // 16 * 16
        spans_of = {None: pl.ds(0, rows), 0: pl.ds(0, first), 1: pl.ds(first, rows - first)}
        width = ref.shape[-1] // (2 * slices)
        columns = pl.ds(pl.multiple_of((core * slices + chip_at) * width, width), width)
        if len(ref.shape) == 2:
            return ref.at[spans_of[half], columns]
        return ref.at[shard_at(step), spans_of[half], columns]

    def core_region(ref, weight, step):
        if shapes[weight] == "rows":
            return ref.at[shard_at(step), core]
        width = ref.shape[-1] // 2
        return ref.at[shard_at(step), :, pl.ds(pl.multiple_of(core * width, width), width)]

    pending = []

    def send(source, target, slot, partner):
        copy = pltpu.make_async_remote_copy(
            src_ref=source,
            dst_ref=target,
            send_sem=send_sem.at[slot],
            recv_sem=recv_sem.at[slot],
            device_id=partner,
            device_id_type=pl.DeviceIdType.MESH,
        )
        copy.start()
        pending.append(copy)
        return copy

    copies = {}
    local = []

    def slot_of(weight, step, kind):
        return (weight * 3 + step - 1) * 8 + kind

    def shard_sends(weight):
        source = region(shard_refs[weight], weight, 0, chip, None)
        target = region(full_refs[weight], weight, 0, chip, None)
        copies[weight, 2, 0] = send(source, target, slot_of(weight, 2, 0), to_two)
        copies[weight, 1, 0] = send(source, target, slot_of(weight, 1, 0), to_one)
        target = full_refs[weight].at[own_shard]
        copy = pltpu.make_async_copy(shard_refs[weight], target, local_sem.at[weight])
        copy.start()
        local.append(copy)

    def shard_forward(weight):
        copies[weight, 2, 0].wait_recv()
        piece = region(full_refs[weight], weight, 2, chip, None)
        copies[weight, 3, 0] = send(piece, piece, slot_of(weight, 3, 0), to_one)

    def plane_sends(weight, step):
        lead = region(full_refs[weight], weight, step, chip, 0)
        rest = region(full_refs[weight], weight, step, chip, 1)
        for kind, piece, partner in ((1, lead, to_x), (2, rest, to_y), (3, lead, to_y), (4, rest, to_x)):
            copies[weight, step, kind] = send(piece, piece, slot_of(weight, step, kind), partner)

    def plane_forward(weight, step):
        copies[weight, step, 1].wait_recv()
        lead = region(full_refs[weight], weight, step, toggled(chip, 1), 0)
        copies[weight, step, 5] = send(lead, lead, slot_of(weight, step, 5), to_y)
        copies[weight, step, 2].wait_recv()
        rest = region(full_refs[weight], weight, step, toggled(chip, 2), 1)
        copies[weight, step, 6] = send(rest, rest, slot_of(weight, step, 6), to_x)

    def core_send(weight, step):
        for kind in (3, 4, 5, 6):
            copies[weight, step, kind].wait_recv()
        piece = core_region(full_refs[weight], weight, step)
        copies[weight, step, 7] = send(piece, piece, slot_of(weight, step, 7), to_core)

    chip_order = (3, 1, 2, 0)

    def start_loads():
        loads = {}
        for chip_bits in chip_order:
            owner_chip = owner_at(2 * chip_bits) // 2
            for part in range(3):
                width = columns_ref.shape[2] // 3
                total = qkv_ref.shape[1] // 3
                first = pl.multiple_of(part * total + owner_chip * width, width)
                loads[chip_bits, part] = pltpu.make_async_copy(
                    qkv_ref.at[:, pl.ds(first, width)],
                    columns_ref.at[chip_bits, :, pl.ds(part * width, width)],
                    load_sem.at[chip_bits * 3 + part],
                )
                loads[chip_bits, part].start()
        return loads

    def project(chip_bits, loads):
        for part in range(3):
            loads[chip_bits, part].wait()
        rows, own_width = (act_ref.shape[0], held_ref.shape[2] // 3)
        product = jnp.dot(
            act_ref[...], columns_ref[chip_bits], preferred_element_type=jnp.float32
        )
        for core_at in (0, 1):
            slot = 2 * chip_bits + core + core_at - 2 * core * core_at
            for part in range(3):
                first = (2 * part + core_at) * own_width
                piece = product[:, first : first + own_width]
                if part < 2:
                    half = HEAD_WIDTH // 2
                    turned = []
                    for base in range(0, own_width, HEAD_WIDTH):
                        turned += [piece[:, base + half : base + HEAD_WIDTH], piece[:, base : base + half]]
                    piece = piece * cosine_ref[...] - jnp.concatenate(turned, axis=1) * sine_ref[...]
                held_ref[slot, :, part * own_width : (part + 1) * own_width] = piece.astype(jnp.bfloat16)
        target = heads_ref.at[pl.ds(pl.multiple_of(own_ctx * rows, rows), rows), :]
        for core_bit in (0, 1):
            relation = 2 * chip_bits + core_bit
            if relation == 0:
                copy = pltpu.make_async_copy(held_ref.at[0], target, own_sem.at[0])
                copy.start()
                local.append(copy)
                continue
            copy = pltpu.make_async_remote_copy(
                src_ref=held_ref.at[relation],
                dst_ref=target,
                send_sem=head_send.at[relation],
                recv_sem=head_recv.at[relation],
                device_id={"ctx": owner_at(relation)},
                device_id_type=pl.DeviceIdType.MESH,
            )
            copy.start()
            pending.append(copy)
            arriving.append(copy)

    arriving = []
    sent = 1
    if projects:
        loads = start_loads()
        for weight in range(count):
            shard_sends(weight)
        sent = count
        for chip_bits in chip_order:
            project(chip_bits, loads)
    else:
        shard_sends(0)
    for weight in range(count):
        if weight + 1 >= sent and weight + 1 < count:
            shard_sends(weight + 1)
        shard_forward(weight)
        copies[weight, 1, 0].wait_recv()
        if shapes[weight] == "small":
            copies[weight, 3, 0].wait_recv()
            continue
        plane_sends(weight, 1)
        plane_sends(weight, 2)
        copies[weight, 3, 0].wait_recv()
        plane_sends(weight, 3)
        for step in (1, 2, 3):
            plane_forward(weight, step)
        if weight > 0 and shapes[weight - 1] != "small":
            for step in (1, 2, 3):
                core_send(weight - 1, step)
    for step in (1, 2, 3):
        core_send(count - 1, step)
    for weight in range(count):
        if shapes[weight] != "small":
            for step in (1, 2, 3):
                copies[weight, step, 7].wait_recv()
    for copy in arriving:
        copy.wait_recv()
    for copy in pending:
        copy.wait_send()
    for copy in local:
        copy.wait()


def gather_weights(weights, projection=None):
    shards, ctx_count = (lax.axis_size("fsdp"), lax.axis_size("ctx"))
    slices = ctx_count // 2
    shapes, views, outs = ([], [], [])
    for weight in weights:
        rows, columns = weight.shape
        if rows % (32 * ctx_count) == 0:
            shapes.append("rows")
            views.append(weight.reshape(2, slices, rows // ctx_count, columns))
            outs.append((shards, 2, slices, rows // ctx_count, columns))
        elif rows == 16:
            shapes.append("small")
            views.append(weight)
            outs.append((shards, rows, columns))
        elif columns % (128 * ctx_count) == 0 and rows % 16 == 0:
            shapes.append("columns")
            views.append(weight)
            outs.append((shards, rows, columns))
    if shards != 4 or ctx_count != 8 or len(views) < len(weights):
        return [lax.all_gather(weight, "fsdp", axis=0, tiled=True) for weight in weights]
    slots = len(views) * 24
    vmem, anywhere, dma = (
        pl.BlockSpec(memory_space=pltpu.VMEM),
        pl.BlockSpec(memory_space=pl.ANY),
        pltpu.SemaphoreType.DMA,
    )
    in_specs = [vmem] * len(views)
    scratch = [dma((slots,)), dma((slots,)), dma((len(views),))]
    if projection is not None:
        act_attn, qkv_full = projection[:2]
        rows, own_columns = (act_attn.shape[0], qkv_full.shape[1] // ctx_count)
        views += list(projection)
        in_specs += [vmem, anywhere, vmem, vmem]
        outs.append((ctx_count * rows, own_columns))
        scratch += [
            pltpu.VMEM((slices, qkv_full.shape[0], 2 * own_columns), jnp.bfloat16),
            pltpu.VMEM((ctx_count, rows, own_columns), jnp.bfloat16),
            dma((3 * slices,)),
            dma((ctx_count,)),
            dma((ctx_count,)),
            dma((1,)),
        ]
    held = pl.pallas_call(
        functools.partial(gather_kernel, shapes, projection is not None),
        out_shape=tuple(jax.ShapeDtypeStruct(out, jnp.bfloat16) for out in outs),
        in_specs=in_specs,
        out_specs=tuple(anywhere for out in outs),
        scratch_shapes=scratch,
        compiler_params=pltpu.CompilerParams(
            collective_id=0 if projection is None else 2,
            has_side_effects=True,
            vmem_limit_bytes=60 * 1024 * 1024,
        ),
        name="gather_weights" if projection is None else "gather_and_project",
    )(*views)
    return [whole.reshape(-1, whole.shape[-1]) for whole in held]


def sum_kernel(plan, lead_rows, *refs):
    weights = len(plan)
    left_refs, right_refs = (refs[:weights], refs[weights : 2 * weights])
    small_ref = refs[2 * weights]
    out_refs = refs[2 * weights + 1 : 3 * weights + 1]
    small_out = refs[3 * weights + 1]
    scratch = list(refs[3 * weights + 2 :])
    turned_refs = [scratch.pop(0) for weight in plan]
    whole_refs = [scratch.pop(0) for weight in plan]
    chunks = [(w, t) for w, (kind, count, width) in enumerate(plan) for t in range(count)]
    units = {}
    for number in range(len(chunks)):
        for half in (0, 1):
            units[number, half] = [scratch.pop(0) for stage in range(5)]
    small_held = scratch.pop(0)
    send_sem, recv_sem, local_sem, pair_send, pair_recv, small_send, small_recv, near_sem = scratch
    own_ctx, own_shard = (lax.axis_index("ctx"), lax.axis_index("fsdp"))
    core, chip = (own_ctx % 2, own_ctx // 2)
    own_x, own_y = (chip % 2, chip // 2)
    low_bit, high_bit = (own_shard % 2, own_shard // 2)
    partners = [{"ctx": toggled(own_ctx, bit)} for bit in (1, 2, 4)]
    partners += [{"fsdp": toggled(own_shard, bit)} for bit in (1, 2)]
    barrier = pltpu.get_barrier_semaphore()
    for partner in partners:
        pl.semaphore_signal(
            barrier, inc=1, device_id=partner, device_id_type=pl.DeviceIdType.MESH
        )
    pl.semaphore_wait(barrier, len(partners))
    to_core, to_x, to_y, to_one, to_two = partners
    pending = []

    def send(source, target, sent, got, partner):
        copy = pltpu.make_async_remote_copy(
            src_ref=source,
            dst_ref=target,
            send_sem=sent,
            recv_sem=got,
            device_id=partner,
            device_id_type=pl.DeviceIdType.MESH,
        )
        copy.start()
        pending.append(copy)
        return copy

    rows = left_refs[0].shape[-2]
    pairs = []
    for w, (kind, count, width) in enumerate(plan):
        span = count * width if kind == "rows" else 4 * width
        if len(right_refs[w].shape) == 3:
            own_half, other_half = (right_refs[w].at[core], right_refs[w].at[1 - core])
        else:
            own_half = right_refs[w].at[:, pl.ds(pl.multiple_of(core * span, span), span)]
            other_half = right_refs[w].at[:, pl.ds(pl.multiple_of((1 - core) * span, span), span)]
        near = pltpu.make_async_copy(own_half, whole_refs[w].at[pl.ds(0, rows)], near_sem.at[w])
        near.start()
        far = send(
            other_half,
            whole_refs[w].at[pl.ds(rows, rows)],
            pair_send.at[2 * w],
            pair_recv.at[2 * w],
            to_core,
        )
        pairs.append([near, far])

    def turn(w):
        left, turned = (left_refs[w], turned_refs[w])
        if len(left.shape) == 3:
            for z in range(left.shape[0]):
                turned[z, :, :rows] = left[z].astype(jnp.float32).T.astype(jnp.bfloat16)
        else:
            deep = left.shape[1] // 4
            for z in range(4):
                turned[z, :, :rows] = (
                    left[:, z * deep : (z + 1) * deep].astype(jnp.float32).T.astype(jnp.bfloat16)
                )

    def send_turned(w):
        pairs[w].append(
            send(
                turned_refs[w].at[:, :, pl.ds(0, rows)],
                turned_refs[w].at[:, :, pl.ds(rows, rows)],
                pair_send.at[2 * w + 1],
                pair_recv.at[2 * w + 1],
                to_core,
            )
        )

    copies = {}

    def hop(number, half, stage, source, target, partner):
        slot = (number * 2 + half) * 8 + stage
        copies[number, half, stage] = send(
            source, target, send_sem.at[slot], recv_sem.at[slot], partner
        )

    def product(number):
        w, t = chunks[number]
        kind, count, width = plan[w]
        if t == 0:
            near, far, turned = pairs[w]
            near.wait()
            far.wait_recv()
            turned.wait_recv()
        first, second = (units[number, 0][0], units[number, 1][0])

        def each(z, carried):
            if kind == "rows":
                part = jnp.dot(
                    turned_refs[w][z],
                    whole_refs[w][:, t * width : (t + 1) * width],
                    preferred_element_type=jnp.float32,
                ).astype(jnp.bfloat16)
                deep = first.shape[3]
                for s in range(4):
                    first[z, s // 2, s % 2] = part[2 * s * deep : (2 * s + 1) * deep]
                    second[z, s // 2, s % 2] = part[(2 * s + 1) * deep : (2 * s + 2) * deep]
            else:
                part = jnp.dot(
                    turned_refs[w][z], whole_refs[w][...], preferred_element_type=jnp.float32
                ).astype(jnp.bfloat16)
                column = first.shape[4]
                for s in range(4):
                    piece = part[:, s * column : (s + 1) * column]
                    first[z, s // 2, s % 2] = piece[:lead_rows]
                    second[z, s // 2, s % 2] = piece[lead_rows:]
            return carried

        lax.fori_loop(0, 4, each, 0)

    def stage_one(number):
        hop(number, 0, 0, units[number, 0][0].at[:, :, 1 - own_x], units[number, 0][1], to_x)
        hop(number, 1, 0, units[number, 1][0].at[:, 1 - own_y], units[number, 1][1], to_y)

    def add(target, source_at, count):
        def each(i, carried):
            target[i] = (
                target[i].astype(jnp.float32) + source_at(i).astype(jnp.float32)
            ).astype(jnp.bfloat16)
            return carried

        lax.fori_loop(0, count, each, 0)

    def stage_two(number):
        held, got = (units[number, 0][0], units[number, 0][1])
        copies[number, 0, 0].wait_recv()
        add(got, lambda z: held[z, :, own_x], 4)
        held_b, got_b = (units[number, 1][0], units[number, 1][1])
        copies[number, 1, 0].wait_recv()
        add(got_b, lambda z: held_b[z, own_y], 4)
        hop(number, 0, 1, got.at[:, 1 - own_y], units[number, 0][2], to_y)
        hop(number, 1, 1, got_b.at[:, 1 - own_x], units[number, 1][2], to_x)

    def stage_three(number):
        for half in (0, 1):
            held, got = (units[number, half][1], units[number, half][2])
            own = own_y if half == 0 else own_x
            copies[number, half, 1].wait_recv()
            add(got, lambda z: held[z, own], 4)
        for half in (0, 1):
            got = units[number, half][2]
            for high in (0, 1):
                hop(
                    number,
                    half,
                    2 + 4 * high,
                    got.at[2 * high + 1 - low_bit],
                    units[number, half][3].at[high],
                    to_one,
                )

    def stage_four(number):
        for half in (0, 1):
            held, got = (units[number, half][2], units[number, half][3])
            copies[number, half, 2].wait_recv()
            copies[number, half, 6].wait_recv()
            add(got, lambda high: held[2 * high + low_bit], 2)
        for half in (0, 1):
            got = units[number, half][3]
            hop(number, half, 3, got.at[1 - high_bit], units[number, half][4].at[0], to_two)

    def final_region(number, half, chip_at):
        w, t = chunks[number]
        kind, count, width = plan[w]
        deep = units[number, half][4].shape[1]
        if kind == "rows":
            start = pl.multiple_of((2 * chip_at + half) * deep, deep)
            column = pl.multiple_of((core * count + t) * width, width)
            return out_refs[w].at[pl.ds(start, deep), pl.ds(column, width)]
        column = pl.multiple_of((core * 4 + chip_at) * width, width)
        return out_refs[w].at[pl.ds(half * lead_rows, deep), pl.ds(column, width)]

    local = []

    def stage_five(number):
        for half in (0, 1):
            held, got = (units[number, half][3], units[number, half][4])
            copies[number, half, 3].wait_recv()
            add(got, lambda i: held[high_bit], 1)
        for half in (0, 1):
            got = units[number, half][4].at[0]
            target = final_region(number, half, chip)
            hop(number, half, 4, got, target, to_x if half == 0 else to_y)
            hop(number, half, 5, got, target, to_y if half == 0 else to_x)
            copy = pltpu.make_async_copy(got, target, local_sem.at[number * 2 + half])
            copy.start()
            local.append(copy)

    def stage_six(number):
        for half in (0, 1):
            copies[number, half, 4].wait_recv()
            piece = final_region(number, half, toggled(chip, 1 if half == 0 else 2))
            hop(number, half, 7, piece, piece, to_y if half == 0 else to_x)

    def stage_seven(number):
        w, t = chunks[number]
        kind, count, width = plan[w]
        for half in (0, 1):
            copies[number, half, 5].wait_recv()
            copies[number, half, 7].wait_recv()
            local[number * 2 + half].wait()
        span = width if kind == "rows" else 4 * width
        at = core * count + t if kind == "rows" else core
        piece = out_refs[w].at[:, pl.ds(pl.multiple_of(at * span, span), span)]
        slot = len(chunks) * 16 + number
        copies[number, 2, 0] = send(
            piece, piece, send_sem.at[slot], recv_sem.at[slot], to_core
        )

    small_copies = []

    def small_step(step):
        if step > 0:
            small_copies[step - 1].wait_recv()
            small_held[2 * step] = small_held[2 * step - 2] + small_held[2 * step - 1]
            if step == 3:
                small_out[0] = small_held[6]
        else:
            small_held[0] = small_ref[...]
        if step < 5:
            small_copies.append(
                send(
                    small_held.at[2 * step],
                    small_held.at[2 * step + 1],
                    small_send.at[step],
                    small_recv.at[step],
                    partners[step],
                )
            )
        else:
            small_out[1] = small_held[10]

    turn(0)
    for w in range(1, weights):
        turn(w)
        send_turned(w - 1)
    stages = [
        (stage_two, 1),
        (stage_three, 2),
        (stage_four, 3),
        (stage_five, 4),
        (stage_six, 5),
        (stage_seven, 6),
    ]
    small_at = 0
    for tick in range(len(chunks) + 7):
        if tick < len(chunks):
            product(tick)
            if tick == 0:
                send_turned(weights - 1)
            stage_one(tick)
        for stage, lag in stages:
            if 0 <= tick - lag < len(chunks):
                stage(tick - lag)
        if small_at < 6:
            small_step(small_at)
            small_at += 1
    for number in range(len(chunks)):
        copies[number, 2, 0].wait_recv()
    for copy in pending:
        copy.wait_send()


def sum_weights(products, small):
    rows = small.shape[0]
    plan, scratch, outs, lefts, rights, turned, whole, pieces = ([], [], [], [], [], [], [], [])
    lead_rows = 0
    for kind, left, right, count in products:
        tokens = left.shape[-2]
        if kind == "rows":
            deep = left.shape[1] // 4
            span = right.shape[-1] // (1 if right.ndim == 3 else 2)
            width = span // count
            outs.append(jax.ShapeDtypeStruct((deep, 2 * span), jnp.bfloat16))
            halves = (deep // 8, deep // 8)
        else:
            deep = left.shape[2]
            span = right.shape[-1] // 2
            width = span // 4
            lead_rows = deep // 2 // 16 * 16
            outs.append(jax.ShapeDtypeStruct((deep, 2 * span), jnp.bfloat16))
            halves = (lead_rows, deep - lead_rows)
        plan.append((kind, count, width))
        lefts.append(left)
        rights.append(right)
        turned.append(pltpu.VMEM((4, deep, 2 * tokens), jnp.bfloat16))
        whole.append(pltpu.VMEM((2 * tokens, span), jnp.bfloat16))
        for chunk in range(count):
            for deep_half in halves:
                for lead in ((4, 2, 2), (4, 2), (4,), (2,), (1,)):
                    pieces.append(pltpu.VMEM(lead + (deep_half, width), jnp.bfloat16))
    chunk_count = sum(count for kind, count, width in plan)
    scratch = turned + whole + pieces
    scratch += [pltpu.VMEM((11,) + small.shape, jnp.float32)]
    dma = pltpu.SemaphoreType.DMA
    slots = chunk_count * 17
    scratch += [dma((slots,)), dma((slots,)), dma((2 * chunk_count,))]
    scratch += [dma((2 * len(plan),)), dma((2 * len(plan),)), dma((5,)), dma((5,)), dma((len(plan),))]
    vmem, anywhere = (
        pl.BlockSpec(memory_space=pltpu.VMEM),
        pl.BlockSpec(memory_space=pl.ANY),
    )
    return pl.pallas_call(
        functools.partial(sum_kernel, plan, lead_rows),
        out_shape=tuple(outs) + (jax.ShapeDtypeStruct((2,) + small.shape, jnp.float32),),
        in_specs=[vmem] * len(plan) + [anywhere] * len(plan) + [vmem],
        out_specs=(anywhere,) * len(plan) + (vmem,),
        scratch_shapes=scratch,
        compiler_params=pltpu.CompilerParams(
            collective_id=1, has_side_effects=True, vmem_limit_bytes=60 * 1024 * 1024
        ),
        name="sum_weights",
    )(*lefts, *rights, small)


def layer_norm(rows_in, gain_vec):
    row_mean = jnp.mean(rows_in, axis=-1, keepdims=True)
    centred = rows_in - row_mean
    variance = jnp.mean(centred * centred, axis=-1, keepdims=True)
    return centred * lax.rsqrt(variance + norm_eps) * gain_vec


def rotate(projected, cosine, sine):
    row_count, width = projected.shape
    half_width = HEAD_WIDTH // 2
    by_head = projected.reshape(row_count, width // HEAD_WIDTH, HEAD_WIDTH)
    turned = jnp.concatenate([by_head[..., half_width:], by_head[..., :half_width]], axis=-1)
    return (by_head * cosine[:, None, :] - turned * sine[:, None, :]).reshape(row_count, width)


def swap(value, axis, bit):
    pairs = [(i, i ^ bit) for i in range(lax.axis_size(axis))]
    return lax.ppermute(value, axis, pairs)


def bit_of(axis, bit):
    return (lax.axis_index(axis) // bit) % 2 == 1


def bits_below(count):
    return [1 << i for i in range(count.bit_length() - 1)]


def reduce_pieces(pieces, labels, order):
    labels = list(labels)
    for axis, bit in order:
        at = labels.index((axis, bit))
        labels.pop(at)
        first = lax.index_in_dim(pieces, 0, at, keepdims=False)
        second = lax.index_in_dim(pieces, 1, at, keepdims=False)
        upper = bit_of(axis, bit)
        arrived = swap(jnp.where(upper, first, second), axis, bit)
        kept = jnp.where(upper, second, first)
        pieces = (kept.astype(jnp.float32) + arrived.astype(jnp.float32)).astype(jnp.bfloat16)
    return pieces


def gather_pieces(piece, labels, order):
    held = []
    for axis, bit in reversed(order):
        arrived = swap(piece, axis, bit)
        upper = bit_of(axis, bit)
        held = [label for label in labels if label in held or label == (axis, bit)]
        piece = jnp.stack(
            [jnp.where(upper, arrived, piece), jnp.where(upper, piece, arrived)],
            axis=held.index((axis, bit)),
        )
    return piece


def keep_and_send(first, second):
    upper = bit_of("ctx", 1)
    return (jnp.where(upper, second, first), jnp.where(upper, first, second))


def core_product(left, first, second):
    kept, sent = keep_and_send(first, second)
    left_all = jnp.concatenate([left, swap(left, "ctx", 1)], axis=0)
    right_all = jnp.concatenate([kept, swap(sent, "ctx", 1)], axis=0)
    return lax.dot_general(
        left_all, right_all, (((0,), (0,)), ((), ())), preferred_element_type=jnp.float32
    ).astype(jnp.bfloat16)


def shard_sum(product, by_columns):
    shards = lax.axis_size("fsdp")
    slices = lax.axis_size("ctx") // 2
    rows, columns = product.shape
    shard_labels = [("fsdp", bit) for bit in reversed(bits_below(shards))]
    slice_labels = [("ctx", 2 * bit) for bit in reversed(bits_below(slices))]
    if by_columns:
        cut = product.reshape(shards, rows // shards, slices, columns // slices)
        cut = jnp.transpose(cut, (0, 2, 1, 3))
    else:
        cut = product.reshape(shards, slices, rows // shards // slices, columns)
    parts = []
    half = cut.shape[2] // 2
    tail = list(reversed(shard_labels))
    for lead, orders in (
        (cut[:, :, :half], list(reversed(slice_labels))),
        (cut[:, :, half:], slice_labels),
    ):
        pieces = lead.reshape((2,) * (len(shard_labels) + len(slice_labels)) + lead.shape[2:])
        piece = reduce_pieces(pieces, shard_labels + slice_labels, orders + tail)
        whole = gather_pieces(piece, slice_labels, orders)
        parts.append(whole.reshape((slices,) + piece.shape))
    both = jnp.concatenate(parts, axis=1)
    if by_columns:
        return jnp.transpose(both, (1, 0, 2)).reshape(rows // shards, columns)
    return both.reshape(rows // shards, columns)


def join_cores(own):
    other = swap(own, "ctx", 1)
    upper = bit_of("ctx", 1)
    return jnp.concatenate(
        [jnp.where(upper, other, own), jnp.where(upper, own, other)], axis=1
    ).astype(jnp.float32)


def sum_over(value, axes):
    for axis in axes:
        for bit in bits_below(lax.axis_size(axis)):
            value = value + swap(value, axis, bit)
    return value


def own_shard(vector):
    width = vector.shape[0] // lax.axis_size("fsdp")
    return lax.dynamic_slice_in_dim(vector, lax.axis_index("fsdp") * width, width, 0)


def weight_sums(
    hidden,
    grad_mlp_low,
    act_mlp,
    grad_leading,
    grad_trailing,
    act_attn,
    grad_projected,
    attn_low,
    grad_attn_low,
    small,
):
    shards, ctx_count = (lax.axis_size("fsdp"), lax.axis_size("ctx"))
    rows, ff_width = hidden.shape
    model_width = act_mlp.shape[1]
    if shards != 4 or ctx_count != 8 or model_width % 1024 != 0 or ff_width % 64 != 0:
        half, half_three = (model_width // 2, 3 * model_width // 2)
        pairs = (
            (hidden, grad_mlp_low[:, :half], grad_mlp_low[:, half:]),
            (act_mlp, grad_leading, grad_trailing),
            (act_attn, grad_projected[:, :half_three], grad_projected[:, half_three:]),
            (attn_low, grad_attn_low[:, :half], grad_attn_low[:, half:]),
        )
        totals = [
            join_cores(shard_sum(core_product(*pair), at == 0)) for at, pair in enumerate(pairs)
        ]
        over_pack = sum_over(small, ("ctx",))
        return totals + [jnp.stack([over_pack, sum_over(over_pack, ("fsdp",))])]
    padded = -(-ff_width // 384) * 384
    sides = jnp.stack(
        [
            jnp.pad(side, ((0, 0), (0, padded - ff_width)))
            for side in (grad_leading, grad_trailing)
        ]
    )
    by_shard = jnp.transpose(hidden.reshape(rows, shards, ff_width // shards), (1, 0, 2))
    total_out, total_in, total_qkv, total_attn, small_sums = sum_weights(
        [
            ("columns", by_shard, grad_mlp_low, 1),
            ("rows", act_mlp, sides, 3),
            ("rows", act_attn, grad_projected, 3),
            ("rows", attn_low, grad_attn_low, 1),
        ],
        small,
    )
    total_in = jnp.concatenate(
        [total_in[:, :ff_width], total_in[:, padded : padded + ff_width]], axis=1
    )
    return [
        total.astype(jnp.float32) for total in (total_out, total_in, total_qkv, total_attn)
    ] + [small_sums]


def per_device(
    inputs,
    cotangent,
    lengths,
    piece_route,
    gain_one,
    qkv_weight,
    attn_out,
    gain_two,
    geglu_in,
    geglu_out,
):
    ctx_count = lax.axis_size("ctx")
    own_index = lax.axis_index("ctx")
    row_count = inputs.shape[1]
    model_width = inputs.shape[2]
    piece_rows = row_count // ctx_count
    tokens = row_count * ctx_count
    own_heads = model_width // HEAD_WIDTH // ctx_count
    own_width = own_heads * HEAD_WIDTH
    block_q = math.gcd(tokens, 256)
    block_k = math.gcd(tokens, 512)
    lengths_row = lengths[0]
    own_route = piece_route[0, 0]
    slot_ids = jnp.arange(ctx_count, dtype=jnp.int32)
    outgoing = jnp.sum(
        slot_ids[None, :] * (own_route[None, :] == slot_ids[:, None]).astype(jnp.int32), axis=1
    )

    def exchange(blocks):
        return lax.all_to_all(blocks, "ctx", split_axis=0, concat_axis=0, tiled=True)

    def to_slots(rows_in):
        return jnp.take(rows_in.reshape(ctx_count, piece_rows, model_width), outgoing, axis=0)

    def to_heads(rows_in):
        by_heads = rows_in.reshape(row_count, ctx_count, -1)
        return exchange(jnp.transpose(by_heads, (1, 0, 2))).reshape(tokens, -1)

    def to_rows(heads_in):
        return exchange(heads_in.reshape(ctx_count, row_count, -1))

    arrived = exchange(to_slots(inputs[0]))
    grad_arrived = exchange(to_slots(cotangent[0]))
    residual = arrived.reshape(row_count, model_width).astype(jnp.float32)
    places = own_index * row_count + jnp.arange(row_count, dtype=jnp.int32)
    unused_begin, unused_end, offset, is_valid = spans(places, lengths_row)
    pack_begin, pack_end, pack_offset, unused_valid = spans(
        jnp.arange(tokens, dtype=jnp.int32), lengths_row
    )
    grad_final = jnp.where(
        is_valid[:, None], grad_arrived.reshape(row_count, model_width).astype(jnp.float32), 0.0
    )
    gains = jnp.pad(jnp.stack([gain_one, gain_two]), ((0, 14), (0, 0)))
    gains_full, qkv_full = gather_weights([gains, qkv_weight])
    gains_full = gains_full.reshape(-1, 16, gains.shape[1])
    gain_attn = gains_full[:, 0].reshape(-1).astype(jnp.float32)
    gain_mlp = gains_full[:, 1].reshape(-1).astype(jnp.float32)
    act_attn = layer_norm(residual, gain_attn).astype(jnp.bfloat16)
    later = [attn_out, geglu_in, geglu_out]
    if lax.axis_size("fsdp") == 4 and ctx_count == 8 and own_width == 128:
        attn_full, in_full, out_full, qkv_heads = gather_weights(
            later, (act_attn, qkv_full) + rotary_tables(offset, own_heads)
        )
    else:
        attn_full, in_full, out_full = gather_weights(later)
        projected = jnp.dot(act_attn, qkv_full, preferred_element_type=jnp.float32)
        cosine, sine = rotary_tables(offset, 1)
        queries, keys = (
            rotate(projected[:, :model_width], cosine, sine).astype(jnp.bfloat16),
            rotate(projected[:, model_width : 2 * model_width], cosine, sine).astype(jnp.bfloat16),
        )
        values = projected[:, 2 * model_width :].astype(jnp.bfloat16)
        joined = jnp.stack(
            [part.reshape(row_count, ctx_count, own_width) for part in (queries, keys, values)], axis=2
        )
        qkv_heads = to_heads(joined.reshape(row_count, -1))
    low, high = key_range(pack_begin, pack_end, block_q, block_k)
    pack_begin, pack_end = (pack_begin[None, :], pack_end[None, :])
    attended_heads, log_total = attention_forward(
        qkv_heads, pack_begin, pack_end, low, high, own_heads, block_q, block_k
    )
    attn_low = jnp.transpose(to_rows(attended_heads.astype(jnp.bfloat16)), (1, 0, 2)).reshape(
        row_count, model_width
    )
    branch_attn = jnp.dot(attn_low, attn_full, preferred_element_type=jnp.float32)
    middle = residual + branch_attn
    act_mlp = layer_norm(middle, gain_mlp).astype(jnp.bfloat16)
    up_both = jnp.dot(act_mlp, in_full, preferred_element_type=jnp.float32)
    ff_width = up_both.shape[1] // 2
    hidden = (jax.nn.gelu(up_both[:, :ff_width], approximate=False) * up_both[:, ff_width:]).astype(
        jnp.bfloat16
    )
    branch_mlp = jnp.dot(hidden, out_full, preferred_element_type=jnp.float32)
    final_rows = jnp.where(is_valid[:, None], middle + branch_mlp, 0.0)
    square_sums = jnp.stack(
        [
            jnp.sum(final_rows * final_rows),
            jnp.sum(jnp.where(is_valid[:, None], branch_attn * branch_attn, 0.0)),
            jnp.sum(jnp.where(is_valid[:, None], branch_mlp * branch_mlp, 0.0)),
        ]
    )
    out_slots = final_rows.astype(jnp.bfloat16).reshape(ctx_count, piece_rows, model_width)
    back_out = exchange(out_slots)
    block_out = jnp.take(back_out, own_route, axis=0).reshape(1, row_count, model_width)
    grad_mlp_low = grad_final.astype(jnp.bfloat16)
    grad_hidden = lax.dot_general(
        grad_mlp_low, out_full, NT, preferred_element_type=jnp.float32
    )

    def gated(leading, trailing):
        return jax.nn.gelu(leading, approximate=False) * trailing

    unused_gate, gate_back = jax.vjp(gated, up_both[:, :ff_width], up_both[:, ff_width:])
    grad_leading, grad_trailing = gate_back(grad_hidden)
    grad_leading, grad_trailing = (
        grad_leading.astype(jnp.bfloat16),
        grad_trailing.astype(jnp.bfloat16),
    )
    grad_up = jnp.concatenate([grad_leading, grad_trailing], axis=1)
    grad_act_mlp = lax.dot_general(grad_up, in_full, NT, preferred_element_type=jnp.float32)
    unused_norm, norm_back_mlp = jax.vjp(layer_norm, middle, gain_mlp)
    grad_middle_norm, grad_gain_mlp = norm_back_mlp(grad_act_mlp)
    grad_middle = grad_final + grad_middle_norm
    grad_attn_low = grad_middle.astype(jnp.bfloat16)
    grad_attended = lax.dot_general(
        grad_attn_low, attn_full, NT, preferred_element_type=jnp.float32
    ).astype(jnp.bfloat16)
    pack_cosine, pack_sine = rotary_tables(pack_offset, own_heads)
    block_back = math.gcd(tokens, 256)
    low_back, high_back = key_range(pack_begin[0], pack_end[0], block_q, block_back)
    grad_heads = attention_backward(
        qkv_heads,
        attended_heads,
        to_heads(grad_attended),
        log_total,
        pack_begin,
        pack_end,
        low_back,
        high_back,
        pack_cosine,
        pack_sine,
        own_heads,
        block_q,
        block_back,
    )
    grad_projected = jnp.transpose(
        to_rows(grad_heads).reshape(ctx_count, row_count, 3, own_width), (1, 2, 0, 3)
    ).reshape(row_count, 3 * model_width)
    grad_act_attn = lax.dot_general(
        grad_projected, qkv_full, NT, preferred_element_type=jnp.float32
    )
    unused_first, norm_back_attn = jax.vjp(layer_norm, residual, gain_attn)
    grad_resid_norm, grad_gain_attn = norm_back_attn(grad_act_attn)
    grad_residual = (grad_middle + grad_resid_norm).astype(jnp.bfloat16)
    back_grad = exchange(grad_residual.reshape(ctx_count, piece_rows, model_width))
    grad_inputs = jnp.take(back_grad, own_route, axis=0).reshape(1, row_count, model_width)
    small = jnp.stack(
        [grad_gain_attn, grad_gain_mlp, jnp.pad(square_sums, (0, model_width - 3))]
        + [jnp.zeros((model_width,), jnp.float32)] * 5
    )
    total_out, total_in, total_qkv, total_attn, small_sums = weight_sums(
        hidden,
        grad_mlp_low,
        act_mlp,
        grad_leading,
        grad_trailing,
        act_attn,
        grad_projected,
        attn_low,
        grad_attn_low,
        small,
    )
    total_gain_one = own_shard(small_sums[1, 0])
    total_gain_two = own_shard(small_sums[1, 1])
    total_squares = small_sums[0, 2, :3]
    valid_count = jnp.sum(lengths_row).astype(jnp.float32)
    rms_stats = jnp.sqrt(total_squares / (valid_count * model_width))[None, :]
    return (
        block_out,
        grad_inputs,
        total_gain_one,
        total_qkv,
        total_attn,
        total_gain_two,
        total_in,
        total_out,
        rms_stats,
    )


def solution(mesh):
    placed = (
        P("fsdp", "ctx", None),
        P("fsdp", "ctx", None),
        P("fsdp", None),
        P("fsdp", "ctx", None),
        P("fsdp"),
        P("fsdp", None),
        P("fsdp", None),
        P("fsdp"),
        P("fsdp", None),
        P("fsdp", None),
    )
    return jax.shard_map(
        per_device,
        mesh=mesh,
        in_specs=placed,
        out_specs=(
            P("fsdp", "ctx", None),
            P("fsdp", "ctx", None),
            P("fsdp"),
            P("fsdp", None),
            P("fsdp", None),
            P("fsdp"),
            P("fsdp", None),
            P("fsdp", None),
            P("fsdp", None),
        ),
        check_vma=False,
    )
```

profile of v0, /device:TPU:1, one launch (start us, length us, event | category | flops | bytes accessed | tf_op | source)
XLA Modules:
  0.0 573.8 jit_solution(4642519773407609963)
XLA Ops:
  0.7 0.9 select_reduce_fusion.6
  2.4 0.6 gather_fusion
  3.1 1.3 broadcast_select_fusion.2
  4.4 5.2 all-to-all-start
  10.4 0.6 fusion.45
  11.1 0.6 fusion.30.refs_0_
  11.7 39.7 %gather_weights.1 = (bf16[4,16,256]{2,1,0:T(8,128)(2,1)}, bf16[4,2,4,32,3072]{4,3,2,1,0:T(8,128)(2,1)}) custom-call(bf16[16,256]{1,0:T(8,128)(2,1)} %fusion.30.refs_0_, bf16[2,4,32,3072]{3,2,1,0:T(8,128)(2,1)} %bitcast.143), custom_call_target="tpu_custom_call" | custom-call | tf_op jit(solution)/shard_map/gather_weights/pallas_call | solution.py:547
  51.4 0.8 slice_convert_fusion
  52.5 0.8 fusion.27
  53.8 0.8 multiply_sine_fusion.1
  54.6 1.1 pad_maximum_fusion.3
  55.7 1.3 compare_select_fusion.1
  57.0 3.5 all-to-all-start.3
  61.2 1.2 fusion.16.refs_3_.refs_2_
  62.4 97.0 %gather_and_project.1 = (bf16[4,2,4,32,1024]{4,3,2,1,0:T(8,128)(2,1)}, bf16[4,2,4,32,5248]{4,3,2,1,0:T(8,128)(2,1)}, bf16[4,656,1024]{2,1,0:T(8,128)(2,1)}, bf16[3072,384]{1,0:T(8,128)(2,1)}) custom-call(bf16[2,4,32,1024]{3,2,1,0:T(8,128)(2,1)} %bitcast.149, bf16[2,4,32,5248]{3,2,1,0:T(8,128)(2,1)} %bitcast.139, bf16[656,1024]{1,0:T(8,128)(2,1)} %refs_2_.1, ...), custom_call_target="tpu_custom_call" | custom-call | tf_op jit(solution)/shard_map/gather_and_project/pallas_call | solution.py:547
  159.4 32.2 %attention_forward.1 = (f32[3072,128]{1,0:T(8,128)}, f32[12,1,512]{2,1,0:T(1,128)}) custom-call(s32[12]{0:T(128)} %get-tuple-element.76.low_ref, s32[12]{0:T(128)} %get-tuple-element.77.high_ref, s32[1,3072]{1,0:T(1,128)} %get-tuple-element.89.begin_ref, s32[1,3072]{1,0:T(1,128)} %get-tuple-element.88.end_ref, bf16[3072,384]{1,0:T(8,128)(2,1)} %get-tuple-element.25.qkv_ref), custom_call_target="tpu_custom_call" | custom-call | flops 2415919104 | bytes 4718592 | tf_op jit(solution)/shard_map/attention_forward/pallas_call | solution.py:97
  191.6 2.4 convert_element_type.123
  193.9 3.7 all-to-all-start.1
  197.6 0.7 fusion.31
  198.3 0.7 add_compare_fusion.1
  199.1 7.5 %all-to-all-done.1 = bf16[8,384,128]{2,1,0:T(8,128)(2,1)S(1)} async-done(((bf16[8,384,128]{2,1,0:T(8,128)(2,1)}), bf16[8,384,128]{2,1,0:T(8,128)(2,1)S(1)}, u32[]{:S(2)}, u32[]{:S(2)}) %all-to-all-start.1) | async-done | bytes 786464 | tf_op jit(solution)/shard_map/all_to_all | solution.py:1097
  206.7 4.1 fusion.42
  211.3 0.9 copy-done.20
  212.2 4.5 fusion.46
  216.7 16.2 %add_convert_fusion = (bf16[384,2624]{1,0:T(8,128)(2,1)S(1)}, f32[384,2624]{1,0:T(8,128)}, f32[384,2624]{1,0:T(8,128)}) fusion(f32[384,5248]{1,0:T(8,128)S(1)} %fusion.46, bf16[384,1024]{1,0:T(8,128)(2,1)S(1)} %bitcast.146, bf16[2624,1024]{1,0:T(8,128)(2,1)} %bitcast.171), kind=kOutput, calls=%fused_computation.8 | convolution fusion | flops 2137153536 | bytes 24297472 | tf_op jit(solution)/shard_map/dot_general | solution.py:1173
  233.0 7.9 %multiply_convert_fusion = (bf16[384,2624]{1,0:T(8,128)(2,1)S(1)}, bf16[384,2624]{1,0:T(8,128)(2,1)S(1)}) fusion(f32[384,2624]{1,0:T(8,128)} %get-tuple-element.85, f32[384,2624]{1,0:T(8,128)} %get-tuple-element.54, f32[384,5248]{1,0:T(8,128)} %copy-done.3), kind=kLoop, calls=%fused_computation.7 | loop fusion | flops 6045696 | bytes 20152320 | tf_op jit(solution)/shard_map/convert_element_type | solution.py:1184
  240.9 9.1 %fusion.6 = f32[384,1024]{1,0:T(8,128)S(1)} fusion(bf16[1024,5248]{1,0:T(8,128)(2,1)} %bitcast.169, bf16[384,2624]{1,0:T(8,128)(2,1)S(1)} %get-tuple-element.59, bf16[384,2624]{1,0:T(8,128)(2,1)S(1)} %get-tuple-element.53), kind=kOutput, calls=%fused_computation.23 | convolution fusion | flops 4135256064 | bytes 16351232 | tf_op jit(solution)/shard_map/dot_general | solution.py:1187
  250.0 7.6 %multiply_reduce_fusion = (f32[]{:T(128)}, f32[]{:T(128)}, f32[384]{0:T(512)S(1)}, f32[1024]{0:T(1024)S(1)}, f32[]{:T(128)}, /*index=5*/bf16[384,1024]{1,0:T(8,128)(2,1)}) fusion(f32[384,1024]{1,0:T(8,128)S(1)} %get-tuple-element.56, pred[384]{0:T(512)(128)(4,1)S(1)} %fusion.31, f32[384,1024]{1,0:T(8,128)S(1)} %fusion.6, f32[1024]{0:T(1024)S(1)} %bitcast.157, ...), kind=kOutput, calls=%fused_computation.56 | convolution fusion | flops 2070674048 | bytes 12907404 | tf_op jit(solution)/shard_map/dot_general | solution.py:1160
  257.7 2.0 fusion.40
  260.0 1.3 copy-done.11
  261.2 1.0 fusion.22
  262.3 1.0 copy.72
  263.3 7.6 %all-to-all-start.4 = ((bf16[8,384,128]{2,1,0:T(8,128)(2,1)}), bf16[8,384,128]{2,1,0:T(8,128)(2,1)}, u32[]{:S(2)}, u32[]{:S(2)}) async-start(bf16[8,384,128]{2,1,0:T(8,128)(2,1)} %bitcast.137), calls=%async_computation.4 | async-start | bytes 1572864 | tf_op jit(solution)/shard_map/all_to_all | solution.py:1097
  270.9 8.2 %multiply_sine_fusion = (f32[3072,32]{1,0:T(8,128)}, f32[3072,32]{1,0:T(8,128)}, f32[3072,32]{1,0:T(8,128)}) fusion(f32[3072]{0:T(1024)S(1)} %subtract_convert_fusion, f32[32]{0:T(128)S(1)} %multiply_power_fusion), kind=kLoop, calls=%fused_computation.33 | loop fusion | flops 196608 | bytes 1192064 | tf_op jit(solution)/shard_map/sin | solution.py:274
  279.1 0.9 all-to-all-done.4
  280.0 7.7 %all-to-all-start.2 = ((bf16[8,48,1024]{2,1,0:T(8,128)(2,1)}), bf16[8,48,1024]{2,1,0:T(8,128)(2,1)}, u32[]{:S(2)}, u32[]{:S(2)}) async-start(bf16[8,48,1024]{2,1,0:T(8,128)(2,1)} %bitcast.145), calls=%async_computation.2 | async-start | bytes 1572864 | tf_op jit(solution)/shard_map/all_to_all | solution.py:1097
  287.7 9.7 %pad_maximum_fusion.1 = (f32[3072,128]{1,0:T(8,128)}, f32[3072,128]{1,0:T(8,128)}) fusion(f32[3072,32]{1,0:T(8,128)} %get-tuple-element.72, f32[3072,32]{1,0:T(8,128)} %get-tuple-element.71, f32[3072,32]{1,0:T(8,128)} %get-tuple-element.70), kind=kLoop, calls=%fused_computation.37 | loop fusion | flops 2359296 | bytes 4325376 | tf_op jit(solution)/shard_map/concatenate | solution.py:276
  297.4 44.9 %attention_backward.1 = bf16[3072,384]{1,0:T(8,128)(2,1)} custom-call(s32[12]{0:T(128)} %get-tuple-element.51.low_ref, s32[12]{0:T(128)} %get-tuple-element.52.high_ref, s32[1,3072]{1,0:T(1,128)} %get-tuple-element.89.begin_ref, s32[1,3072]{1,0:T(1,128)} %get-tuple-element.88.end_ref, bf16[3072,384]{1,0:T(8,128)(2,1)} %get-tuple-element.25.qkv_ref, ...), custom_call_target="tpu_custom_call" | custom-call | flops 6039797760 | bytes 11796480 | tf_op jit(solution)/shard_map/attention_backward/pallas_call | solution.py:223
  342.3 4.3 copy.54
  346.5 5.4 all-to-all-start.5
  352.6 4.0 copy.56
  356.6 4.1 copy.57
  360.8 2.0 select_maximum_fusion
  362.7 2.1 copy_bitcast_fusion.1.refs_3_
  364.9 1.9 pad_bitcast_fusion
  367.2 2.4 pad_maximum_fusion.refs_5_
  369.6 2.7 gather_fusion.1
  372.3 5.6 all-to-all-done.5
  377.9 4.4 copy.55
  382.3 3.8 copy.71
  386.1 4.9 fusion.18
  391.1 0.8 fusion.17
  391.9 1.9 fusion.21
  393.8 7.1 %all-to-all-start.6 = ((bf16[8,48,1024]{2,1,0:T(8,128)(2,1)}), bf16[8,48,1024]{2,1,0:T(8,128)(2,1)S(1)}, u32[]{:S(2)}, u32[]{:S(2)}) async-start(bf16[8,48,1024]{2,1,0:T(8,128)(2,1)} %bitcast.138), calls=%async_computation.6 | async-start | bytes 1572864 | tf_op jit(solution)/shard_map/all_to_all | solution.py:1097
  400.9 0.7 stack.53.refs_8_
  401.5 155.6 %sum_weights.1 = (bf16[656,1024]{1,0:T(8,128)(2,1)}, bf16[256,5376]{1,0:T(8,128)(2,1)}, bf16[256,3072]{1,0:T(8,128)(2,1)}, bf16[256,1024]{1,0:T(8,128)(2,1)}, f32[2,8,1024]{2,1,0:T(8,128)}) custom-call(bf16[4,384,656]{2,1,0:T(8,128)(2,1)} %bitcast.132, bf16[384,1024]{1,0:T(8,128)(2,1)} %copy-done.7, bf16[384,1024]{1,0:T(8,128)(2,1)} %fusion.16.refs_3_.refs_2_, ...), custom_call_target="tpu_custom_call" | custom-call | tf_op jit(solution)/shard_map/sum_weights/pallas_call | solution.py:884
  557.1 0.8 fusion.44
  558.0 3.6 convert_element_type.141
  561.6 1.1 convert_element_type.142
  564.0 1.1 copy-done.16
  565.1 1.9 convert_element_type.144
  567.0 1.2 sqrt_bitcast_fusion
  568.2 3.0 maximum_convert_fusion
  572.3 1.3 broadcast_select_fusion
  (93 shorter events, 7.3 us)
Async XLA Ops:
  0.6 1.2 copy-start
  0.7 1.7 copy-start.17
  3.0 6.6 %copy-start.19 = (s32[1,6]{1,0:T(1,128)S(1)}, s32[1,6]{1,0:T(1,128)}, u32[]{:S(2)}) copy-start(s32[1,6]{1,0:T(1,128)} %param.14) | copy-start | bytes 76
  3.0 8.0 %copy-start.21 = (bf16[256]{0:T(256)(128)(2,1)S(1)}, bf16[256]{0:T(256)(128)(2,1)}, u32[]{:S(2)}) copy-start(bf16[256]{0:T(256)(128)(2,1)} %param.19) | copy-start | bytes 1540
  3.0 8.0 %copy-start.22 = (bf16[256]{0:T(256)(128)(2,1)S(1)}, bf16[256]{0:T(256)(128)(2,1)}, u32[]{:S(2)}) copy-start(bf16[256]{0:T(256)(128)(2,1)} %param.16) | copy-start | bytes 1540
  4.4 52.6 %all-to-all-start = ((bf16[8,48,1024]{2,1,0:T(8,128)(2,1)}), bf16[8,48,1024]{2,1,0:T(8,128)(2,1)S(1)}, u32[]{:S(2)}, u32[]{:S(2)}) async-start(bf16[8,48,1024]{2,1,0:T(8,128)(2,1)} %get-tuple-element.83), calls=%async_computation | async-start | bytes 1572864 | tf_op jit(solution)/shard_map/all_to_all | solution.py:1097
  57.0 137.0 %all-to-all-start.3 = ((bf16[8,48,1024]{2,1,0:T(8,128)(2,1)}), bf16[8,48,1024]{2,1,0:T(8,128)(2,1)S(1)}, u32[]{:S(2)}, u32[]{:S(2)}) async-start(bf16[8,48,1024]{2,1,0:T(8,128)(2,1)} %get-tuple-element.82), calls=%async_computation.3 | async-start | bytes 1572864 | tf_op jit(solution)/shard_map/all_to_all | solution.py:1097
  193.9 12.7 %all-to-all-start.1 = ((bf16[8,384,128]{2,1,0:T(8,128)(2,1)}), bf16[8,384,128]{2,1,0:T(8,128)(2,1)S(1)}, u32[]{:S(2)}, u32[]{:S(2)}) async-start(bf16[8,384,128]{2,1,0:T(8,128)(2,1)} %bitcast.16), calls=%async_computation.1 | async-start | bytes 1572864 | tf_op jit(solution)/shard_map/all_to_all | solution.py:1097
  206.7 4.1 copy-start.6
  206.7 5.5 copy-start.20
  211.3 5.4 copy-start.7
  216.7 16.3 %copy-start.3 = (f32[384,5248]{1,0:T(8,128)}, f32[384,5248]{1,0:T(8,128)S(1)}, u32[]{:S(2)}) copy-start(f32[384,5248]{1,0:T(8,128)S(1)} %fusion.46) | copy-start | bytes 24182788
  233.0 7.9 %copy-start.12 = (bf16[384,2624]{1,0:T(8,128)(2,1)}, bf16[384,2624]{1,0:T(8,128)(2,1)S(1)}, u32[]{:S(2)}) copy-start(bf16[384,2624]{1,0:T(8,128)(2,1)S(1)} %get-tuple-element.53) | copy-start | bytes 6045700
  240.8 9.2 %copy-start.4 = (bf16[384,2624]{1,0:T(8,128)(2,1)}, bf16[384,2624]{1,0:T(8,128)(2,1)S(1)}, u32[]{:S(2)}) copy-start(bf16[384,2624]{1,0:T(8,128)(2,1)S(1)} %get-tuple-element.59) | copy-start | bytes 6045700
  240.8 9.2 %copy-start.5 = (bf16[384,2624]{1,0:T(8,128)(2,1)}, bf16[384,2624]{1,0:T(8,128)(2,1)S(1)}, u32[]{:S(2)}) copy-start(bf16[384,2624]{1,0:T(8,128)(2,1)S(1)} %get-tuple-element.60) | copy-start | bytes 6045700
  240.9 9.2 %copy-start.14 = (f32[384,1024]{1,0:T(8,128)S(1)}, f32[384,1024]{1,0:T(8,128)}, u32[]{:S(2)}) copy-start(f32[384,1024]{1,0:T(8,128)} %get-tuple-element.84) | copy-start | bytes 4718596
  250.0 7.7 %copy-start.15 = (f32[384,1024]{1,0:T(8,128)}, f32[384,1024]{1,0:T(8,128)S(1)}, u32[]{:S(2)}) copy-start(f32[384,1024]{1,0:T(8,128)S(1)} %fusion.6) | copy-start | bytes 4718596
  259.6 1.6 copy-start.11
  261.2 1.0 copy-start.8
  263.3 16.7 %all-to-all-start.4 = ((bf16[8,384,128]{2,1,0:T(8,128)(2,1)}), bf16[8,384,128]{2,1,0:T(8,128)(2,1)}, u32[]{:S(2)}, u32[]{:S(2)}) async-start(bf16[8,384,128]{2,1,0:T(8,128)(2,1)} %bitcast.137), calls=%async_computation.4 | async-start | bytes 1572864 | tf_op jit(solution)/shard_map/all_to_all | solution.py:1097
  280.0 66.6 %all-to-all-start.2 = ((bf16[8,48,1024]{2,1,0:T(8,128)(2,1)}), bf16[8,48,1024]{2,1,0:T(8,128)(2,1)}, u32[]{:S(2)}, u32[]{:S(2)}) async-start(bf16[8,48,1024]{2,1,0:T(8,128)(2,1)} %bitcast.145), calls=%async_computation.2 | async-start | bytes 1572864 | tf_op jit(solution)/shard_map/all_to_all | solution.py:1097
  346.5 5.4 copy-start.23
  346.5 31.4 %all-to-all-start.5 = ((bf16[8,384,384]{1,2,0:T(8,128)(2,1)}), bf16[8,384,384]{1,2,0:T(8,128)(2,1)}, u32[]{:S(2)}, u32[]{:S(2)}) async-start(bf16[8,384,384]{1,2,0:T(8,128)(2,1)} %copy.54), calls=%async_computation.5 | async-start | bytes 4718592 | tf_op jit(solution)/shard_map/all_to_all | solution.py:1097
  364.9 2.2 copy-start.13
  382.3 3.8 copy-start.2
  393.8 177.3 %all-to-all-start.6 = ((bf16[8,48,1024]{2,1,0:T(8,128)(2,1)}), bf16[8,48,1024]{2,1,0:T(8,128)(2,1)S(1)}, u32[]{:S(2)}, u32[]{:S(2)}) async-start(bf16[8,48,1024]{2,1,0:T(8,128)(2,1)} %bitcast.138), calls=%async_computation.6 | async-start | bytes 1572864 | tf_op jit(solution)/shard_map/all_to_all | solution.py:1097
  558.0 3.6 copy-start.18
  558.0 5.8 %copy-start.10 = (bf16[256,5376]{1,0:T(8,128)(2,1)S(1)}, bf16[256,5376]{1,0:T(8,128)(2,1)}, u32[]{:S(2)}) copy-start(bf16[256,5376]{1,0:T(8,128)(2,1)} %get-tuple-element.34) | copy-start | bytes 8257540
  563.8 1.3 copy-start.16
  568.2 5.5 copy-start.1
  571.2 1.1 copy-start.9
where the time goes:
time: 584 us; the launch traced here: 574 us
  Pallas kernels  369 us (63%)
  other arithmetic  62.6 us (11%)
  matrix products  47.5 us (8%)
  starting transfers between devices  40.2 us (7%)
  local copies, waits for them, and re-layouts  38.3 us (7%)
  waiting for transfers between devices  14 us (2%)
    pallas_call x1, Pallas kernels, sum_weights(): pl.pallas_call(functools.partial(sum_kernel, plan, lead_rows), out_shape=...  156 us
    pallas_call x2, Pallas kernels, gather_weights(): pl.pallas_call(functools.partial(gather_kernel, shapes, projection is not...  137 us
    pallas_call x1, Pallas kernels, attention_backward(): pl.pallas_call(functools.partial(backward_kernel, head_count, block_q, bl...  44.9 us
    all_to_all x7, starting transfers between devices, exchange(): lax.all_to_all(blocks, 'ctx', split_axis=0, concat_axis=0, tiled=True)  40.2 us
    pallas_call x1, Pallas kernels, attention_forward(): pl.pallas_call(functools.partial(forward_kernel, head_count, block_q, blo...  32.2 us
    dot_general x1, matrix products, per_device(): lax.dot_general(grad_mlp_low, out_full, NT, preferred_element_type=jnp.fl...  16.2 us
    all_to_all x7, waiting for transfers between devices, exchange(): lax.all_to_all(blocks, 'ctx', split_axis=0, concat_axis=0, tiled=True)  14 us
  transfers between devices with their start and end apart: 7, of which 3 were waited for; matrix products, arithmetic and copies ran while one was open for 12% of the time, Pallas kernels for 64%

commit v1 on v0

--- a/solution.py
+++ b/solution.py
@@ -140,11 +140,9 @@
     log_ref,
     cosine_ref,
     sine_ref,
-    out_ref,
-    turned_ref,
-    key_acc,
-    value_acc,
+    *refs,
 ):
+    out_ref, turned_ref, key_acc, value_acc = refs[-4:]
     width = attended_ref.shape[1]
     step = pl.program_id(0)
 
@@ -213,7 +211,7 @@
 
 
 def attention_backward(
-    qkv, attended, grads, log_total, begin, end, low, high, cosine, sine, head_count, block_q, block_k
+    qkv, attended, grads, log_total, begin, end, low, high, cosine, sine, after, head_count, block_q, block_k
 ):
     tokens = qkv.shape[0]
     width = head_count * HEAD_WIDTH
@@ -235,7 +233,8 @@
                 pl.BlockSpec((1, 1, head_count * block_q), lambda i, *_: (i, 0, 0)),
                 whole((tokens, width)),
                 whole((tokens, width)),
-            ],
+            ]
+            + [pl.BlockSpec(memory_space=pl.ANY)] * len(after),
             out_specs=whole((tokens, 3 * width)),
             scratch_shapes=[
                 pltpu.VMEM((width, tokens), jnp.bfloat16),
@@ -247,7 +246,7 @@
             flops=pairs * 1280, bytes_accessed=tokens * width * 30, transcendentals=pairs
         ),
         name="attention_backward",
-    )(low, high, begin, end, qkv, attended, grads, log_total, cosine, sine)
+    )(low, high, begin, end, qkv, attended, grads, log_total, cosine, sine, *after)
 
 
 def spans(places, lengths_row):
@@ -560,37 +559,76 @@
     return [whole.reshape(-1, whole.shape[-1]) for whole in held]
 
 
-def sum_kernel(plan, lead_rows, *refs):
-    weights = len(plan)
-    left_refs, right_refs = (refs[:weights], refs[weights : 2 * weights])
-    small_ref = refs[2 * weights]
-    out_refs = refs[2 * weights + 1 : 3 * weights + 1]
-    small_out = refs[3 * weights + 1]
-    scratch = list(refs[3 * weights + 2 :])
-    turned_refs = [scratch.pop(0) for weight in plan]
-    whole_refs = [scratch.pop(0) for weight in plan]
-    chunks = [(w, t) for w, (kind, count, width) in enumerate(plan) for t in range(count)]
-    units = {}
-    for number in range(len(chunks)):
-        for half in (0, 1):
-            units[number, half] = [scratch.pop(0) for stage in range(5)]
-    small_held = scratch.pop(0)
-    send_sem, recv_sem, local_sem, pair_send, pair_recv, small_send, small_recv, near_sem = scratch
-    own_ctx, own_shard = (lax.axis_index("ctx"), lax.axis_index("fsdp"))
-    core, chip = (own_ctx % 2, own_ctx // 2)
-    own_x, own_y = (chip % 2, chip // 2)
-    low_bit, high_bit = (own_shard % 2, own_shard // 2)
-    partners = [{"ctx": toggled(own_ctx, bit)} for bit in (1, 2, 4)]
-    partners += [{"fsdp": toggled(own_shard, bit)} for bit in (1, 2)]
-    barrier = pltpu.get_barrier_semaphore()
-    for partner in partners:
-        pl.semaphore_signal(
-            barrier, inc=1, device_id=partner, device_id_type=pl.DeviceIdType.MESH
-        )
-    pl.semaphore_wait(barrier, len(partners))
-    to_core, to_x, to_y, to_one, to_two = partners
-    pending = []
-
+def pair_steps(plan, lead_rows, left_refs, right_refs, turned_refs, whole_refs, sems, core, send_core):
+    pair_send, pair_recv, near_sem = sems
+    rows = left_refs[0].shape[0] if left_refs else 0
+    pairs = []
+    for w, (kind, count, width, deep, halves) in enumerate(plan):
+        span = count * width if kind == "rows" else 4 * width
+        if len(right_refs[w].shape) == 3:
+            own_half, other_half = (right_refs[w].at[core], right_refs[w].at[1 - core])
+        else:
+            own_half = right_refs[w].at[:, pl.ds(pl.multiple_of(core * span, span), span)]
+            other_half = right_refs[w].at[:, pl.ds(pl.multiple_of((1 - core) * span, span), span)]
+        near = pltpu.make_async_copy(own_half, whole_refs[w].at[pl.ds(0, rows)], near_sem.at[w])
+        near.start()
+        target = whole_refs[w].at[pl.ds(rows, rows)]
+        far = send_core(other_half, target, pair_send.at[2 * w], pair_recv.at[2 * w])
+        pairs.append([near, far])
+
+    def turn(w):
+        left, turned = (left_refs[w], turned_refs[w])
+        block = 512
+        for first in range(0, left.shape[1], block):
+            last = min(first + block, left.shape[1])
+            turned[first:last, :rows] = (
+                left[:, first:last].astype(jnp.float32).T.astype(jnp.bfloat16)
+            )
+        pairs[w].append(
+            send_core(
+                turned.at[:, pl.ds(0, rows)],
+                turned.at[:, pl.ds(rows, rows)],
+                pair_send.at[2 * w + 1],
+                pair_recv.at[2 * w + 1],
+            )
+        )
+
+    def multiply(w, t, first, second):
+        kind, count, width, deep, halves = plan[w]
+        if t == 0:
+            near, far, turned = pairs[w]
+            near.wait()
+            far.wait_recv()
+            turned.wait_recv()
+
+        def each(z, carried):
+            left = turned_refs[w][pl.ds(pl.multiple_of(z * deep, 16), deep), :]
+            if kind == "rows":
+                part = jnp.dot(
+                    left,
+                    whole_refs[w][:, t * width : (t + 1) * width],
+                    preferred_element_type=jnp.float32,
+                ).astype(jnp.bfloat16)
+                piece_rows = first.shape[3]
+                for s in range(4):
+                    first[z, s // 2, s % 2] = part[2 * s * piece_rows : (2 * s + 1) * piece_rows]
+                    second[z, s // 2, s % 2] = part[(2 * s + 1) * piece_rows : (2 * s + 2) * piece_rows]
+            else:
+                part = jnp.dot(
+                    left, whole_refs[w][...], preferred_element_type=jnp.float32
+                ).astype(jnp.bfloat16)
+                for s in range(4):
+                    piece = part[:, s * width : (s + 1) * width]
+                    first[z, s // 2, s % 2] = piece[:lead_rows]
+                    second[z, s // 2, s % 2] = piece[lead_rows:]
+            return carried
+
+        lax.fori_loop(0, 4, each, 0)
+
+    return (turn, multiply)
+
+
+def remote_send(pending):
     def send(source, target, sent, got, partner):
         copy = pltpu.make_async_remote_copy(
             src_ref=source,
@@ -604,49 +642,194 @@
         pending.append(copy)
         return copy
 
-    rows = left_refs[0].shape[-2]
-    pairs = []
-    for w, (kind, count, width) in enumerate(plan):
-        span = count * width if kind == "rows" else 4 * width
-        if len(right_refs[w].shape) == 3:
-            own_half, other_half = (right_refs[w].at[core], right_refs[w].at[1 - core])
-        else:
-            own_half = right_refs[w].at[:, pl.ds(pl.multiple_of(core * span, span), span)]
-            other_half = right_refs[w].at[:, pl.ds(pl.multiple_of((1 - core) * span, span), span)]
-        near = pltpu.make_async_copy(own_half, whole_refs[w].at[pl.ds(0, rows)], near_sem.at[w])
-        near.start()
-        far = send(
-            other_half,
-            whole_refs[w].at[pl.ds(rows, rows)],
-            pair_send.at[2 * w],
-            pair_recv.at[2 * w],
-            to_core,
-        )
-        pairs.append([near, far])
-
-    def turn(w):
-        left, turned = (left_refs[w], turned_refs[w])
-        if len(left.shape) == 3:
-            for z in range(left.shape[0]):
-                turned[z, :, :rows] = left[z].astype(jnp.float32).T.astype(jnp.bfloat16)
-        else:
-            deep = left.shape[1] // 4
-            for z in range(4):
-                turned[z, :, :rows] = (
-                    left[:, z * deep : (z + 1) * deep].astype(jnp.float32).T.astype(jnp.bfloat16)
+    return send
+
+
+def product_kernel(plan, lead_rows, *refs):
+    weights = len(plan)
+    left_refs, right_refs = (refs[:weights], refs[weights : 2 * weights])
+    out_refs = refs[2 * weights : 6 * weights]
+    scratch = list(refs[6 * weights :])
+    turned_refs = [scratch.pop(0) for weight in plan]
+    whole_refs = [scratch.pop(0) for weight in plan]
+    chunks = [(w, t) for w, entry in enumerate(plan) for t in range(entry[1])]
+    held = [(scratch.pop(0), scratch.pop(0)) for chunk in chunks]
+    pair_send, pair_recv, near_sem, store_sem = scratch
+    own_ctx = lax.axis_index("ctx")
+    core, chip = (own_ctx % 2, own_ctx // 2)
+    own_x, own_y = (chip % 2, chip // 2)
+    to_core = {"ctx": toggled(own_ctx, 1)}
+    barrier = pltpu.get_barrier_semaphore()
+    pl.semaphore_signal(barrier, inc=1, device_id=to_core, device_id_type=pl.DeviceIdType.MESH)
+    pl.semaphore_wait(barrier, 1)
+    pending = []
+    send = remote_send(pending)
+    turn, multiply = pair_steps(
+        plan,
+        lead_rows,
+        left_refs,
+        right_refs,
+        turned_refs,
+        whole_refs,
+        (pair_send, pair_recv, near_sem),
+        core,
+        lambda *copied: send(*copied, to_core),
+    )
+    for w in range(weights):
+        turn(w)
+    stores = []
+    for number, (w, t) in enumerate(chunks):
+        first, second = held[number]
+        multiply(w, t, first, second)
+        sides = (
+            lambda at: first.at[:, at, own_x],
+            lambda at: first.at[:, at, 1 - own_x],
+            lambda at: second.at[:, own_y, at],
+            lambda at: second.at[:, 1 - own_y, at],
+        )
+        for side, source_at in enumerate(sides):
+            for at in (0, 1):
+                copy = pltpu.make_async_copy(
+                    source_at(at),
+                    out_refs[4 * w + side].at[at, t],
+                    store_sem.at[8 * number + 2 * side + at],
                 )
-
-    def send_turned(w):
-        pairs[w].append(
-            send(
-                turned_refs[w].at[:, :, pl.ds(0, rows)],
-                turned_refs[w].at[:, :, pl.ds(rows, rows)],
-                pair_send.at[2 * w + 1],
-                pair_recv.at[2 * w + 1],
-                to_core,
-            )
-        )
-
+                copy.start()
+                stores.append(copy)
+    for copy in stores:
+        copy.wait()
+    for copy in pending:
+        copy.wait_send()
+
+
+def weight_plan(kind, left, right, count):
+    deep = left.shape[1] // 4
+    if kind == "rows":
+        span = right.shape[-1] // (1 if right.ndim == 3 else 2)
+        return (kind, count, span // count, deep, (deep // 8, deep // 8))
+    lead_rows = deep // 2 // 16 * 16
+    return (kind, count, right.shape[-1] // 8, deep, (lead_rows, deep - lead_rows))
+
+
+def plan_span(entry):
+    return entry[1] * entry[2] if entry[0] == "rows" else 4 * entry[2]
+
+
+def plan_lead(plan):
+    return max([0] + [entry[4][0] for entry in plan if entry[0] == "columns"])
+
+
+def pair_scratch(plan, tokens):
+    turned = [pltpu.VMEM((4 * entry[3], 2 * tokens), jnp.bfloat16) for entry in plan]
+    return turned + [pltpu.VMEM((2 * tokens, plan_span(entry)), jnp.bfloat16) for entry in plan]
+
+
+def early_sums(products):
+    plan = [weight_plan(*product) for product in products]
+    lefts, rights = ([product[1] for product in products], [product[2] for product in products])
+    vmem, anywhere, dma = (
+        pl.BlockSpec(memory_space=pltpu.VMEM),
+        pl.BlockSpec(memory_space=pl.ANY),
+        pltpu.SemaphoreType.DMA,
+    )
+    outs, held = ([], [])
+    for kind, count, width, deep, halves in plan:
+        for half in halves:
+            outs += [jax.ShapeDtypeStruct((2, count, 4, half, width), jnp.bfloat16)] * 2
+        for chunk in range(count):
+            held += [pltpu.VMEM((4, 2, 2, half, width), jnp.bfloat16) for half in halves]
+    chunk_count = sum(entry[1] for entry in plan)
+    scratch = pair_scratch(plan, lefts[0].shape[0]) + held
+    scratch += [dma((2 * len(plan),)), dma((2 * len(plan),)), dma((len(plan),)), dma((8 * chunk_count,))]
+    sides = pl.pallas_call(
+        functools.partial(product_kernel, plan, plan_lead(plan)),
+        out_shape=tuple(outs),
+        in_specs=[vmem] * len(plan) + [anywhere] * len(plan),
+        out_specs=(anywhere,) * len(outs),
+        scratch_shapes=scratch,
+        compiler_params=pltpu.CompilerParams(
+            collective_id=3, has_side_effects=True, vmem_limit_bytes=60 * 1024 * 1024
+        ),
+        name="early_products",
+    )(*lefts, *rights)
+    arrays = []
+    for w in range(len(plan)):
+        for part, bit in ((0, 2), (2, 4)):
+            kept, sent = sides[4 * w + part : 4 * w + part + 2]
+            arrays.append((kept, swap(sent, "ctx", bit)))
+    return (plan, arrays)
+
+
+def second_step(held, early):
+    plan, arrays = early
+    held, arrays = lax.optimization_barrier((held, arrays))
+    chip = lax.axis_index("ctx") // 2
+    flat = []
+    for at, (kept, arrived) in enumerate(arrays):
+        bit, own = ((4, chip // 2), (2, chip % 2))[at % 2]
+        other = [
+            lax.dynamic_index_in_dim(side, 1 - own, 0, keepdims=False).astype(jnp.float32)
+            for side in (kept, arrived)
+        ]
+        flat += [kept, arrived, swap((other[0] + other[1]).astype(jnp.bfloat16), "ctx", bit)]
+    return (held, (plan, flat))
+
+
+def sum_kernel(early, late, lead_rows, *refs):
+    weights, products = (len(early) + len(late), len(late))
+    left_refs, right_refs = (refs[:products], refs[products : 2 * products])
+    refs = refs[2 * products :]
+    early_refs, refs = (refs[: 6 * len(early)], refs[6 * len(early) :])
+    small_ref, out_refs, small_out = (refs[0], refs[1 : weights + 1], refs[weights + 1])
+    scratch = list(refs[weights + 2 :])
+    turned_refs = [scratch.pop(0) for weight in late]
+    whole_refs = [scratch.pop(0) for weight in late]
+    plan = early + late
+    chunks = [(w, t) for w, entry in enumerate(plan) for t in range(entry[1])]
+    early_count = sum(entry[1] for entry in early)
+    units = {}
+    for number in range(len(chunks)):
+        for half in (0, 1):
+            units[number, half] = [scratch.pop(0) for stage in range(5)]
+    small_held = scratch.pop(0)
+    send_sem, recv_sem, local_sem, load_sem, pair_send, pair_recv, small_send, small_recv, near_sem = scratch
+    own_ctx, own_shard = (lax.axis_index("ctx"), lax.axis_index("fsdp"))
+    core, chip = (own_ctx % 2, own_ctx // 2)
+    own_x, own_y = (chip % 2, chip // 2)
+    low_bit, high_bit = (own_shard % 2, own_shard // 2)
+    loads = {}
+    for number in range(early_count):
+        w, t = chunks[number]
+        for half in (0, 1):
+            own = own_y if half == 0 else own_x
+            kept, arrived, twice = early_refs[6 * w + 3 * half : 6 * w + 3 * half + 3]
+            for at, source in enumerate((kept.at[own, t], arrived.at[own, t], twice.at[t])):
+                slot = (number * 2 + half) * 3 + at
+                copy = pltpu.make_async_copy(source, units[number, half][at], load_sem.at[slot])
+                copy.start()
+                loads[number, half, at] = copy
+    partners = [{"ctx": toggled(own_ctx, bit)} for bit in (1, 2, 4)]
+    partners += [{"fsdp": toggled(own_shard, bit)} for bit in (1, 2)]
+    barrier = pltpu.get_barrier_semaphore()
+    for partner in partners:
+        pl.semaphore_signal(
+            barrier, inc=1, device_id=partner, device_id_type=pl.DeviceIdType.MESH
+        )
+    pl.semaphore_wait(barrier, len(partners))
+    to_core, to_x, to_y, to_one, to_two = partners
+    pending = []
+    send = remote_send(pending)
+    turn, multiply = pair_steps(
+        late,
+        lead_rows,
+        left_refs,
+        right_refs,
+        turned_refs,
+        whole_refs,
+        (pair_send, pair_recv, near_sem),
+        core,
+        lambda *copied: send(*copied, to_core),
+    )
     copies = {}
 
     def hop(number, half, stage, source, target, partner):
@@ -655,41 +838,9 @@
             source, target, send_sem.at[slot], recv_sem.at[slot], partner
         )
 
-    def product(number):
+    def stage_one(number):
         w, t = chunks[number]
-        kind, count, width = plan[w]
-        if t == 0:
-            near, far, turned = pairs[w]
-            near.wait()
-            far.wait_recv()
-            turned.wait_recv()
-        first, second = (units[number, 0][0], units[number, 1][0])
-
-        def each(z, carried):
-            if kind == "rows":
-                part = jnp.dot(
-                    turned_refs[w][z],
-                    whole_refs[w][:, t * width : (t + 1) * width],
-                    preferred_element_type=jnp.float32,
-                ).astype(jnp.bfloat16)
-                deep = first.shape[3]
-                for s in range(4):
-                    first[z, s // 2, s % 2] = part[2 * s * deep : (2 * s + 1) * deep]
-                    second[z, s // 2, s % 2] = part[(2 * s + 1) * deep : (2 * s + 2) * deep]
-            else:
-                part = jnp.dot(
-                    turned_refs[w][z], whole_refs[w][...], preferred_element_type=jnp.float32
-                ).astype(jnp.bfloat16)
-                column = first.shape[4]
-                for s in range(4):
-                    piece = part[:, s * column : (s + 1) * column]
-                    first[z, s // 2, s % 2] = piece[:lead_rows]
-                    second[z, s // 2, s % 2] = piece[lead_rows:]
-            return carried
-
-        lax.fori_loop(0, 4, each, 0)
-
-    def stage_one(number):
+        multiply(w - len(early), t, units[number, 0][0], units[number, 1][0])
         hop(number, 0, 0, units[number, 0][0].at[:, :, 1 - own_x], units[number, 0][1], to_x)
         hop(number, 1, 0, units[number, 1][0].at[:, 1 - own_y], units[number, 1][1], to_y)
 
@@ -714,10 +865,16 @@
 
     def stage_three(number):
         for half in (0, 1):
-            held, got = (units[number, half][1], units[number, half][2])
+            kept, held, got = units[number, half][:3]
             own = own_y if half == 0 else own_x
-            copies[number, half, 1].wait_recv()
-            add(got, lambda z: held[z, own], 4)
+            if number < early_count:
+                for at in range(3):
+                    loads[number, half, at].wait()
+                add(held, lambda z: kept[z], 4)
+                add(got, lambda z: held[z], 4)
+            else:
+                copies[number, half, 1].wait_recv()
+                add(got, lambda z: held[z, own], 4)
         for half in (0, 1):
             got = units[number, half][2]
             for high in (0, 1):
@@ -742,7 +899,7 @@
 
     def final_region(number, half, chip_at):
         w, t = chunks[number]
-        kind, count, width = plan[w]
+        kind, count, width = plan[w][:3]
         deep = units[number, half][4].shape[1]
         if kind == "rows":
             start = pl.multiple_of((2 * chip_at + half) * deep, deep)
@@ -751,7 +908,7 @@
         column = pl.multiple_of((core * 4 + chip_at) * width, width)
         return out_refs[w].at[pl.ds(half * lead_rows, deep), pl.ds(column, width)]
 
-    local = []
+    local = {}
 
     def stage_five(number):
         for half in (0, 1):
@@ -765,7 +922,7 @@
             hop(number, half, 5, got, target, to_y if half == 0 else to_x)
             copy = pltpu.make_async_copy(got, target, local_sem.at[number * 2 + half])
             copy.start()
-            local.append(copy)
+            local[number, half] = copy
 
     def stage_six(number):
         for half in (0, 1):
@@ -775,11 +932,11 @@
 
     def stage_seven(number):
         w, t = chunks[number]
-        kind, count, width = plan[w]
+        kind, count, width = plan[w][:3]
         for half in (0, 1):
             copies[number, half, 5].wait_recv()
             copies[number, half, 7].wait_recv()
-            local[number * 2 + half].wait()
+            local[number, half].wait()
         span = width if kind == "rows" else 4 * width
         at = core * count + t if kind == "rows" else core
         piece = out_refs[w].at[:, pl.ds(pl.multiple_of(at * span, span), span)]
@@ -811,28 +968,17 @@
         else:
             small_out[1] = small_held[10]
 
-    turn(0)
-    for w in range(1, weights):
+    stages = (stage_one, stage_two, stage_three, stage_four, stage_five, stage_six, stage_seven)
+    small_at = 0
+    stage_three(0)
+    for w in range(len(late)):
         turn(w)
-        send_turned(w - 1)
-    stages = [
-        (stage_two, 1),
-        (stage_three, 2),
-        (stage_four, 3),
-        (stage_five, 4),
-        (stage_six, 5),
-        (stage_seven, 6),
-    ]
-    small_at = 0
-    for tick in range(len(chunks) + 7):
-        if tick < len(chunks):
-            product(tick)
-            if tick == 0:
-                send_turned(weights - 1)
-            stage_one(tick)
-        for stage, lag in stages:
-            if 0 <= tick - lag < len(chunks):
-                stage(tick - lag)
+    for tick in range(len(chunks) + len(stages)):
+        for lag, stage in enumerate(stages):
+            for number in range(len(chunks)):
+                start = number - 2 if number < early_count else number - early_count
+                if start + lag == tick and (number >= early_count or (lag >= 2 and number + lag > 2)):
+                    stage(number)
         if small_at < 6:
             small_step(small_at)
             small_at += 1
@@ -842,56 +988,41 @@
         copy.wait_send()
 
 
-def sum_weights(products, small):
-    rows = small.shape[0]
-    plan, scratch, outs, lefts, rights, turned, whole, pieces = ([], [], [], [], [], [], [], [])
-    lead_rows = 0
-    for kind, left, right, count in products:
-        tokens = left.shape[-2]
-        if kind == "rows":
-            deep = left.shape[1] // 4
-            span = right.shape[-1] // (1 if right.ndim == 3 else 2)
-            width = span // count
-            outs.append(jax.ShapeDtypeStruct((deep, 2 * span), jnp.bfloat16))
-            halves = (deep // 8, deep // 8)
-        else:
-            deep = left.shape[2]
-            span = right.shape[-1] // 2
-            width = span // 4
-            lead_rows = deep // 2 // 16 * 16
-            outs.append(jax.ShapeDtypeStruct((deep, 2 * span), jnp.bfloat16))
-            halves = (lead_rows, deep - lead_rows)
-        plan.append((kind, count, width))
-        lefts.append(left)
-        rights.append(right)
-        turned.append(pltpu.VMEM((4, deep, 2 * tokens), jnp.bfloat16))
-        whole.append(pltpu.VMEM((2 * tokens, span), jnp.bfloat16))
+def sum_weights(early, early_arrays, products, small):
+    late = [weight_plan(*product) for product in products]
+    lefts, rights = ([product[1] for product in products], [product[2] for product in products])
+    plan = early + late
+    pieces = []
+    for w, (kind, count, width, deep, halves) in enumerate(plan):
+        leads = [(4, 2, 2), (4, 2), (4,), (2,), (1,)]
+        if w < len(early):
+            leads[:2] = [(4,), (4,)]
         for chunk in range(count):
-            for deep_half in halves:
-                for lead in ((4, 2, 2), (4, 2), (4,), (2,), (1,)):
-                    pieces.append(pltpu.VMEM(lead + (deep_half, width), jnp.bfloat16))
-    chunk_count = sum(count for kind, count, width in plan)
-    scratch = turned + whole + pieces
+            for half in halves:
+                pieces += [pltpu.VMEM(lead + (half, width), jnp.bfloat16) for lead in leads]
+    outs = [jax.ShapeDtypeStruct((entry[3], 2 * plan_span(entry)), jnp.bfloat16) for entry in plan]
+    chunk_count = sum(entry[1] for entry in plan)
+    scratch = pair_scratch(late, lefts[0].shape[0]) + pieces
     scratch += [pltpu.VMEM((11,) + small.shape, jnp.float32)]
     dma = pltpu.SemaphoreType.DMA
     slots = chunk_count * 17
-    scratch += [dma((slots,)), dma((slots,)), dma((2 * chunk_count,))]
-    scratch += [dma((2 * len(plan),)), dma((2 * len(plan),)), dma((5,)), dma((5,)), dma((len(plan),))]
+    scratch += [dma((slots,)), dma((slots,)), dma((2 * chunk_count,)), dma((6 * chunk_count,))]
+    scratch += [dma((2 * len(late),)), dma((2 * len(late),)), dma((5,)), dma((5,)), dma((len(late),))]
     vmem, anywhere = (
         pl.BlockSpec(memory_space=pltpu.VMEM),
         pl.BlockSpec(memory_space=pl.ANY),
     )
     return pl.pallas_call(
-        functools.partial(sum_kernel, plan, lead_rows),
+        functools.partial(sum_kernel, early, late, plan_lead(plan)),
         out_shape=tuple(outs) + (jax.ShapeDtypeStruct((2,) + small.shape, jnp.float32),),
-        in_specs=[vmem] * len(plan) + [anywhere] * len(plan) + [vmem],
+        in_specs=[vmem] * len(late) + [anywhere] * (len(late) + len(early_arrays)) + [vmem],
         out_specs=(anywhere,) * len(plan) + (vmem,),
         scratch_shapes=scratch,
         compiler_params=pltpu.CompilerParams(
             collective_id=1, has_side_effects=True, vmem_limit_bytes=60 * 1024 * 1024
         ),
         name="sum_weights",
-    )(*lefts, *rights, small)
+    )(*lefts, *rights, *early_arrays, small)
 
 
 def layer_norm(rows_in, gain_vec):
@@ -1022,11 +1153,12 @@
     attn_low,
     grad_attn_low,
     small,
+    early,
 ):
     shards, ctx_count = (lax.axis_size("fsdp"), lax.axis_size("ctx"))
     rows, ff_width = hidden.shape
     model_width = act_mlp.shape[1]
-    if shards != 4 or ctx_count != 8 or model_width % 1024 != 0 or ff_width % 64 != 0:
+    if early is None:
         half, half_three = (model_width // 2, 3 * model_width // 2)
         pairs = (
             (hidden, grad_mlp_low[:, :half], grad_mlp_low[:, half:]),
@@ -1039,6 +1171,23 @@
         ]
         over_pack = sum_over(small, ("ctx",))
         return totals + [jnp.stack([over_pack, sum_over(over_pack, ("fsdp",))])]
+    total_out, total_in, total_attn, total_qkv, small_sums = sum_weights(
+        *early, [("rows", act_attn, grad_projected, 3)], small
+    )
+    padded = total_in.shape[1] // 2
+    total_in = jnp.concatenate(
+        [total_in[:, :ff_width], total_in[:, padded : padded + ff_width]], axis=1
+    )
+    return [
+        total.astype(jnp.float32) for total in (total_out, total_in, total_qkv, total_attn)
+    ] + [small_sums]
+
+
+def weight_sums_early(hidden, grad_mlp_low, act_mlp, grad_leading, grad_trailing, attn_low, grad_attn_low):
+    shards, ctx_count = (lax.axis_size("fsdp"), lax.axis_size("ctx"))
+    ff_width = hidden.shape[1]
+    if shards != 4 or ctx_count != 8 or act_mlp.shape[1] % 1024 != 0 or ff_width % 64 != 0:
+        return None
     padded = -(-ff_width // 384) * 384
     sides = jnp.stack(
         [
@@ -1046,22 +1195,13 @@
             for side in (grad_leading, grad_trailing)
         ]
     )
-    by_shard = jnp.transpose(hidden.reshape(rows, shards, ff_width // shards), (1, 0, 2))
-    total_out, total_in, total_qkv, total_attn, small_sums = sum_weights(
+    return early_sums(
         [
-            ("columns", by_shard, grad_mlp_low, 1),
+            ("columns", hidden, grad_mlp_low, 1),
             ("rows", act_mlp, sides, 3),
-            ("rows", act_attn, grad_projected, 3),
             ("rows", attn_low, grad_attn_low, 1),
-        ],
-        small,
-    )
-    total_in = jnp.concatenate(
-        [total_in[:, :ff_width], total_in[:, padded : padded + ff_width]], axis=1
-    )
-    return [
-        total.astype(jnp.float32) for total in (total_out, total_in, total_qkv, total_attn)
-    ] + [small_sums]
+        ]
+    )
 
 
 def per_device(
@@ -1192,6 +1332,9 @@
     grad_attended = lax.dot_general(
         grad_attn_low, attn_full, NT, preferred_element_type=jnp.float32
     ).astype(jnp.bfloat16)
+    early = weight_sums_early(
+        hidden, grad_mlp_low, act_mlp, grad_leading, grad_trailing, attn_low, grad_attn_low
+    )
     pack_cosine, pack_sine = rotary_tables(pack_offset, own_heads)
     block_back = math.gcd(tokens, 256)
     low_back, high_back = key_range(pack_begin[0], pack_end[0], block_q, block_back)
@@ -1206,10 +1349,13 @@
         high_back,
         pack_cosine,
         pack_sine,
+        [] if early is None else [early[1][0][0]],
         own_heads,
         block_q,
         block_back,
     )
+    if early is not None:
+        grad_heads, early = second_step(grad_heads, early)
     grad_projected = jnp.transpose(
         to_rows(grad_heads).reshape(ctx_count, row_count, 3, own_width), (1, 2, 0, 3)
     ).reshape(row_count, 3 * model_width)
@@ -1236,6 +1382,7 @@
         attn_low,
         grad_attn_low,
         small,
+        early,
     )
     total_gain_one = own_shard(small_sums[1, 0])
     total_gain_two = own_shard(small_sums[1, 1])

time: 584 us -> 574 us (0.983)
  Pallas kernels: 369 us -> 314 us
  waiting for transfers between devices: 14 us -> 50 us
  other arithmetic: 62.6 us -> 75.5 us
  starting transfers between devices: 40.2 us -> 48.9 us
  local copies, waits for them, and re-layouts: 38.3 us -> 30.8 us
    pallas_call x1 -> x2, Pallas kernels: 156 us -> 106 us  [the longest x1 82.4 us: sum_weights(): pl.pallas_call(functools.partial(sum_kernel, early, late, plan_lead(plan)...]
    ppermute x0 -> x12, waiting for transfers between devices: none -> 38.1 us  [swap(): return lax.ppermute(value, axis, pairs)]
    ppermute x0 -> x12, starting transfers between devices: none -> 11.5 us  [swap(): return lax.ppermute(value, axis, pairs)]
    convert_element_type x1 -> x7, other arithmetic: 0.3 us -> 11.5 us  [the longest x6 9.81 us: second_step(): (other[0] + other[1]).astype(jnp.bfloat16)]
  transfers between devices with their start and end apart: 7 -> 19, of which waited for: 3 -> 4; matrix products, arithmetic and copies ran while one was open for 12% -> 15% of each run, Pallas kernels for 64% -> 56%
where the time goes in v1:
time: 574 us; the launch traced here: 565 us
  Pallas kernels  314 us (55%)
  other arithmetic  75.5 us (13%)
  waiting for transfers between devices  50 us (9%)
  starting transfers between devices  48.9 us (9%)
  matrix products  43.4 us (8%)
  local copies, waits for them, and re-layouts  30.8 us (5%)
    pallas_call x2, Pallas kernels, gather_weights(): pl.pallas_call(functools.partial(gather_kernel, shapes, projection is not...  137 us
    pallas_call x1, Pallas kernels, sum_weights(): pl.pallas_call(functools.partial(sum_kernel, early, late, plan_lead(plan)...  82.4 us
    pallas_call x1, Pallas kernels, attention_backward(): pl.pallas_call(functools.partial(backward_kernel, head_count, block_q, bl...  42.5 us
    ppermute x12, waiting for transfers between devices, swap(): return lax.ppermute(value, axis, pairs)  38.1 us
    all_to_all x7, starting transfers between devices, exchange(): lax.all_to_all(blocks, 'ctx', split_axis=0, concat_axis=0, tiled=True)  37.4 us
    pallas_call x1, Pallas kernels, attention_forward(): pl.pallas_call(functools.partial(forward_kernel, head_count, block_q, blo...  29.5 us
    pallas_call x1, Pallas kernels, early_sums(): pl.pallas_call(functools.partial(product_kernel, plan, plan_lead(plan)),...  23.1 us
    dot_general x1, matrix products, per_device(): lax.dot_general(grad_mlp_low, out_full, NT, preferred_element_type=jnp.fl...  13.7 us
  transfers between devices with their start and end apart: 19, of which 4 were waited for; matrix products, arithmetic and copies ran while one was open for 15% of the time, Pallas kernels for 56%

profile of v1, /device:TPU:1, one launch (start us, length us, event | category | flops | bytes accessed | tf_op | source)
XLA Modules:
  0.0 565.3 jit_solution(12816168531010834979)
XLA Ops:
  3.1 1.3 broadcast_select_fusion.2
  4.4 5.2 all-to-all-start
  11.7 39.7 %gather_weights.1 = (bf16[4,16,256]{2,1,0:T(8,128)(2,1)}, bf16[4,2,4,32,3072]{4,3,2,1,0:T(8,128)(2,1)}) custom-call(bf16[16,256]{1,0:T(8,128)(2,1)} %fusion.36.refs_0_, bf16[2,4,32,3072]{3,2,1,0:T(8,128)(2,1)} %bitcast.150), custom_call_target="tpu_custom_call" | custom-call | tf_op jit(solution)/shard_map/gather_weights/pallas_call | solution.py:546
  54.6 1.1 pad_maximum_fusion.3
  55.7 1.3 compare_select_fusion.1
  57.0 3.5 all-to-all-start.3
  61.3 1.2 fusion.16.refs_3_.refs_0_
  62.4 97.0 %gather_and_project.1 = (bf16[4,2,4,32,1024]{4,3,2,1,0:T(8,128)(2,1)}, bf16[4,2,4,32,5248]{4,3,2,1,0:T(8,128)(2,1)}, bf16[4,656,1024]{2,1,0:T(8,128)(2,1)}, bf16[3072,384]{1,0:T(8,128)(2,1)}) custom-call(bf16[2,4,32,1024]{3,2,1,0:T(8,128)(2,1)} %bitcast.156, bf16[2,4,32,5248]{3,2,1,0:T(8,128)(2,1)} %bitcast.146, bf16[656,1024]{1,0:T(8,128)(2,1)} %refs_2_.1, ...), custom_call_target="tpu_custom_call" | custom-call | tf_op jit(solution)/shard_map/gather_and_project/pallas_call | solution.py:546
  159.4 29.5 %attention_forward.1 = (f32[3072,128]{1,0:T(8,128)}, f32[12,1,512]{2,1,0:T(1,128)}) custom-call(s32[12]{0:T(128)} %get-tuple-element.126.low_ref, s32[12]{0:T(128)} %get-tuple-element.127.high_ref, s32[1,3072]{1,0:T(1,128)} %get-tuple-element.141.begin_ref, s32[1,3072]{1,0:T(1,128)} %get-tuple-element.140.end_ref, bf16[3072,384]{1,0:T(8,128)(2,1)} %get-tuple-element.50.qkv_ref), custom_call_target="tpu_custom_call" | custom-call | flops 2415919104 | bytes 4718592 | tf_op jit(solution)/shard_map/attention_forward/pallas_call | solution.py:97
  188.9 2.4 convert_element_type.303
  191.3 3.7 all-to-all-start.1
  196.3 1.1 select_convert_fusion
  197.4 6.6 %all-to-all-done.1 = bf16[8,384,128]{2,1,0:T(8,128)(2,1)S(1)} async-done(((bf16[8,384,128]{2,1,0:T(8,128)(2,1)}), bf16[8,384,128]{2,1,0:T(8,128)(2,1)S(1)}, u32[]{:S(2)}, u32[]{:S(2)}) %all-to-all-start.1) | async-done | bytes 786464 | tf_op jit(solution)/shard_map/all_to_all | solution.py:1237
  204.0 4.1 fusion.48
  209.5 4.5 fusion.52
  214.1 13.7 %add_convert_fusion = (bf16[384,2624]{1,0:T(8,128)(2,1)}, f32[384,2624]{1,0:T(8,128)}, f32[384,2624]{1,0:T(8,128)}) fusion(f32[384,5248]{1,0:T(8,128)S(1)} %fusion.52, bf16[384,1024]{1,0:T(8,128)(2,1)S(1)} %bitcast.153, bf16[2624,1024]{1,0:T(8,128)(2,1)S(1)} %bitcast.181), kind=kOutput, calls=%fused_computation.8 | convolution fusion | flops 2137153536 | bytes 24297472 | tf_op jit(solution)/shard_map/dot_general | solution.py:1313
  227.8 7.1 %multiply_convert_fusion = (bf16[384,2624]{1,0:T(8,128)(2,1)}, bf16[384,2624]{1,0:T(8,128)(2,1)}) fusion(f32[384,2624]{1,0:T(8,128)} %get-tuple-element.135, f32[384,2624]{1,0:T(8,128)} %get-tuple-element.104, f32[384,5248]{1,0:T(8,128)S(1)} %fusion.52), kind=kLoop, calls=%fused_computation.7 | loop fusion | flops 6045696 | bytes 20152320 | tf_op jit(solution)/shard_map/convert_element_type | solution.py:1324
  234.9 3.2 pad_bitcast_fusion
  238.0 7.5 %fusion.6 = f32[384,1024]{1,0:T(8,128)S(1)} fusion(bf16[1024,5248]{1,0:T(8,128)(2,1)} %bitcast.176, bf16[384,2624]{1,0:T(8,128)(2,1)S(1)} %copy-done.3, bf16[384,2624]{1,0:T(8,128)(2,1)S(1)} %copy-done.14), kind=kOutput, calls=%fused_computation.23 | convolution fusion | flops 4135256064 | bytes 16351232 | tf_op jit(solution)/shard_map/dot_general | solution.py:1327
  245.6 1.5 pad_bitcast_fusion.1
  248.3 7.0 %multiply_reduce_fusion = (f32[]{:T(128)}, f32[]{:T(128)}, f32[384]{0:T(512)S(1)}, f32[1024]{0:T(1024)}, f32[]{:T(128)}, /*index=5*/bf16[384,1024]{1,0:T(8,128)(2,1)}) fusion(f32[384,1024]{1,0:T(8,128)S(1)} %get-tuple-element.106, pred[384]{0:T(512)(128)(4,1)S(1)} %fusion.37, f32[384,1024]{1,0:T(8,128)S(1)} %fusion.6, f32[1024]{0:T(1024)S(1)} %bitcast.164, ...), kind=kOutput, calls=%fused_computation.56 | convolution fusion | flops 2070674048 | bytes 12907404 | tf_op jit(solution)/shard_map/dot_general | solution.py:1300
  256.0 1.2 fusion.21
  257.8 1.0 fusion.22
  258.8 1.0 copy.63
  259.9 7.6 %all-to-all-start.4 = ((bf16[8,384,128]{2,1,0:T(8,128)(2,1)}), bf16[8,384,128]{2,1,0:T(8,128)(2,1)}, u32[]{:S(2)}, u32[]{:S(2)}) async-start(bf16[8,384,128]{2,1,0:T(8,128)(2,1)} %bitcast.145), calls=%async_computation.4 | async-start | bytes 1572864 | tf_op jit(solution)/shard_map/all_to_all | solution.py:1237
  267.4 4.7 pad_maximum_fusion.refs_4_
  273.1 23.1 %early_products.1 = (bf16[2,1,4,320,128]{4,3,2,1,0:T(8,128)(2,1)}, bf16[2,1,4,320,128]{4,3,2,1,0:T(8,128)(2,1)}, bf16[2,1,4,336,128]{4,3,2,1,0:T(8,128)(2,1)}, b...) custom-call(bf16[384,2624]{1,0:T(8,128)(2,1)} %get-tuple-element.110, ...), custom_call_target="tpu_custom_call" | custom-call | tf_op jit(solution)/shard_map/early_products/pallas_call | solution.py:744
  296.2 1.4 collective-permute-start.2
  297.6 1.2 collective-permute-start.3
  298.8 8.3 %multiply_sine_fusion = (f32[3072,32]{1,0:T(8,128)}, f32[3072,32]{1,0:T(8,128)}, f32[3072,32]{1,0:T(8,128)}) fusion(f32[3072]{0:T(1024)S(1)} %subtract_convert_fusion, f32[32]{0:T(128)S(1)} %multiply_power_fusion), kind=kLoop, calls=%fused_computation.33 | loop fusion | flops 196608 | bytes 1192064 | tf_op jit(solution)/shard_map/sin | solution.py:273
  307.4 1.4 collective-permute-start.4
  308.8 6.2 %all-to-all-start.2 = ((bf16[8,48,1024]{2,1,0:T(8,128)(2,1)}), bf16[8,48,1024]{2,1,0:T(8,128)(2,1)}, u32[]{:S(2)}, u32[]{:S(2)}) async-start(bf16[8,48,1024]{2,1,0:T(8,128)(2,1)} %bitcast.152), calls=%async_computation.2 | async-start | bytes 1572864 | tf_op jit(solution)/shard_map/all_to_all | solution.py:1237
  315.0 9.3 %pad_maximum_fusion.1 = (f32[3072,128]{1,0:T(8,128)}, f32[3072,128]{1,0:T(8,128)}) fusion(f32[3072,32]{1,0:T(8,128)} %get-tuple-element.122, f32[3072,32]{1,0:T(8,128)} %get-tuple-element.121, f32[3072,32]{1,0:T(8,128)} %get-tuple-element.120), kind=kLoop, calls=%fused_computation.37 | loop fusion | flops 2359296 | bytes 4325376 | tf_op jit(solution)/shard_map/concatenate | solution.py:275
  324.3 23.4 %collective-permute-done.4.refs_15_ = bf16[2,1,4,32,512]{4,3,2,1,0:T(8,128)(2,1)S(1)} collective-permute-done((bf16[2,1,4,32,512]{4,3,2,1,0:T(8,128)(2,1)}, bf16[2,1,4,32,512]{4,3,2,1,0:T(8,128)(2,1)S(1)}, u32[]{:S(2)}, u32[]{:S(2)}) %collective-permute-start.4) | collective-permute-done | bytes 262176 | tf_op jit(solution)/shard_map/ppermute | solution.py:1045
  347.7 1.1 collective-permute-start.5
  348.9 42.5 %attention_backward.1 = bf16[3072,384]{1,0:T(8,128)(2,1)} custom-call(s32[12]{0:T(128)} %get-tuple-element.101.low_ref, s32[12]{0:T(128)} %get-tuple-element.102.high_ref, s32[1,3072]{1,0:T(1,128)} %get-tuple-element.141.begin_ref, s32[1,3072]{1,0:T(1,128)} %get-tuple-element.140.end_ref, bf16[3072,384]{1,0:T(8,128)(2,1)} %get-tuple-element.50.qkv_ref, ...), custom_call_target="tpu_custom_call" | custom-call | flops 6039797760 | bytes 11796480 | tf_op jit(solution)/shard_map/attention_backward/pallas_call | solution.py:221
  391.4 4.3 copy.47
  395.7 6.7 %all-to-all-start.5 = ((bf16[8,384,384]{1,2,0:T(8,128)(2,1)}), bf16[8,384,384]{1,2,0:T(8,128)(2,1)}, u32[]{:S(2)}, u32[]{:S(2)}) async-start(bf16[8,384,384]{1,2,0:T(8,128)(2,1)} %copy.47), calls=%async_computation.5 | async-start | bytes 4718592 | tf_op jit(solution)/shard_map/all_to_all | solution.py:1237
  403.7 2.6 select_maximum_fusion
  406.3 2.6 gather_fusion.1
  408.9 2.0 fusion.28
  411.0 1.4 collective-permute-start.6
  412.3 1.9 fusion.27
  414.3 1.2 collective-permute-start.7
  415.5 2.1 fusion.24
  417.9 2.1 fusion.25
  420.8 1.3 collective-permute-start.10
  423.1 5.3 all-to-all-done.5
  428.3 4.4 copy.48
  432.8 5.7 %fusion.18 = (f32[384]{0:T(512)S(1)}, f32[384,1024]{1,0:T(8,128)S(1)}) fusion(bf16[8,48,1024]{2,1,0:T(8,128)(2,1)S(1)} %all-to-all-done, f32[1024]{0:T(1024)S(1)} %bitcast.160, f32[384]{0:T(512)S(1)} %div.127, bf16[1024,3072]{1,0:T(8,128)(2,1)} %bitcast.144, bf16[48,8,24,128]{3,2,1,0:T(8,128)(2,1)} %bitcast.140), kind=kOutput, calls=%fused_computation.51 | convolution fusion | flops 2417884672 | bytes 11017216 | tf_op jit(solution)/shard_map/dot_general | solution.py:1362
  438.5 1.3 fusion.17
  439.8 14.7 %collective-permute-done.10.refs_16_ = bf16[1,4,32,512]{3,2,1,0:T(8,128)(2,1)S(1)} collective-permute-done((bf16[1,4,32,512]{3,2,1,0:T(8,128)(2,1)}, bf16[1,4,32,512]{3,2,1,0:T(8,128)(2,1)S(1)}, u32[]{:S(2)}, u32[]{:S(2)}) %collective-permute-start.10) | collective-permute-done | bytes 131104 | tf_op jit(solution)/shard_map/ppermute | solution.py:1045
  454.5 1.7 collective-permute-start.11
  456.2 1.7 add_convert_fusion.1
  457.9 2.0 copy.62
  459.9 4.5 all-to-all-start.6
  465.8 82.4 %sum_weights.1 = (bf16[656,1024]{1,0:T(8,128)(2,1)}, bf16[256,5376]{1,0:T(8,128)(2,1)}, bf16[256,1024]{1,0:T(8,128)(2,1)}, bf16[256,3072]{1,0:T(8,128)(2,1)}, f32[2,8,1024]{2,1,0:T(8,128)}) custom-call(bf16[384,1024]{1,0:T(8,128)(2,1)} %fusion.16.refs_3_.refs_0_, bf16[384,3072]{1,0:T(8,128)(2,1)} %bitcast.142, ...), custom_call_target="tpu_custom_call" | custom-call | tf_op jit(solution)/shard_map/sum_weights/pallas_call | solution.py:1015
  549.1 3.6 convert_element_type.345
  552.7 1.1 convert_element_type.346
  555.1 1.1 copy-done.16
  556.2 1.9 convert_element_type.348
  558.1 1.2 sqrt_bitcast_fusion
  559.3 3.0 maximum_convert_fusion
  563.4 1.3 broadcast_select_fusion
  (159 shorter events, 22.2 us)
Async XLA Ops:
  0.6 1.2 copy-start
  0.7 1.7 copy-start.17
  3.0 6.6 %copy-start.31 = (s32[1,6]{1,0:T(1,128)S(1)}, s32[1,6]{1,0:T(1,128)}, u32[]{:S(2)}) copy-start(s32[1,6]{1,0:T(1,128)} %param.14) | copy-start | bytes 76
  3.0 8.0 %copy-start.37 = (bf16[256]{0:T(256)(128)(2,1)S(1)}, bf16[256]{0:T(256)(128)(2,1)}, u32[]{:S(2)}) copy-start(bf16[256]{0:T(256)(128)(2,1)} %param.19) | copy-start | bytes 1540
  3.0 8.0 %copy-start.38 = (bf16[256]{0:T(256)(128)(2,1)S(1)}, bf16[256]{0:T(256)(128)(2,1)}, u32[]{:S(2)}) copy-start(bf16[256]{0:T(256)(128)(2,1)} %param.16) | copy-start | bytes 1540
  4.4 52.6 %all-to-all-start = ((bf16[8,48,1024]{2,1,0:T(8,128)(2,1)}), bf16[8,48,1024]{2,1,0:T(8,128)(2,1)S(1)}, u32[]{:S(2)}, u32[]{:S(2)}) async-start(bf16[8,48,1024]{2,1,0:T(8,128)(2,1)} %get-tuple-element.133), calls=%async_computation | async-start | bytes 1572864 | tf_op jit(solution)/shard_map/all_to_all | solution.py:1237
  57.0 134.3 %all-to-all-start.3 = ((bf16[8,48,1024]{2,1,0:T(8,128)(2,1)}), bf16[8,48,1024]{2,1,0:T(8,128)(2,1)S(1)}, u32[]{:S(2)}, u32[]{:S(2)}) async-start(bf16[8,48,1024]{2,1,0:T(8,128)(2,1)} %get-tuple-element.132), calls=%async_computation.3 | async-start | bytes 1572864 | tf_op jit(solution)/shard_map/all_to_all | solution.py:1237
  61.2 98.2 %copy-start.26 = (f32[384]{0:T(512)}, f32[384]{0:T(512)S(1)}, u32[]{:S(2)}) copy-start(f32[384]{0:T(512)S(1)} %add.177) | copy-start | bytes 4612
  191.3 12.7 %all-to-all-start.1 = ((bf16[8,384,128]{2,1,0:T(8,128)(2,1)}), bf16[8,384,128]{2,1,0:T(8,128)(2,1)S(1)}, u32[]{:S(2)}, u32[]{:S(2)}) async-start(bf16[8,384,128]{2,1,0:T(8,128)(2,1)} %bitcast.16), calls=%async_computation.1 | async-start | bytes 1572864 | tf_op jit(solution)/shard_map/all_to_all | solution.py:1237
  195.6 60.4 %copy-start.33 = (pred[384]{0:T(512)(128)(4,1)}, pred[384]{0:T(512)(128)(4,1)S(1)}, u32[]{:S(2)}) copy-start(pred[384]{0:T(512)(128)(4,1)S(1)} %fusion.37) | copy-start | bytes 1156
  204.0 4.1 copy-start.5
  204.0 5.5 copy-start.36
  208.4 5.7 %slice-start = ((s8[5373952]{0:T(1024)(128)(4,1)}), s8[4194304]{0:T(1024)(128)(4,1)S(1)}, s32[]{:S(2)}) async-start(s8[5373952]{0:T(1024)(128)(4,1)} %bitcast.179), calls=%async_computation.7 | async-start | bytes 8388608
  208.7 5.4 copy-start.7
  209.5 4.5 copy-start.18
  209.5 4.5 slice-start.1
  234.9 3.2 copy-start.3
  234.9 3.2 copy-start.14
  245.6 2.3 copy-start.4
  245.6 2.8 copy-start.15
  255.9 1.9 copy-start.13
  257.2 1.7 copy-start.8
  259.9 48.9 %all-to-all-start.4 = ((bf16[8,384,128]{2,1,0:T(8,128)(2,1)}), bf16[8,384,128]{2,1,0:T(8,128)(2,1)}, u32[]{:S(2)}, u32[]{:S(2)}) async-start(bf16[8,384,128]{2,1,0:T(8,128)(2,1)} %bitcast.145), calls=%async_computation.4 | async-start | bytes 1572864 | tf_op jit(solution)/shard_map/all_to_all | solution.py:1237
  267.4 4.7 copy-start.6
  296.2 95.2 %collective-permute-start.2 = (bf16[2,3,4,32,896]{4,3,2,1,0:T(8,128)(2,1)}, bf16[2,3,4,32,896]{4,3,2,1,0:T(8,128)(2,1)}, u32[]{:S(2)}, u32[]{:S(2)}) collective-permute-start(bf16[2,3,4,32,896]{4,3,2,1,0:T(8,128)(2,1)} %get-tuple-element.61), channel_id=1, source_target_pairs={{0,8},{4,12},{8,0},{12,4},{16,24},{20,28},{24,16},{28,20},{1,9},{5... | collective-permute-start | bytes 4128776 | tf_op jit(solution)/shard_map/ppermute | solution.py:1045
  297.6 93.7 %collective-permute-start.3 = (bf16[2,3,4,32,896]{4,3,2,1,0:T(8,128)(2,1)}, bf16[2,3,4,32,896]{4,3,2,1,0:T(8,128)(2,1)}, u32[]{:S(2)}, u32[]{:S(2)}) collective-permute-start(bf16[2,3,4,32,896]{4,3,2,1,0:T(8,128)(2,1)} %get-tuple-element.63), channel_id=1, source_target_pairs={{0,16},{4,20},{8,24},{12,28},{16,0},{20,4},{24,8},{28,12},{1,17},{... | collective-permute-start | bytes 4128776 | tf_op jit(solution)/shard_map/ppermute | solution.py:1045
  307.1 84.2 %collective-permute-start = (bf16[2,1,4,320,128]{4,3,2,1,0:T(8,128)(2,1)}, bf16[2,1,4,320,128]{4,3,2,1,0:T(8,128)(2,1)}, u32[]{:S(2)}, u32[]{:S(2)}) collective-permute-start(bf16[2,1,4,320,128]{4,3,2,1,0:T(8,128)(2,1)} %get-tuple-element.57), channel_id=1, source_target_pairs={{0,8},{4,12},{8,0},{12,4},{16,24},{20,28},{24,16},{28,20},{1,9},{5... | collective-permute-start | bytes 1966088 | tf_op jit(solution)/shard_map/ppermute | solution.py:1045
  307.4 84.0 %collective-permute-start.1 = (bf16[2,1,4,336,128]{4,3,2,1,0:T(8,128)(2,1)}, bf16[2,1,4,336,128]{4,3,2,1,0:T(8,128)(2,1)}, u32[]{:S(2)}, u32[]{:S(2)}) collective-permute-start(bf16[2,1,4,336,128]{4,3,2,1,0:T(8,128)(2,1)} %get-tuple-element.59), channel_id=1, source_target_pairs={{0,16},{4,20},{8,24},{12,28},{16,0},{20,4},{24,8},{28,12},{1,17},{... | collective-permute-start | bytes 2064392 | tf_op jit(solution)/shard_map/ppermute | solution.py:1045
  307.4 40.3 %collective-permute-start.4 = (bf16[2,1,4,32,512]{4,3,2,1,0:T(8,128)(2,1)}, bf16[2,1,4,32,512]{4,3,2,1,0:T(8,128)(2,1)S(1)}, u32[]{:S(2)}, u32[]{:S(2)}) collective-permute-start(bf16[2,1,4,32,512]{4,3,2,1,0:T(8,128)(2,1)} %get-tuple-element.65), channel_id=1, source_target_pairs={{0,8},{4,12},{8,0},{12,4},{16,24},{20,28},{24,16},{28,20},{1,9},{5... | collective-permute-start | bytes 786440 | tf_op jit(solution)/shard_map/ppermute | solution.py:1045
  308.8 86.8 %all-to-all-start.2 = ((bf16[8,48,1024]{2,1,0:T(8,128)(2,1)}), bf16[8,48,1024]{2,1,0:T(8,128)(2,1)}, u32[]{:S(2)}, u32[]{:S(2)}) async-start(bf16[8,48,1024]{2,1,0:T(8,128)(2,1)} %bitcast.152), calls=%async_computation.2 | async-start | bytes 1572864 | tf_op jit(solution)/shard_map/all_to_all | solution.py:1237
  347.7 43.6 %copy-start.21 = (bf16[2,1,4,32,512]{4,3,2,1,0:T(8,128)(2,1)}, bf16[2,1,4,32,512]{4,3,2,1,0:T(8,128)(2,1)S(1)}, u32[]{:S(2)}) copy-start(bf16[2,1,4,32,512]{4,3,2,1,0:T(8,128)(2,1)S(1)} %collective-permute-done.4.refs_15_) | copy-start | bytes 786436
  347.7 43.6 %collective-permute-start.5 = (bf16[2,1,4,32,512]{4,3,2,1,0:T(8,128)(2,1)}, bf16[2,1,4,32,512]{4,3,2,1,0:T(8,128)(2,1)}, u32[]{:S(2)}, u32[]{:S(2)}) collective-permute-start(bf16[2,1,4,32,512]{4,3,2,1,0:T(8,128)(2,1)} %get-tuple-element.67), channel_id=1, source_target_pairs={{0,16},{4,20},{8,24},{12,28},{16,0},{20,4},{24,8},{28,12},{1,17},{... | collective-permute-start | bytes 786440 | tf_op jit(solution)/shard_map/ppermute | solution.py:1045
  395.7 7.4 %copy-start.39 = (s32[1,1,8]{2,1,0:T(1,128)S(1)}, s32[1,1,8]{2,1,0:T(1,128)}, u32[]{:S(2)}) copy-start(s32[1,1,8]{2,1,0:T(1,128)} %param.15) | copy-start | bytes 100
  395.7 32.7 %all-to-all-start.5 = ((bf16[8,384,384]{1,2,0:T(8,128)(2,1)}), bf16[8,384,384]{1,2,0:T(8,128)(2,1)}, u32[]{:S(2)}, u32[]{:S(2)}) async-start(bf16[8,384,384]{1,2,0:T(8,128)(2,1)} %copy.47), calls=%async_computation.5 | async-start | bytes 4718592 | tf_op jit(solution)/shard_map/all_to_all | solution.py:1237
  403.1 9.3 %copy-start.30 = (s32[1024]{0:T(1024)}, s32[1024]{0:T(1024)S(1)}, u32[]{:S(2)}) copy-start(s32[1024]{0:T(1024)S(1)} %pad_clamp_fusion) | copy-start | bytes 12292
  408.9 6.6 %copy-start.10 = (bf16[2,3,4,32,896]{4,3,2,1,0:T(8,128)(2,1)S(1)}, bf16[2,3,4,32,896]{4,3,2,1,0:T(8,128)(2,1)}, u32[]{:S(2)}) copy-start(bf16[2,3,4,32,896]{4,3,2,1,0:T(8,128)(2,1)} %get-tuple-element.73.refs_8_) | copy-start | bytes 4128772
  408.9 8.9 %copy-start.11 = (bf16[2,3,4,32,896]{4,3,2,1,0:T(8,128)(2,1)S(1)}, bf16[2,3,4,32,896]{4,3,2,1,0:T(8,128)(2,1)}, u32[]{:S(2)}) copy-start(bf16[2,3,4,32,896]{4,3,2,1,0:T(8,128)(2,1)} %get-tuple-element.75.refs_11_) | copy-start | bytes 4128772
  411.0 54.2 %collective-permute-start.6 = (bf16[1,4,320,128]{3,2,1,0:T(8,128)(2,1)}, bf16[1,4,320,128]{3,2,1,0:T(8,128)(2,1)}, u32[]{:S(2)}, u32[]{:S(2)}) collective-permute-start(bf16[1,4,320,128]{3,2,1,0:T(8,128)(2,1)} %fusion.28), channel_id=1, source_target_pairs={{0,16},{4,20},{8,24},{12,28},{16,0},{20,4},{24,8},{28,12},{1,17},{... | collective-permute-start | bytes 983048 | tf_op jit(solution)/shard_map/ppermute | solution.py:1045
  414.3 5.8 %copy-start.19 = (bf16[2,1,4,32,512]{4,3,2,1,0:T(8,128)(2,1)S(1)}, bf16[2,1,4,32,512]{4,3,2,1,0:T(8,128)(2,1)}, u32[]{:S(2)}) copy-start(bf16[2,1,4,32,512]{4,3,2,1,0:T(8,128)(2,1)} %get-tuple-element.77.refs_14_) | copy-start | bytes 786436
  414.3 5.8 %copy-start.22 = (bf16[2,1,4,32,512]{4,3,2,1,0:T(8,128)(2,1)S(1)}, bf16[2,1,4,32,512]{4,3,2,1,0:T(8,128)(2,1)}, u32[]{:S(2)}) copy-start(bf16[2,1,4,32,512]{4,3,2,1,0:T(8,128)(2,1)} %copy-done.21) | copy-start | bytes 786436
  414.3 7.9 %copy-start.20 = (bf16[2,1,4,32,512]{4,3,2,1,0:T(8,128)(2,1)S(1)}, bf16[2,1,4,32,512]{4,3,2,1,0:T(8,128)(2,1)}, u32[]{:S(2)}) copy-start(bf16[2,1,4,32,512]{4,3,2,1,0:T(8,128)(2,1)} %get-tuple-element.79.refs_17_) | copy-start | bytes 786436
  414.3 50.8 %collective-permute-start.7 = (bf16[1,4,336,128]{3,2,1,0:T(8,128)(2,1)}, bf16[1,4,336,128]{3,2,1,0:T(8,128)(2,1)}, u32[]{:S(2)}, u32[]{:S(2)}) collective-permute-start(bf16[1,4,336,128]{3,2,1,0:T(8,128)(2,1)} %fusion.27), channel_id=1, source_target_pairs={{0,8},{4,12},{8,0},{12,4},{16,24},{20,28},{24,16},{28,20},{1,9},{5... | collective-permute-start | bytes 1032200 | tf_op jit(solution)/shard_map/ppermute | solution.py:1045
  417.6 47.6 %collective-permute-start.8 = (bf16[3,4,32,896]{3,2,1,0:T(8,128)(2,1)}, bf16[3,4,32,896]{3,2,1,0:T(8,128)(2,1)}, u32[]{:S(2)}, u32[]{:S(2)}) collective-permute-start(bf16[3,4,32,896]{3,2,1,0:T(8,128)(2,1)} %fusion.24), channel_id=1, source_target_pairs={{0,16},{4,20},{8,24},{12,28},{16,0},{20,4},{24,8},{28,12},{1,17},{... | collective-permute-start | bytes 2064392 | tf_op jit(solution)/shard_map/ppermute | solution.py:1045
  420.0 45.2 %collective-permute-start.9 = (bf16[3,4,32,896]{3,2,1,0:T(8,128)(2,1)}, bf16[3,4,32,896]{3,2,1,0:T(8,128)(2,1)}, u32[]{:S(2)}, u32[]{:S(2)}) collective-permute-start(bf16[3,4,32,896]{3,2,1,0:T(8,128)(2,1)} %fusion.25), channel_id=1, source_target_pairs={{0,8},{4,12},{8,0},{12,4},{16,24},{20,28},{24,16},{28,20},{1,9},{5... | collective-permute-start | bytes 2064392 | tf_op jit(solution)/shard_map/ppermute | solution.py:1045
  420.8 33.7 %collective-permute-start.10 = (bf16[1,4,32,512]{3,2,1,0:T(8,128)(2,1)}, bf16[1,4,32,512]{3,2,1,0:T(8,128)(2,1)S(1)}, u32[]{:S(2)}, u32[]{:S(2)}) collective-permute-start(bf16[1,4,32,512]{3,2,1,0:T(8,128)(2,1)} %fusion.30), channel_id=1, source_target_pairs={{0,16},{4,20},{8,24},{12,28},{16,0},{20,4},{24,8},{28,12},{1,17},{... | collective-permute-start | bytes 393224 | tf_op jit(solution)/shard_map/ppermute | solution.py:1045
  432.8 5.7 %copy-start.27 = (f32[384]{0:T(512)S(1)}, f32[384]{0:T(512)}, u32[]{:S(2)}) copy-start(f32[384]{0:T(512)} %copy-done.26) | copy-start | bytes 4612
  438.5 17.8 %copy-start.34 = (pred[384]{0:T(512)(128)(4,1)S(1)}, pred[384]{0:T(512)(128)(4,1)}, u32[]{:S(2)}) copy-start(pred[384]{0:T(512)(128)(4,1)} %copy-done.33) | copy-start | bytes 1156
  439.8 18.1 %copy-start.2 = (bf16[384,3,8,128]{3,2,1,0:T(8,128)(2,1)S(1)}, bf16[384,3,8,128]{3,2,1,0:T(8,128)(2,1)}, u32[]{:S(2)}) copy-start(bf16[384,3,8,128]{3,2,1,0:T(8,128)(2,1)} %copy.48) | copy-start | bytes 7077892
  454.5 3.4 copy-start.24
  454.5 10.6 %collective-permute-start.11 = (bf16[1,4,32,512]{3,2,1,0:T(8,128)(2,1)S(1)}, bf16[1,4,32,512]{3,2,1,0:T(8,128)(2,1)S(1)}, u32[]{:S(2)}, u32[]{:S(2)}) collective-permute-start(bf16[1,4,32,512]{3,2,1,0:T(8,128)(2,1)S(1)} %fusion.31), channel_id=1, source_target_pairs={{0,8},{4,12},{8,0},{12,4},{16,24},{20,28},{24,16},{28,20},{1,9},{5... | collective-permute-start | bytes 393224 | tf_op jit(solution)/shard_map/ppermute | solution.py:1045
  457.9 6.6 %copy-start.28 = (f32[1024]{0:T(1024)S(1)}, f32[1024]{0:T(1024)}, u32[]{:S(2)}) copy-start(f32[1024]{0:T(1024)} %get-tuple-element.88) | copy-start | bytes 12292
  457.9 6.6 %copy-start.29 = (f32[1024]{0:T(1024)S(1)}, f32[1024]{0:T(1024)}, u32[]{:S(2)}) copy-start(f32[1024]{0:T(1024)} %select_maximum_fusion) | copy-start | bytes 12292
  457.9 6.6 %copy-start.32 = (f32[1024]{0:T(1024)S(1)}, f32[1024]{0:T(1024)}, u32[]{:S(2)}) copy-start(f32[1024]{0:T(1024)} %get-tuple-element.93) | copy-start | bytes 12292
  459.9 102.4 %all-to-all-start.6 = ((bf16[8,48,1024]{2,1,0:T(8,128)(2,1)}), bf16[8,48,1024]{2,1,0:T(8,128)(2,1)S(1)}, u32[]{:S(2)}, u32[]{:S(2)}) async-start(bf16[8,48,1024]{2,1,0:T(8,128)(2,1)} %bitcast.34), calls=%async_computation.6 | async-start | bytes 1572864 | tf_op jit(solution)/shard_map/all_to_all | solution.py:1237
  465.1 0.7 copy-start.25
  549.1 3.6 copy-start.23
  549.1 5.8 %copy-start.12 = (bf16[256,5376]{1,0:T(8,128)(2,1)S(1)}, bf16[256,5376]{1,0:T(8,128)(2,1)}, u32[]{:S(2)}) copy-start(bf16[256,5376]{1,0:T(8,128)(2,1)} %get-tuple-element.84) | copy-start | bytes 8257540
  554.9 1.3 copy-start.16
  559.3 3.9 copy-start.35
  559.3 5.5 copy-start.1
  562.3 1.1 copy-start.9

commit v2 on v1

--- a/solution.py
+++ b/solution.py
@@ -275,6 +275,31 @@
         jnp.concatenate([cosine, cosine] * head_count, axis=1),
         jnp.concatenate([sine, -sine] * head_count, axis=1),
     )
+
+
+def pack_rotary_tables(lengths_row, tokens, head_count):
+    half, step = (HEAD_WIDTH // 2, math.gcd(tokens, 128))
+    inverse = 160000.0 ** (-2.0 * jnp.arange(half, dtype=jnp.float32) / HEAD_WIDTH)
+    inverse = jnp.tile(inverse, 2 * head_count)[None, :]
+    sign = jnp.tile(jnp.repeat(jnp.asarray([1.0, -1.0], jnp.float32), half), head_count)[None, :]
+    coarse = jnp.arange(0, tokens, step).astype(jnp.float32)[:, None] * inverse
+    fine = jnp.arange(step).astype(jnp.float32)[:, None] * inverse
+    begins = jnp.cumsum(lengths_row) - lengths_row
+    start = begins.astype(jnp.float32)[:, None] * inverse
+    cos_a, sin_a = (jnp.cos(coarse)[:, None, :], jnp.sin(coarse)[:, None, :])
+    cos_b, sin_b = (jnp.cos(fine)[None], jnp.sin(fine)[None])
+    cos_place = (cos_a * cos_b - sin_a * sin_b).reshape(tokens, -1)
+    sin_place = (sin_a * cos_b + cos_a * sin_b).reshape(tokens, -1)
+    place = lax.broadcasted_iota(jnp.int32, cos_place.shape, 0)
+    cos_all, sin_all = (jnp.cos(start), jnp.sin(start))
+    cos_start, sin_start = (cos_all[:1], sin_all[:1])
+    for at in range(1, lengths_row.shape[0]):
+        later = place >= begins[at]
+        cos_start = jnp.where(later, cos_all[at][None, :], cos_start)
+        sin_start = jnp.where(later, sin_all[at][None, :], sin_start)
+    cosine = cos_place * cos_start + sin_place * sin_start
+    sine = sin_place * cos_start - cos_place * sin_start
+    return (cosine, sine * sign)
 
 
 def toggled(index, bit):
@@ -559,22 +584,42 @@
     return [whole.reshape(-1, whole.shape[-1]) for whole in held]
 
 
-def pair_steps(plan, lead_rows, left_refs, right_refs, turned_refs, whole_refs, sems, core, send_core):
+def pair_steps(plan, lead_rows, left_refs, right_refs, turned_refs, whole_refs, sems, core, pending, send):
     pair_send, pair_recv, near_sem = sems
+    to_core = {"ctx": toggled(lax.axis_index("ctx"), 1)}
+
+    def send_core(source, target, sent, got, start=True):
+        return send(source, target, sent, got, to_core, start)
+
     rows = left_refs[0].shape[0] if left_refs else 0
     pairs = []
-    for w, (kind, count, width, deep, halves) in enumerate(plan):
-        span = count * width if kind == "rows" else 4 * width
-        if len(right_refs[w].shape) == 3:
-            own_half, other_half = (right_refs[w].at[core], right_refs[w].at[1 - core])
+    for w, entry in enumerate(plan):
+        span, right = (plan_span(entry), right_refs[w])
+        own_part, other_part = (whole_refs[w].at[pl.ds(0, rows)], whole_refs[w].at[pl.ds(rows, rows)])
+
+        def exchange(own_half, other_half, start=True):
+            near = pltpu.make_async_copy(own_half, own_part, near_sem.at[w])
+            if start:
+                near.start()
+            sems = (pair_send.at[2 * w], pair_recv.at[2 * w])
+            return [near, send_core(other_half, other_part, *sems, start)]
+
+        if entry[5]:
+            ways = [exchange(right[at], right[1 - at], False) for at in (0, 1)]
+            for at in (0, 1):
+
+                @pl.when(core == at)
+                def begin():
+                    for copy in ways[at]:
+                        copy.start()
+
+            pairs.append(ways[0])
+            pending.append(ways[0][1])
         else:
-            own_half = right_refs[w].at[:, pl.ds(pl.multiple_of(core * span, span), span)]
-            other_half = right_refs[w].at[:, pl.ds(pl.multiple_of((1 - core) * span, span), span)]
-        near = pltpu.make_async_copy(own_half, whole_refs[w].at[pl.ds(0, rows)], near_sem.at[w])
-        near.start()
-        target = whole_refs[w].at[pl.ds(rows, rows)]
-        far = send_core(other_half, target, pair_send.at[2 * w], pair_recv.at[2 * w])
-        pairs.append([near, far])
+            halves = [
+                right.at[:, pl.ds(pl.multiple_of(at * span, span), span)] for at in (core, 1 - core)
+            ]
+            pairs.append(exchange(*halves))
 
     def turn(w):
         left, turned = (left_refs[w], turned_refs[w])
@@ -594,7 +639,7 @@
         )
 
     def multiply(w, t, first, second):
-        kind, count, width, deep, halves = plan[w]
+        kind, count, width, deep, halves, parted = plan[w]
         if t == 0:
             near, far, turned = pairs[w]
             near.wait()
@@ -604,11 +649,13 @@
         def each(z, carried):
             left = turned_refs[w][pl.ds(pl.multiple_of(z * deep, 16), deep), :]
             if kind == "rows":
+                last = min((t + 1) * width, whole_refs[w].shape[1])
                 part = jnp.dot(
-                    left,
-                    whole_refs[w][:, t * width : (t + 1) * width],
-                    preferred_element_type=jnp.float32,
+                    left, whole_refs[w][:, t * width : last], preferred_element_type=jnp.float32
                 ).astype(jnp.bfloat16)
+                if last < (t + 1) * width:
+                    empty = jnp.zeros((deep, (t + 1) * width - last), jnp.bfloat16)
+                    part = jnp.concatenate([part, empty], axis=1)
                 piece_rows = first.shape[3]
                 for s in range(4):
                     first[z, s // 2, s % 2] = part[2 * s * piece_rows : (2 * s + 1) * piece_rows]
@@ -629,7 +676,7 @@
 
 
 def remote_send(pending):
-    def send(source, target, sent, got, partner):
+    def send(source, target, sent, got, partner, start=True):
         copy = pltpu.make_async_remote_copy(
             src_ref=source,
             dst_ref=target,
@@ -638,18 +685,25 @@
             device_id=partner,
             device_id_type=pl.DeviceIdType.MESH,
         )
-        copy.start()
-        pending.append(copy)
+        if start:
+            copy.start()
+            pending.append(copy)
         return copy
 
     return send
 
 
 def product_kernel(plan, lead_rows, *refs):
-    weights = len(plan)
-    left_refs, right_refs = (refs[:weights], refs[weights : 2 * weights])
-    out_refs = refs[2 * weights : 6 * weights]
-    scratch = list(refs[6 * weights :])
+    groups, places = early_places(plan)
+    weights, outs = (len(plan), 4 * len(groups))
+    left_refs, refs = (refs[:weights], refs[weights:])
+    right_refs = []
+    for entry in plan:
+        held = 2 if entry[5] else 1
+        right_refs.append(refs[:held] if held == 2 else refs[0])
+        refs = refs[held:]
+    out_refs = refs[:outs]
+    scratch = list(refs[outs:])
     turned_refs = [scratch.pop(0) for weight in plan]
     whole_refs = [scratch.pop(0) for weight in plan]
     chunks = [(w, t) for w, entry in enumerate(plan) for t in range(entry[1])]
@@ -673,7 +727,8 @@
         whole_refs,
         (pair_send, pair_recv, near_sem),
         core,
-        lambda *copied: send(*copied, to_core),
+        pending,
+        send,
     )
     for w in range(weights):
         turn(w)
@@ -681,6 +736,7 @@
     for number, (w, t) in enumerate(chunks):
         first, second = held[number]
         multiply(w, t, first, second)
+        group, offset = places[number]
         sides = (
             lambda at: first.at[:, at, own_x],
             lambda at: first.at[:, at, 1 - own_x],
@@ -691,7 +747,7 @@
             for at in (0, 1):
                 copy = pltpu.make_async_copy(
                     source_at(at),
-                    out_refs[4 * w + side].at[at, t],
+                    out_refs[4 * group + side].at[at, :, :, pl.ds(offset, plan[w][2])],
                     store_sem.at[8 * number + 2 * side + at],
                 )
                 copy.start()
@@ -705,10 +761,25 @@
 def weight_plan(kind, left, right, count):
     deep = left.shape[1] // 4
     if kind == "rows":
-        span = right.shape[-1] // (1 if right.ndim == 3 else 2)
-        return (kind, count, span // count, deep, (deep // 8, deep // 8))
+        parted = isinstance(right, tuple)
+        span = right[0].shape[1] if parted else right.shape[1] // 2
+        width = -(-span // (128 * count)) * 128
+        return (kind, count, width, deep, (deep // 8, deep // 8), span if parted else 0)
     lead_rows = deep // 2 // 16 * 16
-    return (kind, count, right.shape[-1] // 8, deep, (lead_rows, deep - lead_rows))
+    return (kind, count, right.shape[-1] // 8, deep, (lead_rows, deep - lead_rows), 0)
+
+
+def early_places(plan):
+    groups, places = ([], [])
+    for kind, count, width, deep, halves, parted in plan:
+        found = [at for at, group in enumerate(groups) if group[0] == halves]
+        if not found:
+            groups.append([halves, 0])
+            found = [len(groups) - 1]
+        for chunk in range(count):
+            places.append((found[0], groups[found[0]][1]))
+            groups[found[0]][1] += width
+    return (groups, places)
 
 
 def plan_span(entry):
@@ -721,7 +792,9 @@
 
 def pair_scratch(plan, tokens):
     turned = [pltpu.VMEM((4 * entry[3], 2 * tokens), jnp.bfloat16) for entry in plan]
-    return turned + [pltpu.VMEM((2 * tokens, plan_span(entry)), jnp.bfloat16) for entry in plan]
+    return turned + [
+        pltpu.VMEM((2 * tokens, entry[5] or plan_span(entry)), jnp.bfloat16) for entry in plan
+    ]
 
 
 def early_sums(products):
@@ -732,10 +805,13 @@
         pl.BlockSpec(memory_space=pl.ANY),
         pltpu.SemaphoreType.DMA,
     )
+    rights = [part for right in rights for part in (right if isinstance(right, tuple) else [right])]
+    groups = early_places(plan)[0]
     outs, held = ([], [])
-    for kind, count, width, deep, halves in plan:
+    for halves, columns in groups:
         for half in halves:
-            outs += [jax.ShapeDtypeStruct((2, count, 4, half, width), jnp.bfloat16)] * 2
+            outs += [jax.ShapeDtypeStruct((2, 4, half, columns), jnp.bfloat16)] * 2
+    for kind, count, width, deep, halves, parted in plan:
         for chunk in range(count):
             held += [pltpu.VMEM((4, 2, 2, half, width), jnp.bfloat16) for half in halves]
     chunk_count = sum(entry[1] for entry in plan)
@@ -744,7 +820,7 @@
     sides = pl.pallas_call(
         functools.partial(product_kernel, plan, plan_lead(plan)),
         out_shape=tuple(outs),
-        in_specs=[vmem] * len(plan) + [anywhere] * len(plan),
+        in_specs=[vmem] * len(plan) + [anywhere] * len(rights),
         out_specs=(anywhere,) * len(outs),
         scratch_shapes=scratch,
         compiler_params=pltpu.CompilerParams(
@@ -753,9 +829,9 @@
         name="early_products",
     )(*lefts, *rights)
     arrays = []
-    for w in range(len(plan)):
+    for group in range(len(groups)):
         for part, bit in ((0, 2), (2, 4)):
-            kept, sent = sides[4 * w + part : 4 * w + part + 2]
+            kept, sent = sides[4 * group + part : 4 * group + part + 2]
             arrays.append((kept, swap(sent, "ctx", bit)))
     return (plan, arrays)
 
@@ -779,7 +855,8 @@
     weights, products = (len(early) + len(late), len(late))
     left_refs, right_refs = (refs[:products], refs[products : 2 * products])
     refs = refs[2 * products :]
-    early_refs, refs = (refs[: 6 * len(early)], refs[6 * len(early) :])
+    groups, places = early_places(early)
+    early_refs, refs = (refs[: 6 * len(groups)], refs[6 * len(groups) :])
     small_ref, out_refs, small_out = (refs[0], refs[1 : weights + 1], refs[weights + 1])
     scratch = list(refs[weights + 2 :])
     turned_refs = [scratch.pop(0) for weight in late]
@@ -799,11 +876,13 @@
     low_bit, high_bit = (own_shard % 2, own_shard // 2)
     loads = {}
     for number in range(early_count):
-        w, t = chunks[number]
+        w, (group, offset) = (chunks[number][0], places[number])
         for half in (0, 1):
             own = own_y if half == 0 else own_x
-            kept, arrived, twice = early_refs[6 * w + 3 * half : 6 * w + 3 * half + 3]
-            for at, source in enumerate((kept.at[own, t], arrived.at[own, t], twice.at[t])):
+            kept, arrived, twice = early_refs[6 * group + 3 * half : 6 * group + 3 * half + 3]
+            columns = pl.ds(offset, plan[w][2])
+            sources = (kept.at[own, :, :, columns], arrived.at[own, :, :, columns], twice.at[:, :, columns])
+            for at, source in enumerate(sources):
                 slot = (number * 2 + half) * 3 + at
                 copy = pltpu.make_async_copy(source, units[number, half][at], load_sem.at[slot])
                 copy.start()
@@ -828,7 +907,8 @@
         whole_refs,
         (pair_send, pair_recv, near_sem),
         core,
-        lambda *copied: send(*copied, to_core),
+        pending,
+        send,
     )
     copies = {}
 
@@ -993,7 +1073,7 @@
     lefts, rights = ([product[1] for product in products], [product[2] for product in products])
     plan = early + late
     pieces = []
-    for w, (kind, count, width, deep, halves) in enumerate(plan):
+    for w, (kind, count, width, deep, halves, parted) in enumerate(plan):
         leads = [(4, 2, 2), (4, 2), (4,), (2,), (1,)]
         if w < len(early):
             leads[:2] = [(4,), (4,)]
@@ -1188,17 +1268,10 @@
     ff_width = hidden.shape[1]
     if shards != 4 or ctx_count != 8 or act_mlp.shape[1] % 1024 != 0 or ff_width % 64 != 0:
         return None
-    padded = -(-ff_width // 384) * 384
-    sides = jnp.stack(
-        [
-            jnp.pad(side, ((0, 0), (0, padded - ff_width)))
-            for side in (grad_leading, grad_trailing)
-        ]
-    )
     return early_sums(
         [
             ("columns", hidden, grad_mlp_low, 1),
-            ("rows", act_mlp, sides, 3),
+            ("rows", act_mlp, (grad_leading, grad_trailing), 3),
             ("rows", attn_low, grad_attn_low, 1),
         ]
     )
@@ -1251,7 +1324,7 @@
     residual = arrived.reshape(row_count, model_width).astype(jnp.float32)
     places = own_index * row_count + jnp.arange(row_count, dtype=jnp.int32)
     unused_begin, unused_end, offset, is_valid = spans(places, lengths_row)
-    pack_begin, pack_end, pack_offset, unused_valid = spans(
+    pack_begin, pack_end, unused_offset, unused_valid = spans(
         jnp.arange(tokens, dtype=jnp.int32), lengths_row
     )
     grad_final = jnp.where(
@@ -1335,7 +1408,7 @@
     early = weight_sums_early(
         hidden, grad_mlp_low, act_mlp, grad_leading, grad_trailing, attn_low, grad_attn_low
     )
-    pack_cosine, pack_sine = rotary_tables(pack_offset, own_heads)
+    pack_cosine, pack_sine = pack_rotary_tables(lengths_row, tokens, own_heads)
     block_back = math.gcd(tokens, 256)
     low_back, high_back = key_range(pack_begin[0], pack_end[0], block_q, block_back)
     grad_heads = attention_backward(

time: 574 us -> 536 us (0.934)
  waiting for transfers between devices: 50 us -> 14.7 us
  matrix products: 43.4 us -> 49.9 us
  other arithmetic: 75.5 us -> 69.6 us
    ppermute x12 -> x8, waiting for transfers between devices: 38.1 us -> 1.4 us  [swap(): return lax.ppermute(value, axis, pairs)]
    concatenate x2 -> x1, other arithmetic: 10.4 us -> 1.12 us  [rotary_tables(): jnp.concatenate([cosine, cosine] * head_count, axis=1)]
    sin x2 -> x1, other arithmetic: 9.02 us -> 0.76 us  [rotary_tables(): cosine, sine = (jnp.cos(angles), jnp.sin(angles))]
    mul x0 -> x1, other arithmetic: none -> 6.9 us  [pack_rotary_tables(): return (cosine, sine * sign)]
    add x0 -> x1, other arithmetic: none -> 6.87 us  [pack_rotary_tables(): cosine = cos_place * cos_start + sin_place * sin_start]
    ppermute x12 -> x8, starting transfers between devices: 11.5 us -> 6.17 us  [swap(): return lax.ppermute(value, axis, pairs)]
  transfers between devices with their start and end apart: 19 -> 15, of which waited for: 4 -> 4; matrix products, arithmetic and copies ran while one was open for 15% -> 16% of each run, Pallas kernels for 56% -> 60%
where the time goes in v2:
time: 536 us; the launch traced here: 527 us
  Pallas kernels  316 us (59%)
  other arithmetic  69.6 us (13%)
  matrix products  49.9 us (9%)
  starting transfers between devices  44.8 us (8%)
  local copies, waits for them, and re-layouts  29.6 us (6%)
  waiting for transfers between devices  14.7 us (3%)
    pallas_call x2, Pallas kernels, gather_weights(): pl.pallas_call(functools.partial(gather_kernel, shapes, projection is not...  137 us
    pallas_call x1, Pallas kernels, sum_weights(): pl.pallas_call(functools.partial(sum_kernel, early, late, plan_lead(plan)...  82.2 us
    pallas_call x1, Pallas kernels, attention_backward(): pl.pallas_call(functools.partial(backward_kernel, head_count, block_q, bl...  43.5 us
    all_to_all x7, starting transfers between devices, exchange(): lax.all_to_all(blocks, 'ctx', split_axis=0, concat_axis=0, tiled=True)  38.6 us
    pallas_call x1, Pallas kernels, attention_forward(): pl.pallas_call(functools.partial(forward_kernel, head_count, block_q, blo...  30.1 us
    pallas_call x1, Pallas kernels, early_sums(): pl.pallas_call(functools.partial(product_kernel, plan, plan_lead(plan)),...  23.1 us
    dot_general x1, matrix products, per_device(): lax.dot_general(grad_mlp_low, out_full, NT, preferred_element_type=jnp.fl...  13.7 us
    all_to_all x7, waiting for transfers between devices, exchange(): lax.all_to_all(blocks, 'ctx', split_axis=0, concat_axis=0, tiled=True)  13.3 us
  transfers between devices with their start and end apart: 15, of which 4 were waited for; matrix products, arithmetic and copies ran while one was open for 16% of the time, Pallas kernels for 60%

profile of v2, /device:TPU:1, one launch (start us, length us, event | category | flops | bytes accessed | tf_op | source)
XLA Modules:
  0.0 526.7 jit_solution(6482973005606992744)
XLA Ops:
  0.7 0.9 select_reduce_fusion.6
  3.1 1.3 broadcast_select_fusion.2
  4.4 5.2 all-to-all-start
  11.7 39.7 %gather_weights.1 = (bf16[4,16,256]{2,1,0:T(8,128)(2,1)}, bf16[4,2,4,32,3072]{4,3,2,1,0:T(8,128)(2,1)}) custom-call(bf16[16,256]{1,0:T(8,128)(2,1)} %fusion.36.refs_0_, bf16[2,4,32,3072]{3,2,1,0:T(8,128)(2,1)} %bitcast.191), custom_call_target="tpu_custom_call" | custom-call | tf_op jit(solution)/shard_map/gather_weights/pallas_call | solution.py:571
  56.6 1.3 iota_compare_fusion.3
  57.9 1.1 pad_maximum_fusion
  59.7 1.3 compare_select_fusion.1
  61.0 3.5 all-to-all-start.3
  65.2 1.2 fusion.19.refs_3_.refs_0_
  66.4 97.0 %gather_and_project.1 = (bf16[4,2,4,32,1024]{4,3,2,1,0:T(8,128)(2,1)}, bf16[4,2,4,32,5248]{4,3,2,1,0:T(8,128)(2,1)}, bf16[4,656,1024]{2,1,0:T(8,128)(2,1)}, bf16[3072,384]{1,0:T(8,128)(2,1)}) custom-call(bf16[2,4,32,1024]{3,2,1,0:T(8,128)(2,1)} %bitcast.197, bf16[2,4,32,5248]{3,2,1,0:T(8,128)(2,1)} %bitcast.187, bf16[656,1024]{1,0:T(8,128)(2,1)} %refs_2_.1, ...), custom_call_target="tpu_custom_call" | custom-call | tf_op jit(solution)/shard_map/gather_and_project/pallas_call | solution.py:571
  163.4 30.1 %attention_forward.1 = (f32[3072,128]{1,0:T(8,128)}, f32[12,1,512]{2,1,0:T(1,128)}) custom-call(s32[12]{0:T(128)} %get-tuple-element.129.low_ref, s32[12]{0:T(128)} %get-tuple-element.130.high_ref, s32[1,3072]{1,0:T(1,128)} %get-tuple-element.149.begin_ref, s32[1,3072]{1,0:T(1,128)} %get-tuple-element.148.end_ref, bf16[3072,384]{1,0:T(8,128)(2,1)} %get-tuple-element.42.qkv_ref), custom_call_target="tpu_custom_call" | custom-call | flops 2415919104 | bytes 4718592 | tf_op jit(solution)/shard_map/attention_forward/pallas_call | solution.py:97
  193.6 2.4 convert_element_type.202
  195.9 4.3 all-to-all-start.1
  201.2 1.4 iota_compare_fusion.5
  202.6 1.7 multiply_subtract_fusion
  204.3 1.1 select_convert_fusion
  205.3 4.0 all-to-all-done.1
  209.3 4.0 fusion.49
  214.0 8.0 %fusion.54 = f32[384,5248]{1,0:T(8,128)S(1)} fusion(bf16[384,1024]{1,0:T(8,128)(2,1)S(1)} %multiply_convert_fusion.2.refs_1_, bf16[1024,5248]{1,0:T(8,128)(2,1)} %bitcast.217), kind=kOutput, calls=%fused_computation.194 | convolution fusion | flops 4127195136 | bytes 19595264 | tf_op jit(solution)/shard_map/dot_general | solution.py:1368
  222.1 13.7 %add_convert_fusion = (bf16[384,2624]{1,0:T(8,128)(2,1)S(1)}, f32[384,2624]{1,0:T(8,128)}, f32[384,2624]{1,0:T(8,128)}) fusion(f32[384,5248]{1,0:T(8,128)S(1)} %fusion.54, bf16[384,1024]{1,0:T(8,128)(2,1)S(1)} %bitcast.194, bf16[2624,1024]{1,0:T(8,128)(2,1)S(1)} %bitcast.222), kind=kOutput, calls=%fused_computation.7 | convolution fusion | flops 2137153536 | bytes 24297472 | tf_op jit(solution)/shard_map/dot_general | solution.py:1386
  235.8 7.9 %multiply_convert_fusion = (bf16[384,2624]{1,0:T(8,128)(2,1)S(1)}, bf16[384,2624]{1,0:T(8,128)(2,1)S(1)}) fusion(f32[384,2624]{1,0:T(8,128)} %get-tuple-element.143, f32[384,2624]{1,0:T(8,128)} %get-tuple-element.90, f32[384,5248]{1,0:T(8,128)} %copy-done.5), kind=kLoop, calls=%fused_computation.6 | loop fusion | flops 6045696 | bytes 20152320 | tf_op jit(solution)/shard_map/convert_element_type | solution.py:1397
  243.7 10.5 %fusion.6 = f32[384,1024]{1,0:T(8,128)} fusion(bf16[1024,5248]{1,0:T(8,128)(2,1)} %bitcast.218, bf16[384,2624]{1,0:T(8,128)(2,1)S(1)} %get-tuple-element.95.refs_5_, bf16[384,2624]{1,0:T(8,128)(2,1)S(1)} %get-tuple-element.89.refs_4_), kind=kOutput, calls=%fused_computation.22 | convolution fusion | flops 4135256064 | bytes 16351232 | tf_op jit(solution)/shard_map/dot_general | solution.py:1400
  254.3 7.7 %multiply_reduce_fusion = (f32[]{:T(128)}, f32[]{:T(128)}, f32[384]{0:T(512)S(1)}, f32[1024]{0:T(1024)}, f32[]{:T(128)}, /*index=5*/bf16[384,1024]{1,0:T(8,128)(2,1)}) fusion(f32[384,1024]{1,0:T(8,128)S(1)} %get-tuple-element.92, pred[384]{0:T(512)(128)(4,1)S(1)} %fusion.37, f32[384,1024]{1,0:T(8,128)} %fusion.6, f32[1024]{0:T(1024)S(1)} %bitcast.205, ...), kind=kOutput, calls=%fused_computation.58 | convolution fusion | flops 2070674048 | bytes 12907404 | tf_op jit(solution)/shard_map/dot_general | solution.py:1373
  262.6 1.2 fusion.24
  263.9 1.3 copy-done.14
  265.2 1.0 fusion.25
  266.2 1.0 copy.63
  267.3 7.7 %all-to-all-start.4 = ((bf16[8,384,128]{2,1,0:T(8,128)(2,1)}), bf16[8,384,128]{2,1,0:T(8,128)(2,1)}, u32[]{:S(2)}, u32[]{:S(2)}) async-start(bf16[8,384,128]{2,1,0:T(8,128)(2,1)} %bitcast.186), calls=%async_computation.4 | async-start | bytes 1572864 | tf_op jit(solution)/shard_map/all_to_all | solution.py:1310
  275.0 2.2 copy_bitcast_fusion.1.refs_2_
  277.1 23.1 %early_products.1 = (bf16[2,4,320,128]{3,2,1,0:T(8,128)(2,1)}, bf16[2,4,320,128]{3,2,1,0:T(8,128)(2,1)}, bf16[2,4,336,128]{3,2,1,0:T(8,128)(2,1)}, bf16[2,4,336,...) custom-call(bf16[384,2624]{1,0:T(8,128)(2,1)} %copy-done.7, ...), custom_call_target="tpu_custom_call" | custom-call | tf_op jit(solution)/shard_map/early_products/pallas_call | solution.py:820
  300.2 1.4 collective-permute-start.2
  301.7 1.2 collective-permute-start.3
  302.9 6.9 %fusion.13.sine_ref = f32[3072,128]{1,0:T(8,128)} fusion(f32[24,128,128]{2,1,0:T(8,128)} %get-tuple-element.103, f32[24,128,128]{2,1,0:T(8,128)S(1)} %get-tuple-element.102, f32[128]{0:T(128)S(1)} %mul.508, f32[128]{0:T(128)S(1)} %get-tuple-element.115, f32[128]{0:T(128)S(1)} %get-tuple-element.116, f32[128]{0:T(128)S(1)} %get-tuple-element.117, ...), kind=kLoop, calls=%fused_computation.38 | loop fusion | flops 5505024 | bytes 4740608 | tf_op jit(solution)/shard_map/mul | solution.py:302
  310.1 5.3 %all-to-all-start.2 = ((bf16[8,48,1024]{2,1,0:T(8,128)(2,1)}), bf16[8,48,1024]{2,1,0:T(8,128)(2,1)}, u32[]{:S(2)}, u32[]{:S(2)}) async-start(bf16[8,48,1024]{2,1,0:T(8,128)(2,1)} %bitcast.193), calls=%async_computation.2 | async-start | bytes 1572864 | tf_op jit(solution)/shard_map/all_to_all | solution.py:1310
  315.5 6.9 %fusion.11.cosine_ref = f32[3072,128]{1,0:T(8,128)} fusion(f32[24,128,128]{2,1,0:T(8,128)} %get-tuple-element.103, f32[24,128,128]{2,1,0:T(8,128)S(1)} %get-tuple-element.102, f32[128]{0:T(128)S(1)} %get-tuple-element.115, f32[128]{0:T(128)S(1)} %get-tuple-element.116, f32[128]{0:T(128)S(1)} %get-tuple-element.117, f32[128]{0:T(128)S(1)} %get-tuple-element.118, ...), kind=kLoop, calls=%fused_computation.36 | loop fusion | flops 5111808 | bytes 4740096 | tf_op jit(solution)/shard_map/add | solution.py:300
  322.3 43.5 %attention_backward.1 = bf16[3072,384]{1,0:T(8,128)(2,1)} custom-call(s32[12]{0:T(128)} %get-tuple-element.87.low_ref, s32[12]{0:T(128)} %get-tuple-element.88.high_ref, s32[1,3072]{1,0:T(1,128)} %get-tuple-element.149.begin_ref, s32[1,3072]{1,0:T(1,128)} %get-tuple-element.148.end_ref, bf16[3072,384]{1,0:T(8,128)(2,1)} %get-tuple-element.42.qkv_ref, ...), custom_call_target="tpu_custom_call" | custom-call | flops 6039797760 | bytes 11796480 | tf_op jit(solution)/shard_map/attention_backward/pallas_call | solution.py:221
  365.8 4.3 copy.47
  370.1 4.8 all-to-all-start.5
  376.3 2.6 select_maximum_fusion
  378.9 2.8 gather_fusion.1
  381.7 1.9 fusion.30
  383.6 1.4 collective-permute-start.4
  385.0 1.2 fusion.29
  386.2 1.3 collective-permute-start.5
  387.4 2.2 fusion.27
  390.0 1.3 fusion.28
  391.5 9.3 %all-to-all-done.5 = bf16[8,384,384]{1,2,0:T(8,128)(2,1)} async-done(((bf16[8,384,384]{1,2,0:T(8,128)(2,1)}), bf16[8,384,384]{1,2,0:T(8,128)(2,1)}, u32[]{:S(2)}, u32[]{:S(2)}) %all-to-all-start.5) | async-done | bytes 2359328 | tf_op jit(solution)/shard_map/all_to_all | solution.py:1310
  400.9 4.4 copy.48
  405.3 3.8 copy.62
  409.1 4.9 fusion.21
  415.5 1.7 add_convert_fusion.3
  417.2 7.7 %all-to-all-start.6 = ((bf16[8,48,1024]{2,1,0:T(8,128)(2,1)}), bf16[8,48,1024]{2,1,0:T(8,128)(2,1)S(1)}, u32[]{:S(2)}, u32[]{:S(2)}) async-start(bf16[8,48,1024]{2,1,0:T(8,128)(2,1)} %bitcast.51), calls=%async_computation.6 | async-start | bytes 1572864 | tf_op jit(solution)/shard_map/all_to_all | solution.py:1310
  424.8 1.3 stack.41.refs_14_
  426.2 0.9 collective-permute-done.6.refs_10_
  427.6 82.2 %sum_weights.1 = (bf16[656,1024]{1,0:T(8,128)(2,1)}, bf16[256,5376]{1,0:T(8,128)(2,1)}, bf16[256,1024]{1,0:T(8,128)(2,1)}, bf16[256,3072]{1,0:T(8,128)(2,1)}, f32[2,8,1024]{2,1,0:T(8,128)}) custom-call(bf16[384,1024]{1,0:T(8,128)(2,1)} %fusion.19.refs_3_.refs_0_, bf16[384,3072]{1,0:T(8,128)(2,1)} %bitcast.183, ...), custom_call_target="tpu_custom_call" | custom-call | tf_op jit(solution)/shard_map/sum_weights/pallas_call | solution.py:1095
  509.8 0.8 fusion.51
  510.6 3.6 convert_element_type.238
  514.2 1.1 convert_element_type.239
  516.6 1.1 copy-done.18
  517.7 1.9 convert_element_type.241
  519.6 1.2 sqrt_bitcast_fusion
  520.8 3.0 maximum_convert_fusion
  523.8 0.9 gather_fusion.3
  524.9 1.3 broadcast_select_fusion
  (167 shorter events, 17.2 us)
Async XLA Ops:
  0.6 1.2 copy-start
  0.7 1.7 copy-start.19
  3.0 6.6 %copy-start.33 = (s32[1,6]{1,0:T(1,128)S(1)}, s32[1,6]{1,0:T(1,128)}, u32[]{:S(2)}) copy-start(s32[1,6]{1,0:T(1,128)} %param.15) | copy-start | bytes 76
  3.0 8.0 %copy-start.38 = (bf16[256]{0:T(256)(128)(2,1)S(1)}, bf16[256]{0:T(256)(128)(2,1)}, u32[]{:S(2)}) copy-start(bf16[256]{0:T(256)(128)(2,1)} %param.20) | copy-start | bytes 1540
  3.0 8.0 %copy-start.39 = (bf16[256]{0:T(256)(128)(2,1)S(1)}, bf16[256]{0:T(256)(128)(2,1)}, u32[]{:S(2)}) copy-start(bf16[256]{0:T(256)(128)(2,1)} %param.17) | copy-start | bytes 1540
  4.4 56.5 %all-to-all-start = ((bf16[8,48,1024]{2,1,0:T(8,128)(2,1)}), bf16[8,48,1024]{2,1,0:T(8,128)(2,1)S(1)}, u32[]{:S(2)}, u32[]{:S(2)}) async-start(bf16[8,48,1024]{2,1,0:T(8,128)(2,1)} %get-tuple-element.141), calls=%async_computation | async-start | bytes 1572864 | tf_op jit(solution)/shard_map/all_to_all | solution.py:1310
  52.2 13.0 %copy-start.22 = (f32[4,1,256]{2,1,0:T(1,128)}, f32[4,1,256]{2,1,0:T(1,128)S(1)}, u32[]{:S(2)}) copy-start(f32[4,1,256]{2,1,0:T(1,128)S(1)} %get-tuple-element.107) | copy-start | bytes 12292
  61.0 135.0 %all-to-all-start.3 = ((bf16[8,48,1024]{2,1,0:T(8,128)(2,1)}), bf16[8,48,1024]{2,1,0:T(8,128)(2,1)S(1)}, u32[]{:S(2)}, u32[]{:S(2)}) async-start(bf16[8,48,1024]{2,1,0:T(8,128)(2,1)} %get-tuple-element.140), calls=%async_computation.3 | async-start | bytes 1572864 | tf_op jit(solution)/shard_map/all_to_all | solution.py:1310
  64.8 98.6 %copy-start.24 = (f32[384]{0:T(512)}, f32[384]{0:T(512)S(1)}, u32[]{:S(2)}) copy-start(f32[384]{0:T(512)S(1)} %div.134) | copy-start | bytes 4612
  65.2 98.2 %copy-start.30 = (f32[384]{0:T(512)}, f32[384]{0:T(512)S(1)}, u32[]{:S(2)}) copy-start(f32[384]{0:T(512)S(1)} %add.141) | copy-start | bytes 4612
  65.2 98.2 %copy-start.26 = (f32[384]{0:T(512)}, f32[384]{0:T(512)S(1)}, u32[]{:S(2)}) copy-start(f32[384]{0:T(512)S(1)} %rsqrt.22) | copy-start | bytes 4612
  193.6 7.4 %copy-start.41 = (f32[2]{0:T(128)S(1)}, f32[2]{0:T(128)}, u32[]{:S(2)}) copy-start(f32[2]{0:T(128)} %constant.247.clone) | copy-start | bytes 28
  195.9 13.4 %all-to-all-start.1 = ((bf16[8,384,128]{2,1,0:T(8,128)(2,1)}), bf16[8,384,128]{2,1,0:T(8,128)(2,1)}, u32[]{:S(2)}, u32[]{:S(2)}) async-start(bf16[8,384,128]{2,1,0:T(8,128)(2,1)} %bitcast.16), calls=%async_computation.1 | async-start | bytes 1572864 | tf_op jit(solution)/shard_map/all_to_all | solution.py:1310
  201.0 61.6 %copy-start.35 = (pred[384]{0:T(512)(128)(4,1)}, pred[384]{0:T(512)(128)(4,1)S(1)}, u32[]{:S(2)}) copy-start(pred[384]{0:T(512)(128)(4,1)S(1)} %fusion.37) | copy-start | bytes 1156
  213.7 8.3 %slice-start = ((s8[5373952]{0:T(1024)(128)(4,1)}), s8[4194304]{0:T(1024)(128)(4,1)S(1)}, s32[]{:S(2)}) async-start(s8[5373952]{0:T(1024)(128)(4,1)} %bitcast.220), calls=%async_computation.7 | async-start | bytes 8388608
  214.0 8.0 %copy-start.10 = (bf16[384,1024]{1,0:T(8,128)(2,1)}, bf16[384,1024]{1,0:T(8,128)(2,1)S(1)}, u32[]{:S(2)}) copy-start(bf16[384,1024]{1,0:T(8,128)(2,1)S(1)} %multiply_convert_fusion.2.refs_1_) | copy-start | bytes 2359300
  214.0 8.0 %copy-start.20 = (bf16[8,48,1024]{2,1,0:T(8,128)(2,1)S(1)}, bf16[8,48,1024]{2,1,0:T(8,128)(2,1)}, u32[]{:S(2)}) copy-start(bf16[8,48,1024]{2,1,0:T(8,128)(2,1)} %select_convert_fusion) | copy-start | bytes 2359300
  214.0 8.0 %slice-start.1 = ((s8[5373952]{0:T(1024)(128)(4,1)}), s8[1179648]{0:T(1024)(128)(4,1)S(1)}, s32[]{:S(2)}) async-start(s8[5373952]{0:T(1024)(128)(4,1)} %bitcast.220), calls=%async_computation.8 | async-start | bytes 2359296
  222.0 13.8 %copy-start.5 = (f32[384,5248]{1,0:T(8,128)}, f32[384,5248]{1,0:T(8,128)S(1)}, u32[]{:S(2)}) copy-start(f32[384,5248]{1,0:T(8,128)S(1)} %fusion.54) | copy-start | bytes 24182788
  235.8 7.9 %copy-start.15 = (bf16[384,2624]{1,0:T(8,128)(2,1)}, bf16[384,2624]{1,0:T(8,128)(2,1)S(1)}, u32[]{:S(2)}) copy-start(bf16[384,2624]{1,0:T(8,128)(2,1)S(1)} %get-tuple-element.89.refs_4_) | copy-start | bytes 6045700
  243.6 10.6 %copy-start.6 = (bf16[384,2624]{1,0:T(8,128)(2,1)}, bf16[384,2624]{1,0:T(8,128)(2,1)S(1)}, u32[]{:S(2)}) copy-start(bf16[384,2624]{1,0:T(8,128)(2,1)S(1)} %get-tuple-element.95.refs_5_) | copy-start | bytes 6045700
  243.6 10.6 %copy-start.7 = (bf16[384,2624]{1,0:T(8,128)(2,1)}, bf16[384,2624]{1,0:T(8,128)(2,1)S(1)}, u32[]{:S(2)}) copy-start(bf16[384,2624]{1,0:T(8,128)(2,1)S(1)} %get-tuple-element.96.refs_0_) | copy-start | bytes 6045700
  243.7 10.6 %copy-start.16 = (f32[384,1024]{1,0:T(8,128)S(1)}, f32[384,1024]{1,0:T(8,128)}, u32[]{:S(2)}) copy-start(f32[384,1024]{1,0:T(8,128)} %get-tuple-element.142) | copy-start | bytes 4718596
  254.2 7.7 %copy-start.17 = (f32[384,1024]{1,0:T(8,128)S(1)}, f32[384,1024]{1,0:T(8,128)}, u32[]{:S(2)}) copy-start(f32[384,1024]{1,0:T(8,128)} %fusion.6) | copy-start | bytes 4718596
  262.5 1.4 copy-start.2
  262.5 1.4 copy-start.28
  262.6 2.6 copy-start.14
  263.9 2.3 copy-start.11
  267.3 42.8 %all-to-all-start.4 = ((bf16[8,384,128]{2,1,0:T(8,128)(2,1)}), bf16[8,384,128]{2,1,0:T(8,128)(2,1)}, u32[]{:S(2)}, u32[]{:S(2)}) async-start(bf16[8,384,128]{2,1,0:T(8,128)(2,1)} %bitcast.186), calls=%async_computation.4 | async-start | bytes 1572864 | tf_op jit(solution)/shard_map/all_to_all | solution.py:1310
  300.2 65.6 %collective-permute-start.2 = (bf16[2,4,32,3200]{3,2,1,0:T(8,128)(2,1)}, bf16[2,4,32,3200]{3,2,1,0:T(8,128)(2,1)}, u32[]{:S(2)}, u32[]{:S(2)}) collective-permute-start(bf16[2,4,32,3200]{3,2,1,0:T(8,128)(2,1)} %get-tuple-element.53), channel_id=1, source_target_pairs={{0,8},{4,12},{8,0},{12,4},{16,24},{20,28},{24,16},{28,20},{1,9},{5... | collective-permute-start | bytes 4915208 | tf_op jit(solution)/shard_map/ppermute | solution.py:1125
  301.7 64.2 %collective-permute-start.3 = (bf16[2,4,32,3200]{3,2,1,0:T(8,128)(2,1)}, bf16[2,4,32,3200]{3,2,1,0:T(8,128)(2,1)}, u32[]{:S(2)}, u32[]{:S(2)}) collective-permute-start(bf16[2,4,32,3200]{3,2,1,0:T(8,128)(2,1)} %get-tuple-element.55), channel_id=1, source_target_pairs={{0,16},{4,20},{8,24},{12,28},{16,0},{20,4},{24,8},{28,12},{1,17},{... | collective-permute-start | bytes 4915208 | tf_op jit(solution)/shard_map/ppermute | solution.py:1125
  309.8 56.0 %collective-permute-start = (bf16[2,4,320,128]{3,2,1,0:T(8,128)(2,1)}, bf16[2,4,320,128]{3,2,1,0:T(8,128)(2,1)}, u32[]{:S(2)}, u32[]{:S(2)}) collective-permute-start(bf16[2,4,320,128]{3,2,1,0:T(8,128)(2,1)} %get-tuple-element.49), channel_id=1, source_target_pairs={{0,8},{4,12},{8,0},{12,4},{16,24},{20,28},{24,16},{28,20},{1,9},{5... | collective-permute-start | bytes 1966088 | tf_op jit(solution)/shard_map/ppermute | solution.py:1125
  310.0 55.8 %collective-permute-start.1 = (bf16[2,4,336,128]{3,2,1,0:T(8,128)(2,1)}, bf16[2,4,336,128]{3,2,1,0:T(8,128)(2,1)}, u32[]{:S(2)}, u32[]{:S(2)}) collective-permute-start(bf16[2,4,336,128]{3,2,1,0:T(8,128)(2,1)} %get-tuple-element.51), channel_id=1, source_target_pairs={{0,16},{4,20},{8,24},{12,28},{16,0},{20,4},{24,8},{28,12},{1,17},{... | collective-permute-start | bytes 2064392 | tf_op jit(solution)/shard_map/ppermute | solution.py:1125
  310.1 60.0 %all-to-all-start.2 = ((bf16[8,48,1024]{2,1,0:T(8,128)(2,1)}), bf16[8,48,1024]{2,1,0:T(8,128)(2,1)}, u32[]{:S(2)}, u32[]{:S(2)}) async-start(bf16[8,48,1024]{2,1,0:T(8,128)(2,1)} %bitcast.193), calls=%async_computation.2 | async-start | bytes 1572864 | tf_op jit(solution)/shard_map/all_to_all | solution.py:1310
  370.1 5.5 %copy-start.40 = (s32[1,1,8]{2,1,0:T(1,128)S(1)}, s32[1,1,8]{2,1,0:T(1,128)}, u32[]{:S(2)}) copy-start(s32[1,1,8]{2,1,0:T(1,128)} %param.16) | copy-start | bytes 100
  370.1 30.7 %all-to-all-start.5 = ((bf16[8,384,384]{1,2,0:T(8,128)(2,1)}), bf16[8,384,384]{1,2,0:T(8,128)(2,1)}, u32[]{:S(2)}, u32[]{:S(2)}) async-start(bf16[8,384,384]{1,2,0:T(8,128)(2,1)} %copy.47), calls=%async_computation.5 | async-start | bytes 4718592 | tf_op jit(solution)/shard_map/all_to_all | solution.py:1310
  375.7 7.9 %copy-start.34 = (s32[1024]{0:T(1024)}, s32[1024]{0:T(1024)S(1)}, u32[]{:S(2)}) copy-start(s32[1024]{0:T(1024)S(1)} %pad_clamp_fusion) | copy-start | bytes 12292
  378.9 8.5 %copy-start.8 = (bf16[2,4,32,3200]{3,2,1,0:T(8,128)(2,1)S(1)}, bf16[2,4,32,3200]{3,2,1,0:T(8,128)(2,1)}, u32[]{:S(2)}) copy-start(bf16[2,4,32,3200]{3,2,1,0:T(8,128)(2,1)} %get-tuple-element.61.refs_8_) | copy-start | bytes 4915204
  383.6 6.4 %copy-start.9 = (bf16[2,4,32,3200]{3,2,1,0:T(8,128)(2,1)S(1)}, bf16[2,4,32,3200]{3,2,1,0:T(8,128)(2,1)}, u32[]{:S(2)}) copy-start(bf16[2,4,32,3200]{3,2,1,0:T(8,128)(2,1)} %get-tuple-element.63.refs_11_) | copy-start | bytes 4915204
  383.6 42.6 %collective-permute-start.4 = (bf16[4,320,128]{2,1,0:T(8,128)(2,1)}, bf16[4,320,128]{2,1,0:T(8,128)(2,1)}, u32[]{:S(2)}, u32[]{:S(2)}) collective-permute-start(bf16[4,320,128]{2,1,0:T(8,128)(2,1)} %fusion.30), channel_id=1, source_target_pairs={{0,16},{4,20},{8,24},{12,28},{16,0},{20,4},{24,8},{28,12},{1,17},{... | collective-permute-start | bytes 983048 | tf_op jit(solution)/shard_map/ppermute | solution.py:1125
  386.2 40.0 %collective-permute-start.5 = (bf16[4,336,128]{2,1,0:T(8,128)(2,1)S(1)}, bf16[4,336,128]{2,1,0:T(8,128)(2,1)}, u32[]{:S(2)}, u32[]{:S(2)}) collective-permute-start(bf16[4,336,128]{2,1,0:T(8,128)(2,1)S(1)} %fusion.29), channel_id=1, source_target_pairs={{0,8},{4,12},{8,0},{12,4},{16,24},{20,28},{24,16},{28,20},{1,9},{5... | collective-permute-start | bytes 1032200 | tf_op jit(solution)/shard_map/ppermute | solution.py:1125
  389.7 37.4 %collective-permute-start.6 = (bf16[4,32,3200]{2,1,0:T(8,128)(2,1)}, bf16[4,32,3200]{2,1,0:T(8,128)(2,1)}, u32[]{:S(2)}, u32[]{:S(2)}) collective-permute-start(bf16[4,32,3200]{2,1,0:T(8,128)(2,1)} %fusion.27), channel_id=1, source_target_pairs={{0,16},{4,20},{8,24},{12,28},{16,0},{20,4},{24,8},{28,12},{1,17},{... | collective-permute-start | bytes 2457608 | tf_op jit(solution)/shard_map/ppermute | solution.py:1125
  391.4 36.2 %collective-permute-start.7 = (bf16[4,32,3200]{2,1,0:T(8,128)(2,1)S(1)}, bf16[4,32,3200]{2,1,0:T(8,128)(2,1)}, u32[]{:S(2)}, u32[]{:S(2)}) collective-permute-start(bf16[4,32,3200]{2,1,0:T(8,128)(2,1)S(1)} %fusion.28), channel_id=1, source_target_pairs={{0,8},{4,12},{8,0},{12,4},{16,24},{20,28},{24,16},{28,20},{1,9},{5... | collective-permute-start | bytes 2457608 | tf_op jit(solution)/shard_map/ppermute | solution.py:1125
  405.3 3.8 copy-start.4
  405.3 3.8 copy-start.23
  405.3 3.8 copy-start.25
  409.1 5.0 copy-start.31
  409.1 5.0 copy-start.27
  414.1 1.4 copy-start.3
  414.1 1.4 copy-start.29
  414.1 1.4 copy-start.36
  415.5 9.4 %copy-start.32 = (f32[1024]{0:T(1024)S(1)}, f32[1024]{0:T(1024)}, u32[]{:S(2)}) copy-start(f32[1024]{0:T(1024)} %select_maximum_fusion) | copy-start | bytes 12292
  417.2 106.6 %all-to-all-start.6 = ((bf16[8,48,1024]{2,1,0:T(8,128)(2,1)}), bf16[8,48,1024]{2,1,0:T(8,128)(2,1)S(1)}, u32[]{:S(2)}, u32[]{:S(2)}) async-start(bf16[8,48,1024]{2,1,0:T(8,128)(2,1)} %bitcast.51), calls=%async_computation.6 | async-start | bytes 1572864 | tf_op jit(solution)/shard_map/all_to_all | solution.py:1310
  510.6 3.6 copy-start.21
  510.6 5.8 %copy-start.13 = (bf16[256,5376]{1,0:T(8,128)(2,1)S(1)}, bf16[256,5376]{1,0:T(8,128)(2,1)}, u32[]{:S(2)}) copy-start(bf16[256,5376]{1,0:T(8,128)(2,1)} %get-tuple-element.68) | copy-start | bytes 8257540
  516.4 1.3 copy-start.18
  520.8 3.9 copy-start.37
  523.8 1.1 copy-start.12
  523.8 2.5 copy-start.1

commit v3 on v2

--- a/solution.py
+++ b/solution.py
@@ -138,8 +138,6 @@
     attended_ref,
     grad_ref,
     log_ref,
-    cosine_ref,
-    sine_ref,
     *refs,
 ):
     out_ref, turned_ref, key_acc, value_acc = refs[-4:]
@@ -195,23 +193,19 @@
         jnp.zeros((width, head_count * block_q), jnp.float32),
     )
     grad_queries = head_pick(acc, head_count, block_q) * scale
-    out_ref[rows, :width] = turn_back(
-        grad_queries, cosine_ref[rows, :], sine_ref[rows, :], head_count
-    ).astype(jnp.bfloat16)
+    out_ref[rows, :width] = grad_queries.astype(jnp.bfloat16)
 
     @pl.when(step == pl.num_programs(0) - 1)
     def finish():
         @pl.loop(0, pl.num_programs(0))
         def each(index):
             span = pl.ds(pl.multiple_of(index * block_q, block_q), block_q)
-            out_ref[span, width : 2 * width] = turn_back(
-                key_acc[span, :], cosine_ref[span, :], sine_ref[span, :], head_count
-            ).astype(jnp.bfloat16)
+            out_ref[span, width : 2 * width] = key_acc[span, :].astype(jnp.bfloat16)
             out_ref[span, 2 * width :] = value_acc[span, :].astype(jnp.bfloat16)
 
 
 def attention_backward(
-    qkv, attended, grads, log_total, begin, end, low, high, cosine, sine, after, head_count, block_q, block_k
+    qkv, attended, grads, log_total, begin, end, low, high, after, head_count, block_q, block_k
 ):
     tokens = qkv.shape[0]
     width = head_count * HEAD_WIDTH
@@ -231,8 +225,6 @@
                 whole((tokens, width)),
                 whole((tokens, width)),
                 pl.BlockSpec((1, 1, head_count * block_q), lambda i, *_: (i, 0, 0)),
-                whole((tokens, width)),
-                whole((tokens, width)),
             ]
             + [pl.BlockSpec(memory_space=pl.ANY)] * len(after),
             out_specs=whole((tokens, 3 * width)),
@@ -246,7 +238,66 @@
             flops=pairs * 1280, bytes_accessed=tokens * width * 30, transcendentals=pairs
         ),
         name="attention_backward",
-    )(low, high, begin, end, qkv, attended, grads, log_total, cosine, sine, *after)
+    )(low, high, begin, end, qkv, attended, grads, log_total, *after)
+
+
+def rows_kernel(head_count, heads_ref, cosine_ref, sine_ref, query_ref, key_ref, value_ref, out_ref, act_ref):
+    width = heads_ref.shape[2] // 3
+    step = pl.program_id(0)
+    total = out_ref.shape[1] // 3
+    pieces = []
+    for part in range(3):
+        piece = heads_ref[0, :, part * width : (part + 1) * width]
+        if part < 2:
+            piece = turn_back(
+                piece.astype(jnp.float32), cosine_ref[...], sine_ref[...], head_count
+            ).astype(jnp.bfloat16)
+        first = pl.multiple_of(part * total + step * width, width)
+        out_ref[:, pl.ds(first, width)] = piece
+        pieces.append(piece)
+    weights = jnp.concatenate([query_ref[...], key_ref[...], value_ref[...]], axis=1)
+    product = lax.dot_general(
+        jnp.concatenate(pieces, axis=1), weights, NT, preferred_element_type=jnp.float32
+    )
+
+    @pl.when(step == 0)
+    def begin():
+        act_ref[...] = product
+
+    @pl.when(step > 0)
+    def add():
+        act_ref[...] += product
+
+
+def finish_rows(heads, cosine, sine, qkv_full, head_count):
+    owners, rows, columns = heads.shape
+    width = columns // 3
+    depth = qkv_full.shape[0]
+    whole = lambda shape: pl.BlockSpec(shape, lambda i: (0,) * len(shape))
+    part_of = lambda part: pl.BlockSpec((depth, width), lambda i: (0, part * owners + i))
+    return pl.pallas_call(
+        functools.partial(rows_kernel, head_count),
+        out_shape=(
+            jax.ShapeDtypeStruct((rows, owners * columns), jnp.bfloat16),
+            jax.ShapeDtypeStruct((rows, depth), jnp.float32),
+        ),
+        grid=(owners,),
+        in_specs=[
+            pl.BlockSpec((1, rows, columns), lambda i: (i, 0, 0)),
+            whole((rows, width)),
+            whole((rows, width)),
+            part_of(0),
+            part_of(1),
+            part_of(2),
+        ],
+        out_specs=(whole((rows, owners * columns)), whole((rows, depth))),
+        cost_estimate=pl.CostEstimate(
+            flops=2 * rows * depth * owners * columns,
+            bytes_accessed=2 * depth * owners * columns + 4 * rows * owners * columns,
+            transcendentals=0,
+        ),
+        name="finish_rows",
+    )(heads, cosine, sine, qkv_full, qkv_full, qkv_full)
 
 
 def spans(places, lengths_row):
@@ -275,31 +326,6 @@
         jnp.concatenate([cosine, cosine] * head_count, axis=1),
         jnp.concatenate([sine, -sine] * head_count, axis=1),
     )
-
-
-def pack_rotary_tables(lengths_row, tokens, head_count):
-    half, step = (HEAD_WIDTH // 2, math.gcd(tokens, 128))
-    inverse = 160000.0 ** (-2.0 * jnp.arange(half, dtype=jnp.float32) / HEAD_WIDTH)
-    inverse = jnp.tile(inverse, 2 * head_count)[None, :]
-    sign = jnp.tile(jnp.repeat(jnp.asarray([1.0, -1.0], jnp.float32), half), head_count)[None, :]
-    coarse = jnp.arange(0, tokens, step).astype(jnp.float32)[:, None] * inverse
-    fine = jnp.arange(step).astype(jnp.float32)[:, None] * inverse
-    begins = jnp.cumsum(lengths_row) - lengths_row
-    start = begins.astype(jnp.float32)[:, None] * inverse
-    cos_a, sin_a = (jnp.cos(coarse)[:, None, :], jnp.sin(coarse)[:, None, :])
-    cos_b, sin_b = (jnp.cos(fine)[None], jnp.sin(fine)[None])
-    cos_place = (cos_a * cos_b - sin_a * sin_b).reshape(tokens, -1)
-    sin_place = (sin_a * cos_b + cos_a * sin_b).reshape(tokens, -1)
-    place = lax.broadcasted_iota(jnp.int32, cos_place.shape, 0)
-    cos_all, sin_all = (jnp.cos(start), jnp.sin(start))
-    cos_start, sin_start = (cos_all[:1], sin_all[:1])
-    for at in range(1, lengths_row.shape[0]):
-        later = place >= begins[at]
-        cos_start = jnp.where(later, cos_all[at][None, :], cos_start)
-        sin_start = jnp.where(later, sin_all[at][None, :], sin_start)
-    cosine = cos_place * cos_start + sin_place * sin_start
-    sine = sin_place * cos_start - cos_place * sin_start
-    return (cosine, sine * sign)
 
 
 def toggled(index, bit):
@@ -1319,8 +1345,10 @@
     def to_rows(heads_in):
         return exchange(heads_in.reshape(ctx_count, row_count, -1))
 
-    arrived = exchange(to_slots(inputs[0]))
-    grad_arrived = exchange(to_slots(cotangent[0]))
+    both_arrived = exchange(
+        jnp.concatenate([to_slots(inputs[0]), to_slots(cotangent[0])], axis=1)
+    )
+    arrived, grad_arrived = (both_arrived[:, :piece_rows], both_arrived[:, piece_rows:])
     residual = arrived.reshape(row_count, model_width).astype(jnp.float32)
     places = own_index * row_count + jnp.arange(row_count, dtype=jnp.int32)
     unused_begin, unused_end, offset, is_valid = spans(places, lengths_row)
@@ -1337,9 +1365,10 @@
     gain_mlp = gains_full[:, 1].reshape(-1).astype(jnp.float32)
     act_attn = layer_norm(residual, gain_attn).astype(jnp.bfloat16)
     later = [attn_out, geglu_in, geglu_out]
+    row_cosine, row_sine = rotary_tables(offset, own_heads)
     if lax.axis_size("fsdp") == 4 and ctx_count == 8 and own_width == 128:
         attn_full, in_full, out_full, qkv_heads = gather_weights(
-            later, (act_attn, qkv_full) + rotary_tables(offset, own_heads)
+            later, (act_attn, qkv_full, row_cosine, row_sine)
         )
     else:
         attn_full, in_full, out_full = gather_weights(later)
@@ -1380,8 +1409,6 @@
         ]
     )
     out_slots = final_rows.astype(jnp.bfloat16).reshape(ctx_count, piece_rows, model_width)
-    back_out = exchange(out_slots)
-    block_out = jnp.take(back_out, own_route, axis=0).reshape(1, row_count, model_width)
     grad_mlp_low = grad_final.astype(jnp.bfloat16)
     grad_hidden = lax.dot_general(
         grad_mlp_low, out_full, NT, preferred_element_type=jnp.float32
@@ -1408,7 +1435,6 @@
     early = weight_sums_early(
         hidden, grad_mlp_low, act_mlp, grad_leading, grad_trailing, attn_low, grad_attn_low
     )
-    pack_cosine, pack_sine = pack_rotary_tables(lengths_row, tokens, own_heads)
     block_back = math.gcd(tokens, 256)
     low_back, high_back = key_range(pack_begin[0], pack_end[0], block_q, block_back)
     grad_heads = attention_backward(
@@ -1420,8 +1446,6 @@
         pack_end,
         low_back,
         high_back,
-        pack_cosine,
-        pack_sine,
         [] if early is None else [early[1][0][0]],
         own_heads,
         block_q,
@@ -1429,17 +1453,36 @@
     )
     if early is not None:
         grad_heads, early = second_step(grad_heads, early)
-    grad_projected = jnp.transpose(
-        to_rows(grad_heads).reshape(ctx_count, row_count, 3, own_width), (1, 2, 0, 3)
-    ).reshape(row_count, 3 * model_width)
-    grad_act_attn = lax.dot_general(
-        grad_projected, qkv_full, NT, preferred_element_type=jnp.float32
-    )
+    grad_rows = to_rows(grad_heads)
+    if own_width % 128 == 0:
+        grad_projected, grad_act_attn = finish_rows(
+            grad_rows, row_cosine, row_sine, qkv_full, own_heads
+        )
+    else:
+        by_part = jnp.transpose(
+            grad_rows.reshape(ctx_count, row_count, 3, own_width), (2, 1, 0, 3)
+        ).reshape(3, row_count, model_width)
+        cosine, sine = rotary_tables(offset, 1)
+        grad_projected = jnp.concatenate(
+            [
+                rotate(by_part[part].astype(jnp.float32), cosine, -sine).astype(jnp.bfloat16)
+                for part in (0, 1)
+            ]
+            + [by_part[2]],
+            axis=1,
+        )
+        grad_act_attn = lax.dot_general(
+            grad_projected, qkv_full, NT, preferred_element_type=jnp.float32
+        )
     unused_first, norm_back_attn = jax.vjp(layer_norm, residual, gain_attn)
     grad_resid_norm, grad_gain_attn = norm_back_attn(grad_act_attn)
     grad_residual = (grad_middle + grad_resid_norm).astype(jnp.bfloat16)
-    back_grad = exchange(grad_residual.reshape(ctx_count, piece_rows, model_width))
-    grad_inputs = jnp.take(back_grad, own_route, axis=0).reshape(1, row_count, model_width)
+    grad_slots = grad_residual.reshape(ctx_count, piece_rows, model_width)
+    back = exchange(jnp.concatenate([out_slots, grad_slots], axis=1))
+    block_out, grad_inputs = (
+        jnp.take(half, own_route, axis=0).reshape(1, row_count, model_width)
+        for half in (back[:, :piece_rows], back[:, piece_rows:])
+    )
     small = jnp.stack(
         [grad_gain_attn, grad_gain_mlp, jnp.pad(square_sums, (0, model_width - 3))]
         + [jnp.zeros((model_width,), jnp.float32)] * 5

time: 536 us -> 532 us (level)
  waiting for transfers between devices: 14.7 us -> 54.6 us
  local copies, waits for them, and re-layouts: 29.6 us -> 9.81 us
  other arithmetic: 69.6 us -> 55 us
  matrix products: 49.9 us -> 36.3 us
  Pallas kernels: 316 us -> 329 us
  starting transfers between devices: 44.8 us -> 36.9 us
    all_to_all x7 -> x5, waiting for transfers between devices: 13.3 us -> 52.8 us  [exchange(): lax.all_to_all(blocks, 'ctx', split_axis=0, concat_axis=0, tiled=True)]
    pallas_call x0 -> x1, Pallas kernels: none -> 11.4 us  [finish_rows(): pl.pallas_call(functools.partial(rows_kernel, head_count), out_shape=(jax...]
    all_to_all x7 -> x5, starting transfers between devices: 38.6 us -> 30.7 us  [exchange(): lax.all_to_all(blocks, 'ctx', split_axis=0, concat_axis=0, tiled=True)]
    mul x1 -> x0, other arithmetic: 6.9 us -> none  [pack_rotary_tables(): return (cosine, sine * sign)]
    add x1 -> x0, other arithmetic: 6.87 us -> none  [pack_rotary_tables(): cosine = cos_place * cos_start + sin_place * sin_start]
    unnamed x89 -> x40, local copies, waits for them, and re-layouts: 7.52 us -> 1.62 us
  transfers between devices with their start and end apart: 15 -> 13, of which waited for: 4 -> 5; matrix products, arithmetic and copies ran while one was open for 16% -> 8% of each run, Pallas kernels for 60% -> 34%
where the time goes in v3:
time: 532 us; the launch traced here: 524 us
  Pallas kernels  329 us (62%)
  other arithmetic  55 us (10%)
  waiting for transfers between devices  54.6 us (10%)
  starting transfers between devices  36.9 us (7%)
  matrix products  36.3 us (7%)
  local copies, waits for them, and re-layouts  9.81 us (2%)
    pallas_call x2, Pallas kernels, gather_weights(): pl.pallas_call(functools.partial(gather_kernel, shapes, projection is not...  136 us
    pallas_call x1, Pallas kernels, sum_weights(): pl.pallas_call(functools.partial(sum_kernel, early, late, plan_lead(plan)...  85.7 us
    all_to_all x5, waiting for transfers between devices, exchange(): lax.all_to_all(blocks, 'ctx', split_axis=0, concat_axis=0, tiled=True)  52.8 us
    pallas_call x1, Pallas kernels, attention_backward(): pl.pallas_call(functools.partial(backward_kernel, head_count, block_q, bl...  39.6 us
    all_to_all x5, starting transfers between devices, exchange(): lax.all_to_all(blocks, 'ctx', split_axis=0, concat_axis=0, tiled=True)  30.7 us
    pallas_call x1, Pallas kernels, attention_forward(): pl.pallas_call(functools.partial(forward_kernel, head_count, block_q, blo...  30.1 us
    pallas_call x1, Pallas kernels, early_sums(): pl.pallas_call(functools.partial(product_kernel, plan, plan_lead(plan)),...  26.1 us
    pallas_call x1, Pallas kernels, finish_rows(): pl.pallas_call(functools.partial(rows_kernel, head_count), out_shape=(jax...  11.4 us
  transfers between devices with their start and end apart: 13, of which 5 were waited for; matrix products, arithmetic and copies ran while one was open for 8% of the time, Pallas kernels for 34%

profile of v3, /device:TPU:1, one launch (start us, length us, event | category | flops | bytes accessed | tf_op | source)
XLA Modules:
  0.0 523.8 jit_solution(11576113956826397404)
XLA Ops:
  0.7 0.9 select_reduce_fusion.6
  1.6 0.7 compare_and_fusion
  3.7 1.3 pad_maximum_fusion
  5.0 5.3 %all-to-all-start = ((bf16[8,96,1024]{2,1,0:T(8,128)(2,1)}), bf16[8,96,1024]{2,1,0:T(8,128)(2,1)S(1)}, u32[]{:S(2)}, u32[]{:S(2)}) async-start(bf16[8,96,1024]{2,1,0:T(8,128)(2,1)} %pad_maximum_fusion), calls=%async_computation | async-start | bytes 3145728 | tf_op jit(solution)/shard_map/all_to_all | solution.py:1336
  11.1 0.6 fusion.48
  12.0 0.6 fusion.33.refs_0_
  12.6 0.8 multiply_sine_fusion
  13.4 0.7 add_compare_fusion.1
  14.1 39.7 %gather_weights.1 = (bf16[4,16,256]{2,1,0:T(8,128)(2,1)}, bf16[4,2,4,32,3072]{4,3,2,1,0:T(8,128)(2,1)}) custom-call(bf16[16,256]{1,0:T(8,128)(2,1)} %fusion.33.refs_0_, bf16[2,4,32,3072]{3,2,1,0:T(8,128)(2,1)} %bitcast.130), custom_call_target="tpu_custom_call" | custom-call | tf_op jit(solution)/shard_map/gather_weights/pallas_call | solution.py:597
  53.8 0.8 fusion.30
  54.6 1.1 pad_maximum_fusion.2
  55.7 0.6 fusion.38
  56.3 0.8 slice_convert_fusion
  57.1 1.3 compare_select_fusion.1
  59.2 1.2 fusion.16.refs_3_.refs_0_
  60.4 96.4 %gather_and_project.1 = (bf16[4,2,4,32,1024]{4,3,2,1,0:T(8,128)(2,1)}, bf16[4,2,4,32,5248]{4,3,2,1,0:T(8,128)(2,1)}, bf16[4,656,1024]{2,1,0:T(8,128)(2,1)}, bf16[3072,384]{1,0:T(8,128)(2,1)}) custom-call(bf16[2,4,32,1024]{3,2,1,0:T(8,128)(2,1)} %bitcast.136, bf16[2,4,32,5248]{3,2,1,0:T(8,128)(2,1)} %bitcast.126, bf16[656,1024]{1,0:T(8,128)(2,1)} %refs_2_.1, ...), custom_call_target="tpu_custom_call" | custom-call | tf_op jit(solution)/shard_map/gather_and_project/pallas_call | solution.py:597
  156.8 30.1 %attention_forward.1 = (f32[3072,128]{1,0:T(8,128)}, f32[12,1,512]{2,1,0:T(1,128)}) custom-call(s32[12]{0:T(128)} %get-tuple-element.115.low_ref, s32[12]{0:T(128)} %get-tuple-element.116.high_ref, s32[1,3072]{1,0:T(1,128)} %get-tuple-element.127.begin_ref, s32[1,3072]{1,0:T(1,128)} %get-tuple-element.126.end_ref, bf16[3072,384]{1,0:T(8,128)(2,1)} %get-tuple-element.44.qkv_ref), custom_call_target="tpu_custom_call" | custom-call | flops 2415919104 | bytes 4718592 | tf_op jit(solution)/shard_map/attention_forward/pallas_call | solution.py:97
  187.0 2.4 convert_element_type.169
  189.3 3.7 all-to-all-start.1
  193.0 0.7 fusion.34
  193.7 8.4 %all-to-all-done.1 = bf16[8,384,128]{2,1,0:T(8,128)(2,1)S(1)} async-done(((bf16[8,384,128]{2,1,0:T(8,128)(2,1)}), bf16[8,384,128]{2,1,0:T(8,128)(2,1)S(1)}, u32[]{:S(2)}, u32[]{:S(2)}) %all-to-all-start.1) | async-done | bytes 786464 | tf_op jit(solution)/shard_map/all_to_all | solution.py:1336
  202.1 4.1 fusion.44
  206.9 0.8 copy-done.17
  207.6 4.5 fusion.49
  212.1 10.0 %multiply_convert_fusion.1 = (bf16[384,2624]{1,0:T(8,128)(2,1)}, f32[384,2624]{1,0:T(8,128)S(1)}) fusion(f32[384,5248]{1,0:T(8,128)S(1)} %fusion.49), kind=kLoop, calls=%fused_computation.8 | loop fusion | flops 66502656 | bytes 14106624 | tf_op jit(solution)/shard_map/convert_element_type | solution.py:1399
  222.1 9.0 %add_convert_fusion = (bf16[384,2624]{1,0:T(8,128)(2,1)}, bf16[384,2624]{1,0:T(8,128)(2,1)}) fusion(f32[384,2624]{1,0:T(8,128)S(1)} %get-tuple-element.92, f32[384,5248]{1,0:T(8,128)S(1)} %fusion.49, bf16[384,1024]{1,0:T(8,128)(2,1)S(1)} %bitcast.133, bf16[2624,1024]{1,0:T(8,128)(2,1)} %bitcast.159), kind=kOutput, calls=%fused_computation.7 | convolution fusion | flops 2081734656 | bytes 22282240 | tf_op jit(solution)/shard_map/dot_general | solution.py:1413
  231.1 8.9 %fusion.6 = f32[384,1024]{1,0:T(8,128)S(1)} fusion(bf16[1024,5248]{1,0:T(8,128)(2,1)} %bitcast.157, bf16[384,2624]{1,0:T(8,128)(2,1)} %get-tuple-element.98.refs_5_, bf16[384,2624]{1,0:T(8,128)(2,1)} %get-tuple-element.97.refs_4_), kind=kOutput, calls=%fused_computation.22 | convolution fusion | flops 4135256064 | bytes 16351232 | tf_op jit(solution)/shard_map/dot_general | solution.py:1427
  240.0 7.0 %multiply_reduce_fusion = (f32[]{:T(128)}, f32[]{:T(128)}, f32[384]{0:T(512)S(1)}, f32[1024]{0:T(1024)S(1)}, f32[]{:T(128)}, /*index=5*/bf16[384,1024]{1,0:T(8,128)(2,1)}) fusion(f32[384,1024]{1,0:T(8,128)S(1)} %get-tuple-element.94, pred[384]{0:T(512)(128)(4,1)S(1)} %fusion.34, f32[384,1024]{1,0:T(8,128)S(1)} %fusion.6, f32[1024]{0:T(1024)S(1)} %bitcast.144, ...), kind=kOutput, calls=%fused_computation.52 | convolution fusion | flops 2070674048 | bytes 12907404 | tf_op jit(solution)/shard_map/dot_general | solution.py:1402
  248.1 1.0 copy_bitcast_fusion.refs_2_
  249.2 1.5 fusion.21
  250.6 26.1 %early_products.1 = (bf16[2,4,320,128]{3,2,1,0:T(8,128)(2,1)}, bf16[2,4,320,128]{3,2,1,0:T(8,128)(2,1)}, bf16[2,4,336,128]{3,2,1,0:T(8,128)(2,1)}, bf16[2,4,336,...) custom-call(bf16[384,2624]{1,0:T(8,128)(2,1)} %get-tuple-element.91., ...), custom_call_target="tpu_custom_call" | custom-call | tf_op jit(solution)/shard_map/early_products/pallas_call | solution.py:846
  277.3 2.9 fusion.22
  280.2 1.0 copy.44
  281.2 5.1 all-to-all-start.2
  286.4 1.4 collective-permute-start.1
  287.8 1.2 collective-permute-start
  288.9 32.0 %all-to-all-done.2 = bf16[8,384,128]{2,1,0:T(8,128)(2,1)} async-done(((bf16[8,384,128]{2,1,0:T(8,128)(2,1)}), bf16[8,384,128]{2,1,0:T(8,128)(2,1)}, u32[]{:S(2)}, u32[]{:S(2)}) %all-to-all-start.2) | async-done | bytes 786464 | tf_op jit(solution)/shard_map/all_to_all | solution.py:1336
  321.0 39.6 %attention_backward.1 = bf16[3072,384]{1,0:T(8,128)(2,1)} custom-call(s32[12]{0:T(128)} %get-tuple-element.89.low_ref, s32[12]{0:T(128)} %get-tuple-element.90.high_ref, s32[1,3072]{1,0:T(1,128)} %get-tuple-element.127.begin_ref, s32[1,3072]{1,0:T(1,128)} %get-tuple-element.126.end_ref, bf16[3072,384]{1,0:T(8,128)(2,1)} %get-tuple-element.44.qkv_ref, ...), custom_call_target="tpu_custom_call" | custom-call | flops 6039797760 | bytes 11796480 | tf_op jit(solution)/shard_map/attention_backward/pallas_call | solution.py:215
  360.6 8.9 %all-to-all-start.3 = ((bf16[8,384,384]{2,1,0:T(8,128)(2,1)}), bf16[8,384,384]{2,1,0:T(8,128)(2,1)}, u32[]{:S(2)}, u32[]{:S(2)}) async-start(bf16[8,384,384]{2,1,0:T(8,128)(2,1)} %bitcast.127), calls=%async_computation.3 | async-start | bytes 4718592 | tf_op jit(solution)/shard_map/all_to_all | solution.py:1336
  370.2 2.2 select_maximum_fusion
  372.4 2.0 fusion.27
  374.4 1.4 collective-permute-start.4
  375.8 1.2 fusion.26
  376.9 1.3 collective-permute-start.5
  378.2 2.2 fusion.24
  380.7 2.2 fusion.25
  383.0 12.4 %all-to-all-done.3.heads_ref = bf16[8,384,384]{2,1,0:T(8,128)(2,1)} async-done(((bf16[8,384,384]{2,1,0:T(8,128)(2,1)}), bf16[8,384,384]{2,1,0:T(8,128)(2,1)}, u32[]{:S(2)}, u32[]{:S(2)}) %all-to-all-start.3) | async-done | bytes 2359328 | tf_op jit(solution)/shard_map/all_to_all | solution.py:1336
  395.4 11.4 %finish_rows.1 = (bf16[384,3072]{1,0:T(8,128)(2,1)}, f32[384,1024]{1,0:T(8,128)}) custom-call(bf16[8,384,384]{2,1,0:T(8,128)(2,1)} %all-to-all-done.3.heads_ref, f32[384,128]{1,0:T(8,128)} %get-tuple-element.128.refs_5_.cosine_ref, f32[384,128]{1,0:T(8,128)} %get-tuple-element.129.refs_6_.sine_ref, bf16[1024,3072]{1,0:T(8,128)(2,1)} %bitcast.121, ...), custom_call_target="tpu_custom_call" | custom-call | flops 2415919104 | bytes 11010048 | tf_op jit(solution)/shard_map/finish_rows/pallas_call | solution.py:278
  406.8 1.9 fusion.18
  408.7 0.8 fusion.17
  409.5 1.0 add_convert_fusion.3
  410.7 1.3 pad_maximum_fusion.1
  412.0 7.7 %all-to-all-start.4 = ((bf16[8,96,1024]{2,1,0:T(8,128)(2,1)}), bf16[8,96,1024]{2,1,0:T(8,128)(2,1)S(1)}, u32[]{:S(2)}, u32[]{:S(2)}) async-start(bf16[8,96,1024]{2,1,0:T(8,128)(2,1)} %pad_maximum_fusion.1), calls=%async_computation.4 | async-start | bytes 3145728 | tf_op jit(solution)/shard_map/all_to_all | solution.py:1336
  419.7 0.7 stack.41.refs_14_
  420.3 1.3 collective-permute-done.6.refs_10_
  422.1 85.7 %sum_weights.1 = (bf16[656,1024]{1,0:T(8,128)(2,1)}, bf16[256,5376]{1,0:T(8,128)(2,1)}, bf16[256,1024]{1,0:T(8,128)(2,1)}, bf16[256,3072]{1,0:T(8,128)(2,1)}, f32[2,8,1024]{2,1,0:T(8,128)}) custom-call(bf16[384,1024]{1,0:T(8,128)(2,1)} %fusion.16.refs_3_.refs_0_, bf16[384,3072]{1,0:T(8,128)(2,1)} %get-tuple-element.60.refs_1_, ...), custom_call_target="tpu_custom_call" | custom-call | tf_op jit(solution)/shard_map/sum_weights/pallas_call | solution.py:1121
  507.8 0.8 fusion.47
  508.6 3.6 convert_element_type.202
  512.2 1.1 convert_element_type.203
  514.4 1.8 convert_element_type.205
  516.2 1.2 sqrt_bitcast_fusion
  517.7 3.0 maximum_convert_fusion
  520.8 0.6 gather_fusion.3
  522.1 1.3 broadcast_select_fusion
  (93 shorter events, 8.9 us)
Async XLA Ops:
  0.6 1.6 copy-start
  0.7 2.2 copy-start.12
  4.9 5.4 %copy-start.15 = (s32[1,6]{1,0:T(1,128)S(1)}, s32[1,6]{1,0:T(1,128)}, u32[]{:S(2)}) copy-start(s32[1,6]{1,0:T(1,128)} %param.14) | copy-start | bytes 76
  4.9 6.8 %copy-start.18 = (bf16[256]{0:T(256)(128)(2,1)S(1)}, bf16[256]{0:T(256)(128)(2,1)}, u32[]{:S(2)}) copy-start(bf16[256]{0:T(256)(128)(2,1)} %param.19) | copy-start | bytes 1540
  4.9 6.8 %copy-start.19 = (bf16[256]{0:T(256)(128)(2,1)S(1)}, bf16[256]{0:T(256)(128)(2,1)}, u32[]{:S(2)}) copy-start(bf16[256]{0:T(256)(128)(2,1)} %param.16) | copy-start | bytes 1540
  5.0 53.4 %all-to-all-start = ((bf16[8,96,1024]{2,1,0:T(8,128)(2,1)}), bf16[8,96,1024]{2,1,0:T(8,128)(2,1)S(1)}, u32[]{:S(2)}, u32[]{:S(2)}) async-start(bf16[8,96,1024]{2,1,0:T(8,128)(2,1)} %pad_maximum_fusion), calls=%async_computation | async-start | bytes 3145728 | tf_op jit(solution)/shard_map/all_to_all | solution.py:1336
  189.3 12.8 %all-to-all-start.1 = ((bf16[8,384,128]{2,1,0:T(8,128)(2,1)}), bf16[8,384,128]{2,1,0:T(8,128)(2,1)S(1)}, u32[]{:S(2)}, u32[]{:S(2)}) async-start(bf16[8,384,128]{2,1,0:T(8,128)(2,1)} %bitcast.17), calls=%async_computation.1 | async-start | bytes 1572864 | tf_op jit(solution)/shard_map/all_to_all | solution.py:1336
  202.1 4.1 copy-start.4
  202.1 5.5 %copy-start.17 = (bf16[4,2,4,32,5248]{4,3,2,1,0:T(8,128)(2,1)S(1)}, bf16[4,2,4,32,5248]{4,3,2,1,0:T(8,128)(2,1)}, u32[]{:S(2)}) copy-start(bf16[4,2,4,32,5248]{4,3,2,1,0:T(8,128)(2,1)} %get-tuple-element.47) | copy-start | bytes 32243716
  206.9 5.3 %copy-start.8 = (bf16[384,1024]{1,0:T(8,128)(2,1)}, bf16[384,1024]{1,0:T(8,128)(2,1)S(1)}, u32[]{:S(2)}) copy-start(bf16[384,1024]{1,0:T(8,128)(2,1)S(1)} %multiply_convert_fusion.2.refs_1_) | copy-start | bytes 2359300
  231.1 8.9 %copy-start.3 = (bf16[384,2624]{1,0:T(8,128)(2,1)S(1)}, bf16[384,2624]{1,0:T(8,128)(2,1)}, u32[]{:S(2)}) copy-start(bf16[384,2624]{1,0:T(8,128)(2,1)} %get-tuple-element.91.refs_0_) | copy-start | bytes 6045700
  231.1 8.9 %copy-start.10 = (f32[384,1024]{1,0:T(8,128)S(1)}, f32[384,1024]{1,0:T(8,128)}, u32[]{:S(2)}) copy-start(f32[384,1024]{1,0:T(8,128)} %get-tuple-element.123) | copy-start | bytes 4718596
  247.0 1.1 copy-start.5
  276.7 83.8 %collective-permute-start.2 = (bf16[2,4,32,3200]{3,2,1,0:T(8,128)(2,1)}, bf16[2,4,32,3200]{3,2,1,0:T(8,128)(2,1)}, u32[]{:S(2)}, u32[]{:S(2)}) collective-permute-start(bf16[2,4,32,3200]{3,2,1,0:T(8,128)(2,1)} %get-tuple-element.55), channel_id=1, source_target_pairs={{0,8},{4,12},{8,0},{12,4},{16,24},{20,28},{24,16},{28,20},{1,9},{5... | collective-permute-start | bytes 4915208 | tf_op jit(solution)/shard_map/ppermute | solution.py:1151
  277.1 83.5 %collective-permute-start.3 = (bf16[2,4,32,3200]{3,2,1,0:T(8,128)(2,1)}, bf16[2,4,32,3200]{3,2,1,0:T(8,128)(2,1)}, u32[]{:S(2)}, u32[]{:S(2)}) collective-permute-start(bf16[2,4,32,3200]{3,2,1,0:T(8,128)(2,1)} %get-tuple-element.57), channel_id=1, source_target_pairs={{0,16},{4,20},{8,24},{12,28},{16,0},{20,4},{24,8},{28,12},{1,17},{... | collective-permute-start | bytes 4915208 | tf_op jit(solution)/shard_map/ppermute | solution.py:1151
  281.2 39.7 %all-to-all-start.2 = ((bf16[8,384,128]{2,1,0:T(8,128)(2,1)}), bf16[8,384,128]{2,1,0:T(8,128)(2,1)}, u32[]{:S(2)}, u32[]{:S(2)}) async-start(bf16[8,384,128]{2,1,0:T(8,128)(2,1)} %bitcast.124), calls=%async_computation.2 | async-start | bytes 1572864 | tf_op jit(solution)/shard_map/all_to_all | solution.py:1336
  286.4 74.2 %collective-permute-start.1 = (bf16[2,4,336,128]{3,2,1,0:T(8,128)(2,1)}, bf16[2,4,336,128]{3,2,1,0:T(8,128)(2,1)}, u32[]{:S(2)}, u32[]{:S(2)}) collective-permute-start(bf16[2,4,336,128]{3,2,1,0:T(8,128)(2,1)} %get-tuple-element.53), channel_id=1, source_target_pairs={{0,16},{4,20},{8,24},{12,28},{16,0},{20,4},{24,8},{28,12},{1,17},{... | collective-permute-start | bytes 2064392 | tf_op jit(solution)/shard_map/ppermute | solution.py:1151
  287.8 72.8 %collective-permute-start = (bf16[2,4,320,128]{3,2,1,0:T(8,128)(2,1)}, bf16[2,4,320,128]{3,2,1,0:T(8,128)(2,1)}, u32[]{:S(2)}, u32[]{:S(2)}) collective-permute-start(bf16[2,4,320,128]{3,2,1,0:T(8,128)(2,1)} %get-tuple-element.51), channel_id=1, source_target_pairs={{0,8},{4,12},{8,0},{12,4},{16,24},{20,28},{24,16},{28,20},{1,9},{5... | collective-permute-start | bytes 1966088 | tf_op jit(solution)/shard_map/ppermute | solution.py:1151
  360.6 9.6 %copy-start.16 = (s32[1,1,8]{2,1,0:T(1,128)S(1)}, s32[1,1,8]{2,1,0:T(1,128)}, u32[]{:S(2)}) copy-start(s32[1,1,8]{2,1,0:T(1,128)} %param.15) | copy-start | bytes 100
  360.6 34.8 %all-to-all-start.3 = ((bf16[8,384,384]{2,1,0:T(8,128)(2,1)}), bf16[8,384,384]{2,1,0:T(8,128)(2,1)}, u32[]{:S(2)}, u32[]{:S(2)}) async-start(bf16[8,384,384]{2,1,0:T(8,128)(2,1)} %bitcast.127), calls=%async_computation.3 | async-start | bytes 4718592 | tf_op jit(solution)/shard_map/all_to_all | solution.py:1336
  370.2 8.0 %copy-start.6 = (bf16[2,4,32,3200]{3,2,1,0:T(8,128)(2,1)S(1)}, bf16[2,4,32,3200]{3,2,1,0:T(8,128)(2,1)}, u32[]{:S(2)}) copy-start(bf16[2,4,32,3200]{3,2,1,0:T(8,128)(2,1)} %get-tuple-element.65.refs_8_) | copy-start | bytes 4915204
  372.4 8.3 %copy-start.7 = (bf16[2,4,32,3200]{3,2,1,0:T(8,128)(2,1)S(1)}, bf16[2,4,32,3200]{3,2,1,0:T(8,128)(2,1)}, u32[]{:S(2)}) copy-start(bf16[2,4,32,3200]{3,2,1,0:T(8,128)(2,1)} %get-tuple-element.67.refs_11_) | copy-start | bytes 4915204
  374.4 45.9 %collective-permute-start.4 = (bf16[4,320,128]{2,1,0:T(8,128)(2,1)}, bf16[4,320,128]{2,1,0:T(8,128)(2,1)}, u32[]{:S(2)}, u32[]{:S(2)}) collective-permute-start(bf16[4,320,128]{2,1,0:T(8,128)(2,1)} %fusion.27), channel_id=1, source_target_pairs={{0,16},{4,20},{8,24},{12,28},{16,0},{20,4},{24,8},{28,12},{1,17},{... | collective-permute-start | bytes 983048 | tf_op jit(solution)/shard_map/ppermute | solution.py:1151
  376.9 43.4 %collective-permute-start.5 = (bf16[4,336,128]{2,1,0:T(8,128)(2,1)S(1)}, bf16[4,336,128]{2,1,0:T(8,128)(2,1)}, u32[]{:S(2)}, u32[]{:S(2)}) collective-permute-start(bf16[4,336,128]{2,1,0:T(8,128)(2,1)S(1)} %fusion.26), channel_id=1, source_target_pairs={{0,8},{4,12},{8,0},{12,4},{16,24},{20,28},{24,16},{28,20},{1,9},{5... | collective-permute-start | bytes 1032200 | tf_op jit(solution)/shard_map/ppermute | solution.py:1151
  380.4 41.2 %collective-permute-start.6 = (bf16[4,32,3200]{2,1,0:T(8,128)(2,1)}, bf16[4,32,3200]{2,1,0:T(8,128)(2,1)}, u32[]{:S(2)}, u32[]{:S(2)}) collective-permute-start(bf16[4,32,3200]{2,1,0:T(8,128)(2,1)} %fusion.24), channel_id=1, source_target_pairs={{0,16},{4,20},{8,24},{12,28},{16,0},{20,4},{24,8},{28,12},{1,17},{... | collective-permute-start | bytes 2457608 | tf_op jit(solution)/shard_map/ppermute | solution.py:1151
  382.9 39.2 %collective-permute-start.7 = (bf16[4,32,3200]{2,1,0:T(8,128)(2,1)}, bf16[4,32,3200]{2,1,0:T(8,128)(2,1)}, u32[]{:S(2)}, u32[]{:S(2)}) collective-permute-start(bf16[4,32,3200]{2,1,0:T(8,128)(2,1)} %fusion.25), channel_id=1, source_target_pairs={{0,8},{4,12},{8,0},{12,4},{16,24},{20,28},{24,16},{28,20},{1,9},{5... | collective-permute-start | bytes 2457608 | tf_op jit(solution)/shard_map/ppermute | solution.py:1151
  406.8 1.9 copy-start.2
  409.5 1.1 copy-start.13
  412.0 108.7 %all-to-all-start.4 = ((bf16[8,96,1024]{2,1,0:T(8,128)(2,1)}), bf16[8,96,1024]{2,1,0:T(8,128)(2,1)S(1)}, u32[]{:S(2)}, u32[]{:S(2)}) async-start(bf16[8,96,1024]{2,1,0:T(8,128)(2,1)} %pad_maximum_fusion.1), calls=%async_computation.4 | async-start | bytes 3145728 | tf_op jit(solution)/shard_map/all_to_all | solution.py:1336
  508.6 3.6 copy-start.14
  508.6 5.8 %copy-start.11 = (bf16[656,1024]{1,0:T(8,128)(2,1)S(1)}, bf16[656,1024]{1,0:T(8,128)(2,1)}, u32[]{:S(2)}) copy-start(bf16[656,1024]{1,0:T(8,128)(2,1)} %get-tuple-element.73) | copy-start | bytes 4030468
  513.3 4.2 copy-start.9
  521.4 2.0 copy-start.1

commit v4 on v3

--- a/solution.py
+++ b/solution.py
@@ -332,16 +332,19 @@
     return index + bit - 2 * bit * ((index // bit) % 2)
 
 
-def gather_kernel(shapes, projects, *refs):
-    count = len(shapes)
-    shard_refs, refs = (refs[:count], refs[count:])
+def gather_kernel(arrays, parts, projects, *refs):
+    count = len(parts)
+    array_shards, refs = (refs[:arrays], refs[arrays:])
     if projects:
         act_ref, qkv_ref, cosine_ref, sine_ref = refs[:4]
-        heads_ref = refs[4 + count]
-        columns_ref, held_ref, load_sem, head_send, head_recv, own_sem = refs[count + 8 :]
-        refs = refs[4 : 4 + count] + refs[count + 5 : count + 8]
-    full_refs = refs[:count]
-    send_sem, recv_sem, local_sem = refs[count:]
+        heads_ref = refs[4 + arrays]
+        columns_ref, held_ref, load_sem, head_send, head_recv, own_sem = refs[arrays + 8 :]
+        refs = refs[4 : 4 + arrays] + refs[arrays + 5 : arrays + 8]
+    array_fulls = refs[:arrays]
+    send_sem, recv_sem, local_sem = refs[arrays:]
+    shapes = [part[0] for part in parts]
+    shard_refs = [array_shards[part[1]] for part in parts]
+    full_refs = [array_fulls[part[1]] for part in parts]
     shards = lax.axis_size("fsdp")
     slices = lax.axis_size("ctx") // 2
     own_ctx, own_shard = (lax.axis_index("ctx"), lax.axis_index("fsdp"))
@@ -379,9 +382,10 @@
         if shapes[weight] == "rows":
             rows = ref.shape[-2]
             span = pl.ds(0, rows) if half is None else pl.ds(half * (rows // 2), rows // 2)
+            columns = pl.ds(parts[weight][2], parts[weight][3])
             if len(ref.shape) == 4:
-                return ref.at[core, chip_at, span, :]
-            return ref.at[shard_at(step), core, chip_at, span, :]
+                return ref.at[core, chip_at, span, columns]
+            return ref.at[shard_at(step), core, chip_at, span, columns]
         rows = ref.shape[-2]
         first = (rows // 2) // 16 * 16
         spans_of = {None: pl.ds(0, rows), 0: pl.ds(0, first), 1: pl.ds(first, rows - first)}
@@ -393,7 +397,7 @@
 
     def core_region(ref, weight, step):
         if shapes[weight] == "rows":
-            return ref.at[shard_at(step), core]
+            return ref.at[shard_at(step), core, :, :, pl.ds(parts[weight][2], parts[weight][3])]
         width = ref.shape[-1] // 2
         return ref.at[shard_at(step), :, pl.ds(pl.multiple_of(core * width, width), width)]
 
@@ -423,10 +427,11 @@
         target = region(full_refs[weight], weight, 0, chip, None)
         copies[weight, 2, 0] = send(source, target, slot_of(weight, 2, 0), to_two)
         copies[weight, 1, 0] = send(source, target, slot_of(weight, 1, 0), to_one)
-        target = full_refs[weight].at[own_shard]
-        copy = pltpu.make_async_copy(shard_refs[weight], target, local_sem.at[weight])
-        copy.start()
-        local.append(copy)
+        if parts[weight][2] == 0:
+            target = full_refs[weight].at[own_shard]
+            copy = pltpu.make_async_copy(shard_refs[weight], target, local_sem.at[parts[weight][1]])
+            copy.start()
+            local.append(copy)
 
     def shard_forward(weight):
         copies[weight, 2, 0].wait_recv()
@@ -572,7 +577,14 @@
             outs.append((shards, rows, columns))
     if shards != 4 or ctx_count != 8 or len(views) < len(weights):
         return [lax.all_gather(weight, "fsdp", axis=0, tiled=True) for weight in weights]
-    slots = len(views) * 24
+    parts = []
+    for at in sorted(range(len(views)), key=lambda at: (shapes[at] != "small", -views[at].size, at)):
+        columns = views[at].shape[-1]
+        pieces = max(1, min(columns // 1024, views[at].size // (1 << 18))) if shapes[at] == "rows" else 1
+        width = -(-columns // (128 * pieces)) * 128 if pieces > 1 else columns
+        for first in range(0, columns, width):
+            parts.append((shapes[at], at, first, min(width, columns - first)))
+    arrays, slots = (len(views), len(parts) * 24)
     vmem, anywhere, dma = (
         pl.BlockSpec(memory_space=pltpu.VMEM),
         pl.BlockSpec(memory_space=pl.ANY),
@@ -595,7 +607,7 @@
             dma((1,)),
         ]
     held = pl.pallas_call(
-        functools.partial(gather_kernel, shapes, projection is not None),
+        functools.partial(gather_kernel, arrays, parts, projection is not None),
         out_shape=tuple(jax.ShapeDtypeStruct(out, jnp.bfloat16) for out in outs),
         in_specs=in_specs,
         out_specs=tuple(anywhere for out in outs),
@@ -823,7 +835,7 @@
     ]
 
 
-def early_sums(products):
+def early_sums(products, held):
     plan = [weight_plan(*product) for product in products]
     lefts, rights = ([product[1] for product in products], [product[2] for product in products])
     vmem, anywhere, dma = (
@@ -833,15 +845,15 @@
     )
     rights = [part for right in rights for part in (right if isinstance(right, tuple) else [right])]
     groups = early_places(plan)[0]
-    outs, held = ([], [])
+    outs, units = ([], [])
     for halves, columns in groups:
         for half in halves:
             outs += [jax.ShapeDtypeStruct((2, 4, half, columns), jnp.bfloat16)] * 2
     for kind, count, width, deep, halves, parted in plan:
         for chunk in range(count):
-            held += [pltpu.VMEM((4, 2, 2, half, width), jnp.bfloat16) for half in halves]
+            units += [pltpu.VMEM((4, 2, 2, half, width), jnp.bfloat16) for half in halves]
     chunk_count = sum(entry[1] for entry in plan)
-    scratch = pair_scratch(plan, lefts[0].shape[0]) + held
+    scratch = pair_scratch(plan, lefts[0].shape[0]) + units
     scratch += [dma((2 * len(plan),)), dma((2 * len(plan),)), dma((len(plan),)), dma((8 * chunk_count,))]
     sides = pl.pallas_call(
         functools.partial(product_kernel, plan, plan_lead(plan)),
@@ -854,12 +866,13 @@
         ),
         name="early_products",
     )(*lefts, *rights)
+    held, sides = lax.optimization_barrier((held, sides))
     arrays = []
     for group in range(len(groups)):
         for part, bit in ((0, 2), (2, 4)):
             kept, sent = sides[4 * group + part : 4 * group + part + 2]
             arrays.append((kept, swap(sent, "ctx", bit)))
-    return (plan, arrays)
+    return (held, (plan, arrays))
 
 
 def second_step(held, early):
@@ -1289,17 +1302,20 @@
     ] + [small_sums]
 
 
-def weight_sums_early(hidden, grad_mlp_low, act_mlp, grad_leading, grad_trailing, attn_low, grad_attn_low):
+def weight_sums_early(
+    hidden, grad_mlp_low, act_mlp, grad_leading, grad_trailing, attn_low, grad_attn_low, held
+):
     shards, ctx_count = (lax.axis_size("fsdp"), lax.axis_size("ctx"))
     ff_width = hidden.shape[1]
     if shards != 4 or ctx_count != 8 or act_mlp.shape[1] % 1024 != 0 or ff_width % 64 != 0:
-        return None
+        return (held, None)
     return early_sums(
         [
             ("columns", hidden, grad_mlp_low, 1),
             ("rows", act_mlp, (grad_leading, grad_trailing), 3),
             ("rows", attn_low, grad_attn_low, 1),
-        ]
+        ],
+        held,
     )
 
 
@@ -1432,15 +1448,22 @@
     grad_attended = lax.dot_general(
         grad_attn_low, attn_full, NT, preferred_element_type=jnp.float32
     ).astype(jnp.bfloat16)
-    early = weight_sums_early(
-        hidden, grad_mlp_low, act_mlp, grad_leading, grad_trailing, attn_low, grad_attn_low
+    grad_attended_heads, early = weight_sums_early(
+        hidden,
+        grad_mlp_low,
+        act_mlp,
+        grad_leading,
+        grad_trailing,
+        attn_low,
+        grad_attn_low,
+        to_heads(grad_attended),
     )
     block_back = math.gcd(tokens, 256)
     low_back, high_back = key_range(pack_begin[0], pack_end[0], block_q, block_back)
     grad_heads = attention_backward(
         qkv_heads,
         attended_heads,
-        to_heads(grad_attended),
+        grad_attended_heads,
         log_total,
         pack_begin,
         pack_end,

time: 532 us -> 515 us (0.968)
  waiting for transfers between devices: 54.6 us -> 34.3 us
    all_to_all x5, waiting for transfers between devices: 52.8 us -> 21 us  [exchange(): lax.all_to_all(blocks, 'ctx', split_axis=0, concat_axis=0, tiled=True)]
    ppermute x8, waiting for transfers between devices: 1.78 us -> 13.4 us  [swap(): return lax.ppermute(value, axis, pairs)]
    pallas_call x2, Pallas kernels: 136 us -> 143 us  [gather_weights(): pl.pallas_call(functools.partial(gather_kernel, arrays, parts, projection...]
  transfers between devices with their start and end apart: 13 -> 13, of which waited for: 5 -> 6; matrix products, arithmetic and copies ran while one was open for 8% -> 8% of each run, Pallas kernels for 34% -> 40%
where the time goes in v4:
time: 515 us; the launch traced here: 507 us
  Pallas kernels  334 us (65%)
  other arithmetic  54.6 us (11%)
  starting transfers between devices  36.2 us (7%)
  matrix products  34.4 us (7%)
  waiting for transfers between devices  34.3 us (7%)
  local copies, waits for them, and re-layouts  11 us (2%)
    pallas_call x2, Pallas kernels, gather_weights(): pl.pallas_call(functools.partial(gather_kernel, arrays, parts, projection...  143 us
    pallas_call x1, Pallas kernels, sum_weights(): pl.pallas_call(functools.partial(sum_kernel, early, late, plan_lead(plan)...  88.5 us
    pallas_call x1, Pallas kernels, attention_backward(): pl.pallas_call(functools.partial(backward_kernel, head_count, block_q, bl...  38.6 us
    all_to_all x5, starting transfers between devices, exchange(): lax.all_to_all(blocks, 'ctx', split_axis=0, concat_axis=0, tiled=True)  30.2 us
    pallas_call x1, Pallas kernels, attention_forward(): pl.pallas_call(functools.partial(forward_kernel, head_count, block_q, blo...  29.6 us
    pallas_call x1, Pallas kernels, early_sums(): pl.pallas_call(functools.partial(product_kernel, plan, plan_lead(plan)),...  23.1 us
    all_to_all x5, waiting for transfers between devices, exchange(): lax.all_to_all(blocks, 'ctx', split_axis=0, concat_axis=0, tiled=True)  21 us
    ppermute x8, waiting for transfers between devices, swap(): return lax.ppermute(value, axis, pairs)  13.4 us
  transfers between devices with their start and end apart: 13, of which 6 were waited for; matrix products, arithmetic and copies ran while one was open for 8% of the time, Pallas kernels for 40%

profile of v4, /device:TPU:1, one launch (start us, length us, event | category | flops | bytes accessed | tf_op | source)
XLA Modules:
  0.0 506.8 jit_solution(9409646677151485908)
XLA Ops:
  0.7 0.9 select_reduce_fusion.6
  1.6 0.7 compare_and_fusion
  3.7 1.3 pad_maximum_fusion
  5.0 5.3 %all-to-all-start = ((bf16[8,96,1024]{2,1,0:T(8,128)(2,1)}), bf16[8,96,1024]{2,1,0:T(8,128)(2,1)S(1)}, u32[]{:S(2)}, u32[]{:S(2)}) async-start(bf16[8,96,1024]{2,1,0:T(8,128)(2,1)} %pad_maximum_fusion), calls=%async_computation | async-start | bytes 3145728 | tf_op jit(solution)/shard_map/all_to_all | solution.py:1352
  11.1 0.6 fusion.48
  12.0 0.6 fusion.33.refs_0_
  12.6 0.8 multiply_sine_fusion
  13.4 0.7 add_compare_fusion.1
  14.1 43.5 %gather_weights.1 = (bf16[4,16,256]{2,1,0:T(8,128)(2,1)}, bf16[4,2,4,32,3072]{4,3,2,1,0:T(8,128)(2,1)}) custom-call(bf16[16,256]{1,0:T(8,128)(2,1)} %fusion.33.refs_0_, bf16[2,4,32,3072]{3,2,1,0:T(8,128)(2,1)} %bitcast.130), custom_call_target="tpu_custom_call" | custom-call | tf_op jit(solution)/shard_map/gather_weights/pallas_call | solution.py:609
  57.5 0.8 fusion.30
  58.3 1.1 pad_maximum_fusion.2
  60.0 0.8 slice_convert_fusion
  60.8 1.3 compare_select_fusion.1
  62.9 1.2 fusion.16.refs_3_.refs_0_
  64.1 99.4 %gather_and_project.1 = (bf16[4,2,4,32,1024]{4,3,2,1,0:T(8,128)(2,1)}, bf16[4,2,4,32,5248]{4,3,2,1,0:T(8,128)(2,1)}, bf16[4,656,1024]{2,1,0:T(8,128)(2,1)}, bf16[3072,384]{1,0:T(8,128)(2,1)}) custom-call(bf16[2,4,32,1024]{3,2,1,0:T(8,128)(2,1)} %bitcast.136, bf16[2,4,32,5248]{3,2,1,0:T(8,128)(2,1)} %bitcast.126, bf16[656,1024]{1,0:T(8,128)(2,1)} %refs_2_.1, ...), custom_call_target="tpu_custom_call" | custom-call | tf_op jit(solution)/shard_map/gather_and_project/pallas_call | solution.py:609
  163.5 29.6 %attention_forward.1 = (f32[3072,128]{1,0:T(8,128)}, f32[12,1,512]{2,1,0:T(1,128)}) custom-call(s32[12]{0:T(128)} %get-tuple-element.133.low_ref, s32[12]{0:T(128)} %get-tuple-element.134.high_ref, s32[1,3072]{1,0:T(1,128)} %get-tuple-element.145.begin_ref, s32[1,3072]{1,0:T(1,128)} %get-tuple-element.144.end_ref, bf16[3072,384]{1,0:T(8,128)(2,1)} %get-tuple-element.53.qkv_ref), custom_call_target="tpu_custom_call" | custom-call | flops 2415919104 | bytes 4718592 | tf_op jit(solution)/shard_map/attention_forward/pallas_call | solution.py:97
  193.1 2.4 convert_element_type.169
  195.4 3.7 all-to-all-start.1
  199.1 0.7 fusion.34
  199.8 8.6 %all-to-all-done.1 = bf16[8,384,128]{2,1,0:T(8,128)(2,1)S(1)} async-done(((bf16[8,384,128]{2,1,0:T(8,128)(2,1)}), bf16[8,384,128]{2,1,0:T(8,128)(2,1)S(1)}, u32[]{:S(2)}, u32[]{:S(2)}) %all-to-all-start.1) | async-done | bytes 786464 | tf_op jit(solution)/shard_map/all_to_all | solution.py:1352
  208.4 4.1 fusion.44
  213.1 0.8 copy-done.18
  213.9 4.5 fusion.49
  218.4 10.0 %multiply_convert_fusion.1 = (bf16[384,2624]{1,0:T(8,128)(2,1)}, f32[384,2624]{1,0:T(8,128)S(1)}) fusion(f32[384,5248]{1,0:T(8,128)S(1)} %fusion.49), kind=kLoop, calls=%fused_computation.8 | loop fusion | flops 66502656 | bytes 14106624 | tf_op jit(solution)/shard_map/convert_element_type | solution.py:1415
  228.4 9.0 %add_convert_fusion = (bf16[384,2624]{1,0:T(8,128)(2,1)}, bf16[384,2624]{1,0:T(8,128)(2,1)}) fusion(f32[384,2624]{1,0:T(8,128)S(1)} %get-tuple-element.110, f32[384,5248]{1,0:T(8,128)S(1)} %fusion.49, bf16[384,1024]{1,0:T(8,128)(2,1)S(1)} %bitcast.133, bf16[2624,1024]{1,0:T(8,128)(2,1)} %bitcast.159), kind=kOutput, calls=%fused_computation.7 | convolution fusion | flops 2081734656 | bytes 22282240 | tf_op jit(solution)/shard_map/dot_general | solution.py:1429
  237.4 8.9 %fusion.6 = f32[384,1024]{1,0:T(8,128)S(1)} fusion(bf16[1024,5248]{1,0:T(8,128)(2,1)} %bitcast.157, bf16[384,2624]{1,0:T(8,128)(2,1)} %get-tuple-element.116.refs_5_, bf16[384,2624]{1,0:T(8,128)(2,1)} %get-tuple-element.115.refs_4_), kind=kOutput, calls=%fused_computation.22 | convolution fusion | flops 4135256064 | bytes 16351232 | tf_op jit(solution)/shard_map/dot_general | solution.py:1443
  246.3 6.9 %multiply_reduce_fusion = (f32[]{:T(128)}, f32[]{:T(128)}, f32[384]{0:T(512)S(1)}, f32[1024]{0:T(1024)S(1)}, f32[]{:T(128)}, /*index=5*/bf16[384,1024]{1,0:T(8,128)(2,1)}) fusion(f32[384,1024]{1,0:T(8,128)S(1)} %get-tuple-element.112, pred[384]{0:T(512)(128)(4,1)S(1)} %fusion.34, f32[384,1024]{1,0:T(8,128)S(1)} %fusion.6, f32[1024]{0:T(1024)S(1)} %bitcast.144, ...), kind=kOutput, calls=%fused_computation.52 | convolution fusion | flops 2070674048 | bytes 12907404 | tf_op jit(solution)/shard_map/dot_general | solution.py:1418
  253.8 1.2 fusion.21
  255.0 0.7 copy-done.10
  255.6 1.0 fusion.22
  256.7 1.0 copy.44
  257.7 7.3 %all-to-all-start.2 = ((bf16[8,384,128]{2,1,0:T(8,128)(2,1)}), bf16[8,384,128]{2,1,0:T(8,128)(2,1)}, u32[]{:S(2)}, u32[]{:S(2)}) async-start(bf16[8,384,128]{2,1,0:T(8,128)(2,1)} %bitcast.124), calls=%async_computation.2 | async-start | bytes 1572864 | tf_op jit(solution)/shard_map/all_to_all | solution.py:1352
  265.0 2.1 copy_bitcast_fusion.refs_2_
  267.1 23.1 %early_products.1 = (bf16[2,4,320,128]{3,2,1,0:T(8,128)(2,1)}, bf16[2,4,320,128]{3,2,1,0:T(8,128)(2,1)}, bf16[2,4,336,128]{3,2,1,0:T(8,128)(2,1)}, bf16[2,4,336,...) custom-call(bf16[384,2624]{1,0:T(8,128)(2,1)} %get-tuple-element.109, ...), custom_call_target="tpu_custom_call" | custom-call | tf_op jit(solution)/shard_map/early_products/pallas_call | solution.py:858
  290.2 1.4 collective-permute-start.2
  291.7 1.2 collective-permute-start.3
  293.2 38.6 %attention_backward.1 = bf16[3072,384]{1,0:T(8,128)(2,1)} custom-call(s32[12]{0:T(128)} %get-tuple-element.107.low_ref, s32[12]{0:T(128)} %get-tuple-element.108.high_ref, s32[1,3072]{1,0:T(1,128)} %get-tuple-element.145.begin_ref, s32[1,3072]{1,0:T(1,128)} %get-tuple-element.144.end_ref, bf16[3072,384]{1,0:T(8,128)(2,1)} %get-tuple-element.53.qkv_ref, ...), custom_call_target="tpu_custom_call" | custom-call | flops 6039797760 | bytes 11796480 | tf_op jit(solution)/shard_map/attention_backward/pallas_call | solution.py:215
  331.8 10.0 %collective-permute-done.refs_3_ = bf16[2,4,320,128]{3,2,1,0:T(8,128)(2,1)} collective-permute-done((bf16[2,4,320,128]{3,2,1,0:T(8,128)(2,1)}, bf16[2,4,320,128]{3,2,1,0:T(8,128)(2,1)}, u32[]{:S(2)}, u32[]{:S(2)}) %collective-permute-start) | collective-permute-done | bytes 655392 | tf_op jit(solution)/shard_map/ppermute | solution.py:1164
  341.9 1.5 collective-permute-done.1.refs_6_
  343.4 6.2 %all-to-all-start.3 = ((bf16[8,384,384]{2,1,0:T(8,128)(2,1)}), bf16[8,384,384]{2,1,0:T(8,128)(2,1)}, u32[]{:S(2)}, u32[]{:S(2)}) async-start(bf16[8,384,384]{2,1,0:T(8,128)(2,1)} %bitcast.127), calls=%async_computation.3 | async-start | bytes 4718592 | tf_op jit(solution)/shard_map/all_to_all | solution.py:1352
  350.4 2.1 select_maximum_fusion
  352.5 2.0 fusion.27
  354.5 1.4 collective-permute-start.4
  355.9 1.2 fusion.26
  357.1 1.3 collective-permute-start.5
  358.4 2.2 fusion.24
  360.8 2.2 fusion.25
  363.2 12.4 %all-to-all-done.3.heads_ref = bf16[8,384,384]{2,1,0:T(8,128)(2,1)} async-done(((bf16[8,384,384]{2,1,0:T(8,128)(2,1)}), bf16[8,384,384]{2,1,0:T(8,128)(2,1)}, u32[]{:S(2)}, u32[]{:S(2)}) %all-to-all-start.3) | async-done | bytes 2359328 | tf_op jit(solution)/shard_map/all_to_all | solution.py:1352
  375.5 11.4 %finish_rows.1 = (bf16[384,3072]{1,0:T(8,128)(2,1)}, f32[384,1024]{1,0:T(8,128)}) custom-call(bf16[8,384,384]{2,1,0:T(8,128)(2,1)} %all-to-all-done.3.heads_ref, f32[384,128]{1,0:T(8,128)} %get-tuple-element.146.refs_5_.cosine_ref, f32[384,128]{1,0:T(8,128)} %get-tuple-element.147.refs_6_.sine_ref, bf16[1024,3072]{1,0:T(8,128)(2,1)} %bitcast.121, ...), custom_call_target="tpu_custom_call" | custom-call | flops 2415919104 | bytes 11010048 | tf_op jit(solution)/shard_map/finish_rows/pallas_call | solution.py:278
  387.0 1.9 fusion.18
  388.9 0.8 fusion.17
  389.7 1.0 add_convert_fusion.3
  390.8 1.3 pad_maximum_fusion.1
  392.1 7.7 %all-to-all-start.4 = ((bf16[8,96,1024]{2,1,0:T(8,128)(2,1)}), bf16[8,96,1024]{2,1,0:T(8,128)(2,1)S(1)}, u32[]{:S(2)}, u32[]{:S(2)}) async-start(bf16[8,96,1024]{2,1,0:T(8,128)(2,1)} %pad_maximum_fusion.1), calls=%async_computation.4 | async-start | bytes 3145728 | tf_op jit(solution)/shard_map/all_to_all | solution.py:1352
  399.8 0.7 stack.41.refs_14_
  400.5 1.3 collective-permute-done.6.refs_10_
  402.3 88.5 %sum_weights.1 = (bf16[656,1024]{1,0:T(8,128)(2,1)}, bf16[256,5376]{1,0:T(8,128)(2,1)}, bf16[256,1024]{1,0:T(8,128)(2,1)}, bf16[256,3072]{1,0:T(8,128)(2,1)}, f32[2,8,1024]{2,1,0:T(8,128)}) custom-call(bf16[384,1024]{1,0:T(8,128)(2,1)} %fusion.16.refs_3_.refs_0_, bf16[384,3072]{1,0:T(8,128)(2,1)} %get-tuple-element.78.refs_1_, ...), custom_call_target="tpu_custom_call" | custom-call | tf_op jit(solution)/shard_map/sum_weights/pallas_call | solution.py:1134
  490.8 0.8 fusion.47
  491.6 3.6 convert_element_type.202
  495.2 1.1 convert_element_type.203
  497.4 1.8 convert_element_type.205
  499.3 1.2 sqrt_bitcast_fusion
  500.7 3.0 maximum_convert_fusion
  505.0 1.3 broadcast_select_fusion
  (95 shorter events, 9.1 us)
Async XLA Ops:
  0.6 1.6 copy-start
  0.7 2.2 copy-start.13
  4.9 5.4 %copy-start.16 = (s32[1,6]{1,0:T(1,128)S(1)}, s32[1,6]{1,0:T(1,128)}, u32[]{:S(2)}) copy-start(s32[1,6]{1,0:T(1,128)} %param.14) | copy-start | bytes 76
  4.9 6.8 %copy-start.19 = (bf16[256]{0:T(256)(128)(2,1)S(1)}, bf16[256]{0:T(256)(128)(2,1)}, u32[]{:S(2)}) copy-start(bf16[256]{0:T(256)(128)(2,1)} %param.19) | copy-start | bytes 1540
  4.9 6.8 %copy-start.20 = (bf16[256]{0:T(256)(128)(2,1)S(1)}, bf16[256]{0:T(256)(128)(2,1)}, u32[]{:S(2)}) copy-start(bf16[256]{0:T(256)(128)(2,1)} %param.16) | copy-start | bytes 1540
  5.0 57.1 %all-to-all-start = ((bf16[8,96,1024]{2,1,0:T(8,128)(2,1)}), bf16[8,96,1024]{2,1,0:T(8,128)(2,1)S(1)}, u32[]{:S(2)}, u32[]{:S(2)}) async-start(bf16[8,96,1024]{2,1,0:T(8,128)(2,1)} %pad_maximum_fusion), calls=%async_computation | async-start | bytes 3145728 | tf_op jit(solution)/shard_map/all_to_all | solution.py:1352
  195.4 12.9 %all-to-all-start.1 = ((bf16[8,384,128]{2,1,0:T(8,128)(2,1)}), bf16[8,384,128]{2,1,0:T(8,128)(2,1)S(1)}, u32[]{:S(2)}, u32[]{:S(2)}) async-start(bf16[8,384,128]{2,1,0:T(8,128)(2,1)} %bitcast.17), calls=%async_computation.1 | async-start | bytes 1572864 | tf_op jit(solution)/shard_map/all_to_all | solution.py:1352
  208.4 4.1 copy-start.4
  208.4 5.5 %copy-start.18 = (bf16[4,2,4,32,5248]{4,3,2,1,0:T(8,128)(2,1)S(1)}, bf16[4,2,4,32,5248]{4,3,2,1,0:T(8,128)(2,1)}, u32[]{:S(2)}) copy-start(bf16[4,2,4,32,5248]{4,3,2,1,0:T(8,128)(2,1)} %get-tuple-element.56) | copy-start | bytes 32243716
  213.1 5.3 %copy-start.7 = (bf16[384,1024]{1,0:T(8,128)(2,1)}, bf16[384,1024]{1,0:T(8,128)(2,1)S(1)}, u32[]{:S(2)}) copy-start(bf16[384,1024]{1,0:T(8,128)(2,1)S(1)} %multiply_convert_fusion.2.refs_1_) | copy-start | bytes 2359300
  237.4 8.9 %copy-start.3 = (bf16[384,2624]{1,0:T(8,128)(2,1)S(1)}, bf16[384,2624]{1,0:T(8,128)(2,1)}, u32[]{:S(2)}) copy-start(bf16[384,2624]{1,0:T(8,128)(2,1)} %get-tuple-element.109.refs_0_) | copy-start | bytes 6045700
  237.4 8.9 %copy-start.11 = (f32[384,1024]{1,0:T(8,128)S(1)}, f32[384,1024]{1,0:T(8,128)}, u32[]{:S(2)}) copy-start(f32[384,1024]{1,0:T(8,128)} %get-tuple-element.141) | copy-start | bytes 4718596
  253.8 1.9 copy-start.10
  255.0 1.7 copy-start.8
  257.7 32.5 %all-to-all-start.2 = ((bf16[8,384,128]{2,1,0:T(8,128)(2,1)}), bf16[8,384,128]{2,1,0:T(8,128)(2,1)}, u32[]{:S(2)}, u32[]{:S(2)}) async-start(bf16[8,384,128]{2,1,0:T(8,128)(2,1)} %bitcast.124), calls=%async_computation.2 | async-start | bytes 1572864 | tf_op jit(solution)/shard_map/all_to_all | solution.py:1352
  290.2 53.2 %collective-permute-start.2 = (bf16[2,4,32,3200]{3,2,1,0:T(8,128)(2,1)}, bf16[2,4,32,3200]{3,2,1,0:T(8,128)(2,1)}, u32[]{:S(2)}, u32[]{:S(2)}) collective-permute-start(bf16[2,4,32,3200]{3,2,1,0:T(8,128)(2,1)} %get-tuple-element.73), channel_id=1, source_target_pairs={{0,8},{4,12},{8,0},{12,4},{16,24},{20,28},{24,16},{28,20},{1,9},{5... | collective-permute-start | bytes 4915208 | tf_op jit(solution)/shard_map/ppermute | solution.py:1164
  291.7 51.8 %collective-permute-start.3 = (bf16[2,4,32,3200]{3,2,1,0:T(8,128)(2,1)}, bf16[2,4,32,3200]{3,2,1,0:T(8,128)(2,1)}, u32[]{:S(2)}, u32[]{:S(2)}) collective-permute-start(bf16[2,4,32,3200]{3,2,1,0:T(8,128)(2,1)} %get-tuple-element.75), channel_id=1, source_target_pairs={{0,16},{4,20},{8,24},{12,28},{16,0},{20,4},{24,8},{28,12},{1,17},{... | collective-permute-start | bytes 4915208 | tf_op jit(solution)/shard_map/ppermute | solution.py:1164
  292.9 50.5 %collective-permute-start.1 = (bf16[2,4,336,128]{3,2,1,0:T(8,128)(2,1)}, bf16[2,4,336,128]{3,2,1,0:T(8,128)(2,1)}, u32[]{:S(2)}, u32[]{:S(2)}) collective-permute-start(bf16[2,4,336,128]{3,2,1,0:T(8,128)(2,1)} %get-tuple-element.71), channel_id=1, source_target_pairs={{0,16},{4,20},{8,24},{12,28},{16,0},{20,4},{24,8},{28,12},{1,17},{... | collective-permute-start | bytes 2064392 | tf_op jit(solution)/shard_map/ppermute | solution.py:1164
  293.1 48.8 %collective-permute-start = (bf16[2,4,320,128]{3,2,1,0:T(8,128)(2,1)}, bf16[2,4,320,128]{3,2,1,0:T(8,128)(2,1)}, u32[]{:S(2)}, u32[]{:S(2)}) collective-permute-start(bf16[2,4,320,128]{3,2,1,0:T(8,128)(2,1)} %get-tuple-element.69), channel_id=1, source_target_pairs={{0,8},{4,12},{8,0},{12,4},{16,24},{20,28},{24,16},{28,20},{1,9},{5... | collective-permute-start | bytes 1966088 | tf_op jit(solution)/shard_map/ppermute | solution.py:1164
  343.4 6.9 %copy-start.17 = (s32[1,1,8]{2,1,0:T(1,128)S(1)}, s32[1,1,8]{2,1,0:T(1,128)}, u32[]{:S(2)}) copy-start(s32[1,1,8]{2,1,0:T(1,128)} %param.15) | copy-start | bytes 100
  343.4 32.1 %all-to-all-start.3 = ((bf16[8,384,384]{2,1,0:T(8,128)(2,1)}), bf16[8,384,384]{2,1,0:T(8,128)(2,1)}, u32[]{:S(2)}, u32[]{:S(2)}) async-start(bf16[8,384,384]{2,1,0:T(8,128)(2,1)} %bitcast.127), calls=%async_computation.3 | async-start | bytes 4718592 | tf_op jit(solution)/shard_map/all_to_all | solution.py:1352
  350.4 8.0 %copy-start.5 = (bf16[2,4,32,3200]{3,2,1,0:T(8,128)(2,1)S(1)}, bf16[2,4,32,3200]{3,2,1,0:T(8,128)(2,1)}, u32[]{:S(2)}) copy-start(bf16[2,4,32,3200]{3,2,1,0:T(8,128)(2,1)} %get-tuple-element.83.refs_8_) | copy-start | bytes 4915204
  352.5 8.3 %copy-start.6 = (bf16[2,4,32,3200]{3,2,1,0:T(8,128)(2,1)S(1)}, bf16[2,4,32,3200]{3,2,1,0:T(8,128)(2,1)}, u32[]{:S(2)}) copy-start(bf16[2,4,32,3200]{3,2,1,0:T(8,128)(2,1)} %get-tuple-element.85.refs_11_) | copy-start | bytes 4915204
  354.5 45.9 %collective-permute-start.4 = (bf16[4,320,128]{2,1,0:T(8,128)(2,1)}, bf16[4,320,128]{2,1,0:T(8,128)(2,1)}, u32[]{:S(2)}, u32[]{:S(2)}) collective-permute-start(bf16[4,320,128]{2,1,0:T(8,128)(2,1)} %fusion.27), channel_id=1, source_target_pairs={{0,16},{4,20},{8,24},{12,28},{16,0},{20,4},{24,8},{28,12},{1,17},{... | collective-permute-start | bytes 983048 | tf_op jit(solution)/shard_map/ppermute | solution.py:1164
  357.1 43.4 %collective-permute-start.5 = (bf16[4,336,128]{2,1,0:T(8,128)(2,1)S(1)}, bf16[4,336,128]{2,1,0:T(8,128)(2,1)}, u32[]{:S(2)}, u32[]{:S(2)}) collective-permute-start(bf16[4,336,128]{2,1,0:T(8,128)(2,1)S(1)} %fusion.26), channel_id=1, source_target_pairs={{0,8},{4,12},{8,0},{12,4},{16,24},{20,28},{24,16},{28,20},{1,9},{5... | collective-permute-start | bytes 1032200 | tf_op jit(solution)/shard_map/ppermute | solution.py:1164
  360.6 41.2 %collective-permute-start.6 = (bf16[4,32,3200]{2,1,0:T(8,128)(2,1)}, bf16[4,32,3200]{2,1,0:T(8,128)(2,1)}, u32[]{:S(2)}, u32[]{:S(2)}) collective-permute-start(bf16[4,32,3200]{2,1,0:T(8,128)(2,1)} %fusion.24), channel_id=1, source_target_pairs={{0,16},{4,20},{8,24},{12,28},{16,0},{20,4},{24,8},{28,12},{1,17},{... | collective-permute-start | bytes 2457608 | tf_op jit(solution)/shard_map/ppermute | solution.py:1164
  363.1 39.2 %collective-permute-start.7 = (bf16[4,32,3200]{2,1,0:T(8,128)(2,1)}, bf16[4,32,3200]{2,1,0:T(8,128)(2,1)}, u32[]{:S(2)}, u32[]{:S(2)}) collective-permute-start(bf16[4,32,3200]{2,1,0:T(8,128)(2,1)} %fusion.25), channel_id=1, source_target_pairs={{0,8},{4,12},{8,0},{12,4},{16,24},{20,28},{24,16},{28,20},{1,9},{5... | collective-permute-start | bytes 2457608 | tf_op jit(solution)/shard_map/ppermute | solution.py:1164
  387.0 1.9 copy-start.2
  389.7 1.1 copy-start.14
  392.1 111.5 %all-to-all-start.4 = ((bf16[8,96,1024]{2,1,0:T(8,128)(2,1)}), bf16[8,96,1024]{2,1,0:T(8,128)(2,1)S(1)}, u32[]{:S(2)}, u32[]{:S(2)}) async-start(bf16[8,96,1024]{2,1,0:T(8,128)(2,1)} %pad_maximum_fusion.1), calls=%async_computation.4 | async-start | bytes 3145728 | tf_op jit(solution)/shard_map/all_to_all | solution.py:1352
  491.6 3.6 copy-start.15
  491.6 5.8 %copy-start.12 = (bf16[656,1024]{1,0:T(8,128)(2,1)S(1)}, bf16[656,1024]{1,0:T(8,128)(2,1)}, u32[]{:S(2)}) copy-start(bf16[656,1024]{1,0:T(8,128)(2,1)} %get-tuple-element.91) | copy-start | bytes 4030468
  496.3 4.2 copy-start.9
  504.4 2.0 copy-start.1

commit v5 on v3

--- a/solution.py
+++ b/solution.py
@@ -36,7 +36,7 @@
 
 
 def forward_kernel(
-    head_count, block_q, block_k, low_ref, high_ref, begin_ref, end_ref, qkv_ref, out_ref, log_ref, turned_ref
+    head_count, block_q, block_k, low_ref, high_ref, begin_ref, end_ref, qkv_ref, out_ref, low_out_ref, log_ref, turned_ref
 ):
     width = out_ref.shape[1]
     step = pl.program_id(0)
@@ -84,7 +84,9 @@
     safe = jnp.where(valid, total, 1.0)
     acc = jnp.where(valid, acc / safe, 0.0)
     log_total = jnp.where(valid, top + jnp.log(safe), 0.0)
-    out_ref[...] = head_pick(acc, head_count, block_q)
+    attended = head_pick(acc, head_count, block_q)
+    out_ref[...] = attended
+    low_out_ref[...] = attended.astype(jnp.bfloat16)
     log_ref[0] = log_total
 
 
@@ -98,6 +100,7 @@
         functools.partial(forward_kernel, head_count, block_q, block_k),
         out_shape=(
             jax.ShapeDtypeStruct((tokens, width), jnp.float32),
+            jax.ShapeDtypeStruct((tokens, width), jnp.bfloat16),
             jax.ShapeDtypeStruct((steps, 1, head_count * block_q), jnp.float32),
         ),
         grid_spec=pltpu.PrefetchScalarGridSpec(
@@ -105,6 +108,7 @@
             grid=(steps,),
             in_specs=[whole((1, tokens)), whole((1, tokens)), whole((tokens, 3 * width))],
             out_specs=(
+                pl.BlockSpec((block_q, width), lambda i, *_: (i, 0)),
                 pl.BlockSpec((block_q, width), lambda i, *_: (i, 0)),
                 pl.BlockSpec((1, 1, head_count * block_q), lambda i, *_: (i, 0, 0)),
             ),
@@ -245,16 +249,18 @@
     width = heads_ref.shape[2] // 3
     step = pl.program_id(0)
     total = out_ref.shape[1] // 3
+    owners = heads_ref.shape[0]
     pieces = []
     for part in range(3):
-        piece = heads_ref[0, :, part * width : (part + 1) * width]
-        if part < 2:
-            piece = turn_back(
-                piece.astype(jnp.float32), cosine_ref[...], sine_ref[...], head_count
-            ).astype(jnp.bfloat16)
-        first = pl.multiple_of(part * total + step * width, width)
-        out_ref[:, pl.ds(first, width)] = piece
-        pieces.append(piece)
+        for owner in range(owners):
+            piece = heads_ref[owner, :, part * width : (part + 1) * width]
+            if part < 2:
+                piece = turn_back(
+                    piece.astype(jnp.float32), cosine_ref[...], sine_ref[...], head_count
+                ).astype(jnp.bfloat16)
+            first = pl.multiple_of(part * total + (step * owners + owner) * width, width)
+            out_ref[:, pl.ds(first, width)] = piece
+            pieces.append(piece)
     weights = jnp.concatenate([query_ref[...], key_ref[...], value_ref[...]], axis=1)
     product = lax.dot_general(
         jnp.concatenate(pieces, axis=1), weights, NT, preferred_element_type=jnp.float32
@@ -274,16 +280,17 @@
     width = columns // 3
     depth = qkv_full.shape[0]
     whole = lambda shape: pl.BlockSpec(shape, lambda i: (0,) * len(shape))
-    part_of = lambda part: pl.BlockSpec((depth, width), lambda i: (0, part * owners + i))
+    steps = owners // 2
+    part_of = lambda part: pl.BlockSpec((depth, 2 * width), lambda i: (0, part * steps + i))
     return pl.pallas_call(
         functools.partial(rows_kernel, head_count),
         out_shape=(
             jax.ShapeDtypeStruct((rows, owners * columns), jnp.bfloat16),
             jax.ShapeDtypeStruct((rows, depth), jnp.float32),
         ),
-        grid=(owners,),
+        grid=(steps,),
         in_specs=[
-            pl.BlockSpec((1, rows, columns), lambda i: (i, 0, 0)),
+            pl.BlockSpec((2, rows, columns), lambda i: (i, 0, 0)),
             whole((rows, width)),
             whole((rows, width)),
             part_of(0),
@@ -619,7 +626,9 @@
 
     rows = left_refs[0].shape[0] if left_refs else 0
     pairs = []
-    for w, entry in enumerate(plan):
+
+    def begin(w):
+        entry = plan[w]
         span, right = (plan_span(entry), right_refs[w])
         own_part, other_part = (whole_refs[w].at[pl.ds(0, rows)], whole_refs[w].at[pl.ds(rows, rows)])
 
@@ -635,7 +644,7 @@
             for at in (0, 1):
 
                 @pl.when(core == at)
-                def begin():
+                def start():
                     for copy in ways[at]:
                         copy.start()
 
@@ -698,7 +707,7 @@
 
         lax.fori_loop(0, 4, each, 0)
 
-    return (turn, multiply)
+    return (begin, turn, multiply)
 
 
 def remote_send(pending):
@@ -744,7 +753,7 @@
     pl.semaphore_wait(barrier, 1)
     pending = []
     send = remote_send(pending)
-    turn, multiply = pair_steps(
+    begin, turn, multiply = pair_steps(
         plan,
         lead_rows,
         left_refs,
@@ -757,6 +766,7 @@
         send,
     )
     for w in range(weights):
+        begin(w)
         turn(w)
     stores = []
     for number, (w, t) in enumerate(chunks):
@@ -823,7 +833,7 @@
     ]
 
 
-def early_sums(products):
+def early_sums(products, held):
     plan = [weight_plan(*product) for product in products]
     lefts, rights = ([product[1] for product in products], [product[2] for product in products])
     vmem, anywhere, dma = (
@@ -833,15 +843,15 @@
     )
     rights = [part for right in rights for part in (right if isinstance(right, tuple) else [right])]
     groups = early_places(plan)[0]
-    outs, held = ([], [])
+    outs, units = ([], [])
     for halves, columns in groups:
         for half in halves:
             outs += [jax.ShapeDtypeStruct((2, 4, half, columns), jnp.bfloat16)] * 2
     for kind, count, width, deep, halves, parted in plan:
         for chunk in range(count):
-            held += [pltpu.VMEM((4, 2, 2, half, width), jnp.bfloat16) for half in halves]
+            units += [pltpu.VMEM((4, 2, 2, half, width), jnp.bfloat16) for half in halves]
     chunk_count = sum(entry[1] for entry in plan)
-    scratch = pair_scratch(plan, lefts[0].shape[0]) + held
+    scratch = pair_scratch(plan, lefts[0].shape[0]) + units
     scratch += [dma((2 * len(plan),)), dma((2 * len(plan),)), dma((len(plan),)), dma((8 * chunk_count,))]
     sides = pl.pallas_call(
         functools.partial(product_kernel, plan, plan_lead(plan)),
@@ -854,12 +864,13 @@
         ),
         name="early_products",
     )(*lefts, *rights)
+    held, sides = lax.optimization_barrier((held, sides))
     arrays = []
     for group in range(len(groups)):
         for part, bit in ((0, 2), (2, 4)):
             kept, sent = sides[4 * group + part : 4 * group + part + 2]
             arrays.append((kept, swap(sent, "ctx", bit)))
-    return (plan, arrays)
+    return (held, (plan, arrays))
 
 
 def second_step(held, early):
@@ -894,7 +905,9 @@
     for number in range(len(chunks)):
         for half in (0, 1):
             units[number, half] = [scratch.pop(0) for stage in range(5)]
-    small_held = scratch.pop(0)
+    sum_refs = [scratch.pop(0) for entry in plan]
+    wide_refs = [scratch.pop(0) for entry in plan]
+    small_held, wide_sem = (scratch.pop(0), scratch.pop(0))
     send_sem, recv_sem, local_sem, load_sem, pair_send, pair_recv, small_send, small_recv, near_sem = scratch
     own_ctx, own_shard = (lax.axis_index("ctx"), lax.axis_index("fsdp"))
     core, chip = (own_ctx % 2, own_ctx // 2)
@@ -924,7 +937,7 @@
     to_core, to_x, to_y, to_one, to_two = partners
     pending = []
     send = remote_send(pending)
-    turn, multiply = pair_steps(
+    begin, turn, multiply = pair_steps(
         late,
         lead_rows,
         left_refs,
@@ -936,6 +949,8 @@
         pending,
         send,
     )
+    for w in range(len(late)):
+        begin(w)
     copies = {}
 
     def hop(number, half, stage, source, target, partner):
@@ -1010,9 +1025,9 @@
         if kind == "rows":
             start = pl.multiple_of((2 * chip_at + half) * deep, deep)
             column = pl.multiple_of((core * count + t) * width, width)
-            return out_refs[w].at[pl.ds(start, deep), pl.ds(column, width)]
+            return sum_refs[w].at[pl.ds(start, deep), pl.ds(column, width)]
         column = pl.multiple_of((core * 4 + chip_at) * width, width)
-        return out_refs[w].at[pl.ds(half * lead_rows, deep), pl.ds(column, width)]
+        return sum_refs[w].at[pl.ds(half * lead_rows, deep), pl.ds(column, width)]
 
     local = {}
 
@@ -1045,11 +1060,43 @@
             local[number, half].wait()
         span = width if kind == "rows" else 4 * width
         at = core * count + t if kind == "rows" else core
-        piece = out_refs[w].at[:, pl.ds(pl.multiple_of(at * span, span), span)]
+        piece = sum_refs[w].at[:, pl.ds(pl.multiple_of(at * span, span), span)]
         slot = len(chunks) * 16 + number
         copies[number, 2, 0] = send(
             piece, piece, send_sem.at[slot], recv_sem.at[slot], to_core
         )
+
+    written = []
+
+    def write(number, source, target):
+        copy = pltpu.make_async_copy(source, target, wide_sem.at[len(written)])
+        copy.start()
+        written.append(copy)
+
+    def stage_eight(number):
+        w, t = chunks[number]
+        kind, count, width, deep, halves, parted = plan[w]
+        copies[number, 2, 0].wait_recv()
+        span = plan_span(plan[w])
+        real, width = (parted or span, width if kind == "rows" else span)
+        columns = min(width, real - t * width)
+        starts = [(at * span + t * width, at * real + t * width) for at in (0, 1)]
+
+        def each(i, carried):
+            block = pl.ds(pl.multiple_of(16 * i, 16), 16)
+            for source, target in starts:
+                wide_refs[w][block, target : target + columns] = sum_refs[w][
+                    block, source : source + columns
+                ].astype(jnp.float32)
+            return carried
+
+        lax.fori_loop(0, deep // 16, each, 0)
+        if real == span:
+            for source, target in starts:
+                place = pl.ds(target, columns)
+                write(number, wide_refs[w].at[:, place], out_refs[w].at[:, place])
+        elif t == count - 1:
+            write(number, wide_refs[w], out_refs[w])
 
     small_copies = []
 
@@ -1075,6 +1122,7 @@
             small_out[1] = small_held[10]
 
     stages = (stage_one, stage_two, stage_three, stage_four, stage_five, stage_six, stage_seven)
+    stages += (stage_eight,)
     small_at = 0
     stage_three(0)
     for w in range(len(late)):
@@ -1088,8 +1136,8 @@
         if small_at < 6:
             small_step(small_at)
             small_at += 1
-    for number in range(len(chunks)):
-        copies[number, 2, 0].wait_recv()
+    for copy in written:
+        copy.wait()
     for copy in pending:
         copy.wait_send()
 
@@ -1106,11 +1154,16 @@
         for chunk in range(count):
             for half in halves:
                 pieces += [pltpu.VMEM(lead + (half, width), jnp.bfloat16) for lead in leads]
-    outs = [jax.ShapeDtypeStruct((entry[3], 2 * plan_span(entry)), jnp.bfloat16) for entry in plan]
+    outs = [
+        jax.ShapeDtypeStruct((entry[3], 2 * (entry[5] or plan_span(entry))), jnp.float32)
+        for entry in plan
+    ]
     chunk_count = sum(entry[1] for entry in plan)
     scratch = pair_scratch(late, lefts[0].shape[0]) + pieces
-    scratch += [pltpu.VMEM((11,) + small.shape, jnp.float32)]
     dma = pltpu.SemaphoreType.DMA
+    scratch += [pltpu.VMEM((entry[3], 2 * plan_span(entry)), jnp.bfloat16) for entry in plan]
+    scratch += [pltpu.VMEM(out.shape, out.dtype) for out in outs]
+    scratch += [pltpu.VMEM((11,) + small.shape, jnp.float32), dma((2 * chunk_count,))]
     slots = chunk_count * 17
     scratch += [dma((slots,)), dma((slots,)), dma((2 * chunk_count,)), dma((6 * chunk_count,))]
     scratch += [dma((2 * len(late),)), dma((2 * len(late),)), dma((5,)), dma((5,)), dma((len(late),))]
@@ -1277,29 +1330,26 @@
         ]
         over_pack = sum_over(small, ("ctx",))
         return totals + [jnp.stack([over_pack, sum_over(over_pack, ("fsdp",))])]
-    total_out, total_in, total_attn, total_qkv, small_sums = sum_weights(
+    total_attn, total_in, total_out, total_qkv, small_sums = sum_weights(
         *early, [("rows", act_attn, grad_projected, 3)], small
     )
-    padded = total_in.shape[1] // 2
-    total_in = jnp.concatenate(
-        [total_in[:, :ff_width], total_in[:, padded : padded + ff_width]], axis=1
-    )
-    return [
-        total.astype(jnp.float32) for total in (total_out, total_in, total_qkv, total_attn)
-    ] + [small_sums]
-
-
-def weight_sums_early(hidden, grad_mlp_low, act_mlp, grad_leading, grad_trailing, attn_low, grad_attn_low):
+    return [total_out, total_in, total_qkv, total_attn, small_sums]
+
+
+def weight_sums_early(
+    hidden, grad_mlp_low, act_mlp, grad_leading, grad_trailing, attn_low, grad_attn_low, held
+):
     shards, ctx_count = (lax.axis_size("fsdp"), lax.axis_size("ctx"))
     ff_width = hidden.shape[1]
     if shards != 4 or ctx_count != 8 or act_mlp.shape[1] % 1024 != 0 or ff_width % 64 != 0:
-        return None
+        return (held, None)
     return early_sums(
         [
+            ("rows", attn_low, grad_attn_low, 1),
+            ("rows", act_mlp, (grad_leading, grad_trailing), 3),
             ("columns", hidden, grad_mlp_low, 1),
-            ("rows", act_mlp, (grad_leading, grad_trailing), 3),
-            ("rows", attn_low, grad_attn_low, 1),
-        ]
+        ],
+        held,
     )
 
 
@@ -1385,10 +1435,10 @@
         qkv_heads = to_heads(joined.reshape(row_count, -1))
     low, high = key_range(pack_begin, pack_end, block_q, block_k)
     pack_begin, pack_end = (pack_begin[None, :], pack_end[None, :])
-    attended_heads, log_total = attention_forward(
+    attended_heads, attended_low, log_total = attention_forward(
         qkv_heads, pack_begin, pack_end, low, high, own_heads, block_q, block_k
     )
-    attn_low = jnp.transpose(to_rows(attended_heads.astype(jnp.bfloat16)), (1, 0, 2)).reshape(
+    attn_low = jnp.transpose(to_rows(attended_low), (1, 0, 2)).reshape(
         row_count, model_width
     )
     branch_attn = jnp.dot(attn_low, attn_full, preferred_element_type=jnp.float32)
@@ -1432,15 +1482,22 @@
     grad_attended = lax.dot_general(
         grad_attn_low, attn_full, NT, preferred_element_type=jnp.float32
     ).astype(jnp.bfloat16)
-    early = weight_sums_early(
-        hidden, grad_mlp_low, act_mlp, grad_leading, grad_trailing, attn_low, grad_attn_low
+    grad_attended_heads, early = weight_sums_early(
+        hidden,
+        grad_mlp_low,
+        act_mlp,
+        grad_leading,
+        grad_trailing,
+        attn_low,
+        grad_attn_low,
+        to_heads(grad_attended),
     )
     block_back = math.gcd(tokens, 256)
     low_back, high_back = key_range(pack_begin[0], pack_end[0], block_q, block_back)
     grad_heads = attention_backward(
         qkv_heads,
         attended_heads,
-        to_heads(grad_attended),
+        grad_attended_heads,
         log_total,
         pack_begin,
         pack_end,

time: 532 us -> 535 us (level)
  local copies, waits for them, and re-layouts: 9.81 us -> 24.4 us
  other arithmetic: 55 us -> 42.7 us
    ppermute x8, waiting for transfers between devices: 1.78 us -> 29 us  [swap(): return lax.ppermute(value, axis, pairs)]
    all_to_all x5, waiting for transfers between devices: 52.8 us -> 26.9 us  [exchange(): lax.all_to_all(blocks, 'ctx', split_axis=0, concat_axis=0, tiled=True)]
    convert_element_type x5 -> x0, other arithmetic: 11.9 us -> none  [the longest x4 9.49 us: weight_sums(): total.astype(jnp.float32)]
    unnamed x40 -> x54, local copies, waits for them, and re-layouts: 1.62 us -> 11.3 us
  transfers between devices with their start and end apart: 13 -> 13, of which waited for: 5 -> 6; matrix products, arithmetic and copies ran while one was open for 8% -> 5% of each run, Pallas kernels for 34% -> 38%
where the time goes in v5:
time: 535 us; the launch traced here: 526 us
  Pallas kernels  327 us (61%)
  waiting for transfers between devices  55.9 us (10%)
  other arithmetic  42.7 us (8%)
  starting transfers between devices  38.7 us (7%)
  matrix products  34.8 us (7%)
  local copies, waits for them, and re-layouts  24.4 us (5%)
    pallas_call x2, Pallas kernels, gather_weights(): pl.pallas_call(functools.partial(gather_kernel, shapes, projection is not...  136 us
    pallas_call x1, Pallas kernels, sum_weights(): pl.pallas_call(functools.partial(sum_kernel, early, late, plan_lead(plan)...  90.9 us
    pallas_call x1, Pallas kernels, attention_backward(): pl.pallas_call(functools.partial(backward_kernel, head_count, block_q, bl...  39.7 us
    all_to_all x5, starting transfers between devices, exchange(): lax.all_to_all(blocks, 'ctx', split_axis=0, concat_axis=0, tiled=True)  30.4 us
    pallas_call x1, Pallas kernels, attention_forward(): pl.pallas_call(functools.partial(forward_kernel, head_count, block_q, blo...  30.4 us
    ppermute x8, waiting for transfers between devices, swap(): return lax.ppermute(value, axis, pairs)  29 us
    all_to_all x5, waiting for transfers between devices, exchange(): lax.all_to_all(blocks, 'ctx', split_axis=0, concat_axis=0, tiled=True)  26.9 us
    pallas_call x1, Pallas kernels, early_sums(): pl.pallas_call(functools.partial(product_kernel, plan, plan_lead(plan)),...  20.9 us
  transfers between devices with their start and end apart: 13, of which 6 were waited for; matrix products, arithmetic and copies ran while one was open for 5% of the time, Pallas kernels for 38%

profile of v5, /device:TPU:1, one launch (start us, length us, event | category | flops | bytes accessed | tf_op | source)
XLA Modules:
  0.0 525.6 jit_solution(17340440015933826739)
XLA Ops:
  0.7 0.9 select_reduce_fusion.6
  3.7 1.3 pad_maximum_fusion
  5.0 5.3 %all-to-all-start = ((bf16[8,96,1024]{2,1,0:T(8,128)(2,1)}), bf16[8,96,1024]{2,1,0:T(8,128)(2,1)S(1)}, u32[]{:S(2)}, u32[]{:S(2)}) async-start(bf16[8,96,1024]{2,1,0:T(8,128)(2,1)} %pad_maximum_fusion), calls=%async_computation | async-start | bytes 3145728 | tf_op jit(solution)/shard_map/all_to_all | solution.py:1386
  12.6 0.8 multiply_sine_fusion
  14.1 39.7 %gather_weights.1 = (bf16[4,16,256]{2,1,0:T(8,128)(2,1)}, bf16[4,2,4,32,3072]{4,3,2,1,0:T(8,128)(2,1)}) custom-call(bf16[16,256]{1,0:T(8,128)(2,1)} %fusion.33.refs_0_, bf16[2,4,32,3072]{3,2,1,0:T(8,128)(2,1)} %bitcast.132), custom_call_target="tpu_custom_call" | custom-call | tf_op jit(solution)/shard_map/gather_weights/pallas_call | solution.py:604
  53.8 0.8 fusion.30
  54.6 1.1 pad_maximum_fusion.2
  56.3 0.8 slice_convert_fusion
  57.1 1.3 compare_select_fusion.1
  59.2 1.2 fusion.16.refs_3_.refs_0_
  60.4 96.4 %gather_and_project.1 = (bf16[4,2,4,32,1024]{4,3,2,1,0:T(8,128)(2,1)}, bf16[4,2,4,32,5248]{4,3,2,1,0:T(8,128)(2,1)}, bf16[4,656,1024]{2,1,0:T(8,128)(2,1)}, bf16[3072,384]{1,0:T(8,128)(2,1)}) custom-call(bf16[2,4,32,1024]{3,2,1,0:T(8,128)(2,1)} %bitcast.139, bf16[2,4,32,5248]{3,2,1,0:T(8,128)(2,1)} %bitcast.128, bf16[656,1024]{1,0:T(8,128)(2,1)} %refs_2_.1, ...), custom_call_target="tpu_custom_call" | custom-call | tf_op jit(solution)/shard_map/gather_and_project/pallas_call | solution.py:604
  156.8 30.4 %attention_forward.1 = (f32[3072,128]{1,0:T(8,128)}, bf16[3072,128]{1,0:T(8,128)(2,1)}, f32[12,1,512]{2,1,0:T(1,128)}) custom-call(s32[12]{0:T(128)} %get-tuple-element.133.low_ref, s32[12]{0:T(128)} %get-tuple-element.134.high_ref, s32[1,3072]{1,0:T(1,128)} %get-tuple-element.145.begin_ref, s32[1,3072]{1,0:T(1,128)} %get-tuple-element.144.end_ref, ...), custom_call_target="tpu_custom_call" | custom-call | flops 2415919104 | bytes 4718592 | tf_op jit(solution)/shard_map/attention_forward/pallas_call | solution.py:99
  187.2 3.7 all-to-all-start.1
  191.5 8.4 %all-to-all-done.1 = bf16[8,384,128]{2,1,0:T(8,128)(2,1)S(1)} async-done(((bf16[8,384,128]{2,1,0:T(8,128)(2,1)}), bf16[8,384,128]{2,1,0:T(8,128)(2,1)S(1)}, u32[]{:S(2)}, u32[]{:S(2)}) %all-to-all-start.1) | async-done | bytes 786464 | tf_op jit(solution)/shard_map/all_to_all | solution.py:1386
  199.9 3.0 fusion.44
  203.6 0.9 copy-done.8
  204.5 0.7 copy-done.20
  205.2 4.5 fusion.48
  209.7 9.2 %multiply_convert_fusion.1 = (bf16[384,2624]{1,0:T(8,128)(2,1)S(1)}, f32[384,2624]{1,0:T(8,128)S(1)}) fusion(f32[384,5248]{1,0:T(8,128)S(1)} %fusion.48), kind=kLoop, calls=%fused_computation.8 | loop fusion | flops 66502656 | bytes 14106624 | tf_op jit(solution)/shard_map/convert_element_type | solution.py:1449
  219.0 10.7 %add_convert_fusion = (bf16[384,2624]{1,0:T(8,128)(2,1)}, bf16[384,2624]{1,0:T(8,128)(2,1)}) fusion(f32[384,2624]{1,0:T(8,128)S(1)} %get-tuple-element.112, f32[384,5248]{1,0:T(8,128)} %copy-done.3, bf16[384,1024]{1,0:T(8,128)(2,1)S(1)} %bitcast.136, bf16[2624,1024]{1,0:T(8,128)(2,1)} %bitcast.162), kind=kOutput, calls=%fused_computation.7 | convolution fusion | flops 2081734656 | bytes 22282240 | tf_op jit(solution)/shard_map/dot_general | solution.py:1463
  229.7 8.7 %fusion.6 = f32[384,1024]{1,0:T(8,128)S(1)} fusion(bf16[1024,5248]{1,0:T(8,128)(2,1)} %bitcast.160, bf16[384,2624]{1,0:T(8,128)(2,1)} %get-tuple-element.118.refs_5_, bf16[384,2624]{1,0:T(8,128)(2,1)} %get-tuple-element.117.refs_4_), kind=kOutput, calls=%fused_computation.22 | convolution fusion | flops 4135256064 | bytes 16351232 | tf_op jit(solution)/shard_map/dot_general | solution.py:1477
  238.4 6.9 %multiply_reduce_fusion = (f32[]{:T(128)}, f32[]{:T(128)}, f32[384]{0:T(512)S(1)}, f32[1024]{0:T(1024)S(1)}, f32[]{:T(128)}, /*index=5*/bf16[384,1024]{1,0:T(8,128)(2,1)}) fusion(f32[384,1024]{1,0:T(8,128)S(1)} %get-tuple-element.114, pred[384]{0:T(512)(128)(4,1)S(1)} %fusion.34, f32[384,1024]{1,0:T(8,128)S(1)} %fusion.6, f32[1024]{0:T(1024)S(1)} %bitcast.147, ...), kind=kOutput, calls=%fused_computation.51 | convolution fusion | flops 2070674048 | bytes 12907404 | tf_op jit(solution)/shard_map/dot_general | solution.py:1452
  245.9 1.2 fusion.21
  247.7 1.0 fusion.22
  248.8 1.0 copy.44
  249.8 7.5 %all-to-all-start.2 = ((bf16[8,384,128]{2,1,0:T(8,128)(2,1)}), bf16[8,384,128]{2,1,0:T(8,128)(2,1)}, u32[]{:S(2)}, u32[]{:S(2)}) async-start(bf16[8,384,128]{2,1,0:T(8,128)(2,1)} %bitcast.126), calls=%async_computation.2 | async-start | bytes 1572864 | tf_op jit(solution)/shard_map/all_to_all | solution.py:1386
  257.3 2.2 copy_bitcast_fusion.refs_0_
  259.5 20.9 %early_products.1 = (bf16[2,4,32,3200]{3,2,1,0:T(8,128)(2,1)}, bf16[2,4,32,3200]{3,2,1,0:T(8,128)(2,1)}, bf16[2,4,32,3200]{3,2,1,0:T(8,128)(2,1)}, bf16[2,4,32,3...) custom-call(bf16[384,1024]{1,0:T(8,128)(2,1)} %copy_bitcast_fusion.r, ...), custom_call_target="tpu_custom_call" | custom-call | tf_op jit(solution)/shard_map/early_products/pallas_call | solution.py:856
  280.4 1.4 collective-permute-start
  281.9 1.2 collective-permute-start.1
  283.4 39.7 %attention_backward.1 = bf16[3072,384]{1,0:T(8,128)(2,1)} custom-call(s32[12]{0:T(128)} %get-tuple-element.109.low_ref, s32[12]{0:T(128)} %get-tuple-element.110.high_ref, s32[1,3072]{1,0:T(1,128)} %get-tuple-element.145.begin_ref, s32[1,3072]{1,0:T(1,128)} %get-tuple-element.144.end_ref, bf16[3072,384]{1,0:T(8,128)(2,1)} %get-tuple-element.54.qkv_ref, ...), custom_call_target="tpu_custom_call" | custom-call | flops 6039797760 | bytes 11796480 | tf_op jit(solution)/shard_map/attention_backward/pallas_call | solution.py:219
  323.1 9.0 %collective-permute-done.2.refs_9_ = bf16[2,4,320,128]{3,2,1,0:T(8,128)(2,1)} collective-permute-done((bf16[2,4,320,128]{3,2,1,0:T(8,128)(2,1)}, bf16[2,4,320,128]{3,2,1,0:T(8,128)(2,1)}, u32[]{:S(2)}, u32[]{:S(2)}) %collective-permute-start.2) | collective-permute-done | bytes 655392 | tf_op jit(solution)/shard_map/ppermute | solution.py:1204
  332.1 1.5 collective-permute-done.3.refs_12_
  333.6 6.1 %all-to-all-start.3 = ((bf16[8,384,384]{2,1,0:T(8,128)(2,1)}), bf16[8,384,384]{2,1,0:T(8,128)(2,1)}, u32[]{:S(2)}, u32[]{:S(2)}) async-start(bf16[8,384,384]{2,1,0:T(8,128)(2,1)} %bitcast.129), calls=%async_computation.3 | async-start | bytes 4718592 | tf_op jit(solution)/shard_map/all_to_all | solution.py:1386
  339.8 2.6 fusion.24
  342.4 1.4 collective-permute-start.4
  343.7 2.2 fusion.25
  346.0 1.2 collective-permute-start.5
  347.2 18.4 %all-to-all-done.3.heads_ref = bf16[8,384,384]{2,1,0:T(8,128)(2,1)} async-done(((bf16[8,384,384]{2,1,0:T(8,128)(2,1)}), bf16[8,384,384]{2,1,0:T(8,128)(2,1)}, u32[]{:S(2)}, u32[]{:S(2)}) %all-to-all-start.3) | async-done | bytes 2359328 | tf_op jit(solution)/shard_map/all_to_all | solution.py:1386
  365.6 8.9 %finish_rows.1 = (bf16[384,3072]{1,0:T(8,128)(2,1)}, f32[384,1024]{1,0:T(8,128)}) custom-call(bf16[8,384,384]{2,1,0:T(8,128)(2,1)} %all-to-all-done.3.heads_ref, f32[384,128]{1,0:T(8,128)} %get-tuple-element.146.refs_5_.cosine_ref, f32[384,128]{1,0:T(8,128)} %get-tuple-element.147.refs_6_.sine_ref, bf16[1024,3072]{1,0:T(8,128)(2,1)} %bitcast.121, ...), custom_call_target="tpu_custom_call" | custom-call | flops 2415919104 | bytes 11010048 | tf_op jit(solution)/shard_map/finish_rows/pallas_call | solution.py:285
  374.5 1.9 fusion.18
  376.4 0.8 fusion.17
  377.2 1.0 add_convert_fusion.3
  378.3 1.3 pad_maximum_fusion.1
  379.6 7.8 %all-to-all-start.4 = ((bf16[8,96,1024]{2,1,0:T(8,128)(2,1)}), bf16[8,96,1024]{2,1,0:T(8,128)(2,1)S(1)}, u32[]{:S(2)}, u32[]{:S(2)}) async-start(bf16[8,96,1024]{2,1,0:T(8,128)(2,1)} %pad_maximum_fusion.1), calls=%async_computation.4 | async-start | bytes 3145728 | tf_op jit(solution)/shard_map/all_to_all | solution.py:1386
  387.4 1.1 fusion.27
  388.5 1.4 collective-permute-start.6
  389.9 1.1 fusion.26
  391.0 1.3 collective-permute-start.7
  392.9 2.0 select_maximum_fusion
  395.6 18.1 %collective-permute-done.6.refs_10_ = bf16[4,320,128]{2,1,0:T(8,128)(2,1)} collective-permute-done((bf16[4,320,128]{2,1,0:T(8,128)(2,1)S(1)}, bf16[4,320,128]{2,1,0:T(8,128)(2,1)}, u32[]{:S(2)}, u32[]{:S(2)}) %collective-permute-start.6) | collective-permute-done | bytes 327712 | tf_op jit(solution)/shard_map/ppermute | solution.py:1204
  414.1 0.7 copy-done.17
  414.8 90.9 %sum_weights.1 = (f32[256,1024]{1,0:T(8,128)}, f32[256,5248]{1,0:T(8,128)}, f32[656,1024]{1,0:T(8,128)}, f32[256,3072]{1,0:T(8,128)}, f32[2,8,1024]{2,1,0:T(8,128)}) custom-call(bf16[384,1024]{1,0:T(8,128)(2,1)} %fusion.16.refs_3_.refs_0_, bf16[384,3072]{1,0:T(8,128)(2,1)} %get-tuple-element.80.refs_1_, ...), custom_call_target="tpu_custom_call" | custom-call | tf_op jit(solution)/shard_map/sum_weights/pallas_call | solution.py:1174
  505.7 0.8 fusion.46
  507.7 1.2 sqrt_bitcast_fusion
  508.9 1.1 fusion.45
  509.9 1.5 gather_fusion.3
  511.4 2.8 gather_fusion.2
  514.2 2.9 broadcast_select_fusion
  517.1 1.7 copy.49
  519.0 1.0 copy.50
  520.0 2.7 copy.51
  522.7 0.9 copy-done.10
  523.6 1.5 copy.52
  (102 shorter events, 12.0 us)
Async XLA Ops:
  0.6 1.6 copy-start
  0.7 2.2 copy-start.15
  4.9 5.4 %copy-start.18 = (s32[1,6]{1,0:T(1,128)S(1)}, s32[1,6]{1,0:T(1,128)}, u32[]{:S(2)}) copy-start(s32[1,6]{1,0:T(1,128)} %param.14) | copy-start | bytes 76
  4.9 6.8 %copy-start.21 = (bf16[256]{0:T(256)(128)(2,1)S(1)}, bf16[256]{0:T(256)(128)(2,1)}, u32[]{:S(2)}) copy-start(bf16[256]{0:T(256)(128)(2,1)} %param.19) | copy-start | bytes 1540
  4.9 6.8 %copy-start.22 = (bf16[256]{0:T(256)(128)(2,1)S(1)}, bf16[256]{0:T(256)(128)(2,1)}, u32[]{:S(2)}) copy-start(bf16[256]{0:T(256)(128)(2,1)} %param.16) | copy-start | bytes 1540
  5.0 53.4 %all-to-all-start = ((bf16[8,96,1024]{2,1,0:T(8,128)(2,1)}), bf16[8,96,1024]{2,1,0:T(8,128)(2,1)S(1)}, u32[]{:S(2)}, u32[]{:S(2)}) async-start(bf16[8,96,1024]{2,1,0:T(8,128)(2,1)} %pad_maximum_fusion), calls=%async_computation | async-start | bytes 3145728 | tf_op jit(solution)/shard_map/all_to_all | solution.py:1386
  187.2 12.8 %all-to-all-start.1 = ((bf16[8,384,128]{2,1,0:T(8,128)(2,1)}), bf16[8,384,128]{2,1,0:T(8,128)(2,1)S(1)}, u32[]{:S(2)}, u32[]{:S(2)}) async-start(bf16[8,384,128]{2,1,0:T(8,128)(2,1)} %bitcast.134), calls=%async_computation.1 | async-start | bytes 1572864 | tf_op jit(solution)/shard_map/all_to_all | solution.py:1386
  199.9 9.7 %copy-start.5 = (bf16[8,384,128]{2,1,0:T(8,128)(2,1)}, bf16[8,384,128]{2,1,0:T(8,128)(2,1)S(1)}, u32[]{:S(2)}) copy-start(bf16[8,384,128]{2,1,0:T(8,128)(2,1)S(1)} %all-to-all-done.1) | copy-start | bytes 2359300
  199.9 5.3 copy-start.20
  203.5 0.9 copy-start.8
  209.7 9.3 %copy-start.3 = (f32[384,5248]{1,0:T(8,128)}, f32[384,5248]{1,0:T(8,128)S(1)}, u32[]{:S(2)}) copy-start(f32[384,5248]{1,0:T(8,128)S(1)} %fusion.48) | copy-start | bytes 24182788
  219.0 19.4 %copy-start.4 = (bf16[384,2624]{1,0:T(8,128)(2,1)}, bf16[384,2624]{1,0:T(8,128)(2,1)S(1)}, u32[]{:S(2)}) copy-start(bf16[384,2624]{1,0:T(8,128)(2,1)S(1)} %get-tuple-element.111.refs_2_) | copy-start | bytes 6045700
  245.9 1.9 copy-start.11
  247.1 1.7 copy-start.9
  249.8 30.6 %all-to-all-start.2 = ((bf16[8,384,128]{2,1,0:T(8,128)(2,1)}), bf16[8,384,128]{2,1,0:T(8,128)(2,1)}, u32[]{:S(2)}, u32[]{:S(2)}) async-start(bf16[8,384,128]{2,1,0:T(8,128)(2,1)} %bitcast.126), calls=%async_computation.2 | async-start | bytes 1572864 | tf_op jit(solution)/shard_map/all_to_all | solution.py:1386
  280.4 53.2 %collective-permute-start = (bf16[2,4,32,3200]{3,2,1,0:T(8,128)(2,1)}, bf16[2,4,32,3200]{3,2,1,0:T(8,128)(2,1)}, u32[]{:S(2)}, u32[]{:S(2)}) collective-permute-start(bf16[2,4,32,3200]{3,2,1,0:T(8,128)(2,1)} %get-tuple-element.71), channel_id=1, source_target_pairs={{0,8},{4,12},{8,0},{12,4},{16,24},{20,28},{24,16},{28,20},{1,9},{5... | collective-permute-start | bytes 4915208 | tf_op jit(solution)/shard_map/ppermute | solution.py:1204
  281.9 51.8 %collective-permute-start.1 = (bf16[2,4,32,3200]{3,2,1,0:T(8,128)(2,1)}, bf16[2,4,32,3200]{3,2,1,0:T(8,128)(2,1)}, u32[]{:S(2)}, u32[]{:S(2)}) collective-permute-start(bf16[2,4,32,3200]{3,2,1,0:T(8,128)(2,1)} %get-tuple-element.73), channel_id=1, source_target_pairs={{0,16},{4,20},{8,24},{12,28},{16,0},{20,4},{24,8},{28,12},{1,17},{... | collective-permute-start | bytes 4915208 | tf_op jit(solution)/shard_map/ppermute | solution.py:1204
  283.1 50.5 %collective-permute-start.3 = (bf16[2,4,336,128]{3,2,1,0:T(8,128)(2,1)}, bf16[2,4,336,128]{3,2,1,0:T(8,128)(2,1)}, u32[]{:S(2)}, u32[]{:S(2)}) collective-permute-start(bf16[2,4,336,128]{3,2,1,0:T(8,128)(2,1)} %get-tuple-element.77), channel_id=1, source_target_pairs={{0,16},{4,20},{8,24},{12,28},{16,0},{20,4},{24,8},{28,12},{1,17},{... | collective-permute-start | bytes 2064392 | tf_op jit(solution)/shard_map/ppermute | solution.py:1204
  283.3 48.7 %collective-permute-start.2 = (bf16[2,4,320,128]{3,2,1,0:T(8,128)(2,1)}, bf16[2,4,320,128]{3,2,1,0:T(8,128)(2,1)}, u32[]{:S(2)}, u32[]{:S(2)}) collective-permute-start(bf16[2,4,320,128]{3,2,1,0:T(8,128)(2,1)} %get-tuple-element.75), channel_id=1, source_target_pairs={{0,8},{4,12},{8,0},{12,4},{16,24},{20,28},{24,16},{28,20},{1,9},{5... | collective-permute-start | bytes 1966088 | tf_op jit(solution)/shard_map/ppermute | solution.py:1204
  333.6 32.0 %all-to-all-start.3 = ((bf16[8,384,384]{2,1,0:T(8,128)(2,1)}), bf16[8,384,384]{2,1,0:T(8,128)(2,1)}, u32[]{:S(2)}, u32[]{:S(2)}) async-start(bf16[8,384,384]{2,1,0:T(8,128)(2,1)} %bitcast.129), calls=%async_computation.3 | async-start | bytes 4718592 | tf_op jit(solution)/shard_map/all_to_all | solution.py:1386
  339.8 4.0 copy-start.6
  342.4 71.7 %collective-permute-start.4 = (bf16[4,32,3200]{2,1,0:T(8,128)(2,1)}, bf16[4,32,3200]{2,1,0:T(8,128)(2,1)}, u32[]{:S(2)}, u32[]{:S(2)}) collective-permute-start(bf16[4,32,3200]{2,1,0:T(8,128)(2,1)} %fusion.24), channel_id=1, source_target_pairs={{0,16},{4,20},{8,24},{12,28},{16,0},{20,4},{24,8},{28,12},{1,17},{... | collective-permute-start | bytes 2457608 | tf_op jit(solution)/shard_map/ppermute | solution.py:1204
  346.0 68.1 %collective-permute-start.5 = (bf16[4,32,3200]{2,1,0:T(8,128)(2,1)}, bf16[4,32,3200]{2,1,0:T(8,128)(2,1)}, u32[]{:S(2)}, u32[]{:S(2)}) collective-permute-start(bf16[4,32,3200]{2,1,0:T(8,128)(2,1)} %fusion.25), channel_id=1, source_target_pairs={{0,8},{4,12},{8,0},{12,4},{16,24},{20,28},{24,16},{28,20},{1,9},{5... | collective-permute-start | bytes 2457608 | tf_op jit(solution)/shard_map/ppermute | solution.py:1204
  374.5 1.9 copy-start.2
  377.2 1.1 copy-start.16
  379.6 7.8 %copy-start.13 = (bf16[2,4,320,128]{3,2,1,0:T(8,128)(2,1)S(1)}, bf16[2,4,320,128]{3,2,1,0:T(8,128)(2,1)}, u32[]{:S(2)}) copy-start(bf16[2,4,320,128]{3,2,1,0:T(8,128)(2,1)} %get-tuple-element.85.refs_8_) | copy-start | bytes 1966084
  379.6 10.3 %copy-start.12 = (bf16[2,4,336,128]{3,2,1,0:T(8,128)(2,1)S(1)}, bf16[2,4,336,128]{3,2,1,0:T(8,128)(2,1)}, u32[]{:S(2)}) copy-start(bf16[2,4,336,128]{3,2,1,0:T(8,128)(2,1)} %get-tuple-element.87.refs_11_) | copy-start | bytes 2064388
  379.6 12.7 %copy-start.19 = (s32[1,1,8]{2,1,0:T(1,128)S(1)}, s32[1,1,8]{2,1,0:T(1,128)}, u32[]{:S(2)}) copy-start(s32[1,1,8]{2,1,0:T(1,128)} %param.15) | copy-start | bytes 100
  379.6 129.3 %all-to-all-start.4 = ((bf16[8,96,1024]{2,1,0:T(8,128)(2,1)}), bf16[8,96,1024]{2,1,0:T(8,128)(2,1)S(1)}, u32[]{:S(2)}, u32[]{:S(2)}) async-start(bf16[8,96,1024]{2,1,0:T(8,128)(2,1)} %pad_maximum_fusion.1), calls=%async_computation.4 | async-start | bytes 3145728 | tf_op jit(solution)/shard_map/all_to_all | solution.py:1386
  388.5 25.2 %collective-permute-start.6 = (bf16[4,320,128]{2,1,0:T(8,128)(2,1)S(1)}, bf16[4,320,128]{2,1,0:T(8,128)(2,1)}, u32[]{:S(2)}, u32[]{:S(2)}) collective-permute-start(bf16[4,320,128]{2,1,0:T(8,128)(2,1)S(1)} %fusion.27), channel_id=1, source_target_pairs={{0,16},{4,20},{8,24},{12,28},{16,0},{20,4},{24,8},{28,12},{1,17},{... | collective-permute-start | bytes 983048 | tf_op jit(solution)/shard_map/ppermute | solution.py:1204
  391.0 23.1 %collective-permute-start.7 = (bf16[4,336,128]{2,1,0:T(8,128)(2,1)S(1)}, bf16[4,336,128]{2,1,0:T(8,128)(2,1)S(1)}, u32[]{:S(2)}, u32[]{:S(2)}) collective-permute-start(bf16[4,336,128]{2,1,0:T(8,128)(2,1)S(1)} %fusion.26), channel_id=1, source_target_pairs={{0,8},{4,12},{8,0},{12,4},{16,24},{20,28},{24,16},{28,20},{1,9},{5... | collective-permute-start | bytes 1032200 | tf_op jit(solution)/shard_map/ppermute | solution.py:1204
  414.1 0.7 copy-start.17
  511.4 5.6 %copy-start.7 = (f32[256,3072]{1,0:T(8,128)S(1)}, f32[256,3072]{1,0:T(8,128)}, u32[]{:S(2)}) copy-start(f32[256,3072]{1,0:T(8,128)} %get-tuple-element.160) | copy-start | bytes 9437188
  514.2 5.8 %slice-start = ((s8[5373952]{0:T(1024)(128)(4,1)}), s8[4194304]{0:T(1024)(128)(4,1)S(1)}, s32[]{:S(2)}) async-start(s8[5373952]{0:T(1024)(128)(4,1)} %bitcast.124), calls=%async_computation.5 | async-start | bytes 8388608
  517.0 1.9 copy-start.14
  517.0 2.9 slice-start.1
  520.0 3.7 copy-start.10
  520.0 5.2 copy-start.1

commit v6 on v5

--- a/solution.py
+++ b/solution.py
@@ -878,13 +878,15 @@
     held, arrays = lax.optimization_barrier((held, arrays))
     chip = lax.axis_index("ctx") // 2
     flat = []
-    for at, (kept, arrived) in enumerate(arrays):
+    for at, (kept, arrived) in sorted(enumerate(arrays), key=lambda pair: (-(pair[0] // 2), pair[0])):
         bit, own = ((4, chip // 2), (2, chip % 2))[at % 2]
         other = [
             lax.dynamic_index_in_dim(side, 1 - own, 0, keepdims=False).astype(jnp.float32)
             for side in (kept, arrived)
         ]
-        flat += [kept, arrived, swap((other[0] + other[1]).astype(jnp.bfloat16), "ctx", bit)]
+        twice = swap((other[0] + other[1]).astype(jnp.bfloat16), "ctx", bit)
+        flat.append((at, [kept, arrived, twice]))
+    flat = [side for at, sides in sorted(flat, key=lambda pair: pair[0]) for side in sides]
     return (held, (plan, flat))
 
 
@@ -905,9 +907,7 @@
     for number in range(len(chunks)):
         for half in (0, 1):
             units[number, half] = [scratch.pop(0) for stage in range(5)]
-    sum_refs = [scratch.pop(0) for entry in plan]
-    wide_refs = [scratch.pop(0) for entry in plan]
-    small_held, wide_sem = (scratch.pop(0), scratch.pop(0))
+    small_held = scratch.pop(0)
     send_sem, recv_sem, local_sem, load_sem, pair_send, pair_recv, small_send, small_recv, near_sem = scratch
     own_ctx, own_shard = (lax.axis_index("ctx"), lax.axis_index("fsdp"))
     core, chip = (own_ctx % 2, own_ctx // 2)
@@ -1025,9 +1025,9 @@
         if kind == "rows":
             start = pl.multiple_of((2 * chip_at + half) * deep, deep)
             column = pl.multiple_of((core * count + t) * width, width)
-            return sum_refs[w].at[pl.ds(start, deep), pl.ds(column, width)]
+            return out_refs[w].at[pl.ds(start, deep), pl.ds(column, width)]
         column = pl.multiple_of((core * 4 + chip_at) * width, width)
-        return sum_refs[w].at[pl.ds(half * lead_rows, deep), pl.ds(column, width)]
+        return out_refs[w].at[pl.ds(half * lead_rows, deep), pl.ds(column, width)]
 
     local = {}
 
@@ -1060,43 +1060,11 @@
             local[number, half].wait()
         span = width if kind == "rows" else 4 * width
         at = core * count + t if kind == "rows" else core
-        piece = sum_refs[w].at[:, pl.ds(pl.multiple_of(at * span, span), span)]
+        piece = out_refs[w].at[:, pl.ds(pl.multiple_of(at * span, span), span)]
         slot = len(chunks) * 16 + number
         copies[number, 2, 0] = send(
             piece, piece, send_sem.at[slot], recv_sem.at[slot], to_core
         )
-
-    written = []
-
-    def write(number, source, target):
-        copy = pltpu.make_async_copy(source, target, wide_sem.at[len(written)])
-        copy.start()
-        written.append(copy)
-
-    def stage_eight(number):
-        w, t = chunks[number]
-        kind, count, width, deep, halves, parted = plan[w]
-        copies[number, 2, 0].wait_recv()
-        span = plan_span(plan[w])
-        real, width = (parted or span, width if kind == "rows" else span)
-        columns = min(width, real - t * width)
-        starts = [(at * span + t * width, at * real + t * width) for at in (0, 1)]
-
-        def each(i, carried):
-            block = pl.ds(pl.multiple_of(16 * i, 16), 16)
-            for source, target in starts:
-                wide_refs[w][block, target : target + columns] = sum_refs[w][
-                    block, source : source + columns
-                ].astype(jnp.float32)
-            return carried
-
-        lax.fori_loop(0, deep // 16, each, 0)
-        if real == span:
-            for source, target in starts:
-                place = pl.ds(target, columns)
-                write(number, wide_refs[w].at[:, place], out_refs[w].at[:, place])
-        elif t == count - 1:
-            write(number, wide_refs[w], out_refs[w])
 
     small_copies = []
 
@@ -1122,7 +1090,6 @@
             small_out[1] = small_held[10]
 
     stages = (stage_one, stage_two, stage_three, stage_four, stage_five, stage_six, stage_seven)
-    stages += (stage_eight,)
     small_at = 0
     stage_three(0)
     for w in range(len(late)):
@@ -1136,8 +1103,8 @@
         if small_at < 6:
             small_step(small_at)
             small_at += 1
-    for copy in written:
-        copy.wait()
+    for number in range(len(chunks)):
+        copies[number, 2, 0].wait_recv()
     for copy in pending:
         copy.wait_send()
 
@@ -1154,16 +1121,11 @@
         for chunk in range(count):
             for half in halves:
                 pieces += [pltpu.VMEM(lead + (half, width), jnp.bfloat16) for lead in leads]
-    outs = [
-        jax.ShapeDtypeStruct((entry[3], 2 * (entry[5] or plan_span(entry))), jnp.float32)
-        for entry in plan
-    ]
+    outs = [jax.ShapeDtypeStruct((entry[3], 2 * plan_span(entry)), jnp.bfloat16) for entry in plan]
     chunk_count = sum(entry[1] for entry in plan)
     scratch = pair_scratch(late, lefts[0].shape[0]) + pieces
     dma = pltpu.SemaphoreType.DMA
-    scratch += [pltpu.VMEM((entry[3], 2 * plan_span(entry)), jnp.bfloat16) for entry in plan]
-    scratch += [pltpu.VMEM(out.shape, out.dtype) for out in outs]
-    scratch += [pltpu.VMEM((11,) + small.shape, jnp.float32), dma((2 * chunk_count,))]
+    scratch += [pltpu.VMEM((11,) + small.shape, jnp.float32)]
     slots = chunk_count * 17
     scratch += [dma((slots,)), dma((slots,)), dma((2 * chunk_count,)), dma((6 * chunk_count,))]
     scratch += [dma((2 * len(late),)), dma((2 * len(late),)), dma((5,)), dma((5,)), dma((len(late),))]
@@ -1333,7 +1295,13 @@
     total_attn, total_in, total_out, total_qkv, small_sums = sum_weights(
         *early, [("rows", act_attn, grad_projected, 3)], small
     )
-    return [total_out, total_in, total_qkv, total_attn, small_sums]
+    padded = total_in.shape[1] // 2
+    total_in = jnp.concatenate(
+        [total_in[:, :ff_width], total_in[:, padded : padded + ff_width]], axis=1
+    )
+    return [
+        total.astype(jnp.float32) for total in (total_out, total_in, total_qkv, total_attn)
+    ] + [small_sums]
 
 
 def weight_sums_early(

time: 535 us -> 510 us (0.953)
  waiting for transfers between devices: 55.9 us -> 34.7 us
  local copies, waits for them, and re-layouts: 24.4 us -> 11 us
  other arithmetic: 42.7 us -> 52.3 us
    ppermute x8, waiting for transfers between devices: 29 us -> 13.9 us  [swap(): return lax.ppermute(value, axis, pairs)]
    convert_element_type x4 -> x8, other arithmetic: 6.95 us -> 17.1 us  [the longest x4 9.49 us: weight_sums(): total.astype(jnp.float32)]
    unnamed x54 -> x44, local copies, waits for them, and re-layouts: 11.3 us -> 1.68 us
    all_to_all x5, waiting for transfers between devices: 26.9 us -> 20.8 us  [exchange(): lax.all_to_all(blocks, 'ctx', split_axis=0, concat_axis=0, tiled=True)]
  transfers between devices with their start and end apart: 13 -> 13, of which waited for: 6 -> 6; matrix products, arithmetic and copies ran while one was open for 5% -> 8% of each run, Pallas kernels for 38% -> 41%
where the time goes in v6:
time: 510 us; the launch traced here: 502 us
  Pallas kernels  331 us (65%)
  other arithmetic  52.3 us (10%)
  starting transfers between devices  36.5 us (7%)
  waiting for transfers between devices  34.7 us (7%)
  matrix products  34.4 us (7%)
  local copies, waits for them, and re-layouts  11 us (2%)
    pallas_call x2, Pallas kernels, gather_weights(): pl.pallas_call(functools.partial(gather_kernel, shapes, projection is not...  136 us
    pallas_call x1, Pallas kernels, sum_weights(): pl.pallas_call(functools.partial(sum_kernel, early, late, plan_lead(plan)...  93 us
    pallas_call x1, Pallas kernels, attention_backward(): pl.pallas_call(functools.partial(backward_kernel, head_count, block_q, bl...  40.7 us
    pallas_call x1, Pallas kernels, attention_forward(): pl.pallas_call(functools.partial(forward_kernel, head_count, block_q, blo...  31 us
    all_to_all x5, starting transfers between devices, exchange(): lax.all_to_all(blocks, 'ctx', split_axis=0, concat_axis=0, tiled=True)  30.5 us
    pallas_call x1, Pallas kernels, early_sums(): pl.pallas_call(functools.partial(product_kernel, plan, plan_lead(plan)),...  21 us
    all_to_all x5, waiting for transfers between devices, exchange(): lax.all_to_all(blocks, 'ctx', split_axis=0, concat_axis=0, tiled=True)  20.8 us
    ppermute x8, waiting for transfers between devices, swap(): return lax.ppermute(value, axis, pairs)  13.9 us
  transfers between devices with their start and end apart: 13, of which 6 were waited for; matrix products, arithmetic and copies ran while one was open for 8% of the time, Pallas kernels for 41%

profile of v6, /device:TPU:1, one launch (start us, length us, event | category | flops | bytes accessed | tf_op | source)
XLA Modules:
  0.0 501.8 jit_solution(9549533170517832496)
XLA Ops:
  0.7 0.9 select_reduce_fusion.6
  1.6 0.7 compare_and_fusion
  3.7 1.3 pad_maximum_fusion
  5.0 5.3 %all-to-all-start = ((bf16[8,96,1024]{2,1,0:T(8,128)(2,1)}), bf16[8,96,1024]{2,1,0:T(8,128)(2,1)S(1)}, u32[]{:S(2)}, u32[]{:S(2)}) async-start(bf16[8,96,1024]{2,1,0:T(8,128)(2,1)} %pad_maximum_fusion), calls=%async_computation | async-start | bytes 3145728 | tf_op jit(solution)/shard_map/all_to_all | solution.py:1354
  11.1 0.6 fusion.48
  12.0 0.6 fusion.33.refs_0_
  12.6 0.8 multiply_sine_fusion
  13.4 0.7 add_compare_fusion.1
  14.1 39.7 %gather_weights.1 = (bf16[4,16,256]{2,1,0:T(8,128)(2,1)}, bf16[4,2,4,32,3072]{4,3,2,1,0:T(8,128)(2,1)}) custom-call(bf16[16,256]{1,0:T(8,128)(2,1)} %fusion.33.refs_0_, bf16[2,4,32,3072]{3,2,1,0:T(8,128)(2,1)} %bitcast.130), custom_call_target="tpu_custom_call" | custom-call | tf_op jit(solution)/shard_map/gather_weights/pallas_call | solution.py:604
  53.8 0.8 fusion.30
  54.6 1.1 pad_maximum_fusion.2
  56.3 0.8 slice_convert_fusion
  57.1 1.3 compare_select_fusion.1
  59.2 1.2 fusion.16.refs_3_.refs_0_
  60.4 96.4 %gather_and_project.1 = (bf16[4,2,4,32,1024]{4,3,2,1,0:T(8,128)(2,1)}, bf16[4,2,4,32,5248]{4,3,2,1,0:T(8,128)(2,1)}, bf16[4,656,1024]{2,1,0:T(8,128)(2,1)}, bf16[3072,384]{1,0:T(8,128)(2,1)}) custom-call(bf16[2,4,32,1024]{3,2,1,0:T(8,128)(2,1)} %bitcast.137, bf16[2,4,32,5248]{3,2,1,0:T(8,128)(2,1)} %bitcast.126, bf16[656,1024]{1,0:T(8,128)(2,1)} %refs_2_.1, ...), custom_call_target="tpu_custom_call" | custom-call | tf_op jit(solution)/shard_map/gather_and_project/pallas_call | solution.py:604
  156.8 31.0 %attention_forward.1 = (f32[3072,128]{1,0:T(8,128)}, bf16[3072,128]{1,0:T(8,128)(2,1)}, f32[12,1,512]{2,1,0:T(1,128)}) custom-call(s32[12]{0:T(128)} %get-tuple-element.135.low_ref, s32[12]{0:T(128)} %get-tuple-element.136.high_ref, s32[1,3072]{1,0:T(1,128)} %get-tuple-element.147.begin_ref, s32[1,3072]{1,0:T(1,128)} %get-tuple-element.146.end_ref, ...), custom_call_target="tpu_custom_call" | custom-call | flops 2415919104 | bytes 4718592 | tf_op jit(solution)/shard_map/attention_forward/pallas_call | solution.py:99
  187.8 3.7 all-to-all-start.1
  191.5 0.7 fusion.34
  192.1 8.4 %all-to-all-done.1 = bf16[8,384,128]{2,1,0:T(8,128)(2,1)S(1)} async-done(((bf16[8,384,128]{2,1,0:T(8,128)(2,1)}), bf16[8,384,128]{2,1,0:T(8,128)(2,1)S(1)}, u32[]{:S(2)}, u32[]{:S(2)}) %all-to-all-start.1) | async-done | bytes 786464 | tf_op jit(solution)/shard_map/all_to_all | solution.py:1354
  200.5 4.1 fusion.44
  205.3 0.8 copy-done.19
  206.1 4.5 fusion.49
  210.6 10.0 %multiply_convert_fusion.1 = (bf16[384,2624]{1,0:T(8,128)(2,1)}, f32[384,2624]{1,0:T(8,128)S(1)}) fusion(f32[384,5248]{1,0:T(8,128)S(1)} %fusion.49), kind=kLoop, calls=%fused_computation.8 | loop fusion | flops 66502656 | bytes 14106624 | tf_op jit(solution)/shard_map/convert_element_type | solution.py:1417
  220.6 9.0 %add_convert_fusion = (bf16[384,2624]{1,0:T(8,128)(2,1)}, bf16[384,2624]{1,0:T(8,128)(2,1)}) fusion(f32[384,2624]{1,0:T(8,128)S(1)} %get-tuple-element.112, f32[384,5248]{1,0:T(8,128)S(1)} %fusion.49, bf16[384,1024]{1,0:T(8,128)(2,1)S(1)} %bitcast.134, bf16[2624,1024]{1,0:T(8,128)(2,1)} %bitcast.160), kind=kOutput, calls=%fused_computation.7 | convolution fusion | flops 2081734656 | bytes 22282240 | tf_op jit(solution)/shard_map/dot_general | solution.py:1431
  229.6 8.9 %fusion.6 = f32[384,1024]{1,0:T(8,128)S(1)} fusion(bf16[1024,5248]{1,0:T(8,128)(2,1)} %bitcast.158, bf16[384,2624]{1,0:T(8,128)(2,1)} %get-tuple-element.118.refs_5_, bf16[384,2624]{1,0:T(8,128)(2,1)} %get-tuple-element.117.refs_4_), kind=kOutput, calls=%fused_computation.22 | convolution fusion | flops 4135256064 | bytes 16351232 | tf_op jit(solution)/shard_map/dot_general | solution.py:1445
  238.5 6.9 %multiply_reduce_fusion = (f32[]{:T(128)}, f32[]{:T(128)}, f32[384]{0:T(512)S(1)}, f32[1024]{0:T(1024)S(1)}, f32[]{:T(128)}, /*index=5*/bf16[384,1024]{1,0:T(8,128)(2,1)}) fusion(f32[384,1024]{1,0:T(8,128)S(1)} %get-tuple-element.114, pred[384]{0:T(512)(128)(4,1)S(1)} %fusion.34, f32[384,1024]{1,0:T(8,128)S(1)} %fusion.6, f32[1024]{0:T(1024)S(1)} %bitcast.145, ...), kind=kOutput, calls=%fused_computation.52 | convolution fusion | flops 2070674048 | bytes 12907404 | tf_op jit(solution)/shard_map/dot_general | solution.py:1420
  245.9 1.2 fusion.21
  247.2 0.7 copy-done.9
  247.8 1.0 fusion.22
  248.8 1.0 copy.44
  249.9 7.6 %all-to-all-start.2 = ((bf16[8,384,128]{2,1,0:T(8,128)(2,1)}), bf16[8,384,128]{2,1,0:T(8,128)(2,1)}, u32[]{:S(2)}, u32[]{:S(2)}) async-start(bf16[8,384,128]{2,1,0:T(8,128)(2,1)} %bitcast.124), calls=%async_computation.2 | async-start | bytes 1572864 | tf_op jit(solution)/shard_map/all_to_all | solution.py:1354
  257.5 2.1 copy_bitcast_fusion.refs_0_
  259.6 21.0 %early_products.1 = (bf16[2,4,32,3200]{3,2,1,0:T(8,128)(2,1)}, bf16[2,4,32,3200]{3,2,1,0:T(8,128)(2,1)}, bf16[2,4,32,3200]{3,2,1,0:T(8,128)(2,1)}, bf16[2,4,32,3...) custom-call(bf16[384,1024]{1,0:T(8,128)(2,1)} %copy_bitcast_fusion.r, ...), custom_call_target="tpu_custom_call" | custom-call | tf_op jit(solution)/shard_map/early_products/pallas_call | solution.py:856
  280.6 1.4 collective-permute-start
  282.0 1.2 collective-permute-start.1
  283.6 40.7 %attention_backward.1 = bf16[3072,384]{1,0:T(8,128)(2,1)} custom-call(s32[12]{0:T(128)} %get-tuple-element.109.low_ref, s32[12]{0:T(128)} %get-tuple-element.110.high_ref, s32[1,3072]{1,0:T(1,128)} %get-tuple-element.147.begin_ref, s32[1,3072]{1,0:T(1,128)} %get-tuple-element.146.end_ref, bf16[3072,384]{1,0:T(8,128)(2,1)} %get-tuple-element.54.qkv_ref, ...), custom_call_target="tpu_custom_call" | custom-call | flops 6039797760 | bytes 11796480 | tf_op jit(solution)/shard_map/attention_backward/pallas_call | solution.py:219
  324.3 8.0 %collective-permute-done.2.refs_9_ = bf16[2,4,320,128]{3,2,1,0:T(8,128)(2,1)} collective-permute-done((bf16[2,4,320,128]{3,2,1,0:T(8,128)(2,1)}, bf16[2,4,320,128]{3,2,1,0:T(8,128)(2,1)}, u32[]{:S(2)}, u32[]{:S(2)}) %collective-permute-start.2) | collective-permute-done | bytes 655392 | tf_op jit(solution)/shard_map/ppermute | solution.py:1166
  332.3 1.5 collective-permute-done.3.refs_12_
  333.8 6.2 %all-to-all-start.3 = ((bf16[8,384,384]{2,1,0:T(8,128)(2,1)}), bf16[8,384,384]{2,1,0:T(8,128)(2,1)}, u32[]{:S(2)}, u32[]{:S(2)}) async-start(bf16[8,384,384]{2,1,0:T(8,128)(2,1)} %bitcast.127), calls=%async_computation.3 | async-start | bytes 4718592 | tf_op jit(solution)/shard_map/all_to_all | solution.py:1354
  340.8 2.1 select_maximum_fusion
  342.9 2.5 fusion.24
  345.4 1.4 collective-permute-start.4
  346.8 2.2 fusion.25
  349.0 1.2 collective-permute-start.5
  350.2 1.8 fusion.27
  352.3 1.1 fusion.26
  353.6 12.4 %all-to-all-done.3.heads_ref = bf16[8,384,384]{2,1,0:T(8,128)(2,1)} async-done(((bf16[8,384,384]{2,1,0:T(8,128)(2,1)}), bf16[8,384,384]{2,1,0:T(8,128)(2,1)}, u32[]{:S(2)}, u32[]{:S(2)}) %all-to-all-start.3) | async-done | bytes 2359328 | tf_op jit(solution)/shard_map/all_to_all | solution.py:1354
  365.9 8.9 %finish_rows.1 = (bf16[384,3072]{1,0:T(8,128)(2,1)}, f32[384,1024]{1,0:T(8,128)}) custom-call(bf16[8,384,384]{2,1,0:T(8,128)(2,1)} %all-to-all-done.3.heads_ref, f32[384,128]{1,0:T(8,128)} %get-tuple-element.148.refs_5_.cosine_ref, f32[384,128]{1,0:T(8,128)} %get-tuple-element.149.refs_6_.sine_ref, bf16[1024,3072]{1,0:T(8,128)(2,1)} %bitcast.121, ...), custom_call_target="tpu_custom_call" | custom-call | flops 2415919104 | bytes 11010048 | tf_op jit(solution)/shard_map/finish_rows/pallas_call | solution.py:285
  374.8 1.9 fusion.18
  376.7 0.8 fusion.17
  377.5 1.0 add_convert_fusion.3
  378.7 1.3 pad_maximum_fusion.1
  380.0 7.7 %all-to-all-start.4 = ((bf16[8,96,1024]{2,1,0:T(8,128)(2,1)}), bf16[8,96,1024]{2,1,0:T(8,128)(2,1)S(1)}, u32[]{:S(2)}, u32[]{:S(2)}) async-start(bf16[8,96,1024]{2,1,0:T(8,128)(2,1)} %pad_maximum_fusion.1), calls=%async_computation.4 | async-start | bytes 3145728 | tf_op jit(solution)/shard_map/all_to_all | solution.py:1354
  387.7 0.7 stack.41.refs_14_
  388.3 3.8 collective-permute-done.6.refs_10_
  392.7 93.0 %sum_weights.1 = (bf16[256,1024]{1,0:T(8,128)(2,1)}, bf16[256,5376]{1,0:T(8,128)(2,1)}, bf16[656,1024]{1,0:T(8,128)(2,1)}, bf16[256,3072]{1,0:T(8,128)(2,1)}, f32[2,8,1024]{2,1,0:T(8,128)}) custom-call(bf16[384,1024]{1,0:T(8,128)(2,1)} %fusion.16.refs_3_.refs_0_, bf16[384,3072]{1,0:T(8,128)(2,1)} %get-tuple-element.80.refs_1_, ...), custom_call_target="tpu_custom_call" | custom-call | tf_op jit(solution)/shard_map/sum_weights/pallas_call | solution.py:1136
  485.7 0.8 fusion.47
  486.6 3.6 convert_element_type.198
  490.1 1.1 convert_element_type.199
  492.3 1.8 convert_element_type.201
  494.2 1.2 sqrt_bitcast_fusion
  495.6 3.0 maximum_convert_fusion
  498.8 0.6 gather_fusion.3
  500.0 1.3 broadcast_select_fusion
  (96 shorter events, 8.7 us)
Async XLA Ops:
  0.6 1.6 copy-start
  0.7 2.2 copy-start.14
  4.9 5.4 %copy-start.17 = (s32[1,6]{1,0:T(1,128)S(1)}, s32[1,6]{1,0:T(1,128)}, u32[]{:S(2)}) copy-start(s32[1,6]{1,0:T(1,128)} %param.14) | copy-start | bytes 76
  4.9 6.8 %copy-start.20 = (bf16[256]{0:T(256)(128)(2,1)S(1)}, bf16[256]{0:T(256)(128)(2,1)}, u32[]{:S(2)}) copy-start(bf16[256]{0:T(256)(128)(2,1)} %param.19) | copy-start | bytes 1540
  4.9 6.8 %copy-start.21 = (bf16[256]{0:T(256)(128)(2,1)S(1)}, bf16[256]{0:T(256)(128)(2,1)}, u32[]{:S(2)}) copy-start(bf16[256]{0:T(256)(128)(2,1)} %param.16) | copy-start | bytes 1540
  5.0 53.4 %all-to-all-start = ((bf16[8,96,1024]{2,1,0:T(8,128)(2,1)}), bf16[8,96,1024]{2,1,0:T(8,128)(2,1)S(1)}, u32[]{:S(2)}, u32[]{:S(2)}) async-start(bf16[8,96,1024]{2,1,0:T(8,128)(2,1)} %pad_maximum_fusion), calls=%async_computation | async-start | bytes 3145728 | tf_op jit(solution)/shard_map/all_to_all | solution.py:1354
  187.8 12.7 %all-to-all-start.1 = ((bf16[8,384,128]{2,1,0:T(8,128)(2,1)}), bf16[8,384,128]{2,1,0:T(8,128)(2,1)S(1)}, u32[]{:S(2)}, u32[]{:S(2)}) async-start(bf16[8,384,128]{2,1,0:T(8,128)(2,1)} %bitcast.132), calls=%async_computation.1 | async-start | bytes 1572864 | tf_op jit(solution)/shard_map/all_to_all | solution.py:1354
  200.5 4.2 copy-start.4
  200.5 5.5 %copy-start.19 = (bf16[4,2,4,32,5248]{4,3,2,1,0:T(8,128)(2,1)S(1)}, bf16[4,2,4,32,5248]{4,3,2,1,0:T(8,128)(2,1)}, u32[]{:S(2)}) copy-start(bf16[4,2,4,32,5248]{4,3,2,1,0:T(8,128)(2,1)} %get-tuple-element.57) | copy-start | bytes 32243716
  205.3 5.3 %copy-start.6 = (bf16[384,1024]{1,0:T(8,128)(2,1)}, bf16[384,1024]{1,0:T(8,128)(2,1)S(1)}, u32[]{:S(2)}) copy-start(bf16[384,1024]{1,0:T(8,128)(2,1)S(1)} %multiply_convert_fusion.2.refs_1_) | copy-start | bytes 2359300
  229.6 8.9 %copy-start.3 = (bf16[384,2624]{1,0:T(8,128)(2,1)S(1)}, bf16[384,2624]{1,0:T(8,128)(2,1)}, u32[]{:S(2)}) copy-start(bf16[384,2624]{1,0:T(8,128)(2,1)} %get-tuple-element.111.refs_2_) | copy-start | bytes 6045700
  229.6 8.9 %copy-start.10 = (f32[384,1024]{1,0:T(8,128)S(1)}, f32[384,1024]{1,0:T(8,128)}, u32[]{:S(2)}) copy-start(f32[384,1024]{1,0:T(8,128)} %get-tuple-element.143) | copy-start | bytes 4718596
  245.9 1.9 copy-start.9
  247.2 1.7 copy-start.7
  249.9 30.7 %all-to-all-start.2 = ((bf16[8,384,128]{2,1,0:T(8,128)(2,1)}), bf16[8,384,128]{2,1,0:T(8,128)(2,1)}, u32[]{:S(2)}, u32[]{:S(2)}) async-start(bf16[8,384,128]{2,1,0:T(8,128)(2,1)} %bitcast.124), calls=%async_computation.2 | async-start | bytes 1572864 | tf_op jit(solution)/shard_map/all_to_all | solution.py:1354
  280.6 53.2 %collective-permute-start = (bf16[2,4,32,3200]{3,2,1,0:T(8,128)(2,1)}, bf16[2,4,32,3200]{3,2,1,0:T(8,128)(2,1)}, u32[]{:S(2)}, u32[]{:S(2)}) collective-permute-start(bf16[2,4,32,3200]{3,2,1,0:T(8,128)(2,1)} %get-tuple-element.71), channel_id=1, source_target_pairs={{0,8},{4,12},{8,0},{12,4},{16,24},{20,28},{24,16},{28,20},{1,9},{5... | collective-permute-start | bytes 4915208 | tf_op jit(solution)/shard_map/ppermute | solution.py:1166
  282.0 51.8 %collective-permute-start.1 = (bf16[2,4,32,3200]{3,2,1,0:T(8,128)(2,1)}, bf16[2,4,32,3200]{3,2,1,0:T(8,128)(2,1)}, u32[]{:S(2)}, u32[]{:S(2)}) collective-permute-start(bf16[2,4,32,3200]{3,2,1,0:T(8,128)(2,1)} %get-tuple-element.73), channel_id=1, source_target_pairs={{0,16},{4,20},{8,24},{12,28},{16,0},{20,4},{24,8},{28,12},{1,17},{... | collective-permute-start | bytes 4915208 | tf_op jit(solution)/shard_map/ppermute | solution.py:1166
  283.3 50.5 %collective-permute-start.3 = (bf16[2,4,336,128]{3,2,1,0:T(8,128)(2,1)}, bf16[2,4,336,128]{3,2,1,0:T(8,128)(2,1)}, u32[]{:S(2)}, u32[]{:S(2)}) collective-permute-start(bf16[2,4,336,128]{3,2,1,0:T(8,128)(2,1)} %get-tuple-element.77), channel_id=1, source_target_pairs={{0,16},{4,20},{8,24},{12,28},{16,0},{20,4},{24,8},{28,12},{1,17},{... | collective-permute-start | bytes 2064392 | tf_op jit(solution)/shard_map/ppermute | solution.py:1166
  283.5 48.8 %collective-permute-start.2 = (bf16[2,4,320,128]{3,2,1,0:T(8,128)(2,1)}, bf16[2,4,320,128]{3,2,1,0:T(8,128)(2,1)}, u32[]{:S(2)}, u32[]{:S(2)}) collective-permute-start(bf16[2,4,320,128]{3,2,1,0:T(8,128)(2,1)} %get-tuple-element.75), channel_id=1, source_target_pairs={{0,8},{4,12},{8,0},{12,4},{16,24},{20,28},{24,16},{28,20},{1,9},{5... | collective-permute-start | bytes 1966088 | tf_op jit(solution)/shard_map/ppermute | solution.py:1166
  333.8 6.9 %copy-start.18 = (s32[1,1,8]{2,1,0:T(1,128)S(1)}, s32[1,1,8]{2,1,0:T(1,128)}, u32[]{:S(2)}) copy-start(s32[1,1,8]{2,1,0:T(1,128)} %param.15) | copy-start | bytes 100
  333.8 32.1 %all-to-all-start.3 = ((bf16[8,384,384]{2,1,0:T(8,128)(2,1)}), bf16[8,384,384]{2,1,0:T(8,128)(2,1)}, u32[]{:S(2)}, u32[]{:S(2)}) async-start(bf16[8,384,384]{2,1,0:T(8,128)(2,1)} %bitcast.127), calls=%async_computation.3 | async-start | bytes 4718592 | tf_op jit(solution)/shard_map/all_to_all | solution.py:1354
  340.7 6.0 %copy-start.5 = (bf16[2,4,32,3200]{3,2,1,0:T(8,128)(2,1)S(1)}, bf16[2,4,32,3200]{3,2,1,0:T(8,128)(2,1)}, u32[]{:S(2)}) copy-start(bf16[2,4,32,3200]{3,2,1,0:T(8,128)(2,1)} %get-tuple-element.83.refs_5_) | copy-start | bytes 4915204
  342.9 7.3 %copy-start.12 = (bf16[2,4,320,128]{3,2,1,0:T(8,128)(2,1)S(1)}, bf16[2,4,320,128]{3,2,1,0:T(8,128)(2,1)}, u32[]{:S(2)}) copy-start(bf16[2,4,320,128]{3,2,1,0:T(8,128)(2,1)} %get-tuple-element.85.refs_8_) | copy-start | bytes 1966084
  345.4 6.8 %copy-start.11 = (bf16[2,4,336,128]{3,2,1,0:T(8,128)(2,1)S(1)}, bf16[2,4,336,128]{3,2,1,0:T(8,128)(2,1)}, u32[]{:S(2)}) copy-start(bf16[2,4,336,128]{3,2,1,0:T(8,128)(2,1)} %get-tuple-element.87.refs_11_) | copy-start | bytes 2064388
  345.4 47.2 %collective-permute-start.4 = (bf16[4,32,3200]{2,1,0:T(8,128)(2,1)}, bf16[4,32,3200]{2,1,0:T(8,128)(2,1)}, u32[]{:S(2)}, u32[]{:S(2)}) collective-permute-start(bf16[4,32,3200]{2,1,0:T(8,128)(2,1)} %fusion.24), channel_id=1, source_target_pairs={{0,16},{4,20},{8,24},{12,28},{16,0},{20,4},{24,8},{28,12},{1,17},{... | collective-permute-start | bytes 2457608 | tf_op jit(solution)/shard_map/ppermute | solution.py:1166
  349.0 43.6 %collective-permute-start.5 = (bf16[4,32,3200]{2,1,0:T(8,128)(2,1)}, bf16[4,32,3200]{2,1,0:T(8,128)(2,1)}, u32[]{:S(2)}, u32[]{:S(2)}) collective-permute-start(bf16[4,32,3200]{2,1,0:T(8,128)(2,1)} %fusion.25), channel_id=1, source_target_pairs={{0,8},{4,12},{8,0},{12,4},{16,24},{20,28},{24,16},{28,20},{1,9},{5... | collective-permute-start | bytes 2457608 | tf_op jit(solution)/shard_map/ppermute | solution.py:1166
  352.0 40.2 %collective-permute-start.6 = (bf16[4,320,128]{2,1,0:T(8,128)(2,1)}, bf16[4,320,128]{2,1,0:T(8,128)(2,1)}, u32[]{:S(2)}, u32[]{:S(2)}) collective-permute-start(bf16[4,320,128]{2,1,0:T(8,128)(2,1)} %fusion.27), channel_id=1, source_target_pairs={{0,16},{4,20},{8,24},{12,28},{16,0},{20,4},{24,8},{28,12},{1,17},{... | collective-permute-start | bytes 983048 | tf_op jit(solution)/shard_map/ppermute | solution.py:1166
  353.3 39.3 %collective-permute-start.7 = (bf16[4,336,128]{2,1,0:T(8,128)(2,1)S(1)}, bf16[4,336,128]{2,1,0:T(8,128)(2,1)}, u32[]{:S(2)}, u32[]{:S(2)}) collective-permute-start(bf16[4,336,128]{2,1,0:T(8,128)(2,1)S(1)} %fusion.26), channel_id=1, source_target_pairs={{0,8},{4,12},{8,0},{12,4},{16,24},{20,28},{24,16},{28,20},{1,9},{5... | collective-permute-start | bytes 1032200 | tf_op jit(solution)/shard_map/ppermute | solution.py:1166
  374.8 1.9 copy-start.2
  377.5 1.1 copy-start.15
  380.0 118.6 %all-to-all-start.4 = ((bf16[8,96,1024]{2,1,0:T(8,128)(2,1)}), bf16[8,96,1024]{2,1,0:T(8,128)(2,1)S(1)}, u32[]{:S(2)}, u32[]{:S(2)}) async-start(bf16[8,96,1024]{2,1,0:T(8,128)(2,1)} %pad_maximum_fusion.1), calls=%async_computation.4 | async-start | bytes 3145728 | tf_op jit(solution)/shard_map/all_to_all | solution.py:1354
  486.5 3.6 copy-start.16
  486.5 5.8 %copy-start.13 = (bf16[656,1024]{1,0:T(8,128)(2,1)S(1)}, bf16[656,1024]{1,0:T(8,128)(2,1)}, u32[]{:S(2)}) copy-start(bf16[656,1024]{1,0:T(8,128)(2,1)} %get-tuple-element.93) | copy-start | bytes 4030468
  491.2 4.2 copy-start.8
  499.4 2.0 copy-start.1

commit v7 on v6

--- a/solution.py
+++ b/solution.py
@@ -903,6 +903,7 @@
     plan = early + late
     chunks = [(w, t) for w, entry in enumerate(plan) for t in range(entry[1])]
     early_count = sum(entry[1] for entry in early)
+    order = sorted(range(early_count), key=lambda number: (-chunks[number][0], number))
     units = {}
     for number in range(len(chunks)):
         for half in (0, 1):
@@ -914,7 +915,7 @@
     own_x, own_y = (chip % 2, chip // 2)
     low_bit, high_bit = (own_shard % 2, own_shard // 2)
     loads = {}
-    for number in range(early_count):
+    for number in order:
         w, (group, offset) = (chunks[number][0], places[number])
         for half in (0, 1):
             own = own_y if half == 0 else own_x
@@ -1091,14 +1092,18 @@
 
     stages = (stage_one, stage_two, stage_three, stage_four, stage_five, stage_six, stage_seven)
     small_at = 0
-    stage_three(0)
+    stage_three(order[0])
     for w in range(len(late)):
         turn(w)
     for tick in range(len(chunks) + len(stages)):
         for lag, stage in enumerate(stages):
             for number in range(len(chunks)):
-                start = number - 2 if number < early_count else number - early_count
-                if start + lag == tick and (number >= early_count or (lag >= 2 and number + lag > 2)):
+                if number >= early_count:
+                    due = number - early_count + lag == tick
+                else:
+                    rank = order.index(number)
+                    due = rank - 2 + lag == tick and lag >= 2 and rank + lag > 2
+                if due:
                     stage(number)
         if small_at < 6:
             small_step(small_at)

time: 510 us -> 505 us (level)
  Pallas kernels: 331 us -> 325 us
  transfers between devices with their start and end apart: 13 -> 13, of which waited for: 6 -> 6; matrix products, arithmetic and copies ran while one was open for 8% -> 8% of each run, Pallas kernels for 41% -> 40%
where the time goes in v7:
time: 505 us; the launch traced here: 498 us
  Pallas kernels  325 us (64%)
  other arithmetic  52.3 us (10%)
  starting transfers between devices  36.5 us (7%)
  waiting for transfers between devices  35.7 us (7%)
  matrix products  34.4 us (7%)
  local copies, waits for them, and re-layouts  11 us (2%)
    pallas_call x2, Pallas kernels, gather_weights(): pl.pallas_call(functools.partial(gather_kernel, shapes, projection is not...  136 us
    pallas_call x1, Pallas kernels, sum_weights(): pl.pallas_call(functools.partial(sum_kernel, early, late, plan_lead(plan)...  89.5 us
    pallas_call x1, Pallas kernels, attention_backward(): pl.pallas_call(functools.partial(backward_kernel, head_count, block_q, bl...  39.7 us
    all_to_all x5, starting transfers between devices, exchange(): lax.all_to_all(blocks, 'ctx', split_axis=0, concat_axis=0, tiled=True)  30.5 us
    pallas_call x1, Pallas kernels, attention_forward(): pl.pallas_call(functools.partial(forward_kernel, head_count, block_q, blo...  30.4 us
    pallas_call x1, Pallas kernels, early_sums(): pl.pallas_call(functools.partial(product_kernel, plan, plan_lead(plan)),...  21 us
    all_to_all x5, waiting for transfers between devices, exchange(): lax.all_to_all(blocks, 'ctx', split_axis=0, concat_axis=0, tiled=True)  20.8 us
    ppermute x8, waiting for transfers between devices, swap(): return lax.ppermute(value, axis, pairs)  14.9 us
  transfers between devices with their start and end apart: 13, of which 6 were waited for; matrix products, arithmetic and copies ran while one was open for 8% of the time, Pallas kernels for 40%

profile of v7, /device:TPU:1, one launch (start us, length us, event | category | flops | bytes accessed | tf_op | source)
XLA Modules:
  0.0 497.6 jit_solution(10236605347314253414)
XLA Ops:
  0.7 0.9 select_reduce_fusion.6
  1.6 0.7 compare_and_fusion
  3.7 1.3 pad_maximum_fusion
  5.0 5.3 %all-to-all-start = ((bf16[8,96,1024]{2,1,0:T(8,128)(2,1)}), bf16[8,96,1024]{2,1,0:T(8,128)(2,1)S(1)}, u32[]{:S(2)}, u32[]{:S(2)}) async-start(bf16[8,96,1024]{2,1,0:T(8,128)(2,1)} %pad_maximum_fusion), calls=%async_computation | async-start | bytes 3145728 | tf_op jit(solution)/shard_map/all_to_all | solution.py:1359
  11.1 0.6 fusion.48
  12.0 0.6 fusion.33.refs_0_
  12.6 0.8 multiply_sine_fusion
  13.4 0.7 add_compare_fusion.1
  14.1 39.7 %gather_weights.1 = (bf16[4,16,256]{2,1,0:T(8,128)(2,1)}, bf16[4,2,4,32,3072]{4,3,2,1,0:T(8,128)(2,1)}) custom-call(bf16[16,256]{1,0:T(8,128)(2,1)} %fusion.33.refs_0_, bf16[2,4,32,3072]{3,2,1,0:T(8,128)(2,1)} %bitcast.130), custom_call_target="tpu_custom_call" | custom-call | tf_op jit(solution)/shard_map/gather_weights/pallas_call | solution.py:604
  53.8 0.8 fusion.30
  54.6 1.1 pad_maximum_fusion.2
  56.3 0.8 slice_convert_fusion
  57.1 1.3 compare_select_fusion.1
  59.2 1.2 fusion.16.refs_3_.refs_0_
  60.4 96.4 %gather_and_project.1 = (bf16[4,2,4,32,1024]{4,3,2,1,0:T(8,128)(2,1)}, bf16[4,2,4,32,5248]{4,3,2,1,0:T(8,128)(2,1)}, bf16[4,656,1024]{2,1,0:T(8,128)(2,1)}, bf16[3072,384]{1,0:T(8,128)(2,1)}) custom-call(bf16[2,4,32,1024]{3,2,1,0:T(8,128)(2,1)} %bitcast.137, bf16[2,4,32,5248]{3,2,1,0:T(8,128)(2,1)} %bitcast.126, bf16[656,1024]{1,0:T(8,128)(2,1)} %refs_2_.1, ...), custom_call_target="tpu_custom_call" | custom-call | tf_op jit(solution)/shard_map/gather_and_project/pallas_call | solution.py:604
  156.8 30.4 %attention_forward.1 = (f32[3072,128]{1,0:T(8,128)}, bf16[3072,128]{1,0:T(8,128)(2,1)}, f32[12,1,512]{2,1,0:T(1,128)}) custom-call(s32[12]{0:T(128)} %get-tuple-element.135.low_ref, s32[12]{0:T(128)} %get-tuple-element.136.high_ref, s32[1,3072]{1,0:T(1,128)} %get-tuple-element.147.begin_ref, s32[1,3072]{1,0:T(1,128)} %get-tuple-element.146.end_ref, ...), custom_call_target="tpu_custom_call" | custom-call | flops 2415919104 | bytes 4718592 | tf_op jit(solution)/shard_map/attention_forward/pallas_call | solution.py:99
  187.2 3.7 all-to-all-start.1
  190.9 0.7 fusion.34
  191.5 8.4 %all-to-all-done.1 = bf16[8,384,128]{2,1,0:T(8,128)(2,1)S(1)} async-done(((bf16[8,384,128]{2,1,0:T(8,128)(2,1)}), bf16[8,384,128]{2,1,0:T(8,128)(2,1)S(1)}, u32[]{:S(2)}, u32[]{:S(2)}) %all-to-all-start.1) | async-done | bytes 786464 | tf_op jit(solution)/shard_map/all_to_all | solution.py:1359
  199.9 4.1 fusion.44
  204.7 0.8 copy-done.19
  205.5 4.5 fusion.49
  209.9 10.0 %multiply_convert_fusion.1 = (bf16[384,2624]{1,0:T(8,128)(2,1)}, f32[384,2624]{1,0:T(8,128)S(1)}) fusion(f32[384,5248]{1,0:T(8,128)S(1)} %fusion.49), kind=kLoop, calls=%fused_computation.8 | loop fusion | flops 66502656 | bytes 14106624 | tf_op jit(solution)/shard_map/convert_element_type | solution.py:1422
  219.9 9.0 %add_convert_fusion = (bf16[384,2624]{1,0:T(8,128)(2,1)}, bf16[384,2624]{1,0:T(8,128)(2,1)}) fusion(f32[384,2624]{1,0:T(8,128)S(1)} %get-tuple-element.112, f32[384,5248]{1,0:T(8,128)S(1)} %fusion.49, bf16[384,1024]{1,0:T(8,128)(2,1)S(1)} %bitcast.134, bf16[2624,1024]{1,0:T(8,128)(2,1)} %bitcast.160), kind=kOutput, calls=%fused_computation.7 | convolution fusion | flops 2081734656 | bytes 22282240 | tf_op jit(solution)/shard_map/dot_general | solution.py:1436
  228.9 8.9 %fusion.6 = f32[384,1024]{1,0:T(8,128)S(1)} fusion(bf16[1024,5248]{1,0:T(8,128)(2,1)} %bitcast.158, bf16[384,2624]{1,0:T(8,128)(2,1)} %get-tuple-element.118.refs_5_, bf16[384,2624]{1,0:T(8,128)(2,1)} %get-tuple-element.117.refs_4_), kind=kOutput, calls=%fused_computation.22 | convolution fusion | flops 4135256064 | bytes 16351232 | tf_op jit(solution)/shard_map/dot_general | solution.py:1450
  237.8 6.9 %multiply_reduce_fusion = (f32[]{:T(128)}, f32[]{:T(128)}, f32[384]{0:T(512)S(1)}, f32[1024]{0:T(1024)S(1)}, f32[]{:T(128)}, /*index=5*/bf16[384,1024]{1,0:T(8,128)(2,1)}) fusion(f32[384,1024]{1,0:T(8,128)S(1)} %get-tuple-element.114, pred[384]{0:T(512)(128)(4,1)S(1)} %fusion.34, f32[384,1024]{1,0:T(8,128)S(1)} %fusion.6, f32[1024]{0:T(1024)S(1)} %bitcast.145, ...), kind=kOutput, calls=%fused_computation.52 | convolution fusion | flops 2070674048 | bytes 12907404 | tf_op jit(solution)/shard_map/dot_general | solution.py:1425
  245.3 1.2 fusion.21
  246.5 0.7 copy-done.9
  247.2 1.0 fusion.22
  248.2 1.0 copy.44
  249.3 7.6 %all-to-all-start.2 = ((bf16[8,384,128]{2,1,0:T(8,128)(2,1)}), bf16[8,384,128]{2,1,0:T(8,128)(2,1)}, u32[]{:S(2)}, u32[]{:S(2)}) async-start(bf16[8,384,128]{2,1,0:T(8,128)(2,1)} %bitcast.124), calls=%async_computation.2 | async-start | bytes 1572864 | tf_op jit(solution)/shard_map/all_to_all | solution.py:1359
  256.9 2.1 copy_bitcast_fusion.refs_0_
  259.0 21.0 %early_products.1 = (bf16[2,4,32,3200]{3,2,1,0:T(8,128)(2,1)}, bf16[2,4,32,3200]{3,2,1,0:T(8,128)(2,1)}, bf16[2,4,32,3200]{3,2,1,0:T(8,128)(2,1)}, bf16[2,4,32,3...) custom-call(bf16[384,1024]{1,0:T(8,128)(2,1)} %copy_bitcast_fusion.r, ...), custom_call_target="tpu_custom_call" | custom-call | tf_op jit(solution)/shard_map/early_products/pallas_call | solution.py:856
  280.0 1.4 collective-permute-start
  281.4 1.2 collective-permute-start.1
  283.0 39.7 %attention_backward.1 = bf16[3072,384]{1,0:T(8,128)(2,1)} custom-call(s32[12]{0:T(128)} %get-tuple-element.109.low_ref, s32[12]{0:T(128)} %get-tuple-element.110.high_ref, s32[1,3072]{1,0:T(1,128)} %get-tuple-element.147.begin_ref, s32[1,3072]{1,0:T(1,128)} %get-tuple-element.146.end_ref, bf16[3072,384]{1,0:T(8,128)(2,1)} %get-tuple-element.54.qkv_ref, ...), custom_call_target="tpu_custom_call" | custom-call | flops 6039797760 | bytes 11796480 | tf_op jit(solution)/shard_map/attention_backward/pallas_call | solution.py:219
  322.7 9.0 %collective-permute-done.2.refs_9_ = bf16[2,4,320,128]{3,2,1,0:T(8,128)(2,1)} collective-permute-done((bf16[2,4,320,128]{3,2,1,0:T(8,128)(2,1)}, bf16[2,4,320,128]{3,2,1,0:T(8,128)(2,1)}, u32[]{:S(2)}, u32[]{:S(2)}) %collective-permute-start.2) | collective-permute-done | bytes 655392 | tf_op jit(solution)/shard_map/ppermute | solution.py:1171
  331.6 1.5 collective-permute-done.3.refs_12_
  333.2 6.2 %all-to-all-start.3 = ((bf16[8,384,384]{2,1,0:T(8,128)(2,1)}), bf16[8,384,384]{2,1,0:T(8,128)(2,1)}, u32[]{:S(2)}, u32[]{:S(2)}) async-start(bf16[8,384,384]{2,1,0:T(8,128)(2,1)} %bitcast.127), calls=%async_computation.3 | async-start | bytes 4718592 | tf_op jit(solution)/shard_map/all_to_all | solution.py:1359
  340.2 2.1 select_maximum_fusion
  342.2 2.5 fusion.24
  344.8 1.4 collective-permute-start.4
  346.2 2.2 fusion.25
  348.4 1.2 collective-permute-start.5
  349.6 1.8 fusion.27
  351.6 1.1 fusion.26
  352.9 12.4 %all-to-all-done.3.heads_ref = bf16[8,384,384]{2,1,0:T(8,128)(2,1)} async-done(((bf16[8,384,384]{2,1,0:T(8,128)(2,1)}), bf16[8,384,384]{2,1,0:T(8,128)(2,1)}, u32[]{:S(2)}, u32[]{:S(2)}) %all-to-all-start.3) | async-done | bytes 2359328 | tf_op jit(solution)/shard_map/all_to_all | solution.py:1359
  365.3 8.9 %finish_rows.1 = (bf16[384,3072]{1,0:T(8,128)(2,1)}, f32[384,1024]{1,0:T(8,128)}) custom-call(bf16[8,384,384]{2,1,0:T(8,128)(2,1)} %all-to-all-done.3.heads_ref, f32[384,128]{1,0:T(8,128)} %get-tuple-element.148.refs_5_.cosine_ref, f32[384,128]{1,0:T(8,128)} %get-tuple-element.149.refs_6_.sine_ref, bf16[1024,3072]{1,0:T(8,128)(2,1)} %bitcast.121, ...), custom_call_target="tpu_custom_call" | custom-call | flops 2415919104 | bytes 11010048 | tf_op jit(solution)/shard_map/finish_rows/pallas_call | solution.py:285
  374.2 1.9 fusion.18
  376.1 0.8 fusion.17
  376.9 1.0 add_convert_fusion.3
  378.0 1.3 pad_maximum_fusion.1
  379.4 7.7 %all-to-all-start.4 = ((bf16[8,96,1024]{2,1,0:T(8,128)(2,1)}), bf16[8,96,1024]{2,1,0:T(8,128)(2,1)S(1)}, u32[]{:S(2)}, u32[]{:S(2)}) async-start(bf16[8,96,1024]{2,1,0:T(8,128)(2,1)} %pad_maximum_fusion.1), calls=%async_computation.4 | async-start | bytes 3145728 | tf_op jit(solution)/shard_map/all_to_all | solution.py:1359
  387.0 0.7 stack.41.refs_14_
  387.7 3.8 collective-permute-done.6.refs_10_
  392.0 89.5 %sum_weights.1 = (bf16[256,1024]{1,0:T(8,128)(2,1)}, bf16[256,5376]{1,0:T(8,128)(2,1)}, bf16[656,1024]{1,0:T(8,128)(2,1)}, bf16[256,3072]{1,0:T(8,128)(2,1)}, f32[2,8,1024]{2,1,0:T(8,128)}) custom-call(bf16[384,1024]{1,0:T(8,128)(2,1)} %fusion.16.refs_3_.refs_0_, bf16[384,3072]{1,0:T(8,128)(2,1)} %get-tuple-element.80.refs_1_, ...), custom_call_target="tpu_custom_call" | custom-call | tf_op jit(solution)/shard_map/sum_weights/pallas_call | solution.py:1141
  481.5 0.8 fusion.47
  482.4 3.6 convert_element_type.198
  485.9 1.1 convert_element_type.199
  488.1 1.8 convert_element_type.201
  490.0 1.2 sqrt_bitcast_fusion
  491.4 3.0 maximum_convert_fusion
  494.6 0.6 gather_fusion.3
  495.8 1.3 broadcast_select_fusion
  (96 shorter events, 8.7 us)
Async XLA Ops:
  0.6 1.6 copy-start
  0.7 2.2 copy-start.14
  4.9 5.4 %copy-start.17 = (s32[1,6]{1,0:T(1,128)S(1)}, s32[1,6]{1,0:T(1,128)}, u32[]{:S(2)}) copy-start(s32[1,6]{1,0:T(1,128)} %param.14) | copy-start | bytes 76
  4.9 6.8 %copy-start.20 = (bf16[256]{0:T(256)(128)(2,1)S(1)}, bf16[256]{0:T(256)(128)(2,1)}, u32[]{:S(2)}) copy-start(bf16[256]{0:T(256)(128)(2,1)} %param.19) | copy-start | bytes 1540
  4.9 6.8 %copy-start.21 = (bf16[256]{0:T(256)(128)(2,1)S(1)}, bf16[256]{0:T(256)(128)(2,1)}, u32[]{:S(2)}) copy-start(bf16[256]{0:T(256)(128)(2,1)} %param.16) | copy-start | bytes 1540
  5.0 53.4 %all-to-all-start = ((bf16[8,96,1024]{2,1,0:T(8,128)(2,1)}), bf16[8,96,1024]{2,1,0:T(8,128)(2,1)S(1)}, u32[]{:S(2)}, u32[]{:S(2)}) async-start(bf16[8,96,1024]{2,1,0:T(8,128)(2,1)} %pad_maximum_fusion), calls=%async_computation | async-start | bytes 3145728 | tf_op jit(solution)/shard_map/all_to_all | solution.py:1359
  187.2 12.7 %all-to-all-start.1 = ((bf16[8,384,128]{2,1,0:T(8,128)(2,1)}), bf16[8,384,128]{2,1,0:T(8,128)(2,1)S(1)}, u32[]{:S(2)}, u32[]{:S(2)}) async-start(bf16[8,384,128]{2,1,0:T(8,128)(2,1)} %bitcast.132), calls=%async_computation.1 | async-start | bytes 1572864 | tf_op jit(solution)/shard_map/all_to_all | solution.py:1359
  199.9 4.2 copy-start.4
  199.9 5.5 %copy-start.19 = (bf16[4,2,4,32,5248]{4,3,2,1,0:T(8,128)(2,1)S(1)}, bf16[4,2,4,32,5248]{4,3,2,1,0:T(8,128)(2,1)}, u32[]{:S(2)}) copy-start(bf16[4,2,4,32,5248]{4,3,2,1,0:T(8,128)(2,1)} %get-tuple-element.57) | copy-start | bytes 32243716
  204.7 5.3 %copy-start.6 = (bf16[384,1024]{1,0:T(8,128)(2,1)}, bf16[384,1024]{1,0:T(8,128)(2,1)S(1)}, u32[]{:S(2)}) copy-start(bf16[384,1024]{1,0:T(8,128)(2,1)S(1)} %multiply_convert_fusion.2.refs_1_) | copy-start | bytes 2359300
  228.9 8.9 %copy-start.3 = (bf16[384,2624]{1,0:T(8,128)(2,1)S(1)}, bf16[384,2624]{1,0:T(8,128)(2,1)}, u32[]{:S(2)}) copy-start(bf16[384,2624]{1,0:T(8,128)(2,1)} %get-tuple-element.111.refs_2_) | copy-start | bytes 6045700
  228.9 8.9 %copy-start.10 = (f32[384,1024]{1,0:T(8,128)S(1)}, f32[384,1024]{1,0:T(8,128)}, u32[]{:S(2)}) copy-start(f32[384,1024]{1,0:T(8,128)} %get-tuple-element.143) | copy-start | bytes 4718596
  245.3 1.9 copy-start.9
  246.5 1.7 copy-start.7
  249.3 30.7 %all-to-all-start.2 = ((bf16[8,384,128]{2,1,0:T(8,128)(2,1)}), bf16[8,384,128]{2,1,0:T(8,128)(2,1)}, u32[]{:S(2)}, u32[]{:S(2)}) async-start(bf16[8,384,128]{2,1,0:T(8,128)(2,1)} %bitcast.124), calls=%async_computation.2 | async-start | bytes 1572864 | tf_op jit(solution)/shard_map/all_to_all | solution.py:1359
  280.0 53.2 %collective-permute-start = (bf16[2,4,32,3200]{3,2,1,0:T(8,128)(2,1)}, bf16[2,4,32,3200]{3,2,1,0:T(8,128)(2,1)}, u32[]{:S(2)}, u32[]{:S(2)}) collective-permute-start(bf16[2,4,32,3200]{3,2,1,0:T(8,128)(2,1)} %get-tuple-element.71), channel_id=1, source_target_pairs={{0,8},{4,12},{8,0},{12,4},{16,24},{20,28},{24,16},{28,20},{1,9},{5... | collective-permute-start | bytes 4915208 | tf_op jit(solution)/shard_map/ppermute | solution.py:1171
  281.4 51.8 %collective-permute-start.1 = (bf16[2,4,32,3200]{3,2,1,0:T(8,128)(2,1)}, bf16[2,4,32,3200]{3,2,1,0:T(8,128)(2,1)}, u32[]{:S(2)}, u32[]{:S(2)}) collective-permute-start(bf16[2,4,32,3200]{3,2,1,0:T(8,128)(2,1)} %get-tuple-element.73), channel_id=1, source_target_pairs={{0,16},{4,20},{8,24},{12,28},{16,0},{20,4},{24,8},{28,12},{1,17},{... | collective-permute-start | bytes 4915208 | tf_op jit(solution)/shard_map/ppermute | solution.py:1171
  282.6 50.5 %collective-permute-start.3 = (bf16[2,4,336,128]{3,2,1,0:T(8,128)(2,1)}, bf16[2,4,336,128]{3,2,1,0:T(8,128)(2,1)}, u32[]{:S(2)}, u32[]{:S(2)}) collective-permute-start(bf16[2,4,336,128]{3,2,1,0:T(8,128)(2,1)} %get-tuple-element.77), channel_id=1, source_target_pairs={{0,16},{4,20},{8,24},{12,28},{16,0},{20,4},{24,8},{28,12},{1,17},{... | collective-permute-start | bytes 2064392 | tf_op jit(solution)/shard_map/ppermute | solution.py:1171
  282.9 48.8 %collective-permute-start.2 = (bf16[2,4,320,128]{3,2,1,0:T(8,128)(2,1)}, bf16[2,4,320,128]{3,2,1,0:T(8,128)(2,1)}, u32[]{:S(2)}, u32[]{:S(2)}) collective-permute-start(bf16[2,4,320,128]{3,2,1,0:T(8,128)(2,1)} %get-tuple-element.75), channel_id=1, source_target_pairs={{0,8},{4,12},{8,0},{12,4},{16,24},{20,28},{24,16},{28,20},{1,9},{5... | collective-permute-start | bytes 1966088 | tf_op jit(solution)/shard_map/ppermute | solution.py:1171
  333.2 6.9 %copy-start.18 = (s32[1,1,8]{2,1,0:T(1,128)S(1)}, s32[1,1,8]{2,1,0:T(1,128)}, u32[]{:S(2)}) copy-start(s32[1,1,8]{2,1,0:T(1,128)} %param.15) | copy-start | bytes 100
  333.2 32.1 %all-to-all-start.3 = ((bf16[8,384,384]{2,1,0:T(8,128)(2,1)}), bf16[8,384,384]{2,1,0:T(8,128)(2,1)}, u32[]{:S(2)}, u32[]{:S(2)}) async-start(bf16[8,384,384]{2,1,0:T(8,128)(2,1)} %bitcast.127), calls=%async_computation.3 | async-start | bytes 4718592 | tf_op jit(solution)/shard_map/all_to_all | solution.py:1359
  340.1 6.0 %copy-start.5 = (bf16[2,4,32,3200]{3,2,1,0:T(8,128)(2,1)S(1)}, bf16[2,4,32,3200]{3,2,1,0:T(8,128)(2,1)}, u32[]{:S(2)}) copy-start(bf16[2,4,32,3200]{3,2,1,0:T(8,128)(2,1)} %get-tuple-element.83.refs_5_) | copy-start | bytes 4915204
  342.2 7.3 %copy-start.12 = (bf16[2,4,320,128]{3,2,1,0:T(8,128)(2,1)S(1)}, bf16[2,4,320,128]{3,2,1,0:T(8,128)(2,1)}, u32[]{:S(2)}) copy-start(bf16[2,4,320,128]{3,2,1,0:T(8,128)(2,1)} %get-tuple-element.85.refs_8_) | copy-start | bytes 1966084
  344.8 6.8 %copy-start.11 = (bf16[2,4,336,128]{3,2,1,0:T(8,128)(2,1)S(1)}, bf16[2,4,336,128]{3,2,1,0:T(8,128)(2,1)}, u32[]{:S(2)}) copy-start(bf16[2,4,336,128]{3,2,1,0:T(8,128)(2,1)} %get-tuple-element.87.refs_11_) | copy-start | bytes 2064388
  344.8 47.2 %collective-permute-start.4 = (bf16[4,32,3200]{2,1,0:T(8,128)(2,1)}, bf16[4,32,3200]{2,1,0:T(8,128)(2,1)}, u32[]{:S(2)}, u32[]{:S(2)}) collective-permute-start(bf16[4,32,3200]{2,1,0:T(8,128)(2,1)} %fusion.24), channel_id=1, source_target_pairs={{0,16},{4,20},{8,24},{12,28},{16,0},{20,4},{24,8},{28,12},{1,17},{... | collective-permute-start | bytes 2457608 | tf_op jit(solution)/shard_map/ppermute | solution.py:1171
  348.4 43.6 %collective-permute-start.5 = (bf16[4,32,3200]{2,1,0:T(8,128)(2,1)}, bf16[4,32,3200]{2,1,0:T(8,128)(2,1)}, u32[]{:S(2)}, u32[]{:S(2)}) collective-permute-start(bf16[4,32,3200]{2,1,0:T(8,128)(2,1)} %fusion.25), channel_id=1, source_target_pairs={{0,8},{4,12},{8,0},{12,4},{16,24},{20,28},{24,16},{28,20},{1,9},{5... | collective-permute-start | bytes 2457608 | tf_op jit(solution)/shard_map/ppermute | solution.py:1171
  351.4 40.2 %collective-permute-start.6 = (bf16[4,320,128]{2,1,0:T(8,128)(2,1)}, bf16[4,320,128]{2,1,0:T(8,128)(2,1)}, u32[]{:S(2)}, u32[]{:S(2)}) collective-permute-start(bf16[4,320,128]{2,1,0:T(8,128)(2,1)} %fusion.27), channel_id=1, source_target_pairs={{0,16},{4,20},{8,24},{12,28},{16,0},{20,4},{24,8},{28,12},{1,17},{... | collective-permute-start | bytes 983048 | tf_op jit(solution)/shard_map/ppermute | solution.py:1171
  352.7 39.3 %collective-permute-start.7 = (bf16[4,336,128]{2,1,0:T(8,128)(2,1)S(1)}, bf16[4,336,128]{2,1,0:T(8,128)(2,1)}, u32[]{:S(2)}, u32[]{:S(2)}) collective-permute-start(bf16[4,336,128]{2,1,0:T(8,128)(2,1)S(1)} %fusion.26), channel_id=1, source_target_pairs={{0,8},{4,12},{8,0},{12,4},{16,24},{20,28},{24,16},{28,20},{1,9},{5... | collective-permute-start | bytes 1032200 | tf_op jit(solution)/shard_map/ppermute | solution.py:1171
  374.2 1.9 copy-start.2
  376.9 1.1 copy-start.15
  379.4 115.0 %all-to-all-start.4 = ((bf16[8,96,1024]{2,1,0:T(8,128)(2,1)}), bf16[8,96,1024]{2,1,0:T(8,128)(2,1)S(1)}, u32[]{:S(2)}, u32[]{:S(2)}) async-start(bf16[8,96,1024]{2,1,0:T(8,128)(2,1)} %pad_maximum_fusion.1), calls=%async_computation.4 | async-start | bytes 3145728 | tf_op jit(solution)/shard_map/all_to_all | solution.py:1359
  482.3 3.6 copy-start.16
  482.3 5.8 %copy-start.13 = (bf16[656,1024]{1,0:T(8,128)(2,1)S(1)}, bf16[656,1024]{1,0:T(8,128)(2,1)}, u32[]{:S(2)}) copy-start(bf16[656,1024]{1,0:T(8,128)(2,1)} %get-tuple-element.93) | copy-start | bytes 4030468
  487.0 4.2 copy-start.8
  495.2 2.0 copy-start.1

commit v8 on v7

--- a/solution.py
+++ b/solution.py
@@ -1346,7 +1346,7 @@
     tokens = row_count * ctx_count
     own_heads = model_width // HEAD_WIDTH // ctx_count
     own_width = own_heads * HEAD_WIDTH
-    block_q = math.gcd(tokens, 256)
+    block_q = math.gcd(tokens, 384)
     block_k = math.gcd(tokens, 512)
     lengths_row = lengths[0]
     own_route = piece_route[0, 0]

time: 505 us -> 501 us (level)
  no operation moved by 1% of the time
where the time goes in v8:
time: 501 us; the launch traced here: 494 us
  Pallas kernels  321 us (64%)
  other arithmetic  52.3 us (10%)
  waiting for transfers between devices  37.3 us (7%)
  starting transfers between devices  36.5 us (7%)
  matrix products  34.4 us (7%)
  local copies, waits for them, and re-layouts  11 us (2%)
    pallas_call x2, Pallas kernels, gather_weights(): pl.pallas_call(functools.partial(gather_kernel, shapes, projection is not...  136 us
    pallas_call x1, Pallas kernels, sum_weights(): pl.pallas_call(functools.partial(sum_kernel, early, late, plan_lead(plan)...  88.6 us
    pallas_call x1, Pallas kernels, attention_backward(): pl.pallas_call(functools.partial(backward_kernel, head_count, block_q, bl...  38 us
    all_to_all x5, starting transfers between devices, exchange(): lax.all_to_all(blocks, 'ctx', split_axis=0, concat_axis=0, tiled=True)  30.5 us
    pallas_call x1, Pallas kernels, attention_forward(): pl.pallas_call(functools.partial(forward_kernel, head_count, block_q, blo...  27.9 us
    pallas_call x1, Pallas kernels, early_sums(): pl.pallas_call(functools.partial(product_kernel, plan, plan_lead(plan)),...  21 us
    all_to_all x5, waiting for transfers between devices, exchange(): lax.all_to_all(blocks, 'ctx', split_axis=0, concat_axis=0, tiled=True)  20.8 us
    ppermute x8, waiting for transfers between devices, swap(): return lax.ppermute(value, axis, pairs)  16.5 us
  transfers between devices with their start and end apart: 13, of which 6 were waited for; matrix products, arithmetic and copies ran while one was open for 8% of the time, Pallas kernels for 40%

profile of v8, /device:TPU:1, one launch (start us, length us, event | category | flops | bytes accessed | tf_op | source)
XLA Modules:
  0.0 494.3 jit_solution(7437460627856281163)
XLA Ops:
  0.7 0.9 select_reduce_fusion.6
  1.6 0.7 compare_and_fusion
  3.7 1.3 pad_maximum_fusion
  5.0 5.3 %all-to-all-start = ((bf16[8,96,1024]{2,1,0:T(8,128)(2,1)}), bf16[8,96,1024]{2,1,0:T(8,128)(2,1)S(1)}, u32[]{:S(2)}, u32[]{:S(2)}) async-start(bf16[8,96,1024]{2,1,0:T(8,128)(2,1)} %pad_maximum_fusion), calls=%async_computation | async-start | bytes 3145728 | tf_op jit(solution)/shard_map/all_to_all | solution.py:1359
  11.1 0.6 fusion.48
  12.0 0.6 fusion.33.refs_0_
  12.6 0.8 multiply_sine_fusion
  13.4 0.7 add_compare_fusion.1
  14.0 39.7 %gather_weights.1 = (bf16[4,16,256]{2,1,0:T(8,128)(2,1)}, bf16[4,2,4,32,3072]{4,3,2,1,0:T(8,128)(2,1)}) custom-call(bf16[16,256]{1,0:T(8,128)(2,1)} %fusion.33.refs_0_, bf16[2,4,32,3072]{3,2,1,0:T(8,128)(2,1)} %bitcast.130), custom_call_target="tpu_custom_call" | custom-call | tf_op jit(solution)/shard_map/gather_weights/pallas_call | solution.py:604
  53.8 0.8 fusion.32
  54.6 1.1 pad_maximum_fusion.2
  56.3 0.8 slice_convert_fusion
  57.1 1.3 compare_select_fusion.1
  59.3 1.2 fusion.16.refs_3_.refs_0_
  60.5 96.4 %gather_and_project.1 = (bf16[4,2,4,32,1024]{4,3,2,1,0:T(8,128)(2,1)}, bf16[4,2,4,32,5248]{4,3,2,1,0:T(8,128)(2,1)}, bf16[4,656,1024]{2,1,0:T(8,128)(2,1)}, bf16[3072,384]{1,0:T(8,128)(2,1)}) custom-call(bf16[2,4,32,1024]{3,2,1,0:T(8,128)(2,1)} %bitcast.137, bf16[2,4,32,5248]{3,2,1,0:T(8,128)(2,1)} %bitcast.126, bf16[656,1024]{1,0:T(8,128)(2,1)} %refs_2_.1, ...), custom_call_target="tpu_custom_call" | custom-call | tf_op jit(solution)/shard_map/gather_and_project/pallas_call | solution.py:604
  156.9 27.9 %attention_forward.1 = (f32[3072,128]{1,0:T(8,128)}, bf16[3072,128]{1,0:T(8,128)(2,1)}, f32[8,1,768]{2,1,0:T(1,128)}) custom-call(s32[8]{0:T(128)} %get-tuple-element.135.low_ref, s32[8]{0:T(128)} %get-tuple-element.136.high_ref, s32[1,3072]{1,0:T(1,128)} %get-tuple-element.147.begin_ref, s32[1,3072]{1,0:T(1,128)} %get-tuple-element.146.end_ref, ...), custom_call_target="tpu_custom_call" | custom-call | flops 2415919104 | bytes 4718592 | tf_op jit(solution)/shard_map/attention_forward/pallas_call | solution.py:99
  184.8 3.7 all-to-all-start.1
  188.5 0.7 fusion.34
  189.1 8.4 %all-to-all-done.1 = bf16[8,384,128]{2,1,0:T(8,128)(2,1)S(1)} async-done(((bf16[8,384,128]{2,1,0:T(8,128)(2,1)}), bf16[8,384,128]{2,1,0:T(8,128)(2,1)S(1)}, u32[]{:S(2)}, u32[]{:S(2)}) %all-to-all-start.1) | async-done | bytes 786464 | tf_op jit(solution)/shard_map/all_to_all | solution.py:1359
  197.5 4.1 fusion.44
  202.3 0.8 copy-done.19
  203.1 4.5 fusion.49
  207.6 10.0 %multiply_convert_fusion.1 = (bf16[384,2624]{1,0:T(8,128)(2,1)}, f32[384,2624]{1,0:T(8,128)S(1)}) fusion(f32[384,5248]{1,0:T(8,128)S(1)} %fusion.49), kind=kLoop, calls=%fused_computation.8 | loop fusion | flops 66502656 | bytes 14106624 | tf_op jit(solution)/shard_map/convert_element_type | solution.py:1422
  217.6 9.0 %add_convert_fusion = (bf16[384,2624]{1,0:T(8,128)(2,1)}, bf16[384,2624]{1,0:T(8,128)(2,1)}) fusion(f32[384,2624]{1,0:T(8,128)S(1)} %get-tuple-element.112, f32[384,5248]{1,0:T(8,128)S(1)} %fusion.49, bf16[384,1024]{1,0:T(8,128)(2,1)S(1)} %bitcast.134, bf16[2624,1024]{1,0:T(8,128)(2,1)} %bitcast.160), kind=kOutput, calls=%fused_computation.7 | convolution fusion | flops 2081734656 | bytes 22282240 | tf_op jit(solution)/shard_map/dot_general | solution.py:1436
  226.6 8.9 %fusion.6 = f32[384,1024]{1,0:T(8,128)S(1)} fusion(bf16[1024,5248]{1,0:T(8,128)(2,1)} %bitcast.158, bf16[384,2624]{1,0:T(8,128)(2,1)} %get-tuple-element.118.refs_5_, bf16[384,2624]{1,0:T(8,128)(2,1)} %get-tuple-element.117.refs_4_), kind=kOutput, calls=%fused_computation.22 | convolution fusion | flops 4135256064 | bytes 16351232 | tf_op jit(solution)/shard_map/dot_general | solution.py:1450
  235.5 6.9 %multiply_reduce_fusion = (f32[]{:T(128)}, f32[]{:T(128)}, f32[384]{0:T(512)S(1)}, f32[1024]{0:T(1024)S(1)}, f32[]{:T(128)}, /*index=5*/bf16[384,1024]{1,0:T(8,128)(2,1)}) fusion(f32[384,1024]{1,0:T(8,128)S(1)} %get-tuple-element.114, pred[384]{0:T(512)(128)(4,1)S(1)} %fusion.34, f32[384,1024]{1,0:T(8,128)S(1)} %fusion.6, f32[1024]{0:T(1024)S(1)} %bitcast.145, ...), kind=kOutput, calls=%fused_computation.52 | convolution fusion | flops 2070674048 | bytes 12907404 | tf_op jit(solution)/shard_map/dot_general | solution.py:1425
  242.9 1.2 fusion.21
  244.1 0.7 copy-done.9
  244.8 1.0 fusion.22
  245.8 1.0 copy.44
  246.9 7.6 %all-to-all-start.2 = ((bf16[8,384,128]{2,1,0:T(8,128)(2,1)}), bf16[8,384,128]{2,1,0:T(8,128)(2,1)}, u32[]{:S(2)}, u32[]{:S(2)}) async-start(bf16[8,384,128]{2,1,0:T(8,128)(2,1)} %bitcast.124), calls=%async_computation.2 | async-start | bytes 1572864 | tf_op jit(solution)/shard_map/all_to_all | solution.py:1359
  254.4 2.1 copy_bitcast_fusion.refs_0_
  256.6 21.0 %early_products.1 = (bf16[2,4,32,3200]{3,2,1,0:T(8,128)(2,1)}, bf16[2,4,32,3200]{3,2,1,0:T(8,128)(2,1)}, bf16[2,4,32,3200]{3,2,1,0:T(8,128)(2,1)}, bf16[2,4,32,3...) custom-call(bf16[384,1024]{1,0:T(8,128)(2,1)} %copy_bitcast_fusion.r, ...), custom_call_target="tpu_custom_call" | custom-call | tf_op jit(solution)/shard_map/early_products/pallas_call | solution.py:856
  277.6 1.4 collective-permute-start
  279.0 1.2 collective-permute-start.1
  280.6 38.0 %attention_backward.1 = bf16[3072,384]{1,0:T(8,128)(2,1)} custom-call(s32[8]{0:T(128)} %get-tuple-element.109.low_ref, s32[8]{0:T(128)} %get-tuple-element.110.high_ref, s32[1,3072]{1,0:T(1,128)} %get-tuple-element.147.begin_ref, s32[1,3072]{1,0:T(1,128)} %get-tuple-element.146.end_ref, bf16[3072,384]{1,0:T(8,128)(2,1)} %get-tuple-element.54.qkv_ref, ...), custom_call_target="tpu_custom_call" | custom-call | flops 6039797760 | bytes 11796480 | tf_op jit(solution)/shard_map/attention_backward/pallas_call | solution.py:219
  318.6 10.6 %collective-permute-done.2.refs_9_ = bf16[2,4,320,128]{3,2,1,0:T(8,128)(2,1)} collective-permute-done((bf16[2,4,320,128]{3,2,1,0:T(8,128)(2,1)}, bf16[2,4,320,128]{3,2,1,0:T(8,128)(2,1)}, u32[]{:S(2)}, u32[]{:S(2)}) %collective-permute-start.2) | collective-permute-done | bytes 655392 | tf_op jit(solution)/shard_map/ppermute | solution.py:1171
  329.2 1.5 collective-permute-done.3.refs_12_
  330.8 6.2 %all-to-all-start.3 = ((bf16[8,384,384]{2,1,0:T(8,128)(2,1)}), bf16[8,384,384]{2,1,0:T(8,128)(2,1)}, u32[]{:S(2)}, u32[]{:S(2)}) async-start(bf16[8,384,384]{2,1,0:T(8,128)(2,1)} %bitcast.127), calls=%async_computation.3 | async-start | bytes 4718592 | tf_op jit(solution)/shard_map/all_to_all | solution.py:1359
  337.7 2.1 select_maximum_fusion
  339.8 2.5 fusion.24
  342.4 1.4 collective-permute-start.4
  343.8 2.2 fusion.25
  346.0 1.2 collective-permute-start.5
  347.2 1.8 fusion.27
  349.2 1.1 fusion.26
  350.5 12.4 %all-to-all-done.3.heads_ref = bf16[8,384,384]{2,1,0:T(8,128)(2,1)} async-done(((bf16[8,384,384]{2,1,0:T(8,128)(2,1)}), bf16[8,384,384]{2,1,0:T(8,128)(2,1)}, u32[]{:S(2)}, u32[]{:S(2)}) %all-to-all-start.3) | async-done | bytes 2359328 | tf_op jit(solution)/shard_map/all_to_all | solution.py:1359
  362.9 8.9 %finish_rows.1 = (bf16[384,3072]{1,0:T(8,128)(2,1)}, f32[384,1024]{1,0:T(8,128)}) custom-call(bf16[8,384,384]{2,1,0:T(8,128)(2,1)} %all-to-all-done.3.heads_ref, f32[384,128]{1,0:T(8,128)} %get-tuple-element.148.refs_5_.cosine_ref, f32[384,128]{1,0:T(8,128)} %get-tuple-element.149.refs_6_.sine_ref, bf16[1024,3072]{1,0:T(8,128)(2,1)} %bitcast.121, ...), custom_call_target="tpu_custom_call" | custom-call | flops 2415919104 | bytes 11010048 | tf_op jit(solution)/shard_map/finish_rows/pallas_call | solution.py:285
  371.8 1.9 fusion.18
  373.7 0.8 fusion.17
  374.5 1.0 add_convert_fusion.3
  375.6 1.3 pad_maximum_fusion.1
  376.9 7.7 %all-to-all-start.4 = ((bf16[8,96,1024]{2,1,0:T(8,128)(2,1)}), bf16[8,96,1024]{2,1,0:T(8,128)(2,1)S(1)}, u32[]{:S(2)}, u32[]{:S(2)}) async-start(bf16[8,96,1024]{2,1,0:T(8,128)(2,1)} %pad_maximum_fusion.1), calls=%async_computation.4 | async-start | bytes 3145728 | tf_op jit(solution)/shard_map/all_to_all | solution.py:1359
  384.6 0.7 stack.41.refs_14_
  385.3 3.8 collective-permute-done.6.refs_10_
  389.6 88.6 %sum_weights.1 = (bf16[256,1024]{1,0:T(8,128)(2,1)}, bf16[256,5376]{1,0:T(8,128)(2,1)}, bf16[656,1024]{1,0:T(8,128)(2,1)}, bf16[256,3072]{1,0:T(8,128)(2,1)}, f32[2,8,1024]{2,1,0:T(8,128)}) custom-call(bf16[384,1024]{1,0:T(8,128)(2,1)} %fusion.16.refs_3_.refs_0_, bf16[384,3072]{1,0:T(8,128)(2,1)} %get-tuple-element.80.refs_1_, ...), custom_call_target="tpu_custom_call" | custom-call | tf_op jit(solution)/shard_map/sum_weights/pallas_call | solution.py:1141
  478.2 0.8 fusion.47
  479.1 3.6 convert_element_type.198
  482.7 1.1 convert_element_type.199
  484.9 1.8 convert_element_type.201
  486.7 1.2 sqrt_bitcast_fusion
  488.1 3.0 maximum_convert_fusion
  491.3 0.6 gather_fusion.3
  492.5 1.3 broadcast_select_fusion
  (96 shorter events, 8.7 us)
Async XLA Ops:
  0.6 1.6 copy-start
  0.7 2.2 copy-start.14
  4.9 5.4 %copy-start.17 = (s32[1,6]{1,0:T(1,128)S(1)}, s32[1,6]{1,0:T(1,128)}, u32[]{:S(2)}) copy-start(s32[1,6]{1,0:T(1,128)} %param.14) | copy-start | bytes 76
  4.9 6.8 %copy-start.20 = (bf16[256]{0:T(256)(128)(2,1)S(1)}, bf16[256]{0:T(256)(128)(2,1)}, u32[]{:S(2)}) copy-start(bf16[256]{0:T(256)(128)(2,1)} %param.19) | copy-start | bytes 1540
  4.9 6.8 %copy-start.21 = (bf16[256]{0:T(256)(128)(2,1)S(1)}, bf16[256]{0:T(256)(128)(2,1)}, u32[]{:S(2)}) copy-start(bf16[256]{0:T(256)(128)(2,1)} %param.16) | copy-start | bytes 1540
  5.0 53.5 %all-to-all-start = ((bf16[8,96,1024]{2,1,0:T(8,128)(2,1)}), bf16[8,96,1024]{2,1,0:T(8,128)(2,1)S(1)}, u32[]{:S(2)}, u32[]{:S(2)}) async-start(bf16[8,96,1024]{2,1,0:T(8,128)(2,1)} %pad_maximum_fusion), calls=%async_computation | async-start | bytes 3145728 | tf_op jit(solution)/shard_map/all_to_all | solution.py:1359
  184.8 12.7 %all-to-all-start.1 = ((bf16[8,384,128]{2,1,0:T(8,128)(2,1)}), bf16[8,384,128]{2,1,0:T(8,128)(2,1)S(1)}, u32[]{:S(2)}, u32[]{:S(2)}) async-start(bf16[8,384,128]{2,1,0:T(8,128)(2,1)} %bitcast.132), calls=%async_computation.1 | async-start | bytes 1572864 | tf_op jit(solution)/shard_map/all_to_all | solution.py:1359
  197.5 4.2 copy-start.4
  197.5 5.5 %copy-start.19 = (bf16[4,2,4,32,5248]{4,3,2,1,0:T(8,128)(2,1)S(1)}, bf16[4,2,4,32,5248]{4,3,2,1,0:T(8,128)(2,1)}, u32[]{:S(2)}) copy-start(bf16[4,2,4,32,5248]{4,3,2,1,0:T(8,128)(2,1)} %get-tuple-element.57) | copy-start | bytes 32243716
  202.3 5.3 %copy-start.6 = (bf16[384,1024]{1,0:T(8,128)(2,1)}, bf16[384,1024]{1,0:T(8,128)(2,1)S(1)}, u32[]{:S(2)}) copy-start(bf16[384,1024]{1,0:T(8,128)(2,1)S(1)} %multiply_convert_fusion.2.refs_1_) | copy-start | bytes 2359300
  226.6 8.9 %copy-start.3 = (bf16[384,2624]{1,0:T(8,128)(2,1)S(1)}, bf16[384,2624]{1,0:T(8,128)(2,1)}, u32[]{:S(2)}) copy-start(bf16[384,2624]{1,0:T(8,128)(2,1)} %get-tuple-element.111.refs_2_) | copy-start | bytes 6045700
  226.6 8.9 %copy-start.10 = (f32[384,1024]{1,0:T(8,128)S(1)}, f32[384,1024]{1,0:T(8,128)}, u32[]{:S(2)}) copy-start(f32[384,1024]{1,0:T(8,128)} %get-tuple-element.143) | copy-start | bytes 4718596
  242.9 1.9 copy-start.9
  244.1 1.7 copy-start.7
  246.9 30.7 %all-to-all-start.2 = ((bf16[8,384,128]{2,1,0:T(8,128)(2,1)}), bf16[8,384,128]{2,1,0:T(8,128)(2,1)}, u32[]{:S(2)}, u32[]{:S(2)}) async-start(bf16[8,384,128]{2,1,0:T(8,128)(2,1)} %bitcast.124), calls=%async_computation.2 | async-start | bytes 1572864 | tf_op jit(solution)/shard_map/all_to_all | solution.py:1359
  277.6 53.2 %collective-permute-start = (bf16[2,4,32,3200]{3,2,1,0:T(8,128)(2,1)}, bf16[2,4,32,3200]{3,2,1,0:T(8,128)(2,1)}, u32[]{:S(2)}, u32[]{:S(2)}) collective-permute-start(bf16[2,4,32,3200]{3,2,1,0:T(8,128)(2,1)} %get-tuple-element.71), channel_id=1, source_target_pairs={{0,8},{4,12},{8,0},{12,4},{16,24},{20,28},{24,16},{28,20},{1,9},{5... | collective-permute-start | bytes 4915208 | tf_op jit(solution)/shard_map/ppermute | solution.py:1171
  279.0 51.8 %collective-permute-start.1 = (bf16[2,4,32,3200]{3,2,1,0:T(8,128)(2,1)}, bf16[2,4,32,3200]{3,2,1,0:T(8,128)(2,1)}, u32[]{:S(2)}, u32[]{:S(2)}) collective-permute-start(bf16[2,4,32,3200]{3,2,1,0:T(8,128)(2,1)} %get-tuple-element.73), channel_id=1, source_target_pairs={{0,16},{4,20},{8,24},{12,28},{16,0},{20,4},{24,8},{28,12},{1,17},{... | collective-permute-start | bytes 4915208 | tf_op jit(solution)/shard_map/ppermute | solution.py:1171
  280.2 50.5 %collective-permute-start.3 = (bf16[2,4,336,128]{3,2,1,0:T(8,128)(2,1)}, bf16[2,4,336,128]{3,2,1,0:T(8,128)(2,1)}, u32[]{:S(2)}, u32[]{:S(2)}) collective-permute-start(bf16[2,4,336,128]{3,2,1,0:T(8,128)(2,1)} %get-tuple-element.77), channel_id=1, source_target_pairs={{0,16},{4,20},{8,24},{12,28},{16,0},{20,4},{24,8},{28,12},{1,17},{... | collective-permute-start | bytes 2064392 | tf_op jit(solution)/shard_map/ppermute | solution.py:1171
  280.5 48.8 %collective-permute-start.2 = (bf16[2,4,320,128]{3,2,1,0:T(8,128)(2,1)}, bf16[2,4,320,128]{3,2,1,0:T(8,128)(2,1)}, u32[]{:S(2)}, u32[]{:S(2)}) collective-permute-start(bf16[2,4,320,128]{3,2,1,0:T(8,128)(2,1)} %get-tuple-element.75), channel_id=1, source_target_pairs={{0,8},{4,12},{8,0},{12,4},{16,24},{20,28},{24,16},{28,20},{1,9},{5... | collective-permute-start | bytes 1966088 | tf_op jit(solution)/shard_map/ppermute | solution.py:1171
  330.8 6.9 %copy-start.18 = (s32[1,1,8]{2,1,0:T(1,128)S(1)}, s32[1,1,8]{2,1,0:T(1,128)}, u32[]{:S(2)}) copy-start(s32[1,1,8]{2,1,0:T(1,128)} %param.15) | copy-start | bytes 100
  330.8 32.1 %all-to-all-start.3 = ((bf16[8,384,384]{2,1,0:T(8,128)(2,1)}), bf16[8,384,384]{2,1,0:T(8,128)(2,1)}, u32[]{:S(2)}, u32[]{:S(2)}) async-start(bf16[8,384,384]{2,1,0:T(8,128)(2,1)} %bitcast.127), calls=%async_computation.3 | async-start | bytes 4718592 | tf_op jit(solution)/shard_map/all_to_all | solution.py:1359
  337.7 6.0 %copy-start.5 = (bf16[2,4,32,3200]{3,2,1,0:T(8,128)(2,1)S(1)}, bf16[2,4,32,3200]{3,2,1,0:T(8,128)(2,1)}, u32[]{:S(2)}) copy-start(bf16[2,4,32,3200]{3,2,1,0:T(8,128)(2,1)} %get-tuple-element.83.refs_5_) | copy-start | bytes 4915204
  339.8 7.3 %copy-start.12 = (bf16[2,4,320,128]{3,2,1,0:T(8,128)(2,1)S(1)}, bf16[2,4,320,128]{3,2,1,0:T(8,128)(2,1)}, u32[]{:S(2)}) copy-start(bf16[2,4,320,128]{3,2,1,0:T(8,128)(2,1)} %get-tuple-element.85.refs_8_) | copy-start | bytes 1966084
  342.4 6.8 %copy-start.11 = (bf16[2,4,336,128]{3,2,1,0:T(8,128)(2,1)S(1)}, bf16[2,4,336,128]{3,2,1,0:T(8,128)(2,1)}, u32[]{:S(2)}) copy-start(bf16[2,4,336,128]{3,2,1,0:T(8,128)(2,1)} %get-tuple-element.87.refs_11_) | copy-start | bytes 2064388
  342.4 47.2 %collective-permute-start.4 = (bf16[4,32,3200]{2,1,0:T(8,128)(2,1)}, bf16[4,32,3200]{2,1,0:T(8,128)(2,1)}, u32[]{:S(2)}, u32[]{:S(2)}) collective-permute-start(bf16[4,32,3200]{2,1,0:T(8,128)(2,1)} %fusion.24), channel_id=1, source_target_pairs={{0,16},{4,20},{8,24},{12,28},{16,0},{20,4},{24,8},{28,12},{1,17},{... | collective-permute-start | bytes 2457608 | tf_op jit(solution)/shard_map/ppermute | solution.py:1171
  346.0 43.6 %collective-permute-start.5 = (bf16[4,32,3200]{2,1,0:T(8,128)(2,1)}, bf16[4,32,3200]{2,1,0:T(8,128)(2,1)}, u32[]{:S(2)}, u32[]{:S(2)}) collective-permute-start(bf16[4,32,3200]{2,1,0:T(8,128)(2,1)} %fusion.25), channel_id=1, source_target_pairs={{0,8},{4,12},{8,0},{12,4},{16,24},{20,28},{24,16},{28,20},{1,9},{5... | collective-permute-start | bytes 2457608 | tf_op jit(solution)/shard_map/ppermute | solution.py:1171
  349.0 40.2 %collective-permute-start.6 = (bf16[4,320,128]{2,1,0:T(8,128)(2,1)}, bf16[4,320,128]{2,1,0:T(8,128)(2,1)}, u32[]{:S(2)}, u32[]{:S(2)}) collective-permute-start(bf16[4,320,128]{2,1,0:T(8,128)(2,1)} %fusion.27), channel_id=1, source_target_pairs={{0,16},{4,20},{8,24},{12,28},{16,0},{20,4},{24,8},{28,12},{1,17},{... | collective-permute-start | bytes 983048 | tf_op jit(solution)/shard_map/ppermute | solution.py:1171
  350.3 39.3 %collective-permute-start.7 = (bf16[4,336,128]{2,1,0:T(8,128)(2,1)S(1)}, bf16[4,336,128]{2,1,0:T(8,128)(2,1)}, u32[]{:S(2)}, u32[]{:S(2)}) collective-permute-start(bf16[4,336,128]{2,1,0:T(8,128)(2,1)S(1)} %fusion.26), channel_id=1, source_target_pairs={{0,8},{4,12},{8,0},{12,4},{16,24},{20,28},{24,16},{28,20},{1,9},{5... | collective-permute-start | bytes 1032200 | tf_op jit(solution)/shard_map/ppermute | solution.py:1171
  371.8 1.9 copy-start.2
  374.5 1.1 copy-start.15
  376.9 114.2 %all-to-all-start.4 = ((bf16[8,96,1024]{2,1,0:T(8,128)(2,1)}), bf16[8,96,1024]{2,1,0:T(8,128)(2,1)S(1)}, u32[]{:S(2)}, u32[]{:S(2)}) async-start(bf16[8,96,1024]{2,1,0:T(8,128)(2,1)} %pad_maximum_fusion.1), calls=%async_computation.4 | async-start | bytes 3145728 | tf_op jit(solution)/shard_map/all_to_all | solution.py:1359
  479.1 3.6 copy-start.16
  479.1 5.8 %copy-start.13 = (bf16[656,1024]{1,0:T(8,128)(2,1)S(1)}, bf16[656,1024]{1,0:T(8,128)(2,1)}, u32[]{:S(2)}) copy-start(bf16[656,1024]{1,0:T(8,128)(2,1)} %get-tuple-element.93) | copy-start | bytes 4030468
  483.7 4.2 copy-start.8
  491.9 2.0 copy-start.1

commit v9 on v8

--- a/solution.py
+++ b/solution.py
@@ -1298,7 +1298,7 @@
         over_pack = sum_over(small, ("ctx",))
         return totals + [jnp.stack([over_pack, sum_over(over_pack, ("fsdp",))])]
     total_attn, total_in, total_out, total_qkv, small_sums = sum_weights(
-        *early, [("rows", act_attn, grad_projected, 3)], small
+        *early, [("rows", act_attn, grad_projected, 4)], small
     )
     padded = total_in.shape[1] // 2
     total_in = jnp.concatenate(

time: 501 us -> 500 us (level)
  Pallas kernels: 321 us -> 312 us
  waiting for transfers between devices: 37.3 us -> 44.8 us
    ppermute x8, waiting for transfers between devices: 16.5 us -> 24 us  [swap(): return lax.ppermute(value, axis, pairs)]
    pallas_call x1, Pallas kernels: 38 us -> 30.5 us  [attention_backward(): pl.pallas_call(functools.partial(backward_kernel, head_count, block_q, bl...]
    pallas_call x1, Pallas kernels: 27.9 us -> 21.6 us  [attention_forward(): pl.pallas_call(functools.partial(forward_kernel, head_count, block_q, blo...]
    pallas_call x1, Pallas kernels: 88.6 us -> 93.7 us  [sum_weights(): pl.pallas_call(functools.partial(sum_kernel, early, late, plan_lead(plan)...]
  transfers between devices with their start and end apart: 13 -> 13, of which waited for: 6 -> 6; matrix products, arithmetic and copies ran while one was open for 8% -> 8% of each run, Pallas kernels for 40% -> 39%
where the time goes in v9:
time: 500 us; the launch traced here: 493 us
  Pallas kernels  312 us (62%)
  other arithmetic  52.3 us (10%)
  waiting for transfers between devices  44.8 us (9%)
  starting transfers between devices  36.5 us (7%)
  matrix products  34.4 us (7%)
  local copies, waits for them, and re-layouts  11 us (2%)
    pallas_call x2, Pallas kernels, gather_weights(): pl.pallas_call(functools.partial(gather_kernel, shapes, projection is not...  136 us
    pallas_call x1, Pallas kernels, sum_weights(): pl.pallas_call(functools.partial(sum_kernel, early, late, plan_lead(plan)...  93.7 us
    pallas_call x1, Pallas kernels, attention_backward(): pl.pallas_call(functools.partial(backward_kernel, head_count, block_q, bl...  30.5 us
    all_to_all x5, starting transfers between devices, exchange(): lax.all_to_all(blocks, 'ctx', split_axis=0, concat_axis=0, tiled=True)  30.5 us
    ppermute x8, waiting for transfers between devices, swap(): return lax.ppermute(value, axis, pairs)  24 us
    pallas_call x1, Pallas kernels, attention_forward(): pl.pallas_call(functools.partial(forward_kernel, head_count, block_q, blo...  21.6 us
    pallas_call x1, Pallas kernels, early_sums(): pl.pallas_call(functools.partial(product_kernel, plan, plan_lead(plan)),...  21 us
    all_to_all x5, waiting for transfers between devices, exchange(): lax.all_to_all(blocks, 'ctx', split_axis=0, concat_axis=0, tiled=True)  20.8 us
  transfers between devices with their start and end apart: 13, of which 6 were waited for; matrix products, arithmetic and copies ran while one was open for 8% of the time, Pallas kernels for 39%

profile of v9, /device:TPU:1, one launch (start us, length us, event | category | flops | bytes accessed | tf_op | source)
XLA Modules:
  0.0 493.0 jit_solution(8882619343987826932)
XLA Ops:
  0.7 0.9 select_reduce_fusion.6
  1.6 0.7 compare_and_fusion
  3.7 1.3 pad_maximum_fusion
  5.0 5.3 %all-to-all-start = ((bf16[8,96,1024]{2,1,0:T(8,128)(2,1)}), bf16[8,96,1024]{2,1,0:T(8,128)(2,1)S(1)}, u32[]{:S(2)}, u32[]{:S(2)}) async-start(bf16[8,96,1024]{2,1,0:T(8,128)(2,1)} %pad_maximum_fusion), calls=%async_computation | async-start | bytes 3145728 | tf_op jit(solution)/shard_map/all_to_all | solution.py:1359
  11.1 0.6 fusion.48
  12.0 0.6 fusion.33.refs_0_
  12.6 0.8 multiply_sine_fusion
  13.4 0.7 add_compare_fusion.1
  14.0 39.7 %gather_weights.1 = (bf16[4,16,256]{2,1,0:T(8,128)(2,1)}, bf16[4,2,4,32,3072]{4,3,2,1,0:T(8,128)(2,1)}) custom-call(bf16[16,256]{1,0:T(8,128)(2,1)} %fusion.33.refs_0_, bf16[2,4,32,3072]{3,2,1,0:T(8,128)(2,1)} %bitcast.130), custom_call_target="tpu_custom_call" | custom-call | tf_op jit(solution)/shard_map/gather_weights/pallas_call | solution.py:604
  53.8 0.8 fusion.32
  54.6 1.1 pad_maximum_fusion.2
  56.3 0.8 slice_convert_fusion
  57.1 1.3 compare_select_fusion.1
  59.3 1.2 fusion.16.refs_3_.refs_0_
  60.5 96.4 %gather_and_project.1 = (bf16[4,2,4,32,1024]{4,3,2,1,0:T(8,128)(2,1)}, bf16[4,2,4,32,5248]{4,3,2,1,0:T(8,128)(2,1)}, bf16[4,656,1024]{2,1,0:T(8,128)(2,1)}, bf16[3072,384]{1,0:T(8,128)(2,1)}) custom-call(bf16[2,4,32,1024]{3,2,1,0:T(8,128)(2,1)} %bitcast.137, bf16[2,4,32,5248]{3,2,1,0:T(8,128)(2,1)} %bitcast.126, bf16[656,1024]{1,0:T(8,128)(2,1)} %refs_2_.1, ...), custom_call_target="tpu_custom_call" | custom-call | tf_op jit(solution)/shard_map/gather_and_project/pallas_call | solution.py:604
  156.9 21.6 %attention_forward.1 = (f32[3072,128]{1,0:T(8,128)}, bf16[3072,128]{1,0:T(8,128)(2,1)}, f32[8,1,768]{2,1,0:T(1,128)}) custom-call(s32[8]{0:T(128)} %get-tuple-element.135.low_ref, s32[8]{0:T(128)} %get-tuple-element.136.high_ref, s32[1,3072]{1,0:T(1,128)} %get-tuple-element.147.begin_ref, s32[1,3072]{1,0:T(1,128)} %get-tuple-element.146.end_ref, ...), custom_call_target="tpu_custom_call" | custom-call | flops 2415919104 | bytes 4718592 | tf_op jit(solution)/shard_map/attention_forward/pallas_call | solution.py:99
  178.4 3.7 all-to-all-start.1
  182.1 0.7 fusion.34
  182.8 8.4 %all-to-all-done.1 = bf16[8,384,128]{2,1,0:T(8,128)(2,1)S(1)} async-done(((bf16[8,384,128]{2,1,0:T(8,128)(2,1)}), bf16[8,384,128]{2,1,0:T(8,128)(2,1)S(1)}, u32[]{:S(2)}, u32[]{:S(2)}) %all-to-all-start.1) | async-done | bytes 786464 | tf_op jit(solution)/shard_map/all_to_all | solution.py:1359
  191.2 4.1 fusion.44
  195.9 0.8 copy-done.19
  196.7 4.5 fusion.49
  201.2 10.0 %multiply_convert_fusion.1 = (bf16[384,2624]{1,0:T(8,128)(2,1)}, f32[384,2624]{1,0:T(8,128)S(1)}) fusion(f32[384,5248]{1,0:T(8,128)S(1)} %fusion.49), kind=kLoop, calls=%fused_computation.8 | loop fusion | flops 66502656 | bytes 14106624 | tf_op jit(solution)/shard_map/convert_element_type | solution.py:1422
  211.2 9.0 %add_convert_fusion = (bf16[384,2624]{1,0:T(8,128)(2,1)}, bf16[384,2624]{1,0:T(8,128)(2,1)}) fusion(f32[384,2624]{1,0:T(8,128)S(1)} %get-tuple-element.112, f32[384,5248]{1,0:T(8,128)S(1)} %fusion.49, bf16[384,1024]{1,0:T(8,128)(2,1)S(1)} %bitcast.134, bf16[2624,1024]{1,0:T(8,128)(2,1)} %bitcast.160), kind=kOutput, calls=%fused_computation.7 | convolution fusion | flops 2081734656 | bytes 22282240 | tf_op jit(solution)/shard_map/dot_general | solution.py:1436
  220.2 8.9 %fusion.6 = f32[384,1024]{1,0:T(8,128)S(1)} fusion(bf16[1024,5248]{1,0:T(8,128)(2,1)} %bitcast.158, bf16[384,2624]{1,0:T(8,128)(2,1)} %get-tuple-element.118.refs_5_, bf16[384,2624]{1,0:T(8,128)(2,1)} %get-tuple-element.117.refs_4_), kind=kOutput, calls=%fused_computation.22 | convolution fusion | flops 4135256064 | bytes 16351232 | tf_op jit(solution)/shard_map/dot_general | solution.py:1450
  229.1 6.9 %multiply_reduce_fusion = (f32[]{:T(128)}, f32[]{:T(128)}, f32[384]{0:T(512)S(1)}, f32[1024]{0:T(1024)S(1)}, f32[]{:T(128)}, /*index=5*/bf16[384,1024]{1,0:T(8,128)(2,1)}) fusion(f32[384,1024]{1,0:T(8,128)S(1)} %get-tuple-element.114, pred[384]{0:T(512)(128)(4,1)S(1)} %fusion.34, f32[384,1024]{1,0:T(8,128)S(1)} %fusion.6, f32[1024]{0:T(1024)S(1)} %bitcast.145, ...), kind=kOutput, calls=%fused_computation.52 | convolution fusion | flops 2070674048 | bytes 12907404 | tf_op jit(solution)/shard_map/dot_general | solution.py:1425
  236.6 1.2 fusion.21
  237.8 0.7 copy-done.9
  238.4 1.0 fusion.22
  239.5 1.0 copy.44
  240.5 7.6 %all-to-all-start.2 = ((bf16[8,384,128]{2,1,0:T(8,128)(2,1)}), bf16[8,384,128]{2,1,0:T(8,128)(2,1)}, u32[]{:S(2)}, u32[]{:S(2)}) async-start(bf16[8,384,128]{2,1,0:T(8,128)(2,1)} %bitcast.124), calls=%async_computation.2 | async-start | bytes 1572864 | tf_op jit(solution)/shard_map/all_to_all | solution.py:1359
  248.1 2.1 copy_bitcast_fusion.refs_0_
  250.2 21.0 %early_products.1 = (bf16[2,4,32,3200]{3,2,1,0:T(8,128)(2,1)}, bf16[2,4,32,3200]{3,2,1,0:T(8,128)(2,1)}, bf16[2,4,32,3200]{3,2,1,0:T(8,128)(2,1)}, bf16[2,4,32,3...) custom-call(bf16[384,1024]{1,0:T(8,128)(2,1)} %copy_bitcast_fusion.r, ...), custom_call_target="tpu_custom_call" | custom-call | tf_op jit(solution)/shard_map/early_products/pallas_call | solution.py:856
  271.2 1.4 collective-permute-start
  272.7 1.2 collective-permute-start.1
  274.2 30.5 %attention_backward.1 = bf16[3072,384]{1,0:T(8,128)(2,1)} custom-call(s32[8]{0:T(128)} %get-tuple-element.109.low_ref, s32[8]{0:T(128)} %get-tuple-element.110.high_ref, s32[1,3072]{1,0:T(1,128)} %get-tuple-element.147.begin_ref, s32[1,3072]{1,0:T(1,128)} %get-tuple-element.146.end_ref, bf16[3072,384]{1,0:T(8,128)(2,1)} %get-tuple-element.54.qkv_ref, ...), custom_call_target="tpu_custom_call" | custom-call | flops 6039797760 | bytes 11796480 | tf_op jit(solution)/shard_map/attention_backward/pallas_call | solution.py:219
  304.8 18.1 %collective-permute-done.2.refs_9_ = bf16[2,4,320,128]{3,2,1,0:T(8,128)(2,1)} collective-permute-done((bf16[2,4,320,128]{3,2,1,0:T(8,128)(2,1)}, bf16[2,4,320,128]{3,2,1,0:T(8,128)(2,1)}, u32[]{:S(2)}, u32[]{:S(2)}) %collective-permute-start.2) | collective-permute-done | bytes 655392 | tf_op jit(solution)/shard_map/ppermute | solution.py:1171
  322.9 1.5 collective-permute-done.3.refs_12_
  324.4 6.2 %all-to-all-start.3 = ((bf16[8,384,384]{2,1,0:T(8,128)(2,1)}), bf16[8,384,384]{2,1,0:T(8,128)(2,1)}, u32[]{:S(2)}, u32[]{:S(2)}) async-start(bf16[8,384,384]{2,1,0:T(8,128)(2,1)} %bitcast.127), calls=%async_computation.3 | async-start | bytes 4718592 | tf_op jit(solution)/shard_map/all_to_all | solution.py:1359
  331.4 2.1 select_maximum_fusion
  333.5 2.5 fusion.24
  336.0 1.4 collective-permute-start.4
  337.4 2.2 fusion.25
  339.6 1.2 collective-permute-start.5
  340.8 1.8 fusion.27
  342.9 1.1 fusion.26
  344.2 12.4 %all-to-all-done.3.heads_ref = bf16[8,384,384]{2,1,0:T(8,128)(2,1)} async-done(((bf16[8,384,384]{2,1,0:T(8,128)(2,1)}), bf16[8,384,384]{2,1,0:T(8,128)(2,1)}, u32[]{:S(2)}, u32[]{:S(2)}) %all-to-all-start.3) | async-done | bytes 2359328 | tf_op jit(solution)/shard_map/all_to_all | solution.py:1359
  356.6 8.9 %finish_rows.1 = (bf16[384,3072]{1,0:T(8,128)(2,1)}, f32[384,1024]{1,0:T(8,128)}) custom-call(bf16[8,384,384]{2,1,0:T(8,128)(2,1)} %all-to-all-done.3.heads_ref, f32[384,128]{1,0:T(8,128)} %get-tuple-element.148.refs_5_.cosine_ref, f32[384,128]{1,0:T(8,128)} %get-tuple-element.149.refs_6_.sine_ref, bf16[1024,3072]{1,0:T(8,128)(2,1)} %bitcast.121, ...), custom_call_target="tpu_custom_call" | custom-call | flops 2415919104 | bytes 11010048 | tf_op jit(solution)/shard_map/finish_rows/pallas_call | solution.py:285
  365.4 1.9 fusion.18
  367.4 0.8 fusion.17
  368.2 1.0 add_convert_fusion.3
  369.3 1.3 pad_maximum_fusion.1
  370.6 7.7 %all-to-all-start.4 = ((bf16[8,96,1024]{2,1,0:T(8,128)(2,1)}), bf16[8,96,1024]{2,1,0:T(8,128)(2,1)S(1)}, u32[]{:S(2)}, u32[]{:S(2)}) async-start(bf16[8,96,1024]{2,1,0:T(8,128)(2,1)} %pad_maximum_fusion.1), calls=%async_computation.4 | async-start | bytes 3145728 | tf_op jit(solution)/shard_map/all_to_all | solution.py:1359
  378.3 0.7 stack.41.refs_14_
  378.9 3.8 collective-permute-done.6.refs_10_
  383.3 93.7 %sum_weights.1 = (bf16[256,1024]{1,0:T(8,128)(2,1)}, bf16[256,5376]{1,0:T(8,128)(2,1)}, bf16[656,1024]{1,0:T(8,128)(2,1)}, bf16[256,3072]{1,0:T(8,128)(2,1)}, f32[2,8,1024]{2,1,0:T(8,128)}) custom-call(bf16[384,1024]{1,0:T(8,128)(2,1)} %fusion.16.refs_3_.refs_0_, bf16[384,3072]{1,0:T(8,128)(2,1)} %get-tuple-element.80.refs_1_, ...), custom_call_target="tpu_custom_call" | custom-call | tf_op jit(solution)/shard_map/sum_weights/pallas_call | solution.py:1141
  477.0 0.8 fusion.47
  477.8 3.6 convert_element_type.198
  481.4 1.1 convert_element_type.199
  483.6 1.8 convert_element_type.201
  485.5 1.2 sqrt_bitcast_fusion
  486.9 3.0 maximum_convert_fusion
  490.0 0.6 gather_fusion.3
  491.3 1.3 broadcast_select_fusion
  (96 shorter events, 8.7 us)
Async XLA Ops:
  0.6 1.6 copy-start
  0.7 2.2 copy-start.14
  4.9 5.4 %copy-start.17 = (s32[1,6]{1,0:T(1,128)S(1)}, s32[1,6]{1,0:T(1,128)}, u32[]{:S(2)}) copy-start(s32[1,6]{1,0:T(1,128)} %param.14) | copy-start | bytes 76
  4.9 6.8 %copy-start.20 = (bf16[256]{0:T(256)(128)(2,1)S(1)}, bf16[256]{0:T(256)(128)(2,1)}, u32[]{:S(2)}) copy-start(bf16[256]{0:T(256)(128)(2,1)} %param.19) | copy-start | bytes 1540
  4.9 6.8 %copy-start.21 = (bf16[256]{0:T(256)(128)(2,1)S(1)}, bf16[256]{0:T(256)(128)(2,1)}, u32[]{:S(2)}) copy-start(bf16[256]{0:T(256)(128)(2,1)} %param.16) | copy-start | bytes 1540
  5.0 53.5 %all-to-all-start = ((bf16[8,96,1024]{2,1,0:T(8,128)(2,1)}), bf16[8,96,1024]{2,1,0:T(8,128)(2,1)S(1)}, u32[]{:S(2)}, u32[]{:S(2)}) async-start(bf16[8,96,1024]{2,1,0:T(8,128)(2,1)} %pad_maximum_fusion), calls=%async_computation | async-start | bytes 3145728 | tf_op jit(solution)/shard_map/all_to_all | solution.py:1359
  178.4 12.7 %all-to-all-start.1 = ((bf16[8,384,128]{2,1,0:T(8,128)(2,1)}), bf16[8,384,128]{2,1,0:T(8,128)(2,1)S(1)}, u32[]{:S(2)}, u32[]{:S(2)}) async-start(bf16[8,384,128]{2,1,0:T(8,128)(2,1)} %bitcast.132), calls=%async_computation.1 | async-start | bytes 1572864 | tf_op jit(solution)/shard_map/all_to_all | solution.py:1359
  191.2 4.2 copy-start.4
  191.2 5.5 %copy-start.19 = (bf16[4,2,4,32,5248]{4,3,2,1,0:T(8,128)(2,1)S(1)}, bf16[4,2,4,32,5248]{4,3,2,1,0:T(8,128)(2,1)}, u32[]{:S(2)}) copy-start(bf16[4,2,4,32,5248]{4,3,2,1,0:T(8,128)(2,1)} %get-tuple-element.57) | copy-start | bytes 32243716
  195.9 5.3 %copy-start.6 = (bf16[384,1024]{1,0:T(8,128)(2,1)}, bf16[384,1024]{1,0:T(8,128)(2,1)S(1)}, u32[]{:S(2)}) copy-start(bf16[384,1024]{1,0:T(8,128)(2,1)S(1)} %multiply_convert_fusion.2.refs_1_) | copy-start | bytes 2359300
  220.2 8.9 %copy-start.3 = (bf16[384,2624]{1,0:T(8,128)(2,1)S(1)}, bf16[384,2624]{1,0:T(8,128)(2,1)}, u32[]{:S(2)}) copy-start(bf16[384,2624]{1,0:T(8,128)(2,1)} %get-tuple-element.111.refs_2_) | copy-start | bytes 6045700
  220.2 8.9 %copy-start.10 = (f32[384,1024]{1,0:T(8,128)S(1)}, f32[384,1024]{1,0:T(8,128)}, u32[]{:S(2)}) copy-start(f32[384,1024]{1,0:T(8,128)} %get-tuple-element.143) | copy-start | bytes 4718596
  236.6 1.9 copy-start.9
  237.8 1.7 copy-start.7
  240.5 30.7 %all-to-all-start.2 = ((bf16[8,384,128]{2,1,0:T(8,128)(2,1)}), bf16[8,384,128]{2,1,0:T(8,128)(2,1)}, u32[]{:S(2)}, u32[]{:S(2)}) async-start(bf16[8,384,128]{2,1,0:T(8,128)(2,1)} %bitcast.124), calls=%async_computation.2 | async-start | bytes 1572864 | tf_op jit(solution)/shard_map/all_to_all | solution.py:1359
  271.2 53.2 %collective-permute-start = (bf16[2,4,32,3200]{3,2,1,0:T(8,128)(2,1)}, bf16[2,4,32,3200]{3,2,1,0:T(8,128)(2,1)}, u32[]{:S(2)}, u32[]{:S(2)}) collective-permute-start(bf16[2,4,32,3200]{3,2,1,0:T(8,128)(2,1)} %get-tuple-element.71), channel_id=1, source_target_pairs={{0,8},{4,12},{8,0},{12,4},{16,24},{20,28},{24,16},{28,20},{1,9},{5... | collective-permute-start | bytes 4915208 | tf_op jit(solution)/shard_map/ppermute | solution.py:1171
  272.7 51.8 %collective-permute-start.1 = (bf16[2,4,32,3200]{3,2,1,0:T(8,128)(2,1)}, bf16[2,4,32,3200]{3,2,1,0:T(8,128)(2,1)}, u32[]{:S(2)}, u32[]{:S(2)}) collective-permute-start(bf16[2,4,32,3200]{3,2,1,0:T(8,128)(2,1)} %get-tuple-element.73), channel_id=1, source_target_pairs={{0,16},{4,20},{8,24},{12,28},{16,0},{20,4},{24,8},{28,12},{1,17},{... | collective-permute-start | bytes 4915208 | tf_op jit(solution)/shard_map/ppermute | solution.py:1171
  273.9 50.5 %collective-permute-start.3 = (bf16[2,4,336,128]{3,2,1,0:T(8,128)(2,1)}, bf16[2,4,336,128]{3,2,1,0:T(8,128)(2,1)}, u32[]{:S(2)}, u32[]{:S(2)}) collective-permute-start(bf16[2,4,336,128]{3,2,1,0:T(8,128)(2,1)} %get-tuple-element.77), channel_id=1, source_target_pairs={{0,16},{4,20},{8,24},{12,28},{16,0},{20,4},{24,8},{28,12},{1,17},{... | collective-permute-start | bytes 2064392 | tf_op jit(solution)/shard_map/ppermute | solution.py:1171
  274.1 48.8 %collective-permute-start.2 = (bf16[2,4,320,128]{3,2,1,0:T(8,128)(2,1)}, bf16[2,4,320,128]{3,2,1,0:T(8,128)(2,1)}, u32[]{:S(2)}, u32[]{:S(2)}) collective-permute-start(bf16[2,4,320,128]{3,2,1,0:T(8,128)(2,1)} %get-tuple-element.75), channel_id=1, source_target_pairs={{0,8},{4,12},{8,0},{12,4},{16,24},{20,28},{24,16},{28,20},{1,9},{5... | collective-permute-start | bytes 1966088 | tf_op jit(solution)/shard_map/ppermute | solution.py:1171
  324.4 6.9 %copy-start.18 = (s32[1,1,8]{2,1,0:T(1,128)S(1)}, s32[1,1,8]{2,1,0:T(1,128)}, u32[]{:S(2)}) copy-start(s32[1,1,8]{2,1,0:T(1,128)} %param.15) | copy-start | bytes 100
  324.4 32.1 %all-to-all-start.3 = ((bf16[8,384,384]{2,1,0:T(8,128)(2,1)}), bf16[8,384,384]{2,1,0:T(8,128)(2,1)}, u32[]{:S(2)}, u32[]{:S(2)}) async-start(bf16[8,384,384]{2,1,0:T(8,128)(2,1)} %bitcast.127), calls=%async_computation.3 | async-start | bytes 4718592 | tf_op jit(solution)/shard_map/all_to_all | solution.py:1359
  331.4 6.0 %copy-start.5 = (bf16[2,4,32,3200]{3,2,1,0:T(8,128)(2,1)S(1)}, bf16[2,4,32,3200]{3,2,1,0:T(8,128)(2,1)}, u32[]{:S(2)}) copy-start(bf16[2,4,32,3200]{3,2,1,0:T(8,128)(2,1)} %get-tuple-element.83.refs_5_) | copy-start | bytes 4915204
  333.5 7.3 %copy-start.12 = (bf16[2,4,320,128]{3,2,1,0:T(8,128)(2,1)S(1)}, bf16[2,4,320,128]{3,2,1,0:T(8,128)(2,1)}, u32[]{:S(2)}) copy-start(bf16[2,4,320,128]{3,2,1,0:T(8,128)(2,1)} %get-tuple-element.85.refs_8_) | copy-start | bytes 1966084
  336.0 6.8 %copy-start.11 = (bf16[2,4,336,128]{3,2,1,0:T(8,128)(2,1)S(1)}, bf16[2,4,336,128]{3,2,1,0:T(8,128)(2,1)}, u32[]{:S(2)}) copy-start(bf16[2,4,336,128]{3,2,1,0:T(8,128)(2,1)} %get-tuple-element.87.refs_11_) | copy-start | bytes 2064388
  336.0 47.2 %collective-permute-start.4 = (bf16[4,32,3200]{2,1,0:T(8,128)(2,1)}, bf16[4,32,3200]{2,1,0:T(8,128)(2,1)}, u32[]{:S(2)}, u32[]{:S(2)}) collective-permute-start(bf16[4,32,3200]{2,1,0:T(8,128)(2,1)} %fusion.24), channel_id=1, source_target_pairs={{0,16},{4,20},{8,24},{12,28},{16,0},{20,4},{24,8},{28,12},{1,17},{... | collective-permute-start | bytes 2457608 | tf_op jit(solution)/shard_map/ppermute | solution.py:1171
  339.6 43.6 %collective-permute-start.5 = (bf16[4,32,3200]{2,1,0:T(8,128)(2,1)}, bf16[4,32,3200]{2,1,0:T(8,128)(2,1)}, u32[]{:S(2)}, u32[]{:S(2)}) collective-permute-start(bf16[4,32,3200]{2,1,0:T(8,128)(2,1)} %fusion.25), channel_id=1, source_target_pairs={{0,8},{4,12},{8,0},{12,4},{16,24},{20,28},{24,16},{28,20},{1,9},{5... | collective-permute-start | bytes 2457608 | tf_op jit(solution)/shard_map/ppermute | solution.py:1171
  342.6 40.2 %collective-permute-start.6 = (bf16[4,320,128]{2,1,0:T(8,128)(2,1)}, bf16[4,320,128]{2,1,0:T(8,128)(2,1)}, u32[]{:S(2)}, u32[]{:S(2)}) collective-permute-start(bf16[4,320,128]{2,1,0:T(8,128)(2,1)} %fusion.27), channel_id=1, source_target_pairs={{0,16},{4,20},{8,24},{12,28},{16,0},{20,4},{24,8},{28,12},{1,17},{... | collective-permute-start | bytes 983048 | tf_op jit(solution)/shard_map/ppermute | solution.py:1171
  344.0 39.3 %collective-permute-start.7 = (bf16[4,336,128]{2,1,0:T(8,128)(2,1)S(1)}, bf16[4,336,128]{2,1,0:T(8,128)(2,1)}, u32[]{:S(2)}, u32[]{:S(2)}) collective-permute-start(bf16[4,336,128]{2,1,0:T(8,128)(2,1)S(1)} %fusion.26), channel_id=1, source_target_pairs={{0,8},{4,12},{8,0},{12,4},{16,24},{20,28},{24,16},{28,20},{1,9},{5... | collective-permute-start | bytes 1032200 | tf_op jit(solution)/shard_map/ppermute | solution.py:1171
  365.4 1.9 copy-start.2
  368.2 1.1 copy-start.15
  370.6 119.2 %all-to-all-start.4 = ((bf16[8,96,1024]{2,1,0:T(8,128)(2,1)}), bf16[8,96,1024]{2,1,0:T(8,128)(2,1)S(1)}, u32[]{:S(2)}, u32[]{:S(2)}) async-start(bf16[8,96,1024]{2,1,0:T(8,128)(2,1)} %pad_maximum_fusion.1), calls=%async_computation.4 | async-start | bytes 3145728 | tf_op jit(solution)/shard_map/all_to_all | solution.py:1359
  477.8 3.6 copy-start.16
  477.8 5.8 %copy-start.13 = (bf16[656,1024]{1,0:T(8,128)(2,1)S(1)}, bf16[656,1024]{1,0:T(8,128)(2,1)}, u32[]{:S(2)}) copy-start(bf16[656,1024]{1,0:T(8,128)(2,1)} %get-tuple-element.93) | copy-start | bytes 4030468
  482.5 4.2 copy-start.8
  490.6 2.0 copy-start.1
